TPU v7x, 32 devices: a whole 2x2x4 slice. The times are simulated.
32 devices in a mesh: sec: 2 (over core), section: 4 (over y, x), dp: 4 (over z).
Axes of the slice: x: 2, y: 2, z: 4, core: 2. Of those that a mesh axis runs over, the one named last changes fastest.
Arguments:
- enc_states: bfloat16 [4, 128, 4096], P('dp', None, ('sec', 'section')), may hold values from -6 to 6
- norm_gain: float32 [4096], replicated, may hold values from 0.5 to 9, as said below
- kv_weight: bfloat16 [2, 4096, 4096], P('sec', None, 'section'), may hold values from -0.09375 to 0.09375
- queries: bfloat16 [2, 4, 256, 2048], P('sec', 'dp', None, 'section'), may hold values from -6 to 6
- attn_cotangent: bfloat16 [2, 4, 256, 2048], P('sec', 'dp', None, 'section'), may hold values from -6 to 6
- target_lengths: int32 [4], P('dp'), may hold values from 64 to 256, as said below
Outputs:
- attended: bfloat16 [2, 4, 256, 2048], P('sec', 'dp', None, 'section')
- enc_grad: bfloat16 [4, 128, 4096], P('dp', None, ('sec', 'section'))
- gain_grad: float32 [4096], P(('sec', 'section', 'dp'))
- row_dot: float32 [4, 128], P('dp')
Inputs may be any that keep to these rules, and one draw needn't show every extreme that they name: `target_lengths`: some sequence has all 256 tokens live. `norm_gain`: positive gains.
All inputs are finite; a program needn't handle non-finite values.
Results may differ from a plain program's by a relative error of at most 0.012.
The roundings to bfloat16 on the way count: a program that leaves them out, or rounds other values in their place, can miss the bound.
Values may be sent and summed in bfloat16 or wider, within the bound.
No kernel may reach another device: no remote copies, remote signals or barrier semaphores. Data moves between devices by JAX's collectives and lax.ppermute only.
A program may use at most 64 MiB of HBM per device.

v0:
```python
import jax
import jax.numpy as jnp
from jax import lax
from jax.sharding import PartitionSpec as P

HS = 256


def per_device(enc_states, norm_gain, kv_weight, queries, attn_cotangent, target_lengths):
    full_rows = lax.all_gather(enc_states, ("sec", "section"), axis=2, tiled=True)[0]
    own_rows = enc_states[0].astype(jnp.float32)
    feat_count = own_rows.shape[1]
    model_width = full_rows.shape[1]
    enc_count = full_rows.shape[0]
    weight = kv_weight[0]
    query_flat = queries[0, 0]
    dec_count = query_flat.shape[0]
    heads_here = query_flat.shape[1] // HS
    score_scale = HS ** (-0.5)
    rows_float = full_rows.astype(jnp.float32)
    inv_rms = lax.rsqrt(jnp.mean(rows_float * rows_float, axis=-1) + 1e-06)
    memory = (rows_float * inv_rms[:, None] * norm_gain).astype(jnp.bfloat16)
    key_value = jnp.dot(memory, weight, preferred_element_type=jnp.float32)
    key_value = key_value.reshape(enc_count, heads_here, 2, HS)
    key_rows = key_value[:, :, 0].astype(jnp.bfloat16)
    value_rows = key_value[:, :, 1].astype(jnp.bfloat16)
    query_rows = query_flat.reshape(dec_count, heads_here, HS)
    cot_rows = attn_cotangent[0, 0].reshape(dec_count, heads_here, HS)
    scores = (
        jnp.einsum("thd,shd->hts", query_rows, key_rows, preferred_element_type=jnp.float32)
        * score_scale
    )
    exponent = jnp.exp(scores)
    attention = exponent / jnp.sum(exponent, axis=-1, keepdims=True)
    weights_b = attention.astype(jnp.bfloat16)
    attended = jnp.einsum("hts,shd->thd", weights_b, value_rows, preferred_element_type=jnp.float32)
    attended = attended.astype(jnp.bfloat16).reshape(dec_count, heads_here * HS)
    live_rows = jnp.arange(dec_count) < target_lengths[0]
    masked = jnp.where(live_rows[:, None, None], cot_rows, jnp.zeros_like(cot_rows))
    back_prod = jnp.einsum("thd,shd->hts", masked, value_rows, preferred_element_type=jnp.float32)
    score_grad = (
        attention
        * (back_prod - jnp.sum(attention * back_prod, axis=-1, keepdims=True))
        * score_scale
    )
    score_grad = score_grad.astype(jnp.bfloat16)
    key_grad = jnp.einsum(
        "hts,thd->shd", score_grad, query_rows, preferred_element_type=jnp.float32
    )
    value_grad = jnp.einsum("hts,thd->shd", weights_b, masked, preferred_element_type=jnp.float32)
    kv_grad = (
        jnp.stack([key_grad, value_grad], axis=2)
        .reshape(enc_count, 2 * heads_here * HS)
        .astype(jnp.bfloat16)
    )
    contract_last = (((1,), (1,)), ((), ()))
    grad_cols = lax.psum_scatter(
        lax.dot_general(weight, kv_grad, contract_last, preferred_element_type=jnp.float32),
        ("sec", "section"),
        scatter_dimension=0,
        tiled=True,
    )
    memory_grad = grad_cols.T
    offset_own = lax.axis_index(("sec", "section")) * feat_count
    gain_own = lax.dynamic_slice_in_dim(norm_gain, offset_own, feat_count, 0)
    normed_own = own_rows * inv_rms[:, None]
    gain_scaled = memory_grad * gain_own
    row_part = jnp.sum(gain_scaled * normed_own, axis=-1)
    row_dot = lax.psum(row_part, ("sec", "section"))
    enc_grad = (
        inv_rms[:, None] * (gain_scaled - normed_own * row_dot[:, None] / model_width)
    ).astype(jnp.bfloat16)
    gain_term = jnp.sum(memory_grad * normed_own, axis=0)
    gain_grad = lax.psum_scatter(gain_term, "dp", scatter_dimension=0, tiled=True)
    return (attended[None, None], enc_grad[None], gain_grad, row_dot[None])


def solution(mesh):
    placed = (
        P("dp", None, ("sec", "section")),
        P(),
        P("sec", None, "section"),
        P("sec", "dp", None, "section"),
        P("sec", "dp", None, "section"),
        P("dp"),
    )
    return jax.shard_map(
        per_device,
        mesh=mesh,
        in_specs=placed,
        out_specs=(
            P("sec", "dp", None, "section"),
            P("dp", None, ("sec", "section")),
            P(("sec", "section", "dp")),
            P("dp", None),
        ),
        check_vma=False,
    )
```

profile of v0, /device:TPU:0, one launch (start us, length us, event | category | flops | bytes accessed | tf_op | source)
XLA Modules:
  0.0 130.8 jit_solution(16637254228986146248)
XLA Ops:
  7.2 0.0 all-gather.2.cloned.1.call-start
  7.2 0.7 all-gather.2.cloned.1.call-update
  7.9 0.0 reduce-scatter.2.cloned.1.call-start
  7.9 0.0 copy-start.1
  8.0 0.0 copy-start.2
  8.0 11.3 %copy.48 = bf16[1024,4096]{1,0:T(8,128)(2,1)} copy(bf16[1024,4096]{0,1:T(8,128)(2,1)} %bitcast.67) | data formatting | bytes 16777216 | tf_op jit(solution)/shard_map/dot_general | solution.py:23
  19.3 0.0 copy-done.1
  19.3 0.0 copy-start.4
  19.3 0.1 reshape_squeeze.6
  19.4 0.0 copy-done.2
  19.4 0.1 copy.49
  20.2 16.0 %all-gather.2.cloned.1.call-done = bf16[1,128,4096]{2,1,0:T(8,128)(2,1)} async-done(((bf16[1,128,512]{2,1,0:T(8,128)(2,1)}), bf16[1,128,4096]{2,1,0:T(8,128)(2,1)}) %all-gather.2.cloned.1.call-update) | async-done | bytes 1048592 | tf_op jit(solution)/shard_map/all_gather | solution.py:10
  36.2 1.5 %fusion.6 = f32[128]{0:T(128)S(1)} fusion(bf16[1,128,4096]{2,1,0:T(8,128)(2,1)} %all-gather.2.cloned.1.call-done), kind=kLoop, calls=%fused_computation.6 | loop fusion | flops 1572736 | bytes 1049088 | tf_op jit(solution)/shard_map/reduce_sum | solution.py:21
  37.7 0.0 copy-done.4
  37.7 6.6 %convolution_convert_fusion.1 = bf16[128,2,2,256]{3,0,2,1:T(8,128)(2,1)S(1)} fusion(bf16[2,2,256,4096]{3,2,1,0:T(8,128)(2,1)} %bitcast.68, bf16[1,128,4096]{2,1,0:T(8,128)(2,1)} %all-gather.2.cloned.1.call-done, f32[4096]{0:T(1024)S(1)} %copy-done.4, f32[128]{0:T(128)S(1)} %add_rsqrt_fusion), kind=kOutput, calls=%fused_computation.10 | convolution fusion | flops 1075970048 | bytes 9716224 | tf_op jit(solution)/shard_map/dot_general | solution.py:23
  44.4 0.3 fusion.42
  44.6 0.2 fusion.36
  44.8 0.2 fusion.17
  45.0 0.2 fusion.18
  45.3 0.2 copy.40
  45.5 7.7 %fusion.3 = f32[4096,128]{0,1:T(8,128)} fusion(bf16[128,1024]{0,1:T(8,128)(2,1)S(1)} %bitcast.72, bf16[1,4096,1024]{2,1,0:T(8,128)(2,1)} %param.8), kind=kOutput, calls=%fused_computation.3 | convolution fusion | flops 1073741824 | bytes 10747904 | tf_op jit(solution)/shard_map/dot_general | solution.py:58
  53.1 0.0 copy-start.5
  53.2 0.0 copy-start
  53.2 0.0 reduce-scatter.2.cloned.1.call-update
  53.2 0.1 dynamic_slice.3
  53.3 0.5 copy-done.5
  53.8 0.6 dynamic-slice
  55.0 0.3 convolution_convert_fusion
  55.3 0.8 copy.41
  56.2 38.4 %reduce-scatter.2.cloned.1.call-done = f32[512,128]{0,1:T(8,128)} async-done(((f32[4096,128]{0,1:T(8,128)}), f32[512,128]{0,1:T(8,128)}) %reduce-scatter.2.cloned.1.call-update) | async-done | bytes 262160 | tf_op jit(solution)/shard_map/reduce_scatter | solution.py:57
  94.5 0.0 copy-done
  94.5 1.2 fusion.31
  95.7 14.2 %psum.7 = f32[128]{0:T(128)S(1)} all-reduce(f32[128]{0:T(128)S(1)} %get-tuple-element.17), channel_id=1, replica_groups=mesh['sec'=2,'section'=4,'dp'=4] {'sec','section'}, use_global_device_ids=true, to_apply=%region_5.6 | all-reduce | flops 128 | bytes 1024 | tf_op jit(solution)/shard_map/psum | solution.py:69
  109.9 0.0 copy-start.3
  109.9 11.7 %all-reduce = f32[512]{0:T(512)S(1)} all-reduce(f32[512]{0:T(512)S(1)} %get-tuple-element.16), channel_id=3, replica_groups=mesh['sec'=2,'section'=4,'dp'=4] {'dp'}, use_global_device_ids=true, to_apply=%region_7.8.clone | all-reduce | flops 512 | bytes 4096
  121.6 0.6 dynamic-slice.1
  122.2 1.7 %fusion.37 = bf16[1,128,512]{2,1,0:T(8,128)(2,1)} fusion(f32[512,128]{0,1:T(8,128)} %reduce-scatter.2.cloned.1.call-done, bf16[1,128,512]{2,1,0:T(8,128)(2,1)S(1)} %copy-done, f32[128]{0:T(128)S(1)} %psum.7, f32[512]{0:T(512)S(1)} %dynamic_slice.3, f32[128]{0:T(128)S(1)} %add_rsqrt_fusion), kind=kLoop, calls=%fused_computation.44 | loop fusion | flops 524288 | bytes 527360 | tf_op jit(solution)/shard_map/broadcast_in_dim | solution.py:75
  123.9 0.0 copy-done.3
  (3 shorter events, 0.0 us)
Async XLA Ops:
  7.2 29.0 %all-gather.2.cloned.1.call-start = ((), (), s32[]{:S(2)}) async-start(), calls=%async_computation.1 | async-start | bytes 1179648 | tf_op jit(solution)/shard_map/all_gather | solution.py:10
  7.9 86.6 %reduce-scatter.2.cloned.1.call-start = ((), (), s32[]{:S(2)}) async-start(), calls=%async_computation.2 | async-start | bytes 2359296 | tf_op jit(solution)/shard_map/reduce_scatter | solution.py:57
  7.9 11.3 %copy-start.1 = (bf16[1,1,256,512]{3,2,1,0:T(8,128)(2,1)S(1)}, bf16[1,1,256,512]{3,2,1,0:T(8,128)(2,1)}, u32[]{:S(2)}) copy-start(bf16[1,1,256,512]{3,2,1,0:T(8,128)(2,1)} %param.9) | copy-start | bytes 786436
  8.0 11.4 %copy-start.2 = (bf16[1,1,256,512]{3,2,1,0:T(8,128)(2,1)S(1)}, bf16[1,1,256,512]{3,2,1,0:T(8,128)(2,1)}, u32[]{:S(2)}) copy-start(bf16[1,1,256,512]{3,2,1,0:T(8,128)(2,1)} %param.10) | copy-start | bytes 786436
  19.3 18.4 %copy-start.4 = (f32[4096]{0:T(1024)S(1)}, f32[4096]{0:T(1024)}, u32[]{:S(2)}) copy-start(f32[4096]{0:T(1024)} %param.7) | copy-start | bytes 49156
  53.1 0.7 copy-start.5
  53.2 41.4 %copy-start = (bf16[1,128,512]{2,1,0:T(8,128)(2,1)S(1)}, bf16[1,128,512]{2,1,0:T(8,128)(2,1)}, u32[]{:S(2)}) copy-start(bf16[1,128,512]{2,1,0:T(8,128)(2,1)} %param.6) | copy-start | bytes 393220
  109.9 14.0 %copy-start.3 = (f32[128]{0:T(128)}, f32[128]{0:T(128)S(1)}, u32[]{:S(2)}) copy-start(f32[128]{0:T(128)S(1)} %psum.7) | copy-start | bytes 1540
Sparse Core Ops, SparseCore 0:
  9.9 26.2 all-gather.1
  53.3 41.2 reduce-scatter.1
where the time goes:
time: 131 us
  waiting for transfers between devices  55.1 us (42%)
  blocking collectives  25.9 us (20%)
  matrix products  15.5 us (12%)
  between operations  15.5 us (12%)
  local copies, waits for them, and re-layouts  14.3 us (11%)
  other arithmetic  4.46 us (3%)
    reduce_scatter x1, waiting for transfers between devices, per_device(): lax.psum_scatter(lax.dot_general(weight, kv_grad, contract_last, preferre...  38.4 us
    all_gather x1, waiting for transfers between devices, per_device(): lax.all_gather(enc_states, ('sec', 'section'), axis=2, tiled=True)[0]  16 us
    psum x1, blocking collectives, per_device(): row_dot = lax.psum(row_part, ('sec', 'section'))  14.2 us
    unnamed x1, blocking collectives  11.7 us
    dot_general x1, local copies, waits for them, and re-layouts, per_device(): key_value = jnp.dot(memory, weight, preferred_element_type=jnp.float32)  11.3 us
    dot_general x1, matrix products, per_device(): lax.dot_general(weight, kv_grad, contract_last, preferred_element_type=jn...  7.66 us
    dot_general x1, matrix products, per_device(): key_value = jnp.dot(memory, weight, preferred_element_type=jnp.float32)  6.63 us
  transfers between devices with their start and end apart: 2, of which 2 were waited for; matrix products, arithmetic and copies ran while one was open for 10% of the time, Pallas kernels for 0%

commit v1 on v0

v1 whole, which is shorter than its diff:
```python
import functools

import jax
import jax.numpy as jnp
from jax import lax
from jax.experimental import pallas as pl
from jax.experimental.pallas import tpu as pltpu
from jax.sharding import PartitionSpec as P

HS = 256
EPS = 1e-06
LAST = (((1,), (1,)), ((), ()))
FIRST = (((0,), (0,)), ((), ()))
VMEM = pl.BlockSpec(memory_space=pltpu.VMEM)
SMEM = pl.BlockSpec(memory_space=pltpu.SMEM)
ANY = pl.BlockSpec(memory_space=pl.ANY)


def partner(index, step, count):
    return index ^ step


def tree_sum(terms):
    while len(terms) > 1:
        terms = [terms[i] + terms[i + 1] for i in range(0, len(terms), 2)]
    return terms[0]


def main_kernel(
    parts,
    heads,
    where_ref,
    length_ref,
    *refs,
):
    chunk_refs = refs[: 2 * parts]
    (gain_ref, weight_hbm, query_ref, cot_ref) = refs[2 * parts : 2 * parts + 4]
    (att_ref, sib_ref, own_ref, inv_ref, row_ref) = refs[2 * parts + 4 : 2 * parts + 9]
    (weight, memory, kv, kv_grad, sems) = refs[2 * parts + 9 :]
    tokens, feats = chunk_refs[0].shape
    width = weight.shape[0]
    half = width // 2
    blocks = sems.shape[0]
    block = width // blocks

    copies = []
    for b in range(blocks):
        rows = pl.ds(b * block, block)
        copy = pltpu.make_async_copy(weight_hbm.at[rows], weight.at[rows], sems.at[b])
        copy.start()
        copies.append(copy)

    square = None
    for ref in chunk_refs:
        x = ref[...].astype(jnp.float32)
        part = jnp.sum(x * x, axis=1, keepdims=True)
        square = part if square is None else square + part
    inv_rms = lax.rsqrt(square / width + EPS)
    inv_ref[...] = inv_rms
    for j, ref in enumerate(chunk_refs):
        at = pl.multiple_of(where_ref[j] * feats, feats)
        normed = ref[...].astype(jnp.float32) * inv_rms
        memory[:, pl.ds(at, feats)] = (normed * gain_ref[:, pl.ds(at, feats)]).astype(jnp.bfloat16)

    for b in range(blocks):
        copies[b].wait()
        rows = pl.ds(b * block, block)
        product = jnp.dot(memory[:, rows], weight[rows, :], preferred_element_type=jnp.float32)
        if b == 0:
            kv[...] = product
        else:
            kv[...] += product

    scale = HS ** (-0.5)
    live = lax.broadcasted_iota(jnp.int32, (query_ref.shape[0], HS), 0) < length_ref[0]
    row_part = None
    for h in range(heads):
        cols = pl.ds(h * HS, HS)
        key_cols, value_cols = pl.ds(2 * h * HS, HS), pl.ds((2 * h + 1) * HS, HS)
        key_full, value_full = kv[:, key_cols], kv[:, value_cols]
        key_rows, value_rows = key_full.astype(jnp.bfloat16), value_full.astype(jnp.bfloat16)
        query = query_ref[:, cols]
        cot = cot_ref[:, cols]
        masked = jnp.where(live, cot, jnp.zeros_like(cot))
        scores = lax.dot_general(key_rows, query, LAST, preferred_element_type=jnp.float32) * scale
        exponent = jnp.exp(scores)
        attention = exponent * (1.0 / jnp.sum(exponent, axis=0, keepdims=True))
        weights_b = attention.astype(jnp.bfloat16)
        att_ref[:, cols] = lax.dot_general(
            weights_b, value_rows, FIRST, preferred_element_type=jnp.float32
        ).astype(jnp.bfloat16)
        back = lax.dot_general(value_rows, masked, LAST, preferred_element_type=jnp.float32)
        mean = jnp.sum(attention * back, axis=0, keepdims=True)
        score_grad = (attention * (back - mean) * scale).astype(jnp.bfloat16)
        key_grad = jnp.dot(score_grad, query, preferred_element_type=jnp.float32)
        value_grad = jnp.dot(weights_b, masked, preferred_element_type=jnp.float32)
        key_grad, value_grad = key_grad.astype(jnp.bfloat16), value_grad.astype(jnp.bfloat16)
        kv_grad[:, key_cols] = key_grad
        kv_grad[:, value_cols] = value_grad
        here = jnp.sum(
            key_grad.astype(jnp.float32) * key_full + value_grad.astype(jnp.float32) * value_full,
            axis=1,
            keepdims=True,
        )
        row_part = here if row_part is None else row_part + here
    row_ref[...] = jnp.transpose(jnp.broadcast_to(row_part, (tokens, 128)))[0:1, :]

    me = where_ref[2 * parts]
    grad = kv_grad[...]
    tile = half // 4
    for t in range(4):
        rows = pl.ds(pl.multiple_of((1 - me) * half + t * tile, tile), tile)
        sib_ref[:, pl.ds(t * tile, tile)] = lax.dot_general(
            grad, weight[rows, :], LAST, preferred_element_type=jnp.float32
        ).astype(jnp.bfloat16)
    for t in range(4):
        rows = pl.ds(pl.multiple_of(me * half + t * tile, tile), tile)
        own_ref[:, pl.ds(t * tile, tile)] = lax.dot_general(
            grad, weight[rows, :], LAST, preferred_element_type=jnp.float32
        )


def chip_kernel(parts, where_ref, own_ref, sib_ref, row_ref, row_sib_ref, inv_ref, *refs):
    chunk_refs = refs[:parts]
    kept_ref = refs[parts]
    big_refs = refs[parts + 1 : 2 * parts]
    small_refs = refs[2 * parts :]
    feats = chunk_refs[0].shape[1]
    inv_rms = inv_ref[...]
    row = row_ref[...] + row_sib_ref[...]
    for k in range(parts):
        at = pl.multiple_of(where_ref[k] * feats, feats)
        cols = pl.ds(at, feats)
        total = own_ref[:, cols] + sib_ref[:, cols].astype(jnp.float32)
        if k == 0:
            kept_ref[...] = total
        else:
            big_refs[k - 1][...] = total.astype(jnp.bfloat16)
        normed = chunk_refs[k][...].astype(jnp.float32) * inv_rms
        small_refs[k][:, pl.ds(0, feats)] = jnp.sum(total * normed, axis=0, keepdims=True)
        small_refs[k][:, pl.ds(feats, row.shape[1])] = row


def last_kernel(parts, width, where_ref, kept_ref, *refs):
    big_refs = refs[: parts - 1]
    chunk_ref, inv_ref, gain_ref, row_ref, enc_ref = refs[parts - 1 :]
    tokens, feats = chunk_ref.shape
    grad = kept_ref[...]
    for ref in big_refs:
        grad = grad + ref[...].astype(jnp.float32)
    inv_rms = inv_ref[...]
    at = pl.multiple_of(where_ref[0] * feats, feats)
    gain = gain_ref[:, pl.ds(at, feats)]
    normed = chunk_ref[...].astype(jnp.float32) * inv_rms
    row_dot = jnp.transpose(jnp.broadcast_to(row_ref[...], (128, tokens)))[:, 0:1]
    enc_ref[...] = (inv_rms * (gain * grad - normed * (row_dot / width))).astype(jnp.bfloat16)


def per_device(sizes, enc_states, norm_gain, kv_weight, queries, attn_cotangent, target_lengths):
    cores, parts, seqs = sizes
    rows = enc_states[0]
    tokens, feats = rows.shape
    weight = kv_weight[0]
    width = weight.shape[0]
    half = width // 2
    query, cot = queries[0, 0], attn_cotangent[0, 0]
    dec = query.shape[0]
    heads = query.shape[1] // HS
    gain = norm_gain.reshape(1, width)
    core = lax.axis_index("sec")
    section = lax.axis_index("section")
    swap = [(0, 1), (1, 0)]

    def to_section(x, step):
        return lax.ppermute(x, "section", [(i, partner(i, step, parts)) for i in range(parts)])

    def to_core(x):
        return lax.ppermute(x, "sec", swap)

    chunks = [rows] + [to_section(rows, k) for k in range(1, parts)]
    others = [to_core(c) for c in chunks]
    peers = [partner(section, k, parts) for k in range(parts)]
    where = jnp.stack(
        [core * parts + p for p in peers] + [(1 - core) * parts + p for p in peers] + [core]
    ).astype(jnp.int32)

    blocks = 8
    flops = 2 * tokens * width * weight.shape[1]
    att, sib, own, inv_rms, row = pl.pallas_call(
        functools.partial(main_kernel, parts, heads),
        out_shape=(
            jax.ShapeDtypeStruct(query.shape, jnp.bfloat16),
            jax.ShapeDtypeStruct((tokens, half), jnp.bfloat16),
            jax.ShapeDtypeStruct((tokens, half), jnp.float32),
            jax.ShapeDtypeStruct((tokens, 1), jnp.float32),
            jax.ShapeDtypeStruct((1, tokens), jnp.float32),
        ),
        in_specs=[SMEM, SMEM] + [VMEM] * (2 * parts) + [VMEM, ANY, VMEM, VMEM],
        out_specs=(VMEM,) * 5,
        scratch_shapes=[
            pltpu.VMEM(weight.shape, jnp.bfloat16),
            pltpu.VMEM((tokens, width), jnp.bfloat16),
            pltpu.VMEM((tokens, weight.shape[1]), jnp.float32),
            pltpu.VMEM((tokens, weight.shape[1]), jnp.bfloat16),
            pltpu.SemaphoreType.DMA((blocks,)),
        ],
        compiler_params=pltpu.CompilerParams(vmem_limit_bytes=40 << 20),
        cost_estimate=pl.CostEstimate(
            flops=3 * flops, bytes_accessed=2 * weight.size, transcendentals=dec * tokens * heads
        ),
        name="main",
    )(where, target_lengths, *chunks, *others, gain, weight, query, cot)

    row_sib = to_core(row)
    sib_in = to_core(sib)

    where_section = jnp.stack(peers).astype(jnp.int32)
    pieces = pl.pallas_call(
        functools.partial(chip_kernel, parts),
        out_shape=(jax.ShapeDtypeStruct((tokens, feats), jnp.float32),)
        + (jax.ShapeDtypeStruct((tokens, feats), jnp.bfloat16),) * (parts - 1)
        + (jax.ShapeDtypeStruct((1, feats + tokens), jnp.float32),) * parts,
        in_specs=[SMEM] + [VMEM] * (5 + parts),
        out_specs=(VMEM,) * (2 * parts),
        compiler_params=pltpu.CompilerParams(vmem_limit_bytes=16 << 20),
        cost_estimate=pl.CostEstimate(
            flops=4 * tokens * half, bytes_accessed=8 * tokens * half, transcendentals=0
        ),
        name="chip",
    )(where_section, own, sib_in, row, row_sib, inv_rms, *chunks)
    kept, big, small = pieces[0], pieces[1:parts], pieces[parts:]

    small_in = [small[0]] + [to_section(small[k], k) for k in range(1, parts)]
    big_in = [to_section(big[k - 1], k) for k in range(1, parts)]
    sums = tree_sum(small_in)
    gain_term = sums[0, :feats]
    row_dot = sums[:, feats:]
    piece = feats // seqs
    if seqs <= 8:
        dp = lax.axis_index("dp")
        owned = [
            lax.dynamic_slice_in_dim(gain_term, partner(dp, k, seqs) * piece, piece, 0)
            for k in range(seqs)
        ]
        gain_grad = tree_sum(
            [owned[0]]
            + [
                lax.ppermute(owned[k], "dp", [(i, partner(i, k, seqs)) for i in range(seqs)])
                for k in range(1, seqs)
            ]
        )
    else:
        gain_grad = lax.psum_scatter(gain_term, "dp", scatter_dimension=0, tiled=True)

    where_own = (core * parts + section).reshape(1).astype(jnp.int32)
    enc_grad = pl.pallas_call(
        functools.partial(last_kernel, parts, width),
        out_shape=jax.ShapeDtypeStruct((tokens, feats), jnp.bfloat16),
        in_specs=[SMEM] + [VMEM] * (4 + parts),
        out_specs=VMEM,
        compiler_params=pltpu.CompilerParams(vmem_limit_bytes=8 << 20),
        cost_estimate=pl.CostEstimate(
            flops=10 * tokens * feats, bytes_accessed=16 * tokens * feats, transcendentals=0
        ),
        name="last",
    )(where_own, kept, *big_in, rows, inv_rms, gain, row_dot)
    return (att[None, None], enc_grad[None], gain_grad, row_dot)


def solution(mesh):
    sizes = tuple(mesh.shape[a] for a in ("sec", "section", "dp"))
    placed = (
        P("dp", None, ("sec", "section")),
        P(),
        P("sec", None, "section"),
        P("sec", "dp", None, "section"),
        P("sec", "dp", None, "section"),
        P("dp"),
    )
    return jax.shard_map(
        functools.partial(per_device, sizes),
        mesh=mesh,
        in_specs=placed,
        out_specs=(
            P("sec", "dp", None, "section"),
            P("dp", None, ("sec", "section")),
            P(("sec", "section", "dp")),
            P("dp", None),
        ),
        check_vma=False,
    )
```

time: 131 us -> 50 us (0.38)
  waiting for transfers between devices: 55.1 us -> 15 us
  blocking collectives: 25.9 us -> 0 us
  starting transfers between devices: 0.08 us -> 17.1 us
  matrix products: 15.5 us -> 0 us
  between operations: 15.5 us -> 1.35 us
  Pallas kernels: 0 us -> 8.56 us
  local copies, waits for them, and re-layouts: 14.3 us -> 7.02 us
  other arithmetic: 4.46 us -> 0.6 us
    reduce_scatter x1 -> x0, waiting for transfers between devices: 38.4 us -> none  [per_device(): lax.psum_scatter(lax.dot_general(weight, kv_grad, contract_last, preferre...]
    ppermute x0 -> x18, starting transfers between devices: none -> 17.1 us  [the longest x9 11.6 us: to_section(): lax.ppermute(x, 'section', [(i, partner(i, step, parts)) for i in range(p...]
    all_gather x1 -> x0, waiting for transfers between devices: 16 us -> none  [per_device(): lax.all_gather(enc_states, ('sec', 'section'), axis=2, tiled=True)[0]]
    dot_general x6 -> x0, matrix products: 15.2 us -> none  [the longest x1 7.66 us: per_device(): lax.dot_general(weight, kv_grad, contract_last, preferred_element_type=jn...]
    ppermute x0 -> x18, waiting for transfers between devices: none -> 15 us  [the longest x9 11.8 us: to_section(): lax.ppermute(x, 'section', [(i, partner(i, step, parts)) for i in range(p...]
    psum x1 -> x0, blocking collectives: 14.2 us -> none  [per_device(): row_dot = lax.psum(row_part, ('sec', 'section'))]
    unnamed x1 -> x0, blocking collectives: 11.7 us -> none
    dot_general x1 -> x0, local copies, waits for them, and re-layouts: 11.3 us -> none  [per_device(): key_value = jnp.dot(memory, weight, preferred_element_type=jnp.float32)]
  transfers between devices with their start and end apart: 2 -> 18, of which waited for: 2 -> 11; matrix products, arithmetic and copies ran while one was open for 10% -> 1% of each run, Pallas kernels for 0% -> 0%
where the time goes in v1:
time: 50 us; the launch traced here: 49.7 us
  starting transfers between devices  17.1 us (34%)
  waiting for transfers between devices  15 us (30%)
  Pallas kernels  8.56 us (17%)
  local copies, waits for them, and re-layouts  7.02 us (14%)
  between operations  1.35 us (3%)
  other arithmetic  0.6 us (1%)
    ppermute x9, waiting for transfers between devices, to_section(): lax.ppermute(x, 'section', [(i, partner(i, step, parts)) for i in range(p...  11.8 us
    ppermute x9, starting transfers between devices, to_section(): lax.ppermute(x, 'section', [(i, partner(i, step, parts)) for i in range(p...  11.6 us
    unnamed x16, local copies, waits for them, and re-layouts  6.91 us
    pallas_call x1, Pallas kernels, per_device(): pl.pallas_call(functools.partial(main_kernel, parts, heads), out_shape=(j...  6.83 us
    ppermute x3, starting transfers between devices, per_device(): lax.ppermute(owned[k], 'dp', [(i, partner(i, k, seqs)) for i in range(seq...  4.45 us
    ppermute x3, waiting for transfers between devices, per_device(): lax.ppermute(owned[k], 'dp', [(i, partner(i, k, seqs)) for i in range(seq...  1.62 us
    ppermute x6, waiting for transfers between devices, to_core(): return lax.ppermute(x, 'sec', swap)  1.6 us
    ppermute x6, starting transfers between devices, to_core(): return lax.ppermute(x, 'sec', swap)  1.09 us
  transfers between devices with their start and end apart: 18, of which 11 were waited for; matrix products, arithmetic and copies ran while one was open for 1% of the time, Pallas kernels for 0%

profile of v1, /device:TPU:0, one launch (start us, length us, event | category | flops | bytes accessed | tf_op | source)
XLA Modules:
  0.0 49.7 jit_solution(8999906620336422142)
XLA Ops:
  0.6 0.0 copy-start.3
  0.6 3.0 %collective-permute-start = (bf16[128,512]{1,0:T(8,128)(2,1)}, bf16[128,512]{1,0:T(8,128)(2,1)S(1)}, u32[]{:S(2)}, u32[]{:S(2)}) collective-permute-start(bf16[128,512]{1,0:T(8,128)(2,1)} %bitcast.32), channel_id=1, source_target_pairs={{0,4},{4,0},{8,12},{12,8},{1,5},{5,1},{9,13},{13,9},{2,6},{6,2},{1... | collective-permute-start | bytes 393224 | tf_op jit(solution)/shard_map/ppermute | solution.py:175
  3.6 1.5 %collective-permute-start.1 = (bf16[128,512]{1,0:T(8,128)(2,1)}, bf16[128,512]{1,0:T(8,128)(2,1)S(1)}, u32[]{:S(2)}, u32[]{:S(2)}) collective-permute-start(bf16[128,512]{1,0:T(8,128)(2,1)} %bitcast.33), channel_id=1, source_target_pairs={{0,8},{4,12},{8,0},{12,4},{1,9},{5,13},{9,1},{13,5},{2,10},{6,14},... | collective-permute-start | bytes 393224 | tf_op jit(solution)/shard_map/ppermute | solution.py:175
  5.2 0.0 collective-permute-start.2
  5.2 0.0 collective-permute-start.3
  5.2 2.7 %collective-permute-done.refs_1_ = bf16[128,512]{1,0:T(8,128)(2,1)S(1)} collective-permute-done((bf16[128,512]{1,0:T(8,128)(2,1)}, bf16[128,512]{1,0:T(8,128)(2,1)S(1)}, u32[]{:S(2)}, u32[]{:S(2)}) %collective-permute-start) | collective-permute-done | bytes 131104 | tf_op jit(solution)/shard_map/ppermute | solution.py:175
  7.9 0.0 collective-permute-start.4
  7.9 3.8 %collective-permute-done.1.refs_2_ = bf16[128,512]{1,0:T(8,128)(2,1)S(1)} collective-permute-done((bf16[128,512]{1,0:T(8,128)(2,1)}, bf16[128,512]{1,0:T(8,128)(2,1)S(1)}, u32[]{:S(2)}, u32[]{:S(2)}) %collective-permute-start.1) | collective-permute-done | bytes 131104 | tf_op jit(solution)/shard_map/ppermute | solution.py:175
  11.6 0.0 collective-permute-start.5
  11.6 0.0 collective-permute-done.2.refs_3_
  11.6 0.5 %collective-permute-start.6 = (bf16[128,512]{1,0:T(8,128)(2,1)S(1)}, bf16[128,512]{1,0:T(8,128)(2,1)S(1)}, u32[]{:S(2)}, u32[]{:S(2)}) collective-permute-start(bf16[128,512]{1,0:T(8,128)(2,1)S(1)} %collective-permute-done.2.refs_3_), channel_id=1, source_target_pairs={{0,16},{16,0},{1,17},{17,1},{2,18},{18,2},{3,19},{19,3},{4,20},{20... | collective-permute-start | bytes 393224 | tf_op jit(solution)/shard_map/ppermute | solution.py:178
  12.8 0.1 stack.54.where_ref
  12.9 0.0 collective-permute-done.3.refs_4_
  12.9 0.0 collective-permute-done.4.refs_5_
  12.9 0.1 collective-permute-done.5.refs_6_
  13.0 0.2 collective-permute-done.6.refs_7_
  13.2 0.9 %copy-done = bf16[1,128,512]{2,1,0:T(8,128)(2,1)S(1)} copy-done((bf16[1,128,512]{2,1,0:T(8,128)(2,1)S(1)}, bf16[1,128,512]{2,1,0:T(8,128)(2,1)}, u32[]{:S(2)}) %copy-start) | copy-done | bytes 131096
  14.1 0.7 %copy-done.2 = f32[4096]{0:T(1024)S(1)} copy-done((f32[4096]{0:T(1024)S(1)}, f32[4096]{0:T(1024)}, u32[]{:S(2)}) %copy-start.2) | copy-done | bytes 16408
  14.8 3.4 %copy-done.5 = bf16[1,4096,1024]{2,1,0:T(8,128)(2,1)S(1)} copy-done((bf16[1,4096,1024]{2,1,0:T(8,128)(2,1)S(1)}, bf16[1,4096,1024]{2,1,0:T(8,128)(2,1)}, u32[]{:S(2)}) %copy-start.5) | copy-done | bytes 8388632
  18.2 0.9 %copy-done.6 = bf16[1,1,256,512]{3,2,1,0:T(8,128)(2,1)S(1)} copy-done((bf16[1,1,256,512]{3,2,1,0:T(8,128)(2,1)S(1)}, bf16[1,1,256,512]{3,2,1,0:T(8,128)(2,1)}, u32[]{:S(2)}) %copy-start.6) | copy-done | bytes 262168
  19.1 0.9 %copy-done.7 = bf16[1,1,256,512]{3,2,1,0:T(8,128)(2,1)S(1)} copy-done((bf16[1,1,256,512]{3,2,1,0:T(8,128)(2,1)S(1)}, bf16[1,1,256,512]{3,2,1,0:T(8,128)(2,1)}, u32[]{:S(2)}) %copy-start.7) | copy-done | bytes 262168
  20.1 6.8 %main.1 = (bf16[256,512]{1,0:T(8,128)(2,1)}, bf16[128,2048]{1,0:T(8,128)(2,1)S(1)}, f32[128,2048]{1,0:T(8,128)S(1)}, f32[128,1]{1,0:T(8,128)S(1)}, f32[1,128]{1,0:T(1,128)S(1)}) custom-call(s32[9]{0:T(128)S(1)} %stack.54.where_ref, s32[1]{0:T(128)S(6)} %copy.10.length_ref, bf16[128,512]{1,0:T(8,128)(2,1)S(1)} %bitcast.36, ...), custom_call_target="tpu_custom_call" | custom-call | flops 3221225472 | bytes 8388608 | tf_op jit(solution)/shard_map/main/pallas_call | solution.py:189
  26.9 0.4 collective-permute-start.7
  27.3 0.2 collective-permute-start.8
  27.5 0.1 pad_add_fusion.where_ref
  27.6 1.3 %collective-permute-done.8.row_sib_ref = f32[1,128]{1,0:T(1,128)S(1)} collective-permute-done((f32[1,128]{1,0:T(1,128)S(1)}, f32[1,128]{1,0:T(1,128)S(1)}, u32[]{:S(2)}, u32[]{:S(2)}) %collective-permute-start.8) | collective-permute-done | bytes 544 | tf_op jit(solution)/shard_map/ppermute | solution.py:178
  28.9 0.0 collective-permute-done.7.sib_ref
  28.9 0.9 %chip.1 = (f32[128,512]{1,0:T(8,128)S(1)}, bf16[128,512]{1,0:T(8,128)(2,1)S(1)}, bf16[128,512]{1,0:T(8,128)(2,1)S(1)}, bf16[128,512]{1,0:T(8,128)(2,1)S(1)}, f32...) custom-call(s32[4]{0:T(128)S(1)} %pad_add_fusion.where_ref, ...), custom_call_target="tpu_custom_call" | custom-call | flops 1048576 | bytes 2097152 | tf_op jit(solution)/shard_map/chip/pallas_call | solution.py:218
  29.8 1.6 %collective-permute-start.13 = (f32[1,640]{1,0:T(1,128)S(1)}, f32[1,640]{1,0:T(1,128)S(1)}, u32[]{:S(2)}, u32[]{:S(2)}) collective-permute-start(f32[1,640]{1,0:T(1,128)S(1)} %get-tuple-element.28), channel_id=1, source_target_pairs={{0,8},{4,12},{8,0},{12,4},{1,9},{5,13},{9,1},{13,5},{2,10},{6,14},... | collective-permute-start | bytes 7688 | tf_op jit(solution)/shard_map/ppermute | solution.py:175
  31.3 1.0 %collective-permute-start.14 = (f32[1,640]{1,0:T(1,128)S(1)}, f32[1,640]{1,0:T(1,128)S(1)}, u32[]{:S(2)}, u32[]{:S(2)}) collective-permute-start(f32[1,640]{1,0:T(1,128)S(1)} %get-tuple-element.29), channel_id=1, source_target_pairs={{0,12},{4,8},{8,4},{12,0},{1,13},{5,9},{9,5},{13,1},{2,14},{6,10},... | collective-permute-start | bytes 7688 | tf_op jit(solution)/shard_map/ppermute | solution.py:175
  32.3 1.0 %collective-permute-start.12 = (f32[1,640]{1,0:T(1,128)S(1)}, f32[1,640]{1,0:T(1,128)S(1)}, u32[]{:S(2)}, u32[]{:S(2)}) collective-permute-start(f32[1,640]{1,0:T(1,128)S(1)} %get-tuple-element.27), channel_id=1, source_target_pairs={{0,4},{4,0},{8,12},{12,8},{1,5},{5,1},{9,13},{13,9},{2,6},{6,2},{1... | collective-permute-start | bytes 7688 | tf_op jit(solution)/shard_map/ppermute | solution.py:175
  33.3 0.1 collective-permute-done.13
  33.4 2.4 %collective-permute-done.14 = f32[1,640]{1,0:T(1,128)S(1)} collective-permute-done((f32[1,640]{1,0:T(1,128)S(1)}, f32[1,640]{1,0:T(1,128)S(1)}, u32[]{:S(2)}, u32[]{:S(2)}) %collective-permute-start.14) | collective-permute-done | bytes 2592 | tf_op jit(solution)/shard_map/ppermute | solution.py:175
  35.8 0.1 collective-permute-done.12
  35.9 1.6 %collective-permute-start.15 = (f32[128]{0:T(128)S(1)}, f32[128]{0:T(128)S(1)}, u32[]{:S(2)}, u32[]{:S(2)}) collective-permute-start(f32[128]{0:T(128)S(1)} %get-tuple-element.32), channel_id=1, source_target_pairs={{0,1},{1,0},{2,3},{3,2},{4,5},{5,4},{6,7},{7,6},{8,9},{9,8},{10,11... | collective-permute-start | bytes 1544 | tf_op jit(solution)/shard_map/ppermute | solution.py:248
  37.6 2.6 %collective-permute-start.16 = (f32[128]{0:T(128)S(1)}, f32[128]{0:T(128)S(1)}, u32[]{:S(2)}, u32[]{:S(2)}) collective-permute-start(f32[128]{0:T(128)S(1)} %get-tuple-element.31), channel_id=1, source_target_pairs={{0,2},{1,3},{2,0},{3,1},{4,6},{5,7},{6,4},{7,5},{8,10},{9,11},{10,... | collective-permute-start | bytes 1544 | tf_op jit(solution)/shard_map/ppermute | solution.py:248
  40.2 0.2 collective-permute-start.17
  40.4 1.0 %collective-permute-start.9 = (bf16[128,512]{1,0:T(8,128)(2,1)S(1)}, bf16[128,512]{1,0:T(8,128)(2,1)S(1)}, u32[]{:S(2)}, u32[]{:S(2)}) collective-permute-start(bf16[128,512]{1,0:T(8,128)(2,1)S(1)} %get-tuple-element.23), channel_id=1, source_target_pairs={{0,4},{4,0},{8,12},{12,8},{1,5},{5,1},{9,13},{13,9},{2,6},{6,2},{1... | collective-permute-start | bytes 393224 | tf_op jit(solution)/shard_map/ppermute | solution.py:175
  41.4 1.5 %collective-permute-start.10 = (bf16[128,512]{1,0:T(8,128)(2,1)S(1)}, bf16[128,512]{1,0:T(8,128)(2,1)S(1)}, u32[]{:S(2)}, u32[]{:S(2)}) collective-permute-start(bf16[128,512]{1,0:T(8,128)(2,1)S(1)} %get-tuple-element.24), channel_id=1, source_target_pairs={{0,8},{4,12},{8,0},{12,4},{1,9},{5,13},{9,1},{13,5},{2,10},{6,14},... | collective-permute-start | bytes 393224 | tf_op jit(solution)/shard_map/ppermute | solution.py:175
  42.9 0.0 collective-permute-done.15
  42.9 1.0 %collective-permute-start.11 = (bf16[128,512]{1,0:T(8,128)(2,1)S(1)}, bf16[128,512]{1,0:T(8,128)(2,1)S(1)}, u32[]{:S(2)}, u32[]{:S(2)}) collective-permute-start(bf16[128,512]{1,0:T(8,128)(2,1)S(1)} %get-tuple-element.25), channel_id=1, source_target_pairs={{0,12},{4,8},{8,4},{12,0},{1,13},{5,9},{9,5},{13,1},{2,14},{6,10},... | collective-permute-start | bytes 393224 | tf_op jit(solution)/shard_map/ppermute | solution.py:175
  43.9 0.0 collective-permute-done.16
  43.9 1.6 %collective-permute-done.17 = f32[128]{0:T(128)S(1)} collective-permute-done((f32[128]{0:T(128)S(1)}, f32[128]{0:T(128)S(1)}, u32[]{:S(2)}, u32[]{:S(2)}) %collective-permute-start.17) | collective-permute-done | bytes 544 | tf_op jit(solution)/shard_map/ppermute | solution.py:248
  45.5 0.5 %fusion.2 = f32[128]{0:T(128)} fusion(f32[128]{0:T(128)S(1)} %collective-permute-done.15, f32[1,512]{1,0:T(1,128)S(1)} %slice.9, s32[]{:T(128)S(6)} %select_n.12, f32[128]{0:T(128)S(1)} %collective-permute-done.16, f32[128]{0:T(128)S(1)} %collective-permute-done.17), kind=kLoop, calls=%fused_computation.7 | loop fusion | flops 384 | bytes 2564 | tf_op jit(solution)/shard_map/add | solution.py:25
  46.0 0.0 collective-permute-done.9.refs_0_
  46.0 1.1 %collective-permute-done.10.refs_1_ = bf16[128,512]{1,0:T(8,128)(2,1)S(1)} collective-permute-done((bf16[128,512]{1,0:T(8,128)(2,1)S(1)}, bf16[128,512]{1,0:T(8,128)(2,1)S(1)}, u32[]{:S(2)}, u32[]{:S(2)}) %collective-permute-start.10) | collective-permute-done | bytes 131104 | tf_op jit(solution)/shard_map/ppermute | solution.py:175
  47.1 1.7 %collective-permute-done.11.refs_2_ = bf16[128,512]{1,0:T(8,128)(2,1)S(1)} collective-permute-done((bf16[128,512]{1,0:T(8,128)(2,1)S(1)}, bf16[128,512]{1,0:T(8,128)(2,1)S(1)}, u32[]{:S(2)}, u32[]{:S(2)}) %collective-permute-start.11) | collective-permute-done | bytes 131104 | tf_op jit(solution)/shard_map/ppermute | solution.py:175
  48.8 0.9 %last.1 = bf16[128,512]{1,0:T(8,128)(2,1)} custom-call(s32[1]{0:T(128)} %bitcast.where_ref, f32[128,512]{1,0:T(8,128)S(1)} %get-tuple-element.22.kept_ref, bf16[128,512]{1,0:T(8,128)(2,1)S(1)} %collective-permute-done.9.refs_0_, bf16[128,512]{1,0:T(8,128)(2,1)S(1)} %collective-permute-done.10.refs_1_, bf16[128,512]{1,0:T(8,128)(2,1)S(1)} %collective-permute-done.11.refs_2_, ...), custom_call_target="tpu_custom_call" | custom-call | flops 655360 | bytes 1048576 | tf_op jit(solution)/shard_map/last/pallas_call | solution.py:256
  (14 shorter events, 0.0 us)
Async XLA Ops:
  0.6 48.2 %copy-start.3 = (f32[4096]{0:T(1024)S(1)}, f32[4096]{0:T(1024)}, u32[]{:S(2)}) copy-start(f32[4096]{0:T(1024)} %param.7) | copy-start | bytes 49156
  0.6 7.2 %collective-permute-start = (bf16[128,512]{1,0:T(8,128)(2,1)}, bf16[128,512]{1,0:T(8,128)(2,1)S(1)}, u32[]{:S(2)}, u32[]{:S(2)}) collective-permute-start(bf16[128,512]{1,0:T(8,128)(2,1)} %bitcast.32), channel_id=1, source_target_pairs={{0,4},{4,0},{8,12},{12,8},{1,5},{5,1},{9,13},{13,9},{2,6},{6,2},{1... | collective-permute-start | bytes 393224 | tf_op jit(solution)/shard_map/ppermute | solution.py:175
  3.6 8.0 %collective-permute-start.1 = (bf16[128,512]{1,0:T(8,128)(2,1)}, bf16[128,512]{1,0:T(8,128)(2,1)S(1)}, u32[]{:S(2)}, u32[]{:S(2)}) collective-permute-start(bf16[128,512]{1,0:T(8,128)(2,1)} %bitcast.33), channel_id=1, source_target_pairs={{0,8},{4,12},{8,0},{12,4},{1,9},{5,13},{9,1},{13,5},{2,10},{6,14},... | collective-permute-start | bytes 393224 | tf_op jit(solution)/shard_map/ppermute | solution.py:175
  5.2 6.5 %collective-permute-start.2 = (bf16[128,512]{1,0:T(8,128)(2,1)}, bf16[128,512]{1,0:T(8,128)(2,1)S(1)}, u32[]{:S(2)}, u32[]{:S(2)}) collective-permute-start(bf16[128,512]{1,0:T(8,128)(2,1)} %bitcast.34), channel_id=1, source_target_pairs={{0,12},{4,8},{8,4},{12,0},{1,13},{5,9},{9,5},{13,1},{2,14},{6,10},... | collective-permute-start | bytes 393224 | tf_op jit(solution)/shard_map/ppermute | solution.py:175
  5.2 7.7 %collective-permute-start.3 = (bf16[128,512]{1,0:T(8,128)(2,1)}, bf16[128,512]{1,0:T(8,128)(2,1)S(1)}, u32[]{:S(2)}, u32[]{:S(2)}) collective-permute-start(bf16[128,512]{1,0:T(8,128)(2,1)} %bitcast.35), channel_id=1, source_target_pairs={{0,16},{16,0},{1,17},{17,1},{2,18},{18,2},{3,19},{19,3},{4,20},{20... | collective-permute-start | bytes 393224 | tf_op jit(solution)/shard_map/ppermute | solution.py:178
  7.9 5.0 %collective-permute-start.4 = (bf16[128,512]{1,0:T(8,128)(2,1)S(1)}, bf16[128,512]{1,0:T(8,128)(2,1)S(1)}, u32[]{:S(2)}, u32[]{:S(2)}) collective-permute-start(bf16[128,512]{1,0:T(8,128)(2,1)S(1)} %collective-permute-done.refs_1_), channel_id=1, source_target_pairs={{0,16},{16,0},{1,17},{17,1},{2,18},{18,2},{3,19},{19,3},{4,20},{20... | collective-permute-start | bytes 393224 | tf_op jit(solution)/shard_map/ppermute | solution.py:178
  11.6 1.3 %collective-permute-start.5 = (bf16[128,512]{1,0:T(8,128)(2,1)S(1)}, bf16[128,512]{1,0:T(8,128)(2,1)S(1)}, u32[]{:S(2)}, u32[]{:S(2)}) collective-permute-start(bf16[128,512]{1,0:T(8,128)(2,1)S(1)} %collective-permute-done.1.refs_2_), channel_id=1, source_target_pairs={{0,16},{16,0},{1,17},{17,1},{2,18},{18,2},{3,19},{19,3},{4,20},{20... | collective-permute-start | bytes 393224 | tf_op jit(solution)/shard_map/ppermute | solution.py:178
  11.6 1.5 %collective-permute-start.6 = (bf16[128,512]{1,0:T(8,128)(2,1)S(1)}, bf16[128,512]{1,0:T(8,128)(2,1)S(1)}, u32[]{:S(2)}, u32[]{:S(2)}) collective-permute-start(bf16[128,512]{1,0:T(8,128)(2,1)S(1)} %collective-permute-done.2.refs_3_), channel_id=1, source_target_pairs={{0,16},{16,0},{1,17},{17,1},{2,18},{18,2},{3,19},{19,3},{4,20},{20... | collective-permute-start | bytes 393224 | tf_op jit(solution)/shard_map/ppermute | solution.py:178
  13.2 0.9 %copy-start = (bf16[1,128,512]{2,1,0:T(8,128)(2,1)S(1)}, bf16[1,128,512]{2,1,0:T(8,128)(2,1)}, u32[]{:S(2)}) copy-start(bf16[1,128,512]{2,1,0:T(8,128)(2,1)} %param.6) | copy-start | bytes 393220
  14.1 0.7 %copy-start.2 = (f32[4096]{0:T(1024)S(1)}, f32[4096]{0:T(1024)}, u32[]{:S(2)}) copy-start(f32[4096]{0:T(1024)} %param.7) | copy-start | bytes 49156
  14.8 3.4 %copy-start.5 = (bf16[1,4096,1024]{2,1,0:T(8,128)(2,1)S(1)}, bf16[1,4096,1024]{2,1,0:T(8,128)(2,1)}, u32[]{:S(2)}) copy-start(bf16[1,4096,1024]{2,1,0:T(8,128)(2,1)} %param.8) | copy-start | bytes 25165828
  18.2 0.9 %copy-start.6 = (bf16[1,1,256,512]{3,2,1,0:T(8,128)(2,1)S(1)}, bf16[1,1,256,512]{3,2,1,0:T(8,128)(2,1)}, u32[]{:S(2)}) copy-start(bf16[1,1,256,512]{3,2,1,0:T(8,128)(2,1)} %param.9) | copy-start | bytes 786436
  19.1 0.9 %copy-start.7 = (bf16[1,1,256,512]{3,2,1,0:T(8,128)(2,1)S(1)}, bf16[1,1,256,512]{3,2,1,0:T(8,128)(2,1)}, u32[]{:S(2)}) copy-start(bf16[1,1,256,512]{3,2,1,0:T(8,128)(2,1)} %param.10) | copy-start | bytes 786436
  20.1 28.7 %copy-start.1 = (bf16[1,128,512]{2,1,0:T(8,128)(2,1)S(1)}, bf16[1,128,512]{2,1,0:T(8,128)(2,1)}, u32[]{:S(2)}) copy-start(bf16[1,128,512]{2,1,0:T(8,128)(2,1)} %param.6) | copy-start | bytes 393220
  26.9 2.0 %collective-permute-start.7 = (bf16[128,2048]{1,0:T(8,128)(2,1)S(1)}, bf16[128,2048]{1,0:T(8,128)(2,1)S(1)}, u32[]{:S(2)}, u32[]{:S(2)}) collective-permute-start(bf16[128,2048]{1,0:T(8,128)(2,1)S(1)} %get-tuple-element.19), channel_id=1, source_target_pairs={{0,16},{16,0},{1,17},{17,1},{2,18},{18,2},{3,19},{19,3},{4,20},{20... | collective-permute-start | bytes 1572872 | tf_op jit(solution)/shard_map/ppermute | solution.py:178
  27.3 1.6 %collective-permute-start.8 = (f32[1,128]{1,0:T(1,128)S(1)}, f32[1,128]{1,0:T(1,128)S(1)}, u32[]{:S(2)}, u32[]{:S(2)}) collective-permute-start(f32[1,128]{1,0:T(1,128)S(1)} %get-tuple-element.20.row_ref), channel_id=1, source_target_pairs={{0,16},{16,0},{1,17},{17,1},{2,18},{18,2},{3,19},{19,3},{4,20},{20... | collective-permute-start | bytes 1544 | tf_op jit(solution)/shard_map/ppermute | solution.py:178
  29.8 3.7 %collective-permute-start.13 = (f32[1,640]{1,0:T(1,128)S(1)}, f32[1,640]{1,0:T(1,128)S(1)}, u32[]{:S(2)}, u32[]{:S(2)}) collective-permute-start(f32[1,640]{1,0:T(1,128)S(1)} %get-tuple-element.28), channel_id=1, source_target_pairs={{0,8},{4,12},{8,0},{12,4},{1,9},{5,13},{9,1},{13,5},{2,10},{6,14},... | collective-permute-start | bytes 7688 | tf_op jit(solution)/shard_map/ppermute | solution.py:175
  31.3 4.5 %collective-permute-start.14 = (f32[1,640]{1,0:T(1,128)S(1)}, f32[1,640]{1,0:T(1,128)S(1)}, u32[]{:S(2)}, u32[]{:S(2)}) collective-permute-start(f32[1,640]{1,0:T(1,128)S(1)} %get-tuple-element.29), channel_id=1, source_target_pairs={{0,12},{4,8},{8,4},{12,0},{1,13},{5,9},{9,5},{13,1},{2,14},{6,10},... | collective-permute-start | bytes 7688 | tf_op jit(solution)/shard_map/ppermute | solution.py:175
  32.3 3.6 %collective-permute-start.12 = (f32[1,640]{1,0:T(1,128)S(1)}, f32[1,640]{1,0:T(1,128)S(1)}, u32[]{:S(2)}, u32[]{:S(2)}) collective-permute-start(f32[1,640]{1,0:T(1,128)S(1)} %get-tuple-element.27), channel_id=1, source_target_pairs={{0,4},{4,0},{8,12},{12,8},{1,5},{5,1},{9,13},{13,9},{2,6},{6,2},{1... | collective-permute-start | bytes 7688 | tf_op jit(solution)/shard_map/ppermute | solution.py:175
  35.9 7.0 %collective-permute-start.15 = (f32[128]{0:T(128)S(1)}, f32[128]{0:T(128)S(1)}, u32[]{:S(2)}, u32[]{:S(2)}) collective-permute-start(f32[128]{0:T(128)S(1)} %get-tuple-element.32), channel_id=1, source_target_pairs={{0,1},{1,0},{2,3},{3,2},{4,5},{5,4},{6,7},{7,6},{8,9},{9,8},{10,11... | collective-permute-start | bytes 1544 | tf_op jit(solution)/shard_map/ppermute | solution.py:248
  37.6 6.3 %collective-permute-start.16 = (f32[128]{0:T(128)S(1)}, f32[128]{0:T(128)S(1)}, u32[]{:S(2)}, u32[]{:S(2)}) collective-permute-start(f32[128]{0:T(128)S(1)} %get-tuple-element.31), channel_id=1, source_target_pairs={{0,2},{1,3},{2,0},{3,1},{4,6},{5,7},{6,4},{7,5},{8,10},{9,11},{10,... | collective-permute-start | bytes 1544 | tf_op jit(solution)/shard_map/ppermute | solution.py:248
  40.2 5.3 %collective-permute-start.17 = (f32[128]{0:T(128)S(1)}, f32[128]{0:T(128)S(1)}, u32[]{:S(2)}, u32[]{:S(2)}) collective-permute-start(f32[128]{0:T(128)S(1)} %get-tuple-element.30), channel_id=1, source_target_pairs={{0,3},{1,2},{2,1},{3,0},{4,7},{5,6},{6,5},{7,4},{8,11},{9,10},{10,... | collective-permute-start | bytes 1544 | tf_op jit(solution)/shard_map/ppermute | solution.py:248
  40.4 5.6 %collective-permute-start.9 = (bf16[128,512]{1,0:T(8,128)(2,1)S(1)}, bf16[128,512]{1,0:T(8,128)(2,1)S(1)}, u32[]{:S(2)}, u32[]{:S(2)}) collective-permute-start(bf16[128,512]{1,0:T(8,128)(2,1)S(1)} %get-tuple-element.23), channel_id=1, source_target_pairs={{0,4},{4,0},{8,12},{12,8},{1,5},{5,1},{9,13},{13,9},{2,6},{6,2},{1... | collective-permute-start | bytes 393224 | tf_op jit(solution)/shard_map/ppermute | solution.py:175
  41.4 5.7 %collective-permute-start.10 = (bf16[128,512]{1,0:T(8,128)(2,1)S(1)}, bf16[128,512]{1,0:T(8,128)(2,1)S(1)}, u32[]{:S(2)}, u32[]{:S(2)}) collective-permute-start(bf16[128,512]{1,0:T(8,128)(2,1)S(1)} %get-tuple-element.24), channel_id=1, source_target_pairs={{0,8},{4,12},{8,0},{12,4},{1,9},{5,13},{9,1},{13,5},{2,10},{6,14},... | collective-permute-start | bytes 393224 | tf_op jit(solution)/shard_map/ppermute | solution.py:175
  42.9 6.7 %copy-start.4 = (f32[1,128]{1,0:T(1,128)}, f32[1,128]{1,0:T(1,128)S(1)}, u32[]{:S(2)}) copy-start(f32[1,128]{1,0:T(1,128)S(1)} %slice.8.refs_6_) | copy-start | bytes 1540
  42.9 5.9 %collective-permute-start.11 = (bf16[128,512]{1,0:T(8,128)(2,1)S(1)}, bf16[128,512]{1,0:T(8,128)(2,1)S(1)}, u32[]{:S(2)}, u32[]{:S(2)}) collective-permute-start(bf16[128,512]{1,0:T(8,128)(2,1)S(1)} %get-tuple-element.25), channel_id=1, source_target_pairs={{0,12},{4,8},{8,4},{12,0},{1,13},{5,9},{9,5},{13,1},{2,14},{6,10},... | collective-permute-start | bytes 393224 | tf_op jit(solution)/shard_map/ppermute | solution.py:175

commit v2 on v1

v2 whole, which is shorter than its diff:
```python
import functools

import jax
import jax.numpy as jnp
from jax import lax
from jax.experimental import pallas as pl
from jax.experimental.pallas import tpu as pltpu
from jax.sharding import PartitionSpec as P

HS = 256
EPS = 1e-06
LAST = (((1,), (1,)), ((), ()))
FIRST = (((0,), (0,)), ((), ()))
VMEM = pl.BlockSpec(memory_space=pltpu.VMEM)
SMEM = pl.BlockSpec(memory_space=pltpu.SMEM)
ANY = pl.BlockSpec(memory_space=pl.ANY)


def partner(index, step, count):
    return index ^ step


def tree_sum(terms):
    while len(terms) > 1:
        terms = [terms[i] + terms[i + 1] for i in range(0, len(terms), 2)]
    return terms[0]


def direct_sum(terms, axis, count):
    perms = [[(i, partner(i, k, count)) for i in range(count)] for k in range(count)]
    return tree_sum([terms[0]] + [lax.ppermute(terms[k], axis, perms[k]) for k in range(1, count)])


def first_kernel(rows_ref, weight_ref, square_ref):
    own = rows_ref[...].astype(jnp.float32)
    square_ref[...] = jnp.sum(own * own, axis=1, keepdims=True)


def main_kernel(
    parts,
    heads,
    length_ref,
    square_ref,
    *refs,
):
    chunk_refs = refs[: 2 * parts]
    (gain_ref, weight, query_ref, cot_ref) = refs[2 * parts : 2 * parts + 4]
    (att_ref, sib_ref, own_ref, inv_ref, row_ref) = refs[2 * parts + 4 : 2 * parts + 9]
    (memory, kv, kv_grad) = refs[2 * parts + 9 :]
    tokens, feats = chunk_refs[0].shape
    width = weight.shape[0]
    half = width // 2

    square = square_ref[...]
    for ref in chunk_refs[1:]:
        x = ref[...].astype(jnp.float32)
        part = jnp.sum(x * x, axis=1, keepdims=True)
        square = square + part
    inv_rms = lax.rsqrt(square / width + EPS)
    inv_ref[...] = inv_rms
    me, section = lax.axis_index("sec"), lax.axis_index("section")
    for j, ref in enumerate(chunk_refs):
        owner = me if j < parts else 1 - me
        at = pl.multiple_of((owner * parts + partner(section, j % parts, parts)) * feats, feats)
        normed = ref[...].astype(jnp.float32) * inv_rms
        memory[:, pl.ds(at, feats)] = (normed * gain_ref[:, pl.ds(at, feats)]).astype(jnp.bfloat16)

    kv[...] = jnp.dot(memory[...], weight[...], preferred_element_type=jnp.float32)

    scale = HS ** (-0.5)
    live = lax.broadcasted_iota(jnp.int32, (query_ref.shape[0], HS), 0) < length_ref[0]
    row_part = None
    for h in range(heads):
        cols = pl.ds(h * HS, HS)
        key_cols, value_cols = pl.ds(2 * h * HS, HS), pl.ds((2 * h + 1) * HS, HS)
        key_full, value_full = kv[:, key_cols], kv[:, value_cols]
        key_rows, value_rows = key_full.astype(jnp.bfloat16), value_full.astype(jnp.bfloat16)
        query = query_ref[:, cols]
        cot = cot_ref[:, cols]
        masked = jnp.where(live, cot, jnp.zeros_like(cot))
        scores = lax.dot_general(key_rows, query, LAST, preferred_element_type=jnp.float32) * scale
        exponent = jnp.exp(scores)
        attention = exponent * (1.0 / jnp.sum(exponent, axis=0, keepdims=True))
        weights_b = attention.astype(jnp.bfloat16)
        att_ref[:, cols] = lax.dot_general(
            weights_b, value_rows, FIRST, preferred_element_type=jnp.float32
        ).astype(jnp.bfloat16)
        back = lax.dot_general(value_rows, masked, LAST, preferred_element_type=jnp.float32)
        mean = jnp.sum(attention * back, axis=0, keepdims=True)
        score_grad = (attention * (back - mean) * scale).astype(jnp.bfloat16)
        key_grad = jnp.dot(score_grad, query, preferred_element_type=jnp.float32)
        value_grad = jnp.dot(weights_b, masked, preferred_element_type=jnp.float32)
        key_grad, value_grad = key_grad.astype(jnp.bfloat16), value_grad.astype(jnp.bfloat16)
        kv_grad[:, key_cols] = key_grad
        kv_grad[:, value_cols] = value_grad
        here = jnp.sum(
            key_grad.astype(jnp.float32) * key_full + value_grad.astype(jnp.float32) * value_full,
            axis=1,
            keepdims=True,
        )
        row_part = here if row_part is None else row_part + here
    row_ref[...] = jnp.transpose(jnp.broadcast_to(row_part, (tokens, 128)))[0:1, :]

    grad = kv_grad[...]
    tile = half // 4
    for t in range(4):
        rows = pl.ds(pl.multiple_of((1 - me) * half + t * tile, tile), tile)
        sib_ref[:, pl.ds(t * tile, tile)] = lax.dot_general(
            grad, weight[rows, :], LAST, preferred_element_type=jnp.float32
        ).astype(jnp.bfloat16)
    for t in range(4):
        rows = pl.ds(pl.multiple_of(me * half + t * tile, tile), tile)
        own_ref[:, pl.ds(t * tile, tile)] = lax.dot_general(
            grad, weight[rows, :], LAST, preferred_element_type=jnp.float32
        )


def chip_kernel(parts, own_ref, sib_ref, kept_ref, *big_refs):
    feats = kept_ref.shape[1]
    section = lax.axis_index("section")
    for k in range(parts):
        at = pl.multiple_of(partner(section, k, parts) * feats, feats)
        total = own_ref[:, pl.ds(at, feats)] + sib_ref[:, pl.ds(at, feats)].astype(jnp.float32)
        if k == 0:
            kept_ref[...] = total
        else:
            big_refs[k - 1][...] = total.astype(jnp.bfloat16)


def gain_kernel(parts, row_ref, row_sib_ref, inv_ref, *refs):
    chunk_refs, total_refs, small_refs = refs[:parts], refs[parts : 2 * parts], refs[2 * parts :]
    feats = chunk_refs[0].shape[1]
    inv_rms = inv_ref[...]
    row = row_ref[...] + row_sib_ref[...]
    for k in range(parts):
        normed = chunk_refs[k][...].astype(jnp.float32) * inv_rms
        total = total_refs[k][...].astype(jnp.float32)
        small_refs[k][:, pl.ds(0, feats)] = jnp.sum(total * normed, axis=0, keepdims=True)
        small_refs[k][:, pl.ds(feats, row.shape[1])] = row


def last_kernel(parts, width, kept_ref, *refs):
    big_refs = refs[: parts - 1]
    chunk_ref, inv_ref, gain_ref, row_ref, enc_ref = refs[parts - 1 :]
    tokens, feats = chunk_ref.shape
    grad = kept_ref[...]
    for ref in big_refs:
        grad = grad + ref[...].astype(jnp.float32)
    inv_rms = inv_ref[...]
    me = lax.axis_index("sec") * parts + lax.axis_index("section")
    at = pl.multiple_of(me * feats, feats)
    gain = gain_ref[:, pl.ds(at, feats)]
    normed = chunk_ref[...].astype(jnp.float32) * inv_rms
    row_dot = jnp.transpose(jnp.broadcast_to(row_ref[...], (128, tokens)))[:, 0:1]
    enc_ref[...] = (inv_rms * (gain * grad - normed * (row_dot / width))).astype(jnp.bfloat16)


def per_device(sizes, enc_states, norm_gain, kv_weight, queries, attn_cotangent, target_lengths):
    cores, parts, seqs = sizes
    rows = enc_states[0]
    tokens, feats = rows.shape
    weight = kv_weight[0]
    width = weight.shape[0]
    half = width // 2
    query, cot = queries[0, 0], attn_cotangent[0, 0]
    dec = query.shape[0]
    heads = query.shape[1] // HS
    gain = norm_gain.reshape(1, width)
    swap = [(0, 1), (1, 0)]

    def to_section(x, step):
        return lax.ppermute(x, "section", [(i, partner(i, step, parts)) for i in range(parts)])

    def to_core(x):
        return lax.ppermute(x, "sec", swap)

    square = pl.pallas_call(
        first_kernel,
        out_shape=jax.ShapeDtypeStruct((tokens, 1), jnp.float32),
        in_specs=[VMEM, ANY],
        out_specs=VMEM,
        compiler_params=pltpu.CompilerParams(vmem_limit_bytes=16 << 20),
        cost_estimate=pl.CostEstimate(
            flops=20_000_000_000, bytes_accessed=2 * rows.size, transcendentals=0
        ),
        name="first",
    )(rows, weight)
    flops = 2 * tokens * width * weight.shape[1]
    chunks = [rows]
    for k in range(1, parts):
        chunks.append(lax.optimization_barrier((to_section(rows, k), square))[0])
    others = [to_core(c) for c in chunks]
    att, sib, own, inv_rms, row = pl.pallas_call(
        functools.partial(main_kernel, parts, heads),
        out_shape=(
            jax.ShapeDtypeStruct(query.shape, jnp.bfloat16),
            jax.ShapeDtypeStruct((tokens, half), jnp.bfloat16),
            jax.ShapeDtypeStruct((tokens, half), jnp.float32),
            jax.ShapeDtypeStruct((tokens, 1), jnp.float32),
            jax.ShapeDtypeStruct((1, tokens), jnp.float32),
        ),
        in_specs=[SMEM] + [VMEM] * (1 + 2 * parts) + [VMEM, VMEM, VMEM, VMEM],
        out_specs=(VMEM,) * 5,
        scratch_shapes=[
            pltpu.VMEM((tokens, width), jnp.bfloat16),
            pltpu.VMEM((tokens, weight.shape[1]), jnp.float32),
            pltpu.VMEM((tokens, weight.shape[1]), jnp.bfloat16),
        ],
        compiler_params=pltpu.CompilerParams(vmem_limit_bytes=16 << 20),
        cost_estimate=pl.CostEstimate(
            flops=3 * flops, bytes_accessed=2 * weight.size, transcendentals=dec * tokens * heads
        ),
        name="main",
    )(target_lengths, square, *chunks, *others, gain, weight, query, cot)

    row_sib = to_core(row)
    sib_in = to_core(sib)

    kept, *big = pl.pallas_call(
        functools.partial(chip_kernel, parts),
        out_shape=(jax.ShapeDtypeStruct((tokens, feats), jnp.float32),)
        + (jax.ShapeDtypeStruct((tokens, feats), jnp.bfloat16),) * (parts - 1),
        in_specs=[VMEM] * 2,
        out_specs=(VMEM,) * parts,
        compiler_params=pltpu.CompilerParams(vmem_limit_bytes=16 << 20),
        cost_estimate=pl.CostEstimate(
            flops=2 * tokens * half, bytes_accessed=8 * tokens * half, transcendentals=0
        ),
        name="chip",
    )(own, sib_in)
    small = pl.pallas_call(
        functools.partial(gain_kernel, parts),
        out_shape=(jax.ShapeDtypeStruct((1, feats + tokens), jnp.float32),) * parts,
        in_specs=[VMEM] * (3 + 2 * parts),
        out_specs=(VMEM,) * parts,
        compiler_params=pltpu.CompilerParams(vmem_limit_bytes=16 << 20),
        cost_estimate=pl.CostEstimate(
            flops=20_000_000_000, bytes_accessed=8 * tokens * half, transcendentals=0
        ),
        name="gain",
    )(row, row_sib, inv_rms, *chunks, kept, *big)

    big_in = [to_section(big[k - 1], k) for k in range(1, parts)]
    gain_row = direct_sum(small, "section", parts)
    gain_term, row_dot = gain_row[0, :feats], gain_row[:, feats:]
    enc_grad = pl.pallas_call(
        functools.partial(last_kernel, parts, width),
        out_shape=jax.ShapeDtypeStruct((tokens, feats), jnp.bfloat16),
        in_specs=[VMEM] * (4 + parts),
        out_specs=VMEM,
        compiler_params=pltpu.CompilerParams(vmem_limit_bytes=8 << 20),
        cost_estimate=pl.CostEstimate(
            flops=10 * tokens * feats, bytes_accessed=16 * tokens * feats, transcendentals=0
        ),
        name="last",
    )(kept, *big_in, rows, inv_rms, gain, row_dot)
    if seqs <= 8:
        piece = feats // seqs
        dp = lax.axis_index("dp")
        owned = [
            lax.dynamic_slice_in_dim(gain_term, partner(dp, k, seqs) * piece, piece, 0)
            for k in range(seqs)
        ]
        came = [
            lax.ppermute(owned[k], "dp", [(i, partner(i, k, seqs)) for i in range(seqs)])
            for k in reversed(range(1, seqs))
        ]
        enc_grad, first = lax.optimization_barrier((enc_grad, owned[0]))
        gain_grad = tree_sum([first] + came)
    else:
        gain_grad = lax.psum_scatter(gain_term, "dp", scatter_dimension=0, tiled=True)
    return (att[None, None], enc_grad[None], gain_grad, row_dot)


def solution(mesh):
    sizes = tuple(mesh.shape[a] for a in ("sec", "section", "dp"))
    placed = (
        P("dp", None, ("sec", "section")),
        P(),
        P("sec", None, "section"),
        P("sec", "dp", None, "section"),
        P("sec", "dp", None, "section"),
        P("dp"),
    )
    return jax.shard_map(
        functools.partial(per_device, sizes),
        mesh=mesh,
        in_specs=placed,
        out_specs=(
            P("sec", "dp", None, "section"),
            P("dp", None, ("sec", "section")),
            P(("sec", "section", "dp")),
            P("dp", None),
        ),
        check_vma=False,
    )
```

time: 50 us -> 37.2 us (0.74)
  waiting for transfers between devices: 15 us -> 5.2 us
  local copies, waits for them, and re-layouts: 7.02 us -> 4.37 us
  Pallas kernels: 8.56 us -> 7.16 us
  starting transfers between devices: 17.1 us -> 18.4 us
    ppermute x9 -> x6, waiting for transfers between devices: 11.8 us -> 1.58 us  [to_section(): lax.ppermute(x, 'section', [(i, partner(i, step, parts)) for i in range(p...]
    ppermute x0 -> x3, starting transfers between devices: none -> 3.55 us  [direct_sum(): lax.ppermute(terms[k], axis, perms[k])]
    ppermute x9 -> x6, starting transfers between devices: 11.6 us -> 8.04 us  [to_section(): lax.ppermute(x, 'section', [(i, partner(i, step, parts)) for i in range(p...]
    unnamed x16 -> x14, local copies, waits for them, and re-layouts: 6.91 us -> 4.35 us
    pallas_call x1, Pallas kernels: 6.83 us -> 5.82 us  [per_device(): pl.pallas_call(functools.partial(main_kernel, parts, heads), out_shape=(j...]
    ppermute x3, starting transfers between devices: 4.45 us -> 5.24 us  [per_device(): lax.ppermute(owned[k], 'dp', [(i, partner(i, k, seqs)) for i in range(seq...]
    pallas_call x1, Pallas kernels: 0.86 us -> 0.1 us  [per_device(): pl.pallas_call(functools.partial(chip_kernel, parts), out_shape=(jax.Shap...]
  transfers between devices with their start and end apart: 18 -> 18, of which waited for: 11 -> 6; matrix products, arithmetic and copies ran while one was open for 1% -> 0% of each run, Pallas kernels for 0% -> 3%
where the time goes in v2:
time: 37.2 us; the launch traced here: 37 us
  starting transfers between devices  18.4 us (49%)
  Pallas kernels  7.16 us (19%)
  waiting for transfers between devices  5.2 us (14%)
  local copies, waits for them, and re-layouts  4.37 us (12%)
  between operations  1.38 us (4%)
  other arithmetic  0.52 us (1%)
    ppermute x6, starting transfers between devices, to_section(): lax.ppermute(x, 'section', [(i, partner(i, step, parts)) for i in range(p...  8.04 us
    pallas_call x1, Pallas kernels, per_device(): pl.pallas_call(functools.partial(main_kernel, parts, heads), out_shape=(j...  5.82 us
    ppermute x3, starting transfers between devices, per_device(): lax.ppermute(owned[k], 'dp', [(i, partner(i, k, seqs)) for i in range(seq...  5.24 us
    unnamed x14, local copies, waits for them, and re-layouts  4.35 us
    ppermute x3, starting transfers between devices, direct_sum(): lax.ppermute(terms[k], axis, perms[k])  3.55 us
    ppermute x3, waiting for transfers between devices, per_device(): lax.ppermute(owned[k], 'dp', [(i, partner(i, k, seqs)) for i in range(seq...  1.86 us
    ppermute x6, waiting for transfers between devices, to_core(): return lax.ppermute(x, 'sec', swap)  1.76 us
    ppermute x6, waiting for transfers between devices, to_section(): lax.ppermute(x, 'section', [(i, partner(i, step, parts)) for i in range(p...  1.58 us
  transfers between devices with their start and end apart: 18, of which 6 were waited for; matrix products, arithmetic and copies ran while one was open for 0% of the time, Pallas kernels for 3%

profile of v2, /device:TPU:0, one launch (start us, length us, event | category | flops | bytes accessed | tf_op | source)
XLA Modules:
  0.0 37.0 jit_solution(15063986737458736883)
XLA Ops:
  0.6 3.0 %collective-permute-start = (bf16[128,512]{1,0:T(8,128)(2,1)}, bf16[128,512]{1,0:T(8,128)(2,1)S(1)}, u32[]{:S(2)}, u32[]{:S(2)}) collective-permute-start(bf16[128,512]{1,0:T(8,128)(2,1)} %bitcast.15), channel_id=1, source_target_pairs={{0,4},{4,0},{8,12},{12,8},{1,5},{5,1},{9,13},{13,9},{2,6},{6,2},{1... | collective-permute-start | bytes 393224 | tf_op jit(solution)/shard_map/ppermute | solution.py:172
  3.6 1.5 %collective-permute-start.1 = (bf16[128,512]{1,0:T(8,128)(2,1)}, bf16[128,512]{1,0:T(8,128)(2,1)S(1)}, u32[]{:S(2)}, u32[]{:S(2)}) collective-permute-start(bf16[128,512]{1,0:T(8,128)(2,1)} %bitcast.16), channel_id=1, source_target_pairs={{0,8},{4,12},{8,0},{12,4},{1,9},{5,13},{9,1},{13,5},{2,10},{6,14},... | collective-permute-start | bytes 393224 | tf_op jit(solution)/shard_map/ppermute | solution.py:172
  5.2 0.0 collective-permute-start.2
  5.2 0.0 collective-permute-start.3
  5.2 0.9 %copy-done = bf16[1,128,512]{2,1,0:T(8,128)(2,1)S(1)} copy-done((bf16[1,128,512]{2,1,0:T(8,128)(2,1)S(1)}, bf16[1,128,512]{2,1,0:T(8,128)(2,1)}, u32[]{:S(2)}) %copy-start) | copy-done | bytes 131096
  6.1 3.4 %copy-done.4 = bf16[1,4096,1024]{2,1,0:T(8,128)(2,1)S(1)} copy-done((bf16[1,4096,1024]{2,1,0:T(8,128)(2,1)S(1)}, bf16[1,4096,1024]{2,1,0:T(8,128)(2,1)}, u32[]{:S(2)}) %copy-start.4) | copy-done | bytes 8388632
  9.5 0.1 first.1.square_ref
  9.6 0.0 copy-start.1
  9.6 0.0 collective-permute-done.refs_1_
  9.6 0.5 %collective-permute-start.4 = (bf16[128,512]{1,0:T(8,128)(2,1)S(1)}, bf16[128,512]{1,0:T(8,128)(2,1)S(1)}, u32[]{:S(2)}, u32[]{:S(2)}) collective-permute-start(bf16[128,512]{1,0:T(8,128)(2,1)S(1)} %collective-permute-done.refs_1_), channel_id=1, source_target_pairs={{0,16},{16,0},{1,17},{17,1},{2,18},{18,2},{3,19},{19,3},{4,20},{20... | collective-permute-start | bytes 393224 | tf_op jit(solution)/shard_map/ppermute | solution.py:175
  10.2 1.4 %collective-permute-done.1.refs_2_ = bf16[128,512]{1,0:T(8,128)(2,1)S(1)} collective-permute-done((bf16[128,512]{1,0:T(8,128)(2,1)}, bf16[128,512]{1,0:T(8,128)(2,1)S(1)}, u32[]{:S(2)}, u32[]{:S(2)}) %collective-permute-start.1) | collective-permute-done | bytes 131104 | tf_op jit(solution)/shard_map/ppermute | solution.py:172
  11.6 0.0 collective-permute-start.5
  11.6 0.0 collective-permute-done.2.refs_3_
  11.6 0.5 %collective-permute-start.6 = (bf16[128,512]{1,0:T(8,128)(2,1)S(1)}, bf16[128,512]{1,0:T(8,128)(2,1)S(1)}, u32[]{:S(2)}, u32[]{:S(2)}) collective-permute-start(bf16[128,512]{1,0:T(8,128)(2,1)S(1)} %collective-permute-done.2.refs_3_), channel_id=1, source_target_pairs={{0,16},{16,0},{1,17},{17,1},{2,18},{18,2},{3,19},{19,3},{4,20},{20... | collective-permute-start | bytes 393224 | tf_op jit(solution)/shard_map/ppermute | solution.py:175
  12.8 0.0 collective-permute-done.3.refs_4_
  12.8 0.0 collective-permute-done.4.refs_5_
  12.8 0.2 collective-permute-done.5.refs_6_
  13.0 0.2 collective-permute-done.6.refs_7_
  13.2 0.0 copy-done.2
  13.2 0.0 copy-done.5
  13.2 0.0 copy-done.6
  13.2 5.8 %main.1 = (bf16[256,512]{1,0:T(8,128)(2,1)}, bf16[128,2048]{1,0:T(8,128)(2,1)S(1)}, f32[128,2048]{1,0:T(8,128)S(1)}, f32[128,1]{1,0:T(8,128)S(1)}, f32[1,128]{1,0:T(1,128)S(1)}) custom-call(s32[1]{0:T(128)S(6)} %copy.10.length_ref, f32[128,1]{1,0:T(8,128)S(1)} %first.1.square_ref, bf16[128,512]{1,0:T(8,128)(2,1)S(1)} %bitcast.20, ...), custom_call_target="tpu_custom_call" | custom-call | flops 3221225472 | bytes 8388608 | tf_op jit(solution)/shard_map/main/pallas_call | solution.py:193
  19.0 0.3 collective-permute-start.7
  19.3 0.2 collective-permute-start.11
  19.5 1.4 %collective-permute-done.7.sib_ref = bf16[128,2048]{1,0:T(8,128)(2,1)S(1)} collective-permute-done((bf16[128,2048]{1,0:T(8,128)(2,1)S(1)}, bf16[128,2048]{1,0:T(8,128)(2,1)S(1)}, u32[]{:S(2)}, u32[]{:S(2)}) %collective-permute-start.7) | collective-permute-done | bytes 524320 | tf_op jit(solution)/shard_map/ppermute | solution.py:175
  20.9 0.1 chip.1
  21.0 0.0 collective-permute-done.11.row_sib_ref
  21.0 0.3 gain.1
  21.3 1.1 %collective-permute-start.12 = (f32[1,640]{1,0:T(1,128)S(1)}, f32[1,640]{1,0:T(1,128)S(1)}, u32[]{:S(2)}, u32[]{:S(2)}) collective-permute-start(f32[1,640]{1,0:T(1,128)S(1)} %get-tuple-element.35), channel_id=1, source_target_pairs={{0,4},{4,0},{8,12},{12,8},{1,5},{5,1},{9,13},{13,9},{2,6},{6,2},{1... | collective-permute-start | bytes 7688 | tf_op jit(solution)/shard_map/ppermute | solution.py:31
  22.4 1.0 %collective-permute-start.13 = (f32[1,640]{1,0:T(1,128)S(1)}, f32[1,640]{1,0:T(1,128)S(1)}, u32[]{:S(2)}, u32[]{:S(2)}) collective-permute-start(f32[1,640]{1,0:T(1,128)S(1)} %get-tuple-element.36), channel_id=1, source_target_pairs={{0,8},{4,12},{8,0},{12,4},{1,9},{5,13},{9,1},{13,5},{2,10},{6,14},... | collective-permute-start | bytes 7688 | tf_op jit(solution)/shard_map/ppermute | solution.py:31
  23.4 1.4 %collective-permute-start.14 = (f32[1,640]{1,0:T(1,128)S(1)}, f32[1,640]{1,0:T(1,128)S(1)}, u32[]{:S(2)}, u32[]{:S(2)}) collective-permute-start(f32[1,640]{1,0:T(1,128)S(1)} %get-tuple-element.37), channel_id=1, source_target_pairs={{0,12},{4,8},{8,4},{12,0},{1,13},{5,9},{9,5},{13,1},{2,14},{6,10},... | collective-permute-start | bytes 7688 | tf_op jit(solution)/shard_map/ppermute | solution.py:31
  24.8 1.5 %collective-permute-start.10 = (bf16[128,512]{1,0:T(8,128)(2,1)S(1)}, bf16[128,512]{1,0:T(8,128)(2,1)S(1)}, u32[]{:S(2)}, u32[]{:S(2)}) collective-permute-start(bf16[128,512]{1,0:T(8,128)(2,1)S(1)} %get-tuple-element.31.refs_7_), channel_id=1, source_target_pairs={{0,12},{4,8},{8,4},{12,0},{1,13},{5,9},{9,5},{13,1},{2,14},{6,10},... | collective-permute-start | bytes 393224 | tf_op jit(solution)/shard_map/ppermute | solution.py:172
  26.3 1.5 %collective-permute-start.8 = (bf16[128,512]{1,0:T(8,128)(2,1)S(1)}, bf16[128,512]{1,0:T(8,128)(2,1)S(1)}, u32[]{:S(2)}, u32[]{:S(2)}) collective-permute-start(bf16[128,512]{1,0:T(8,128)(2,1)S(1)} %get-tuple-element.29.refs_5_), channel_id=1, source_target_pairs={{0,4},{4,0},{8,12},{12,8},{1,5},{5,1},{9,13},{13,9},{2,6},{6,2},{1... | collective-permute-start | bytes 393224 | tf_op jit(solution)/shard_map/ppermute | solution.py:172
  27.8 0.0 collective-permute-done.12
  27.8 0.5 %collective-permute-start.9 = (bf16[128,512]{1,0:T(8,128)(2,1)S(1)}, bf16[128,512]{1,0:T(8,128)(2,1)S(1)}, u32[]{:S(2)}, u32[]{:S(2)}) collective-permute-start(bf16[128,512]{1,0:T(8,128)(2,1)S(1)} %get-tuple-element.30.refs_6_), channel_id=1, source_target_pairs={{0,8},{4,12},{8,0},{12,4},{1,9},{5,13},{9,1},{13,5},{2,10},{6,14},... | collective-permute-start | bytes 393224 | tf_op jit(solution)/shard_map/ppermute | solution.py:172
  28.3 0.0 collective-permute-done.13
  28.3 0.0 collective-permute-done.14
  28.4 3.7 %collective-permute-start.15 = (f32[128]{0:T(128)S(1)}, f32[128]{0:T(128)S(1)}, u32[]{:S(2)}, u32[]{:S(2)}) collective-permute-start(f32[128]{0:T(128)S(1)} %get-tuple-element.40), channel_id=1, source_target_pairs={{0,3},{1,2},{2,1},{3,0},{4,7},{5,6},{6,5},{7,4},{8,11},{9,10},{10,... | collective-permute-start | bytes 1544 | tf_op jit(solution)/shard_map/ppermute | solution.py:265
  32.1 0.0 collective-permute-start.16
  32.1 0.1 collective-permute-done.10.refs_2_
  32.2 1.6 %collective-permute-start.17 = (f32[128]{0:T(128)S(1)}, f32[128]{0:T(128)S(1)}, u32[]{:S(2)}, u32[]{:S(2)}) collective-permute-start(f32[128]{0:T(128)S(1)} %get-tuple-element.41), channel_id=1, source_target_pairs={{0,1},{1,0},{2,3},{3,2},{4,5},{5,4},{6,7},{7,6},{8,9},{9,8},{10,11... | collective-permute-start | bytes 1544 | tf_op jit(solution)/shard_map/ppermute | solution.py:265
  33.8 0.0 collective-permute-done.8.refs_0_
  33.8 0.0 collective-permute-done.9.refs_1_
  33.8 0.9 %last.1 = bf16[128,512]{1,0:T(8,128)(2,1)} custom-call(f32[128,512]{1,0:T(8,128)S(1)} %get-tuple-element.28.refs_4_.kept_ref, bf16[128,512]{1,0:T(8,128)(2,1)S(1)} %collective-permute-done.8.refs_0_, bf16[128,512]{1,0:T(8,128)(2,1)S(1)} %collective-permute-done.9.refs_1_, bf16[128,512]{1,0:T(8,128)(2,1)S(1)} %collective-permute-done.10.refs_2_, ...), custom_call_target="tpu_custom_call" | custom-call | flops 655360 | bytes 1048576 | tf_op jit(solution)/shard_map/last/pallas_call | solution.py:246
  34.6 0.0 collective-permute-done.15
  34.6 1.9 %collective-permute-done.16 = f32[128]{0:T(128)S(1)} collective-permute-done((f32[128]{0:T(128)S(1)}, f32[128]{0:T(128)S(1)}, u32[]{:S(2)}, u32[]{:S(2)}) %collective-permute-start.16) | collective-permute-done | bytes 544 | tf_op jit(solution)/shard_map/ppermute | solution.py:265
  36.5 0.0 collective-permute-done.17
  36.5 0.5 %add_add_fusion.1 = f32[128]{0:T(128)} fusion(f32[128]{0:T(128)S(1)} %collective-permute-done.16, f32[128]{0:T(128)S(1)} %collective-permute-done.17, f32[128]{0:T(128)S(1)} %get-tuple-element.39, f32[128]{0:T(128)S(1)} %collective-permute-done.15), kind=kLoop, calls=%fused_computation.9 | loop fusion | flops 384 | bytes 2560 | tf_op jit(solution)/shard_map/add | solution.py:25
  (12 shorter events, 0.0 us)
Async XLA Ops:
  0.6 9.0 %collective-permute-start = (bf16[128,512]{1,0:T(8,128)(2,1)}, bf16[128,512]{1,0:T(8,128)(2,1)S(1)}, u32[]{:S(2)}, u32[]{:S(2)}) collective-permute-start(bf16[128,512]{1,0:T(8,128)(2,1)} %bitcast.15), channel_id=1, source_target_pairs={{0,4},{4,0},{8,12},{12,8},{1,5},{5,1},{9,13},{13,9},{2,6},{6,2},{1... | collective-permute-start | bytes 393224 | tf_op jit(solution)/shard_map/ppermute | solution.py:172
  3.6 8.0 %collective-permute-start.1 = (bf16[128,512]{1,0:T(8,128)(2,1)}, bf16[128,512]{1,0:T(8,128)(2,1)S(1)}, u32[]{:S(2)}, u32[]{:S(2)}) collective-permute-start(bf16[128,512]{1,0:T(8,128)(2,1)} %bitcast.16), channel_id=1, source_target_pairs={{0,8},{4,12},{8,0},{12,4},{1,9},{5,13},{9,1},{13,5},{2,10},{6,14},... | collective-permute-start | bytes 393224 | tf_op jit(solution)/shard_map/ppermute | solution.py:172
  5.2 6.5 %collective-permute-start.2 = (bf16[128,512]{1,0:T(8,128)(2,1)}, bf16[128,512]{1,0:T(8,128)(2,1)S(1)}, u32[]{:S(2)}, u32[]{:S(2)}) collective-permute-start(bf16[128,512]{1,0:T(8,128)(2,1)} %bitcast.17), channel_id=1, source_target_pairs={{0,12},{4,8},{8,4},{12,0},{1,13},{5,9},{9,5},{13,1},{2,14},{6,10},... | collective-permute-start | bytes 393224 | tf_op jit(solution)/shard_map/ppermute | solution.py:172
  5.2 7.6 %collective-permute-start.3 = (bf16[128,512]{1,0:T(8,128)(2,1)}, bf16[128,512]{1,0:T(8,128)(2,1)S(1)}, u32[]{:S(2)}, u32[]{:S(2)}) collective-permute-start(bf16[128,512]{1,0:T(8,128)(2,1)} %bitcast.18), channel_id=1, source_target_pairs={{0,16},{16,0},{1,17},{17,1},{2,18},{18,2},{3,19},{19,3},{4,20},{20... | collective-permute-start | bytes 393224 | tf_op jit(solution)/shard_map/ppermute | solution.py:175
  5.2 0.9 %copy-start = (bf16[1,128,512]{2,1,0:T(8,128)(2,1)S(1)}, bf16[1,128,512]{2,1,0:T(8,128)(2,1)}, u32[]{:S(2)}) copy-start(bf16[1,128,512]{2,1,0:T(8,128)(2,1)} %param.6) | copy-start | bytes 393220
  6.1 3.4 %copy-start.4 = (bf16[1,4096,1024]{2,1,0:T(8,128)(2,1)S(1)}, bf16[1,4096,1024]{2,1,0:T(8,128)(2,1)}, u32[]{:S(2)}) copy-start(bf16[1,4096,1024]{2,1,0:T(8,128)(2,1)} %param.8) | copy-start | bytes 25165828
  9.5 3.7 %copy-start.2 = (f32[4096]{0:T(1024)S(1)}, f32[4096]{0:T(1024)}, u32[]{:S(2)}) copy-start(f32[4096]{0:T(1024)} %param.7) | copy-start | bytes 49156
  9.5 3.7 %copy-start.5 = (bf16[1,1,256,512]{3,2,1,0:T(8,128)(2,1)S(1)}, bf16[1,1,256,512]{3,2,1,0:T(8,128)(2,1)}, u32[]{:S(2)}) copy-start(bf16[1,1,256,512]{3,2,1,0:T(8,128)(2,1)} %param.9) | copy-start | bytes 786436
  9.5 3.7 %copy-start.6 = (bf16[1,1,256,512]{3,2,1,0:T(8,128)(2,1)S(1)}, bf16[1,1,256,512]{3,2,1,0:T(8,128)(2,1)}, u32[]{:S(2)}) copy-start(bf16[1,1,256,512]{3,2,1,0:T(8,128)(2,1)} %param.10) | copy-start | bytes 786436
  9.6 11.4 %copy-start.1 = (bf16[1,128,512]{2,1,0:T(8,128)(2,1)S(1)}, bf16[1,128,512]{2,1,0:T(8,128)(2,1)}, u32[]{:S(2)}) copy-start(bf16[1,128,512]{2,1,0:T(8,128)(2,1)} %param.6) | copy-start | bytes 393220
  9.6 3.2 %collective-permute-start.4 = (bf16[128,512]{1,0:T(8,128)(2,1)S(1)}, bf16[128,512]{1,0:T(8,128)(2,1)S(1)}, u32[]{:S(2)}, u32[]{:S(2)}) collective-permute-start(bf16[128,512]{1,0:T(8,128)(2,1)S(1)} %collective-permute-done.refs_1_), channel_id=1, source_target_pairs={{0,16},{16,0},{1,17},{17,1},{2,18},{18,2},{3,19},{19,3},{4,20},{20... | collective-permute-start | bytes 393224 | tf_op jit(solution)/shard_map/ppermute | solution.py:175
  11.6 1.3 %collective-permute-start.5 = (bf16[128,512]{1,0:T(8,128)(2,1)S(1)}, bf16[128,512]{1,0:T(8,128)(2,1)S(1)}, u32[]{:S(2)}, u32[]{:S(2)}) collective-permute-start(bf16[128,512]{1,0:T(8,128)(2,1)S(1)} %collective-permute-done.1.refs_2_), channel_id=1, source_target_pairs={{0,16},{16,0},{1,17},{17,1},{2,18},{18,2},{3,19},{19,3},{4,20},{20... | collective-permute-start | bytes 393224 | tf_op jit(solution)/shard_map/ppermute | solution.py:175
  11.6 1.5 %collective-permute-start.6 = (bf16[128,512]{1,0:T(8,128)(2,1)S(1)}, bf16[128,512]{1,0:T(8,128)(2,1)S(1)}, u32[]{:S(2)}, u32[]{:S(2)}) collective-permute-start(bf16[128,512]{1,0:T(8,128)(2,1)S(1)} %collective-permute-done.2.refs_3_), channel_id=1, source_target_pairs={{0,16},{16,0},{1,17},{17,1},{2,18},{18,2},{3,19},{19,3},{4,20},{20... | collective-permute-start | bytes 393224 | tf_op jit(solution)/shard_map/ppermute | solution.py:175
  19.0 1.9 %collective-permute-start.7 = (bf16[128,2048]{1,0:T(8,128)(2,1)S(1)}, bf16[128,2048]{1,0:T(8,128)(2,1)S(1)}, u32[]{:S(2)}, u32[]{:S(2)}) collective-permute-start(bf16[128,2048]{1,0:T(8,128)(2,1)S(1)} %get-tuple-element.27), channel_id=1, source_target_pairs={{0,16},{16,0},{1,17},{17,1},{2,18},{18,2},{3,19},{19,3},{4,20},{20... | collective-permute-start | bytes 1572872 | tf_op jit(solution)/shard_map/ppermute | solution.py:175
  19.3 1.7 %collective-permute-start.11 = (f32[1,128]{1,0:T(1,128)S(1)}, f32[1,128]{1,0:T(1,128)S(1)}, u32[]{:S(2)}, u32[]{:S(2)}) collective-permute-start(f32[1,128]{1,0:T(1,128)S(1)} %get-tuple-element.33.row_ref), channel_id=1, source_target_pairs={{0,16},{16,0},{1,17},{17,1},{2,18},{18,2},{3,19},{19,3},{4,20},{20... | collective-permute-start | bytes 1544 | tf_op jit(solution)/shard_map/ppermute | solution.py:175
  21.3 6.5 %collective-permute-start.12 = (f32[1,640]{1,0:T(1,128)S(1)}, f32[1,640]{1,0:T(1,128)S(1)}, u32[]{:S(2)}, u32[]{:S(2)}) collective-permute-start(f32[1,640]{1,0:T(1,128)S(1)} %get-tuple-element.35), channel_id=1, source_target_pairs={{0,4},{4,0},{8,12},{12,8},{1,5},{5,1},{9,13},{13,9},{2,6},{6,2},{1... | collective-permute-start | bytes 7688 | tf_op jit(solution)/shard_map/ppermute | solution.py:31
  22.4 5.9 %collective-permute-start.13 = (f32[1,640]{1,0:T(1,128)S(1)}, f32[1,640]{1,0:T(1,128)S(1)}, u32[]{:S(2)}, u32[]{:S(2)}) collective-permute-start(f32[1,640]{1,0:T(1,128)S(1)} %get-tuple-element.36), channel_id=1, source_target_pairs={{0,8},{4,12},{8,0},{12,4},{1,9},{5,13},{9,1},{13,5},{2,10},{6,14},... | collective-permute-start | bytes 7688 | tf_op jit(solution)/shard_map/ppermute | solution.py:31
  23.4 4.9 %collective-permute-start.14 = (f32[1,640]{1,0:T(1,128)S(1)}, f32[1,640]{1,0:T(1,128)S(1)}, u32[]{:S(2)}, u32[]{:S(2)}) collective-permute-start(f32[1,640]{1,0:T(1,128)S(1)} %get-tuple-element.37), channel_id=1, source_target_pairs={{0,12},{4,8},{8,4},{12,0},{1,13},{5,9},{9,5},{13,1},{2,14},{6,10},... | collective-permute-start | bytes 7688 | tf_op jit(solution)/shard_map/ppermute | solution.py:31
  24.8 7.3 %collective-permute-start.10 = (bf16[128,512]{1,0:T(8,128)(2,1)S(1)}, bf16[128,512]{1,0:T(8,128)(2,1)S(1)}, u32[]{:S(2)}, u32[]{:S(2)}) collective-permute-start(bf16[128,512]{1,0:T(8,128)(2,1)S(1)} %get-tuple-element.31.refs_7_), channel_id=1, source_target_pairs={{0,12},{4,8},{8,4},{12,0},{1,13},{5,9},{9,5},{13,1},{2,14},{6,10},... | collective-permute-start | bytes 393224 | tf_op jit(solution)/shard_map/ppermute | solution.py:172
  26.3 7.4 %collective-permute-start.8 = (bf16[128,512]{1,0:T(8,128)(2,1)S(1)}, bf16[128,512]{1,0:T(8,128)(2,1)S(1)}, u32[]{:S(2)}, u32[]{:S(2)}) collective-permute-start(bf16[128,512]{1,0:T(8,128)(2,1)S(1)} %get-tuple-element.29.refs_5_), channel_id=1, source_target_pairs={{0,4},{4,0},{8,12},{12,8},{1,5},{5,1},{9,13},{13,9},{2,6},{6,2},{1... | collective-permute-start | bytes 393224 | tf_op jit(solution)/shard_map/ppermute | solution.py:172
  27.8 5.9 %collective-permute-start.9 = (bf16[128,512]{1,0:T(8,128)(2,1)S(1)}, bf16[128,512]{1,0:T(8,128)(2,1)S(1)}, u32[]{:S(2)}, u32[]{:S(2)}) collective-permute-start(bf16[128,512]{1,0:T(8,128)(2,1)S(1)} %get-tuple-element.30.refs_6_), channel_id=1, source_target_pairs={{0,8},{4,12},{8,0},{12,4},{1,9},{5,13},{9,1},{13,5},{2,10},{6,14},... | collective-permute-start | bytes 393224 | tf_op jit(solution)/shard_map/ppermute | solution.py:172
  28.4 6.2 %collective-permute-start.15 = (f32[128]{0:T(128)S(1)}, f32[128]{0:T(128)S(1)}, u32[]{:S(2)}, u32[]{:S(2)}) collective-permute-start(f32[128]{0:T(128)S(1)} %get-tuple-element.40), channel_id=1, source_target_pairs={{0,3},{1,2},{2,1},{3,0},{4,7},{5,6},{6,5},{7,4},{8,11},{9,10},{10,... | collective-permute-start | bytes 1544 | tf_op jit(solution)/shard_map/ppermute | solution.py:265
  32.1 4.4 %collective-permute-start.16 = (f32[128]{0:T(128)S(1)}, f32[128]{0:T(128)S(1)}, u32[]{:S(2)}, u32[]{:S(2)}) collective-permute-start(f32[128]{0:T(128)S(1)} %get-tuple-element.42), channel_id=1, source_target_pairs={{0,2},{1,3},{2,0},{3,1},{4,6},{5,7},{6,4},{7,5},{8,10},{9,11},{10,... | collective-permute-start | bytes 1544 | tf_op jit(solution)/shard_map/ppermute | solution.py:265
  32.2 4.3 %collective-permute-start.17 = (f32[128]{0:T(128)S(1)}, f32[128]{0:T(128)S(1)}, u32[]{:S(2)}, u32[]{:S(2)}) collective-permute-start(f32[128]{0:T(128)S(1)} %get-tuple-element.41), channel_id=1, source_target_pairs={{0,1},{1,0},{2,3},{3,2},{4,5},{5,4},{6,7},{7,6},{8,9},{9,8},{10,11... | collective-permute-start | bytes 1544 | tf_op jit(solution)/shard_map/ppermute | solution.py:265
  33.8 3.3 %copy-start.3 = (f32[1,128]{1,0:T(1,128)}, f32[1,128]{1,0:T(1,128)S(1)}, u32[]{:S(2)}) copy-start(f32[1,128]{1,0:T(1,128)S(1)} %slice.8.refs_6_) | copy-start | bytes 1540

commit v3 on v2

--- a/solution.py
+++ b/solution.py
@@ -31,16 +31,15 @@
     return tree_sum([terms[0]] + [lax.ppermute(terms[k], axis, perms[k]) for k in range(1, count)])
 
 
-def first_kernel(rows_ref, weight_ref, square_ref):
-    own = rows_ref[...].astype(jnp.float32)
-    square_ref[...] = jnp.sum(own * own, axis=1, keepdims=True)
+def first_kernel(token_ref):
+    token_ref[...] = jnp.zeros_like(token_ref)
 
 
 def main_kernel(
     parts,
     heads,
     length_ref,
-    square_ref,
+    token_ref,
     *refs,
 ):
     chunk_refs = refs[: 2 * parts]
@@ -51,11 +50,12 @@
     width = weight.shape[0]
     half = width // 2
 
-    square = square_ref[...]
-    for ref in chunk_refs[1:]:
+    square = None
+    for ref in chunk_refs:
         x = ref[...].astype(jnp.float32)
-        part = jnp.sum(x * x, axis=1, keepdims=True)
-        square = square + part
+        part = jnp.sum((x * x).reshape(tokens, feats // 128, 128), axis=1)
+        square = part if square is None else square + part
+    square = jnp.sum(square, axis=1, keepdims=True)
     inv_rms = lax.rsqrt(square / width + EPS)
     inv_ref[...] = inv_rms
     me, section = lax.axis_index("sec"), lax.axis_index("section")
@@ -174,21 +174,18 @@
     def to_core(x):
         return lax.ppermute(x, "sec", swap)
 
-    square = pl.pallas_call(
+    token = pl.pallas_call(
         first_kernel,
-        out_shape=jax.ShapeDtypeStruct((tokens, 1), jnp.float32),
-        in_specs=[VMEM, ANY],
+        out_shape=jax.ShapeDtypeStruct((8, 128), jnp.float32),
         out_specs=VMEM,
-        compiler_params=pltpu.CompilerParams(vmem_limit_bytes=16 << 20),
-        cost_estimate=pl.CostEstimate(
-            flops=20_000_000_000, bytes_accessed=2 * rows.size, transcendentals=0
-        ),
+        compiler_params=pltpu.CompilerParams(vmem_limit_bytes=1 << 20),
+        cost_estimate=pl.CostEstimate(flops=20_000_000_000, bytes_accessed=4096, transcendentals=0),
         name="first",
-    )(rows, weight)
+    )()
     flops = 2 * tokens * width * weight.shape[1]
     chunks = [rows]
     for k in range(1, parts):
-        chunks.append(lax.optimization_barrier((to_section(rows, k), square))[0])
+        chunks.append(lax.optimization_barrier((to_section(rows, k), token))[0])
     others = [to_core(c) for c in chunks]
     att, sib, own, inv_rms, row = pl.pallas_call(
         functools.partial(main_kernel, parts, heads),
@@ -199,7 +196,7 @@
             jax.ShapeDtypeStruct((tokens, 1), jnp.float32),
             jax.ShapeDtypeStruct((1, tokens), jnp.float32),
         ),
-        in_specs=[SMEM] + [VMEM] * (1 + 2 * parts) + [VMEM, VMEM, VMEM, VMEM],
+        in_specs=[SMEM, ANY] + [VMEM] * (2 * parts) + [VMEM, VMEM, VMEM, VMEM],
         out_specs=(VMEM,) * 5,
         scratch_shapes=[
             pltpu.VMEM((tokens, width), jnp.bfloat16),
@@ -211,7 +208,7 @@
             flops=3 * flops, bytes_accessed=2 * weight.size, transcendentals=dec * tokens * heads
         ),
         name="main",
-    )(target_lengths, square, *chunks, *others, gain, weight, query, cot)
+    )(target_lengths, token, *chunks, *others, gain, weight, query, cot)
 
     row_sib = to_core(row)
     sib_in = to_core(sib)

time: 37.2 us -> 38.1 us (1.024)
  waiting for transfers between devices: 5.2 us -> 10.2 us
  local copies, waits for them, and re-layouts: 4.37 us -> 0.05 us
  Pallas kernels: 7.16 us -> 7.81 us
  starting transfers between devices: 18.4 us -> 17.9 us
    ppermute x6, waiting for transfers between devices: 1.58 us -> 6.54 us  [to_section(): lax.ppermute(x, 'section', [(i, partner(i, step, parts)) for i in range(p...]
    unnamed x14, local copies, waits for them, and re-layouts: 4.35 us -> 0.03 us
    pallas_call x1, Pallas kernels: 5.82 us -> 6.56 us  [per_device(): pl.pallas_call(functools.partial(main_kernel, parts, heads), out_shape=(j...]
    ppermute x6, starting transfers between devices: 1.55 us -> 1.09 us  [to_core(): return lax.ppermute(x, 'sec', swap)]
  transfers between devices with their start and end apart: 18 -> 18, of which waited for: 6 -> 7; matrix products, arithmetic and copies ran while one was open for 0% -> 0% of each run, Pallas kernels for 3% -> 3%
where the time goes in v3:
time: 38.1 us; the launch traced here: 37.9 us
  starting transfers between devices  17.9 us (47%)
  waiting for transfers between devices  10.2 us (27%)
  Pallas kernels  7.81 us (20%)
  between operations  1.44 us (4%)
  other arithmetic  0.52 us (1%)
    ppermute x6, starting transfers between devices, to_section(): lax.ppermute(x, 'section', [(i, partner(i, step, parts)) for i in range(p...  8.03 us
    pallas_call x1, Pallas kernels, per_device(): pl.pallas_call(functools.partial(main_kernel, parts, heads), out_shape=(j...  6.56 us
    ppermute x6, waiting for transfers between devices, to_section(): lax.ppermute(x, 'section', [(i, partner(i, step, parts)) for i in range(p...  6.54 us
    ppermute x3, starting transfers between devices, per_device(): lax.ppermute(owned[k], 'dp', [(i, partner(i, k, seqs)) for i in range(seq...  5.26 us
    ppermute x3, starting transfers between devices, direct_sum(): lax.ppermute(terms[k], axis, perms[k])  3.55 us
    ppermute x3, waiting for transfers between devices, per_device(): lax.ppermute(owned[k], 'dp', [(i, partner(i, k, seqs)) for i in range(seq...  1.86 us
    ppermute x6, waiting for transfers between devices, to_core(): return lax.ppermute(x, 'sec', swap)  1.76 us
    ppermute x6, starting transfers between devices, to_core(): return lax.ppermute(x, 'sec', swap)  1.09 us
  transfers between devices with their start and end apart: 18, of which 7 were waited for; matrix products, arithmetic and copies ran while one was open for 0% of the time, Pallas kernels for 3%

profile of v3, /device:TPU:0, one launch (start us, length us, event | category | flops | bytes accessed | tf_op | source)
XLA Modules:
  0.0 37.9 jit_solution(265492890408250028)
XLA Ops:
  0.6 0.0 slice-start
  0.6 0.0 copy-start
  0.7 0.0 copy-start.1
  0.7 0.0 slice-start.1
  0.7 0.0 copy-start.3
  0.7 0.0 copy-start.4
  0.7 3.0 %collective-permute-start = (bf16[128,512]{1,0:T(8,128)(2,1)}, bf16[128,512]{1,0:T(8,128)(2,1)S(1)}, u32[]{:S(2)}, u32[]{:S(2)}) collective-permute-start(bf16[128,512]{1,0:T(8,128)(2,1)} %bitcast.15), channel_id=1, source_target_pairs={{0,4},{4,0},{8,12},{12,8},{1,5},{5,1},{9,13},{13,9},{2,6},{6,2},{1... | collective-permute-start | bytes 393224 | tf_op jit(solution)/shard_map/ppermute | solution.py:172
  3.7 1.5 %collective-permute-start.1 = (bf16[128,512]{1,0:T(8,128)(2,1)}, bf16[128,512]{1,0:T(8,128)(2,1)S(1)}, u32[]{:S(2)}, u32[]{:S(2)}) collective-permute-start(bf16[128,512]{1,0:T(8,128)(2,1)} %bitcast.16), channel_id=1, source_target_pairs={{0,8},{4,12},{8,0},{12,4},{1,9},{5,13},{9,1},{13,5},{2,10},{6,14},... | collective-permute-start | bytes 393224 | tf_op jit(solution)/shard_map/ppermute | solution.py:172
  5.2 0.0 collective-permute-start.2
  5.2 0.0 collective-permute-start.3
  5.2 2.7 %collective-permute-done.refs_1_ = bf16[128,512]{1,0:T(8,128)(2,1)S(1)} collective-permute-done((bf16[128,512]{1,0:T(8,128)(2,1)}, bf16[128,512]{1,0:T(8,128)(2,1)S(1)}, u32[]{:S(2)}, u32[]{:S(2)}) %collective-permute-start) | collective-permute-done | bytes 131104 | tf_op jit(solution)/shard_map/ppermute | solution.py:172
  7.9 0.0 collective-permute-start.4
  7.9 3.8 %collective-permute-done.1.refs_2_ = bf16[128,512]{1,0:T(8,128)(2,1)S(1)} collective-permute-done((bf16[128,512]{1,0:T(8,128)(2,1)}, bf16[128,512]{1,0:T(8,128)(2,1)S(1)}, u32[]{:S(2)}, u32[]{:S(2)}) %collective-permute-start.1) | collective-permute-done | bytes 131104 | tf_op jit(solution)/shard_map/ppermute | solution.py:172
  11.7 0.0 collective-permute-start.5
  11.7 0.0 collective-permute-done.2.refs_3_
  11.7 0.5 %collective-permute-start.6 = (bf16[128,512]{1,0:T(8,128)(2,1)S(1)}, bf16[128,512]{1,0:T(8,128)(2,1)S(1)}, u32[]{:S(2)}, u32[]{:S(2)}) collective-permute-start(bf16[128,512]{1,0:T(8,128)(2,1)S(1)} %collective-permute-done.2.refs_3_), channel_id=1, source_target_pairs={{0,16},{16,0},{1,17},{17,1},{2,18},{18,2},{3,19},{19,3},{4,20},{20... | collective-permute-start | bytes 393224 | tf_op jit(solution)/shard_map/ppermute | solution.py:175
  12.9 0.0 collective-permute-done.3.refs_4_
  12.9 0.0 collective-permute-done.4.refs_5_
  12.9 0.2 collective-permute-done.5.refs_6_
  13.0 0.2 collective-permute-done.6.refs_7_
  13.2 0.0 slice-done
  13.3 6.6 %main.1 = (bf16[256,512]{1,0:T(8,128)(2,1)}, bf16[128,2048]{1,0:T(8,128)(2,1)S(1)}, f32[128,2048]{1,0:T(8,128)S(1)}, f32[128,1]{1,0:T(8,128)S(1)}, f32[1,128]{1,0:T(1,128)S(1)}) custom-call(s32[1]{0:T(128)S(6)} %copy.10.length_ref, f32[8,128]{1,0:T(8,128)S(1)} %first.1.token_ref, bf16[128,512]{1,0:T(8,128)(2,1)S(1)} %bitcast.19, ...), custom_call_target="tpu_custom_call" | custom-call | flops 3221225472 | bytes 8388608 | tf_op jit(solution)/shard_map/main/pallas_call | solution.py:190
  19.8 0.4 collective-permute-start.7
  20.2 0.2 collective-permute-start.11
  20.4 1.4 %collective-permute-done.7.sib_ref = bf16[128,2048]{1,0:T(8,128)(2,1)S(1)} collective-permute-done((bf16[128,2048]{1,0:T(8,128)(2,1)S(1)}, bf16[128,2048]{1,0:T(8,128)(2,1)S(1)}, u32[]{:S(2)}, u32[]{:S(2)}) %collective-permute-start.7) | collective-permute-done | bytes 524320 | tf_op jit(solution)/shard_map/ppermute | solution.py:175
  21.8 0.1 chip.1
  21.9 0.0 collective-permute-done.11.row_sib_ref
  21.9 0.3 gain.1
  22.2 1.1 %collective-permute-start.12 = (f32[1,640]{1,0:T(1,128)S(1)}, f32[1,640]{1,0:T(1,128)S(1)}, u32[]{:S(2)}, u32[]{:S(2)}) collective-permute-start(f32[1,640]{1,0:T(1,128)S(1)} %get-tuple-element.35), channel_id=1, source_target_pairs={{0,4},{4,0},{8,12},{12,8},{1,5},{5,1},{9,13},{13,9},{2,6},{6,2},{1... | collective-permute-start | bytes 7688 | tf_op jit(solution)/shard_map/ppermute | solution.py:31
  23.3 1.0 %collective-permute-start.13 = (f32[1,640]{1,0:T(1,128)S(1)}, f32[1,640]{1,0:T(1,128)S(1)}, u32[]{:S(2)}, u32[]{:S(2)}) collective-permute-start(f32[1,640]{1,0:T(1,128)S(1)} %get-tuple-element.36), channel_id=1, source_target_pairs={{0,8},{4,12},{8,0},{12,4},{1,9},{5,13},{9,1},{13,5},{2,10},{6,14},... | collective-permute-start | bytes 7688 | tf_op jit(solution)/shard_map/ppermute | solution.py:31
  24.3 1.4 %collective-permute-start.14 = (f32[1,640]{1,0:T(1,128)S(1)}, f32[1,640]{1,0:T(1,128)S(1)}, u32[]{:S(2)}, u32[]{:S(2)}) collective-permute-start(f32[1,640]{1,0:T(1,128)S(1)} %get-tuple-element.37), channel_id=1, source_target_pairs={{0,12},{4,8},{8,4},{12,0},{1,13},{5,9},{9,5},{13,1},{2,14},{6,10},... | collective-permute-start | bytes 7688 | tf_op jit(solution)/shard_map/ppermute | solution.py:31
  25.8 1.5 %collective-permute-start.10 = (bf16[128,512]{1,0:T(8,128)(2,1)S(1)}, bf16[128,512]{1,0:T(8,128)(2,1)S(1)}, u32[]{:S(2)}, u32[]{:S(2)}) collective-permute-start(bf16[128,512]{1,0:T(8,128)(2,1)S(1)} %get-tuple-element.31.refs_7_), channel_id=1, source_target_pairs={{0,12},{4,8},{8,4},{12,0},{1,13},{5,9},{9,5},{13,1},{2,14},{6,10},... | collective-permute-start | bytes 393224 | tf_op jit(solution)/shard_map/ppermute | solution.py:172
  27.3 1.5 %collective-permute-start.8 = (bf16[128,512]{1,0:T(8,128)(2,1)S(1)}, bf16[128,512]{1,0:T(8,128)(2,1)S(1)}, u32[]{:S(2)}, u32[]{:S(2)}) collective-permute-start(bf16[128,512]{1,0:T(8,128)(2,1)S(1)} %get-tuple-element.29.refs_5_), channel_id=1, source_target_pairs={{0,4},{4,0},{8,12},{12,8},{1,5},{5,1},{9,13},{13,9},{2,6},{6,2},{1... | collective-permute-start | bytes 393224 | tf_op jit(solution)/shard_map/ppermute | solution.py:172
  28.7 0.0 collective-permute-done.12
  28.7 0.5 %collective-permute-start.9 = (bf16[128,512]{1,0:T(8,128)(2,1)S(1)}, bf16[128,512]{1,0:T(8,128)(2,1)S(1)}, u32[]{:S(2)}, u32[]{:S(2)}) collective-permute-start(bf16[128,512]{1,0:T(8,128)(2,1)S(1)} %get-tuple-element.30.refs_6_), channel_id=1, source_target_pairs={{0,8},{4,12},{8,0},{12,4},{1,9},{5,13},{9,1},{13,5},{2,10},{6,14},... | collective-permute-start | bytes 393224 | tf_op jit(solution)/shard_map/ppermute | solution.py:172
  29.3 0.0 collective-permute-done.13
  29.3 0.0 collective-permute-done.14
  29.3 3.7 %collective-permute-start.15 = (f32[128]{0:T(128)S(1)}, f32[128]{0:T(128)S(1)}, u32[]{:S(2)}, u32[]{:S(2)}) collective-permute-start(f32[128]{0:T(128)S(1)} %get-tuple-element.40), channel_id=1, source_target_pairs={{0,3},{1,2},{2,1},{3,0},{4,7},{5,6},{6,5},{7,4},{8,11},{9,10},{10,... | collective-permute-start | bytes 1544 | tf_op jit(solution)/shard_map/ppermute | solution.py:262
  33.0 0.0 collective-permute-start.16
  33.0 0.1 collective-permute-done.10.refs_2_
  33.1 1.6 %collective-permute-start.17 = (f32[128]{0:T(128)S(1)}, f32[128]{0:T(128)S(1)}, u32[]{:S(2)}, u32[]{:S(2)}) collective-permute-start(f32[128]{0:T(128)S(1)} %get-tuple-element.41), channel_id=1, source_target_pairs={{0,1},{1,0},{2,3},{3,2},{4,5},{5,4},{6,7},{7,6},{8,9},{9,8},{10,11... | collective-permute-start | bytes 1544 | tf_op jit(solution)/shard_map/ppermute | solution.py:262
  34.7 0.0 collective-permute-done.8.refs_0_
  34.7 0.0 collective-permute-done.9.refs_1_
  34.7 0.9 %last.1 = bf16[128,512]{1,0:T(8,128)(2,1)} custom-call(f32[128,512]{1,0:T(8,128)S(1)} %get-tuple-element.28.refs_4_.kept_ref, bf16[128,512]{1,0:T(8,128)(2,1)S(1)} %collective-permute-done.8.refs_0_, bf16[128,512]{1,0:T(8,128)(2,1)S(1)} %collective-permute-done.9.refs_1_, bf16[128,512]{1,0:T(8,128)(2,1)S(1)} %collective-permute-done.10.refs_2_, ...), custom_call_target="tpu_custom_call" | custom-call | flops 655360 | bytes 1048576 | tf_op jit(solution)/shard_map/last/pallas_call | solution.py:243
  35.6 0.0 collective-permute-done.15
  35.6 1.9 %collective-permute-done.16 = f32[128]{0:T(128)S(1)} collective-permute-done((f32[128]{0:T(128)S(1)}, f32[128]{0:T(128)S(1)}, u32[]{:S(2)}, u32[]{:S(2)}) %collective-permute-start.16) | collective-permute-done | bytes 544 | tf_op jit(solution)/shard_map/ppermute | solution.py:262
  37.4 0.0 collective-permute-done.17
  37.4 0.5 %add_add_fusion.1 = f32[128]{0:T(128)} fusion(f32[128]{0:T(128)S(1)} %collective-permute-done.16, f32[128]{0:T(128)S(1)} %collective-permute-done.17, f32[128]{0:T(128)S(1)} %get-tuple-element.39, f32[128]{0:T(128)S(1)} %collective-permute-done.15), kind=kLoop, calls=%fused_computation.9 | loop fusion | flops 384 | bytes 2560 | tf_op jit(solution)/shard_map/add | solution.py:25
  (13 shorter events, 0.0 us)
Async XLA Ops:
  0.6 12.6 %slice-start = ((s8[8388608]{0:T(1024)(128)(4,1)}), s8[4194304]{0:T(1024)(128)(4,1)S(1)}, s32[]{:S(2)}) async-start(s8[8388608]{0:T(1024)(128)(4,1)} %bitcast.24), calls=%async_computation | async-start | bytes 8388608
  0.6 12.6 %copy-start = (bf16[1,128,512]{2,1,0:T(8,128)(2,1)S(1)}, bf16[1,128,512]{2,1,0:T(8,128)(2,1)}, u32[]{:S(2)}) copy-start(bf16[1,128,512]{2,1,0:T(8,128)(2,1)} %param.6) | copy-start | bytes 393220
  0.7 12.6 %copy-start.1 = (f32[4096]{0:T(1024)S(1)}, f32[4096]{0:T(1024)}, u32[]{:S(2)}) copy-start(f32[4096]{0:T(1024)} %param.7) | copy-start | bytes 49156
  0.7 12.6 %slice-start.1 = ((s8[8388608]{0:T(1024)(128)(4,1)}), s8[4194304]{0:T(1024)(128)(4,1)S(1)}, s32[]{:S(2)}) async-start(s8[8388608]{0:T(1024)(128)(4,1)} %bitcast.24), calls=%async_computation.1 | async-start | bytes 8388608
  0.7 12.6 %copy-start.3 = (bf16[1,1,256,512]{3,2,1,0:T(8,128)(2,1)S(1)}, bf16[1,1,256,512]{3,2,1,0:T(8,128)(2,1)}, u32[]{:S(2)}) copy-start(bf16[1,1,256,512]{3,2,1,0:T(8,128)(2,1)} %param.9) | copy-start | bytes 786436
  0.7 12.6 %copy-start.4 = (bf16[1,1,256,512]{3,2,1,0:T(8,128)(2,1)S(1)}, bf16[1,1,256,512]{3,2,1,0:T(8,128)(2,1)}, u32[]{:S(2)}) copy-start(bf16[1,1,256,512]{3,2,1,0:T(8,128)(2,1)} %param.10) | copy-start | bytes 786436
  0.7 7.2 %collective-permute-start = (bf16[128,512]{1,0:T(8,128)(2,1)}, bf16[128,512]{1,0:T(8,128)(2,1)S(1)}, u32[]{:S(2)}, u32[]{:S(2)}) collective-permute-start(bf16[128,512]{1,0:T(8,128)(2,1)} %bitcast.15), channel_id=1, source_target_pairs={{0,4},{4,0},{8,12},{12,8},{1,5},{5,1},{9,13},{13,9},{2,6},{6,2},{1... | collective-permute-start | bytes 393224 | tf_op jit(solution)/shard_map/ppermute | solution.py:172
  3.7 8.0 %collective-permute-start.1 = (bf16[128,512]{1,0:T(8,128)(2,1)}, bf16[128,512]{1,0:T(8,128)(2,1)S(1)}, u32[]{:S(2)}, u32[]{:S(2)}) collective-permute-start(bf16[128,512]{1,0:T(8,128)(2,1)} %bitcast.16), channel_id=1, source_target_pairs={{0,8},{4,12},{8,0},{12,4},{1,9},{5,13},{9,1},{13,5},{2,10},{6,14},... | collective-permute-start | bytes 393224 | tf_op jit(solution)/shard_map/ppermute | solution.py:172
  5.2 6.5 %collective-permute-start.2 = (bf16[128,512]{1,0:T(8,128)(2,1)}, bf16[128,512]{1,0:T(8,128)(2,1)S(1)}, u32[]{:S(2)}, u32[]{:S(2)}) collective-permute-start(bf16[128,512]{1,0:T(8,128)(2,1)} %bitcast.17), channel_id=1, source_target_pairs={{0,12},{4,8},{8,4},{12,0},{1,13},{5,9},{9,5},{13,1},{2,14},{6,10},... | collective-permute-start | bytes 393224 | tf_op jit(solution)/shard_map/ppermute | solution.py:172
  5.2 7.6 %collective-permute-start.3 = (bf16[128,512]{1,0:T(8,128)(2,1)}, bf16[128,512]{1,0:T(8,128)(2,1)S(1)}, u32[]{:S(2)}, u32[]{:S(2)}) collective-permute-start(bf16[128,512]{1,0:T(8,128)(2,1)} %bitcast.18), channel_id=1, source_target_pairs={{0,16},{16,0},{1,17},{17,1},{2,18},{18,2},{3,19},{19,3},{4,20},{20... | collective-permute-start | bytes 393224 | tf_op jit(solution)/shard_map/ppermute | solution.py:175
  7.9 4.9 %collective-permute-start.4 = (bf16[128,512]{1,0:T(8,128)(2,1)S(1)}, bf16[128,512]{1,0:T(8,128)(2,1)S(1)}, u32[]{:S(2)}, u32[]{:S(2)}) collective-permute-start(bf16[128,512]{1,0:T(8,128)(2,1)S(1)} %collective-permute-done.refs_1_), channel_id=1, source_target_pairs={{0,16},{16,0},{1,17},{17,1},{2,18},{18,2},{3,19},{19,3},{4,20},{20... | collective-permute-start | bytes 393224 | tf_op jit(solution)/shard_map/ppermute | solution.py:175
  11.7 1.3 %collective-permute-start.5 = (bf16[128,512]{1,0:T(8,128)(2,1)S(1)}, bf16[128,512]{1,0:T(8,128)(2,1)S(1)}, u32[]{:S(2)}, u32[]{:S(2)}) collective-permute-start(bf16[128,512]{1,0:T(8,128)(2,1)S(1)} %collective-permute-done.1.refs_2_), channel_id=1, source_target_pairs={{0,16},{16,0},{1,17},{17,1},{2,18},{18,2},{3,19},{19,3},{4,20},{20... | collective-permute-start | bytes 393224 | tf_op jit(solution)/shard_map/ppermute | solution.py:175
  11.7 1.5 %collective-permute-start.6 = (bf16[128,512]{1,0:T(8,128)(2,1)S(1)}, bf16[128,512]{1,0:T(8,128)(2,1)S(1)}, u32[]{:S(2)}, u32[]{:S(2)}) collective-permute-start(bf16[128,512]{1,0:T(8,128)(2,1)S(1)} %collective-permute-done.2.refs_3_), channel_id=1, source_target_pairs={{0,16},{16,0},{1,17},{17,1},{2,18},{18,2},{3,19},{19,3},{4,20},{20... | collective-permute-start | bytes 393224 | tf_op jit(solution)/shard_map/ppermute | solution.py:175
  19.8 2.0 %collective-permute-start.7 = (bf16[128,2048]{1,0:T(8,128)(2,1)S(1)}, bf16[128,2048]{1,0:T(8,128)(2,1)S(1)}, u32[]{:S(2)}, u32[]{:S(2)}) collective-permute-start(bf16[128,2048]{1,0:T(8,128)(2,1)S(1)} %get-tuple-element.27), channel_id=1, source_target_pairs={{0,16},{16,0},{1,17},{17,1},{2,18},{18,2},{3,19},{19,3},{4,20},{20... | collective-permute-start | bytes 1572872 | tf_op jit(solution)/shard_map/ppermute | solution.py:175
  20.2 1.7 %collective-permute-start.11 = (f32[1,128]{1,0:T(1,128)S(1)}, f32[1,128]{1,0:T(1,128)S(1)}, u32[]{:S(2)}, u32[]{:S(2)}) collective-permute-start(f32[1,128]{1,0:T(1,128)S(1)} %get-tuple-element.33.row_ref), channel_id=1, source_target_pairs={{0,16},{16,0},{1,17},{17,1},{2,18},{18,2},{3,19},{19,3},{4,20},{20... | collective-permute-start | bytes 1544 | tf_op jit(solution)/shard_map/ppermute | solution.py:175
  22.2 6.5 %collective-permute-start.12 = (f32[1,640]{1,0:T(1,128)S(1)}, f32[1,640]{1,0:T(1,128)S(1)}, u32[]{:S(2)}, u32[]{:S(2)}) collective-permute-start(f32[1,640]{1,0:T(1,128)S(1)} %get-tuple-element.35), channel_id=1, source_target_pairs={{0,4},{4,0},{8,12},{12,8},{1,5},{5,1},{9,13},{13,9},{2,6},{6,2},{1... | collective-permute-start | bytes 7688 | tf_op jit(solution)/shard_map/ppermute | solution.py:31
  23.3 6.0 %collective-permute-start.13 = (f32[1,640]{1,0:T(1,128)S(1)}, f32[1,640]{1,0:T(1,128)S(1)}, u32[]{:S(2)}, u32[]{:S(2)}) collective-permute-start(f32[1,640]{1,0:T(1,128)S(1)} %get-tuple-element.36), channel_id=1, source_target_pairs={{0,8},{4,12},{8,0},{12,4},{1,9},{5,13},{9,1},{13,5},{2,10},{6,14},... | collective-permute-start | bytes 7688 | tf_op jit(solution)/shard_map/ppermute | solution.py:31
  24.3 4.9 %collective-permute-start.14 = (f32[1,640]{1,0:T(1,128)S(1)}, f32[1,640]{1,0:T(1,128)S(1)}, u32[]{:S(2)}, u32[]{:S(2)}) collective-permute-start(f32[1,640]{1,0:T(1,128)S(1)} %get-tuple-element.37), channel_id=1, source_target_pairs={{0,12},{4,8},{8,4},{12,0},{1,13},{5,9},{9,5},{13,1},{2,14},{6,10},... | collective-permute-start | bytes 7688 | tf_op jit(solution)/shard_map/ppermute | solution.py:31
  25.8 7.3 %collective-permute-start.10 = (bf16[128,512]{1,0:T(8,128)(2,1)S(1)}, bf16[128,512]{1,0:T(8,128)(2,1)S(1)}, u32[]{:S(2)}, u32[]{:S(2)}) collective-permute-start(bf16[128,512]{1,0:T(8,128)(2,1)S(1)} %get-tuple-element.31.refs_7_), channel_id=1, source_target_pairs={{0,12},{4,8},{8,4},{12,0},{1,13},{5,9},{9,5},{13,1},{2,14},{6,10},... | collective-permute-start | bytes 393224 | tf_op jit(solution)/shard_map/ppermute | solution.py:172
  27.3 7.4 %collective-permute-start.8 = (bf16[128,512]{1,0:T(8,128)(2,1)S(1)}, bf16[128,512]{1,0:T(8,128)(2,1)S(1)}, u32[]{:S(2)}, u32[]{:S(2)}) collective-permute-start(bf16[128,512]{1,0:T(8,128)(2,1)S(1)} %get-tuple-element.29.refs_5_), channel_id=1, source_target_pairs={{0,4},{4,0},{8,12},{12,8},{1,5},{5,1},{9,13},{13,9},{2,6},{6,2},{1... | collective-permute-start | bytes 393224 | tf_op jit(solution)/shard_map/ppermute | solution.py:172
  28.7 6.0 %collective-permute-start.9 = (bf16[128,512]{1,0:T(8,128)(2,1)S(1)}, bf16[128,512]{1,0:T(8,128)(2,1)S(1)}, u32[]{:S(2)}, u32[]{:S(2)}) collective-permute-start(bf16[128,512]{1,0:T(8,128)(2,1)S(1)} %get-tuple-element.30.refs_6_), channel_id=1, source_target_pairs={{0,8},{4,12},{8,0},{12,4},{1,9},{5,13},{9,1},{13,5},{2,10},{6,14},... | collective-permute-start | bytes 393224 | tf_op jit(solution)/shard_map/ppermute | solution.py:172
  29.3 6.2 %collective-permute-start.15 = (f32[128]{0:T(128)S(1)}, f32[128]{0:T(128)S(1)}, u32[]{:S(2)}, u32[]{:S(2)}) collective-permute-start(f32[128]{0:T(128)S(1)} %get-tuple-element.40), channel_id=1, source_target_pairs={{0,3},{1,2},{2,1},{3,0},{4,7},{5,6},{6,5},{7,4},{8,11},{9,10},{10,... | collective-permute-start | bytes 1544 | tf_op jit(solution)/shard_map/ppermute | solution.py:262
  33.0 4.4 %collective-permute-start.16 = (f32[128]{0:T(128)S(1)}, f32[128]{0:T(128)S(1)}, u32[]{:S(2)}, u32[]{:S(2)}) collective-permute-start(f32[128]{0:T(128)S(1)} %get-tuple-element.42), channel_id=1, source_target_pairs={{0,2},{1,3},{2,0},{3,1},{4,6},{5,7},{6,4},{7,5},{8,10},{9,11},{10,... | collective-permute-start | bytes 1544 | tf_op jit(solution)/shard_map/ppermute | solution.py:262
  33.1 4.3 %collective-permute-start.17 = (f32[128]{0:T(128)S(1)}, f32[128]{0:T(128)S(1)}, u32[]{:S(2)}, u32[]{:S(2)}) collective-permute-start(f32[128]{0:T(128)S(1)} %get-tuple-element.41), channel_id=1, source_target_pairs={{0,1},{1,0},{2,3},{3,2},{4,5},{5,4},{6,7},{7,6},{8,9},{9,8},{10,11... | collective-permute-start | bytes 1544 | tf_op jit(solution)/shard_map/ppermute | solution.py:262
  34.7 3.3 %copy-start.2 = (f32[1,128]{1,0:T(1,128)}, f32[1,128]{1,0:T(1,128)S(1)}, u32[]{:S(2)}) copy-start(f32[1,128]{1,0:T(1,128)S(1)} %slice.8.refs_6_) | copy-start | bytes 1540

commit v4 on v3

--- a/solution.py
+++ b/solution.py
@@ -16,19 +16,24 @@
 ANY = pl.BlockSpec(memory_space=pl.ANY)
 
 
-def partner(index, step, count):
-    return index ^ step
+def reverse_bits(step, count):
+    out, bit = 0, 1
+    while bit < count:
+        out = 2 * out + (1 if step & bit else 0)
+        bit *= 2
+    return out
+
+
+def section_step(core, step, count):
+    if isinstance(core, int):
+        return reverse_bits(step, count) if core else step
+    return jnp.where(core == 0, step, reverse_bits(step, count))
 
 
 def tree_sum(terms):
     while len(terms) > 1:
         terms = [terms[i] + terms[i + 1] for i in range(0, len(terms), 2)]
     return terms[0]
-
-
-def direct_sum(terms, axis, count):
-    perms = [[(i, partner(i, k, count)) for i in range(count)] for k in range(count)]
-    return tree_sum([terms[0]] + [lax.ppermute(terms[k], axis, perms[k]) for k in range(1, count)])
 
 
 def first_kernel(token_ref):
@@ -44,8 +49,8 @@
 ):
     chunk_refs = refs[: 2 * parts]
     (gain_ref, weight, query_ref, cot_ref) = refs[2 * parts : 2 * parts + 4]
-    (att_ref, sib_ref, own_ref, inv_ref, row_ref) = refs[2 * parts + 4 : 2 * parts + 9]
-    (memory, kv, kv_grad) = refs[2 * parts + 9 :]
+    (att_ref, sib_ref, kv_grad, inv_ref, row_ref) = refs[2 * parts + 4 : 2 * parts + 9]
+    (memory, kv) = refs[2 * parts + 9 :]
     tokens, feats = chunk_refs[0].shape
     width = weight.shape[0]
     half = width // 2
@@ -53,15 +58,17 @@
     square = None
     for ref in chunk_refs:
         x = ref[...].astype(jnp.float32)
-        part = jnp.sum((x * x).reshape(tokens, feats // 128, 128), axis=1)
-        square = part if square is None else square + part
+        x = x * x
+        for i in range(0, feats, 128):
+            square = x[:, i : i + 128] if square is None else square + x[:, i : i + 128]
     square = jnp.sum(square, axis=1, keepdims=True)
     inv_rms = lax.rsqrt(square / width + EPS)
     inv_ref[...] = inv_rms
     me, section = lax.axis_index("sec"), lax.axis_index("section")
     for j, ref in enumerate(chunk_refs):
         owner = me if j < parts else 1 - me
-        at = pl.multiple_of((owner * parts + partner(section, j % parts, parts)) * feats, feats)
+        peer = section ^ section_step(owner, j % parts, parts)
+        at = pl.multiple_of((owner * parts + peer) * feats, feats)
         normed = ref[...].astype(jnp.float32) * inv_rms
         memory[:, pl.ds(at, feats)] = (normed * gain_ref[:, pl.ds(at, feats)]).astype(jnp.bfloat16)
 
@@ -108,6 +115,13 @@
         sib_ref[:, pl.ds(t * tile, tile)] = lax.dot_general(
             grad, weight[rows, :], LAST, preferred_element_type=jnp.float32
         ).astype(jnp.bfloat16)
+
+
+def back_kernel(grad_ref, weight, own_ref):
+    half = own_ref.shape[1]
+    me = lax.axis_index("sec")
+    grad = grad_ref[...]
+    tile = half // 4
     for t in range(4):
         rows = pl.ds(pl.multiple_of(me * half + t * tile, tile), tile)
         own_ref[:, pl.ds(t * tile, tile)] = lax.dot_general(
@@ -117,9 +131,9 @@
 
 def chip_kernel(parts, own_ref, sib_ref, kept_ref, *big_refs):
     feats = kept_ref.shape[1]
-    section = lax.axis_index("section")
+    me, section = lax.axis_index("sec"), lax.axis_index("section")
     for k in range(parts):
-        at = pl.multiple_of(partner(section, k, parts) * feats, feats)
+        at = pl.multiple_of((section ^ section_step(me, k, parts)) * feats, feats)
         total = own_ref[:, pl.ds(at, feats)] + sib_ref[:, pl.ds(at, feats)].astype(jnp.float32)
         if k == 0:
             kept_ref[...] = total
@@ -139,20 +153,33 @@
         small_refs[k][:, pl.ds(feats, row.shape[1])] = row
 
 
-def last_kernel(parts, width, kept_ref, *refs):
-    big_refs = refs[: parts - 1]
-    chunk_ref, inv_ref, gain_ref, row_ref, enc_ref = refs[parts - 1 :]
+def total_kernel(kept_ref, *refs):
+    total = kept_ref[...]
+    for ref in refs[:-1]:
+        total = total + ref[...].astype(jnp.float32)
+    refs[-1][...] = total
+
+
+def last_kernel(parts, width, grad_ref, chunk_ref, inv_ref, gain_ref, *refs):
+    small_refs, gain_refs, (enc_ref, row_ref, *gain_out) = refs[:parts], refs[parts:-3], refs[-3:]
+    if not gain_refs:
+        small_refs, (enc_ref, row_ref), gain_out = refs[:parts], refs[-2:], ()
     tokens, feats = chunk_ref.shape
-    grad = kept_ref[...]
-    for ref in big_refs:
-        grad = grad + ref[...].astype(jnp.float32)
+    core = lax.axis_index("sec")
+    rows = [ref[:, pl.ds(feats, tokens)] for ref in small_refs]
+    row = tree_sum(
+        [jnp.where(core == 0, rows[k], rows[reverse_bits(k, parts)]) for k in range(parts)]
+    )
+    row_ref[...] = row
+    grad = grad_ref[...]
     inv_rms = inv_ref[...]
-    me = lax.axis_index("sec") * parts + lax.axis_index("section")
-    at = pl.multiple_of(me * feats, feats)
+    at = pl.multiple_of((core * parts + lax.axis_index("section")) * feats, feats)
     gain = gain_ref[:, pl.ds(at, feats)]
     normed = chunk_ref[...].astype(jnp.float32) * inv_rms
-    row_dot = jnp.transpose(jnp.broadcast_to(row_ref[...], (128, tokens)))[:, 0:1]
+    row_dot = jnp.transpose(jnp.broadcast_to(row, (128, tokens)))[:, 0:1]
     enc_ref[...] = (inv_rms * (gain * grad - normed * (row_dot / width))).astype(jnp.bfloat16)
+    for ref in gain_out:
+        ref[...] = tree_sum([g[...] for g in gain_refs])
 
 
 def per_device(sizes, enc_states, norm_gain, kv_weight, queries, attn_cotangent, target_lengths):
@@ -169,7 +196,12 @@
     swap = [(0, 1), (1, 0)]
 
     def to_section(x, step):
-        return lax.ppermute(x, "section", [(i, partner(i, step, parts)) for i in range(parts)])
+        pairs = [
+            (c * parts + i, c * parts + (i ^ section_step(c, step, parts)))
+            for c in range(cores)
+            for i in range(parts)
+        ]
+        return lax.ppermute(x, ("sec", "section"), pairs)
 
     def to_core(x):
         return lax.ppermute(x, "sec", swap)
@@ -187,12 +219,12 @@
     for k in range(1, parts):
         chunks.append(lax.optimization_barrier((to_section(rows, k), token))[0])
     others = [to_core(c) for c in chunks]
-    att, sib, own, inv_rms, row = pl.pallas_call(
+    att, sib, kv_grad, inv_rms, row = pl.pallas_call(
         functools.partial(main_kernel, parts, heads),
         out_shape=(
             jax.ShapeDtypeStruct(query.shape, jnp.bfloat16),
             jax.ShapeDtypeStruct((tokens, half), jnp.bfloat16),
-            jax.ShapeDtypeStruct((tokens, half), jnp.float32),
+            jax.ShapeDtypeStruct((tokens, weight.shape[1]), jnp.bfloat16),
             jax.ShapeDtypeStruct((tokens, 1), jnp.float32),
             jax.ShapeDtypeStruct((1, tokens), jnp.float32),
         ),
@@ -201,7 +233,6 @@
         scratch_shapes=[
             pltpu.VMEM((tokens, width), jnp.bfloat16),
             pltpu.VMEM((tokens, weight.shape[1]), jnp.float32),
-            pltpu.VMEM((tokens, weight.shape[1]), jnp.bfloat16),
         ],
         compiler_params=pltpu.CompilerParams(vmem_limit_bytes=16 << 20),
         cost_estimate=pl.CostEstimate(
@@ -210,6 +241,17 @@
         name="main",
     )(target_lengths, token, *chunks, *others, gain, weight, query, cot)
 
+    own = pl.pallas_call(
+        back_kernel,
+        out_shape=jax.ShapeDtypeStruct((tokens, half), jnp.float32),
+        in_specs=[VMEM, VMEM],
+        out_specs=VMEM,
+        compiler_params=pltpu.CompilerParams(vmem_limit_bytes=16 << 20),
+        cost_estimate=pl.CostEstimate(
+            flops=flops // 2, bytes_accessed=weight.size, transcendentals=0
+        ),
+        name="back",
+    )(kv_grad, weight)
     row_sib = to_core(row)
     sib_in = to_core(sib)
 
@@ -238,34 +280,45 @@
     )(row, row_sib, inv_rms, *chunks, kept, *big)
 
     big_in = [to_section(big[k - 1], k) for k in range(1, parts)]
-    gain_row = direct_sum(small, "section", parts)
-    gain_term, row_dot = gain_row[0, :feats], gain_row[:, feats:]
-    enc_grad = pl.pallas_call(
-        functools.partial(last_kernel, parts, width),
-        out_shape=jax.ShapeDtypeStruct((tokens, feats), jnp.bfloat16),
-        in_specs=[VMEM] * (4 + parts),
+    small_in = [small[0]] + [to_section(small[k], k) for k in range(1, parts)]
+    gain_term = tree_sum([x[:, :feats] for x in small_in])
+    direct = seqs <= 8 and (feats // seqs) % 128 == 0
+    pieces = []
+    if direct:
+        piece = feats // seqs
+        dp = lax.axis_index("dp")
+        pieces = [lax.dynamic_slice_in_dim(gain_term, dp * piece, piece, 1)]
+        for k in reversed(range(1, seqs)):
+            send = lax.dynamic_slice_in_dim(gain_term, (dp ^ k) * piece, piece, 1)
+            pieces.append(lax.ppermute(send, "dp", [(i, i ^ k) for i in range(seqs)]))
+    total = pl.pallas_call(
+        total_kernel,
+        out_shape=jax.ShapeDtypeStruct((tokens, feats), jnp.float32),
+        in_specs=[VMEM] * parts,
         out_specs=VMEM,
         compiler_params=pltpu.CompilerParams(vmem_limit_bytes=8 << 20),
+        cost_estimate=pl.CostEstimate(flops=20_000_000_000, bytes_accessed=4096, transcendentals=0),
+        name="total",
+    )(kept, *big_in)
+    enc_grad, row_dot, *gain_grad = pl.pallas_call(
+        functools.partial(last_kernel, parts, width),
+        out_shape=(
+            jax.ShapeDtypeStruct((tokens, feats), jnp.bfloat16),
+            jax.ShapeDtypeStruct((1, tokens), jnp.float32),
+        )
+        + ((jax.ShapeDtypeStruct(pieces[0].shape, jnp.float32),) if direct else ()),
+        in_specs=[VMEM] * (4 + parts + len(pieces)),
+        out_specs=(VMEM,) * (3 if direct else 2),
+        compiler_params=pltpu.CompilerParams(vmem_limit_bytes=8 << 20),
         cost_estimate=pl.CostEstimate(
             flops=10 * tokens * feats, bytes_accessed=16 * tokens * feats, transcendentals=0
         ),
         name="last",
-    )(kept, *big_in, rows, inv_rms, gain, row_dot)
-    if seqs <= 8:
-        piece = feats // seqs
-        dp = lax.axis_index("dp")
-        owned = [
-            lax.dynamic_slice_in_dim(gain_term, partner(dp, k, seqs) * piece, piece, 0)
-            for k in range(seqs)
-        ]
-        came = [
-            lax.ppermute(owned[k], "dp", [(i, partner(i, k, seqs)) for i in range(seqs)])
-            for k in reversed(range(1, seqs))
-        ]
-        enc_grad, first = lax.optimization_barrier((enc_grad, owned[0]))
-        gain_grad = tree_sum([first] + came)
+    )(total, rows, inv_rms, gain, *small_in, *pieces)
+    if direct:
+        gain_grad = gain_grad[0][0]
     else:
-        gain_grad = lax.psum_scatter(gain_term, "dp", scatter_dimension=0, tiled=True)
+        gain_grad = lax.psum_scatter(gain_term[0], "dp", scatter_dimension=0, tiled=True)
     return (att[None, None], enc_grad[None], gain_grad, row_dot)
 
 

time: 38.1 us -> 36 us (0.945)
  Pallas kernels: 7.81 us -> 6.79 us
  starting transfers between devices: 17.9 us -> 17.3 us
  other arithmetic: 0.52 us -> 0.01 us
    pallas_call x1, Pallas kernels: 6.56 us -> 3.99 us  [per_device(): pl.pallas_call(functools.partial(main_kernel, parts, heads), out_shape=(j...]
    pallas_call x1 -> x3, Pallas kernels: 0.87 us -> 2.42 us  [the longest x1 1.49 us: per_device(): pl.pallas_call(back_kernel, out_shape=jax.ShapeDtypeStruct((tokens, half)...]
    ppermute x12, waiting for transfers between devices: 8.41 us -> 9.96 us  [the longest x9 7.04 us: to_section(): return lax.ppermute(x, ('sec', 'section'), pairs)]
    ppermute x6, waiting for transfers between devices: 1.76 us -> 0.36 us  [to_core(): return lax.ppermute(x, 'sec', swap)]
    ppermute x12, starting transfers between devices: 16.8 us -> 16.2 us  [the longest x9 11.6 us: to_section(): return lax.ppermute(x, ('sec', 'section'), pairs)]
    add x2 -> x1, other arithmetic: 0.52 us -> 0.01 us  [tree_sum(): terms = [terms[i] + terms[i + 1] for i in range(0, len(terms), 2)]]
  transfers between devices with their start and end apart: 18 -> 18, of which waited for: 7 -> 8; matrix products, arithmetic and copies ran while one was open for 0% -> 0% of each run, Pallas kernels for 3% -> 5%
where the time goes in v4:
time: 36 us; the launch traced here: 35.9 us
  starting transfers between devices  17.3 us (48%)
  waiting for transfers between devices  10.3 us (29%)
  Pallas kernels  6.79 us (19%)
  between operations  1.45 us (4%)
    ppermute x9, starting transfers between devices, to_section(): return lax.ppermute(x, ('sec', 'section'), pairs)  11.6 us
    ppermute x9, waiting for transfers between devices, to_section(): return lax.ppermute(x, ('sec', 'section'), pairs)  7.04 us
    ppermute x3, starting transfers between devices, per_device(): pieces.append(lax.ppermute(send, 'dp', [(i, i ^ k) for i in range(seqs)]))  4.6 us
    pallas_call x1, Pallas kernels, per_device(): pl.pallas_call(functools.partial(main_kernel, parts, heads), out_shape=(j...  3.99 us
    ppermute x3, waiting for transfers between devices, per_device(): pieces.append(lax.ppermute(send, 'dp', [(i, i ^ k) for i in range(seqs)]))  2.92 us
    pallas_call x1, Pallas kernels, per_device(): pl.pallas_call(back_kernel, out_shape=jax.ShapeDtypeStruct((tokens, half)...  1.49 us
    ppermute x6, starting transfers between devices, to_core(): return lax.ppermute(x, 'sec', swap)  1.09 us
    pallas_call x1, Pallas kernels, per_device(): pl.pallas_call(functools.partial(last_kernel, parts, width), out_shape=(j...  0.86 us
  transfers between devices with their start and end apart: 18, of which 8 were waited for; matrix products, arithmetic and copies ran while one was open for 0% of the time, Pallas kernels for 5%

profile of v4, /device:TPU:0, one launch (start us, length us, event | category | flops | bytes accessed | tf_op | source)
XLA Modules:
  0.0 35.9 jit_solution(8483971579292934450)
XLA Ops:
  0.6 0.0 slice-start
  0.6 0.0 slice-start.1
  0.7 0.0 copy-start
  0.7 0.0 copy-start.1
  0.7 0.0 copy-start.2
  0.7 3.0 %collective-permute-start = (bf16[128,512]{1,0:T(8,128)(2,1)}, bf16[128,512]{1,0:T(8,128)(2,1)S(1)}, u32[]{:S(2)}, u32[]{:S(2)}) collective-permute-start(bf16[128,512]{1,0:T(8,128)(2,1)} %bitcast.12), channel_id=1, source_target_pairs={{0,4},{4,0},{8,12},{12,8},{16,24},{20,28},{24,16},{28,20},{1,5},{5... | collective-permute-start | bytes 393224 | tf_op jit(solution)/shard_map/ppermute | solution.py:204
  3.7 1.5 %collective-permute-start.1 = (bf16[128,512]{1,0:T(8,128)(2,1)}, bf16[128,512]{1,0:T(8,128)(2,1)S(1)}, u32[]{:S(2)}, u32[]{:S(2)}) collective-permute-start(bf16[128,512]{1,0:T(8,128)(2,1)} %bitcast.13), channel_id=1, source_target_pairs={{0,8},{4,12},{8,0},{12,4},{16,20},{20,16},{24,28},{28,24},{1,9},{5... | collective-permute-start | bytes 393224 | tf_op jit(solution)/shard_map/ppermute | solution.py:204
  5.2 0.0 collective-permute-start.2
  5.2 0.0 collective-permute-start.3
  5.2 2.6 %collective-permute-done.refs_1_ = bf16[128,512]{1,0:T(8,128)(2,1)S(1)} collective-permute-done((bf16[128,512]{1,0:T(8,128)(2,1)}, bf16[128,512]{1,0:T(8,128)(2,1)S(1)}, u32[]{:S(2)}, u32[]{:S(2)}) %collective-permute-start) | collective-permute-done | bytes 131104 | tf_op jit(solution)/shard_map/ppermute | solution.py:204
  7.8 0.0 collective-permute-start.4
  7.8 3.9 %collective-permute-done.1.refs_2_ = bf16[128,512]{1,0:T(8,128)(2,1)S(1)} collective-permute-done((bf16[128,512]{1,0:T(8,128)(2,1)}, bf16[128,512]{1,0:T(8,128)(2,1)S(1)}, u32[]{:S(2)}, u32[]{:S(2)}) %collective-permute-start.1) | collective-permute-done | bytes 131104 | tf_op jit(solution)/shard_map/ppermute | solution.py:204
  11.7 0.0 collective-permute-start.5
  11.7 0.0 collective-permute-done.2.refs_3_
  11.7 0.5 %collective-permute-start.6 = (bf16[128,512]{1,0:T(8,128)(2,1)S(1)}, bf16[128,512]{1,0:T(8,128)(2,1)S(1)}, u32[]{:S(2)}, u32[]{:S(2)}) collective-permute-start(bf16[128,512]{1,0:T(8,128)(2,1)S(1)} %collective-permute-done.2.refs_3_), channel_id=1, source_target_pairs={{0,16},{16,0},{1,17},{17,1},{2,18},{18,2},{3,19},{19,3},{4,20},{20... | collective-permute-start | bytes 393224 | tf_op jit(solution)/shard_map/ppermute | solution.py:207
  12.9 0.0 collective-permute-done.3.refs_4_
  12.9 0.0 collective-permute-done.4.refs_5_
  12.9 0.2 collective-permute-done.5.refs_6_
  13.0 0.2 collective-permute-done.6.refs_7_
  13.2 0.0 copy-done
  13.3 4.0 %main.1 = (bf16[256,512]{1,0:T(8,128)(2,1)}, bf16[128,2048]{1,0:T(8,128)(2,1)S(1)}, bf16[128,1024]{1,0:T(8,128)(2,1)S(1)}, f32[128,1]{1,0:T(8,128)S(1)}, f32[1,128]{1,0:T(1,128)S(1)}) custom-call(s32[1]{0:T(128)S(6)} %copy.10.length_ref, f32[8,128]{1,0:T(8,128)S(1)} %first.1.token_ref, bf16[128,512]{1,0:T(8,128)(2,1)S(1)} %bitcast.16, ...), custom_call_target="tpu_custom_call" | custom-call | flops 3221225472 | bytes 8388608 | tf_op jit(solution)/shard_map/main/pallas_call | solution.py:222
  17.3 0.4 %collective-permute-start.7 = (bf16[128,2048]{1,0:T(8,128)(2,1)S(1)}, bf16[128,2048]{1,0:T(8,128)(2,1)S(1)}, u32[]{:S(2)}, u32[]{:S(2)}) collective-permute-start(bf16[128,2048]{1,0:T(8,128)(2,1)S(1)} %get-tuple-element.28), channel_id=1, source_target_pairs={{0,16},{16,0},{1,17},{17,1},{2,18},{18,2},{3,19},{19,3},{4,20},{20... | collective-permute-start | bytes 1572872 | tf_op jit(solution)/shard_map/ppermute | solution.py:207
  17.7 0.2 collective-permute-start.11
  17.8 1.5 %back.1.own_ref = f32[128,2048]{1,0:T(8,128)S(1)} custom-call(bf16[128,1024]{1,0:T(8,128)(2,1)S(1)} %get-tuple-element.27.grad_ref, bf16[4096,1024]{1,0:T(8,128)(2,1)S(1)} %bitcast.11), custom_call_target="tpu_custom_call" | custom-call | flops 536870912 | bytes 4194304 | tf_op jit(solution)/shard_map/back/pallas_call | solution.py:244
  19.3 0.0 collective-permute-done.7.sib_ref
  19.4 0.1 chip.1
  19.5 0.0 collective-permute-done.11.row_sib_ref
  19.5 0.3 gain.1
  19.7 1.3 %collective-permute-start.12 = (f32[1,640]{1,0:T(1,128)S(1)}, f32[1,640]{1,0:T(1,128)S(1)}, u32[]{:S(2)}, u32[]{:S(2)}) collective-permute-start(f32[1,640]{1,0:T(1,128)S(1)} %get-tuple-element.36), channel_id=1, source_target_pairs={{0,4},{4,0},{8,12},{12,8},{16,24},{20,28},{24,16},{28,20},{1,5},{5... | collective-permute-start | bytes 7688 | tf_op jit(solution)/shard_map/ppermute | solution.py:204
  21.1 1.3 %collective-permute-start.13 = (f32[1,640]{1,0:T(1,128)S(1)}, f32[1,640]{1,0:T(1,128)S(1)}, u32[]{:S(2)}, u32[]{:S(2)}) collective-permute-start(f32[1,640]{1,0:T(1,128)S(1)} %get-tuple-element.37), channel_id=1, source_target_pairs={{0,8},{4,12},{8,0},{12,4},{16,20},{20,16},{24,28},{28,24},{1,9},{5... | collective-permute-start | bytes 7688 | tf_op jit(solution)/shard_map/ppermute | solution.py:204
  22.4 0.9 %collective-permute-start.14 = (f32[1,640]{1,0:T(1,128)S(1)}, f32[1,640]{1,0:T(1,128)S(1)}, u32[]{:S(2)}, u32[]{:S(2)}) collective-permute-start(f32[1,640]{1,0:T(1,128)S(1)} %get-tuple-element.38), channel_id=1, source_target_pairs={{0,12},{4,8},{8,4},{12,0},{16,28},{20,24},{24,20},{28,16},{1,13},{... | collective-permute-start | bytes 7688 | tf_op jit(solution)/shard_map/ppermute | solution.py:204
  23.3 2.0 %collective-permute-start.10 = (bf16[128,512]{1,0:T(8,128)(2,1)S(1)}, bf16[128,512]{1,0:T(8,128)(2,1)S(1)}, u32[]{:S(2)}, u32[]{:S(2)}) collective-permute-start(bf16[128,512]{1,0:T(8,128)(2,1)S(1)} %get-tuple-element.32.refs_7_), channel_id=1, source_target_pairs={{0,12},{4,8},{8,4},{12,0},{16,28},{20,24},{24,20},{28,16},{1,13},{... | collective-permute-start | bytes 393224 | tf_op jit(solution)/shard_map/ppermute | solution.py:204
  25.3 1.0 %collective-permute-start.8 = (bf16[128,512]{1,0:T(8,128)(2,1)S(1)}, bf16[128,512]{1,0:T(8,128)(2,1)S(1)}, u32[]{:S(2)}, u32[]{:S(2)}) collective-permute-start(bf16[128,512]{1,0:T(8,128)(2,1)S(1)} %get-tuple-element.30.refs_5_), channel_id=1, source_target_pairs={{0,4},{4,0},{8,12},{12,8},{16,24},{20,28},{24,16},{28,20},{1,5},{5... | collective-permute-start | bytes 393224 | tf_op jit(solution)/shard_map/ppermute | solution.py:204
  26.3 0.0 collective-permute-done.12.refs_1_
  26.3 0.5 %collective-permute-start.9 = (bf16[128,512]{1,0:T(8,128)(2,1)S(1)}, bf16[128,512]{1,0:T(8,128)(2,1)S(1)}, u32[]{:S(2)}, u32[]{:S(2)}) collective-permute-start(bf16[128,512]{1,0:T(8,128)(2,1)S(1)} %get-tuple-element.31.refs_6_), channel_id=1, source_target_pairs={{0,8},{4,12},{8,0},{12,4},{16,20},{20,16},{24,28},{28,24},{1,9},{5... | collective-permute-start | bytes 393224 | tf_op jit(solution)/shard_map/ppermute | solution.py:204
  26.8 0.0 collective-permute-done.13.refs_2_
  26.8 0.1 collective-permute-done.14.refs_3_
  26.9 3.7 %collective-permute-start.15 = (f32[1,128]{1,0:T(1,128)S(1)}, f32[1,128]{1,0:T(1,128)S(1)}, u32[]{:S(2)}, u32[]{:S(2)}) collective-permute-start(f32[1,128]{1,0:T(1,128)S(1)} %get-tuple-element.44), channel_id=1, source_target_pairs={{0,3},{1,2},{2,1},{3,0},{4,7},{5,6},{6,5},{7,4},{8,11},{9,10},{10,... | collective-permute-start | bytes 1544 | tf_op jit(solution)/shard_map/ppermute | solution.py:293
  30.6 0.0 collective-permute-start.16
  30.6 0.0 collective-permute-done.10.refs_2_
  30.6 0.9 %collective-permute-start.17 = (f32[1,128]{1,0:T(1,128)S(1)}, f32[1,128]{1,0:T(1,128)S(1)}, u32[]{:S(2)}, u32[]{:S(2)}) collective-permute-start(f32[1,128]{1,0:T(1,128)S(1)} %get-tuple-element.42), channel_id=1, source_target_pairs={{0,1},{1,0},{2,3},{3,2},{4,5},{5,4},{6,7},{7,6},{8,9},{9,8},{10,11... | collective-permute-start | bytes 1544 | tf_op jit(solution)/shard_map/ppermute | solution.py:293
  31.5 0.5 %collective-permute-done.8.refs_0_ = bf16[128,512]{1,0:T(8,128)(2,1)S(1)} collective-permute-done((bf16[128,512]{1,0:T(8,128)(2,1)S(1)}, bf16[128,512]{1,0:T(8,128)(2,1)S(1)}, u32[]{:S(2)}, u32[]{:S(2)}) %collective-permute-start.8) | collective-permute-done | bytes 131104 | tf_op jit(solution)/shard_map/ppermute | solution.py:204
  32.0 0.0 collective-permute-done.9.refs_1_
  32.0 0.1 total.1.grad_ref
  32.1 0.2 collective-permute-done.15.refs_5_
  32.3 2.7 %collective-permute-done.16.refs_6_ = f32[1,128]{1,0:T(1,128)S(1)} collective-permute-done((f32[1,128]{1,0:T(1,128)S(1)}, f32[1,128]{1,0:T(1,128)S(1)}, u32[]{:S(2)}, u32[]{:S(2)}) %collective-permute-start.16) | collective-permute-done | bytes 544 | tf_op jit(solution)/shard_map/ppermute | solution.py:293
  35.0 0.0 collective-permute-done.17.refs_7_
  35.0 0.9 %last.1 = (bf16[128,512]{1,0:T(8,128)(2,1)}, f32[1,128]{1,0:T(1,128)}, f32[1,128]{1,0:T(1,128)}) custom-call(f32[128,512]{1,0:T(8,128)S(1)} %total.1.grad_ref, bf16[128,512]{1,0:T(8,128)(2,1)S(1)} %bitcast.18, f32[128,1]{1,0:T(8,128)S(1)} %get-tuple-element.33.inv_ref, f32[1,4096]{1,0:T(1,128)S(1)} %bitcast.20, f32[1,640]{1,0:T(1,128)S(1)} %get-tuple-element.35.refs_0_, ...), custom_call_target="tpu_custom_call" | custom-call | flops 655360 | bytes 1048576 | tf_op jit(solution)/shard_map/last/pallas_call | solution.py:303
  (10 shorter events, 0.0 us)
Async XLA Ops:
  0.6 12.6 %slice-start = ((s8[8388608]{0:T(1024)(128)(4,1)}), s8[4194304]{0:T(1024)(128)(4,1)S(1)}, s32[]{:S(2)}) async-start(s8[8388608]{0:T(1024)(128)(4,1)} %bitcast.8), calls=%async_computation | async-start | bytes 8388608
  0.6 12.6 %slice-start.1 = ((s8[8388608]{0:T(1024)(128)(4,1)}), s8[4194304]{0:T(1024)(128)(4,1)S(1)}, s32[]{:S(2)}) async-start(s8[8388608]{0:T(1024)(128)(4,1)} %bitcast.8), calls=%async_computation.1 | async-start | bytes 8388608
  0.7 12.6 %copy-start = (bf16[1,128,512]{2,1,0:T(8,128)(2,1)S(1)}, bf16[1,128,512]{2,1,0:T(8,128)(2,1)}, u32[]{:S(2)}) copy-start(bf16[1,128,512]{2,1,0:T(8,128)(2,1)} %param.6) | copy-start | bytes 393220
  0.7 12.6 %copy-start.1 = (f32[4096]{0:T(1024)S(1)}, f32[4096]{0:T(1024)}, u32[]{:S(2)}) copy-start(f32[4096]{0:T(1024)} %param.7) | copy-start | bytes 49156
  0.7 12.6 %copy-start.2 = (bf16[1,1,256,512]{3,2,1,0:T(8,128)(2,1)S(1)}, bf16[1,1,256,512]{3,2,1,0:T(8,128)(2,1)}, u32[]{:S(2)}) copy-start(bf16[1,1,256,512]{3,2,1,0:T(8,128)(2,1)} %param.9) | copy-start | bytes 786436
  0.7 12.6 %copy-start.3 = (bf16[1,1,256,512]{3,2,1,0:T(8,128)(2,1)S(1)}, bf16[1,1,256,512]{3,2,1,0:T(8,128)(2,1)}, u32[]{:S(2)}) copy-start(bf16[1,1,256,512]{3,2,1,0:T(8,128)(2,1)} %param.10) | copy-start | bytes 786436
  0.7 7.1 %collective-permute-start = (bf16[128,512]{1,0:T(8,128)(2,1)}, bf16[128,512]{1,0:T(8,128)(2,1)S(1)}, u32[]{:S(2)}, u32[]{:S(2)}) collective-permute-start(bf16[128,512]{1,0:T(8,128)(2,1)} %bitcast.12), channel_id=1, source_target_pairs={{0,4},{4,0},{8,12},{12,8},{16,24},{20,28},{24,16},{28,20},{1,5},{5... | collective-permute-start | bytes 393224 | tf_op jit(solution)/shard_map/ppermute | solution.py:204
  3.7 8.0 %collective-permute-start.1 = (bf16[128,512]{1,0:T(8,128)(2,1)}, bf16[128,512]{1,0:T(8,128)(2,1)S(1)}, u32[]{:S(2)}, u32[]{:S(2)}) collective-permute-start(bf16[128,512]{1,0:T(8,128)(2,1)} %bitcast.13), channel_id=1, source_target_pairs={{0,8},{4,12},{8,0},{12,4},{16,20},{20,16},{24,28},{28,24},{1,9},{5... | collective-permute-start | bytes 393224 | tf_op jit(solution)/shard_map/ppermute | solution.py:204
  5.2 6.5 %collective-permute-start.2 = (bf16[128,512]{1,0:T(8,128)(2,1)}, bf16[128,512]{1,0:T(8,128)(2,1)S(1)}, u32[]{:S(2)}, u32[]{:S(2)}) collective-permute-start(bf16[128,512]{1,0:T(8,128)(2,1)} %bitcast.14), channel_id=1, source_target_pairs={{0,12},{4,8},{8,4},{12,0},{16,28},{20,24},{24,20},{28,16},{1,13},{... | collective-permute-start | bytes 393224 | tf_op jit(solution)/shard_map/ppermute | solution.py:204
  5.2 7.6 %collective-permute-start.3 = (bf16[128,512]{1,0:T(8,128)(2,1)}, bf16[128,512]{1,0:T(8,128)(2,1)S(1)}, u32[]{:S(2)}, u32[]{:S(2)}) collective-permute-start(bf16[128,512]{1,0:T(8,128)(2,1)} %bitcast.15), channel_id=1, source_target_pairs={{0,16},{16,0},{1,17},{17,1},{2,18},{18,2},{3,19},{19,3},{4,20},{20... | collective-permute-start | bytes 393224 | tf_op jit(solution)/shard_map/ppermute | solution.py:207
  7.8 5.1 %collective-permute-start.4 = (bf16[128,512]{1,0:T(8,128)(2,1)S(1)}, bf16[128,512]{1,0:T(8,128)(2,1)S(1)}, u32[]{:S(2)}, u32[]{:S(2)}) collective-permute-start(bf16[128,512]{1,0:T(8,128)(2,1)S(1)} %collective-permute-done.refs_1_), channel_id=1, source_target_pairs={{0,16},{16,0},{1,17},{17,1},{2,18},{18,2},{3,19},{19,3},{4,20},{20... | collective-permute-start | bytes 393224 | tf_op jit(solution)/shard_map/ppermute | solution.py:207
  11.7 1.3 %collective-permute-start.5 = (bf16[128,512]{1,0:T(8,128)(2,1)S(1)}, bf16[128,512]{1,0:T(8,128)(2,1)S(1)}, u32[]{:S(2)}, u32[]{:S(2)}) collective-permute-start(bf16[128,512]{1,0:T(8,128)(2,1)S(1)} %collective-permute-done.1.refs_2_), channel_id=1, source_target_pairs={{0,16},{16,0},{1,17},{17,1},{2,18},{18,2},{3,19},{19,3},{4,20},{20... | collective-permute-start | bytes 393224 | tf_op jit(solution)/shard_map/ppermute | solution.py:207
  11.7 1.5 %collective-permute-start.6 = (bf16[128,512]{1,0:T(8,128)(2,1)S(1)}, bf16[128,512]{1,0:T(8,128)(2,1)S(1)}, u32[]{:S(2)}, u32[]{:S(2)}) collective-permute-start(bf16[128,512]{1,0:T(8,128)(2,1)S(1)} %collective-permute-done.2.refs_3_), channel_id=1, source_target_pairs={{0,16},{16,0},{1,17},{17,1},{2,18},{18,2},{3,19},{19,3},{4,20},{20... | collective-permute-start | bytes 393224 | tf_op jit(solution)/shard_map/ppermute | solution.py:207
  17.3 2.1 %collective-permute-start.7 = (bf16[128,2048]{1,0:T(8,128)(2,1)S(1)}, bf16[128,2048]{1,0:T(8,128)(2,1)S(1)}, u32[]{:S(2)}, u32[]{:S(2)}) collective-permute-start(bf16[128,2048]{1,0:T(8,128)(2,1)S(1)} %get-tuple-element.28), channel_id=1, source_target_pairs={{0,16},{16,0},{1,17},{17,1},{2,18},{18,2},{3,19},{19,3},{4,20},{20... | collective-permute-start | bytes 1572872 | tf_op jit(solution)/shard_map/ppermute | solution.py:207
  17.7 1.8 %collective-permute-start.11 = (f32[1,128]{1,0:T(1,128)S(1)}, f32[1,128]{1,0:T(1,128)S(1)}, u32[]{:S(2)}, u32[]{:S(2)}) collective-permute-start(f32[1,128]{1,0:T(1,128)S(1)} %get-tuple-element.34.row_ref), channel_id=1, source_target_pairs={{0,16},{16,0},{1,17},{17,1},{2,18},{18,2},{3,19},{19,3},{4,20},{20... | collective-permute-start | bytes 1544 | tf_op jit(solution)/shard_map/ppermute | solution.py:207
  19.7 6.5 %collective-permute-start.12 = (f32[1,640]{1,0:T(1,128)S(1)}, f32[1,640]{1,0:T(1,128)S(1)}, u32[]{:S(2)}, u32[]{:S(2)}) collective-permute-start(f32[1,640]{1,0:T(1,128)S(1)} %get-tuple-element.36), channel_id=1, source_target_pairs={{0,4},{4,0},{8,12},{12,8},{16,24},{20,28},{24,16},{28,20},{1,5},{5... | collective-permute-start | bytes 7688 | tf_op jit(solution)/shard_map/ppermute | solution.py:204
  21.1 5.7 %collective-permute-start.13 = (f32[1,640]{1,0:T(1,128)S(1)}, f32[1,640]{1,0:T(1,128)S(1)}, u32[]{:S(2)}, u32[]{:S(2)}) collective-permute-start(f32[1,640]{1,0:T(1,128)S(1)} %get-tuple-element.37), channel_id=1, source_target_pairs={{0,8},{4,12},{8,0},{12,4},{16,20},{20,16},{24,28},{28,24},{1,9},{5... | collective-permute-start | bytes 7688 | tf_op jit(solution)/shard_map/ppermute | solution.py:204
  22.4 4.5 %collective-permute-start.14 = (f32[1,640]{1,0:T(1,128)S(1)}, f32[1,640]{1,0:T(1,128)S(1)}, u32[]{:S(2)}, u32[]{:S(2)}) collective-permute-start(f32[1,640]{1,0:T(1,128)S(1)} %get-tuple-element.38), channel_id=1, source_target_pairs={{0,12},{4,8},{8,4},{12,0},{16,28},{20,24},{24,20},{28,16},{1,13},{... | collective-permute-start | bytes 7688 | tf_op jit(solution)/shard_map/ppermute | solution.py:204
  23.3 7.3 %collective-permute-start.10 = (bf16[128,512]{1,0:T(8,128)(2,1)S(1)}, bf16[128,512]{1,0:T(8,128)(2,1)S(1)}, u32[]{:S(2)}, u32[]{:S(2)}) collective-permute-start(bf16[128,512]{1,0:T(8,128)(2,1)S(1)} %get-tuple-element.32.refs_7_), channel_id=1, source_target_pairs={{0,12},{4,8},{8,4},{12,0},{16,28},{20,24},{24,20},{28,16},{1,13},{... | collective-permute-start | bytes 393224 | tf_op jit(solution)/shard_map/ppermute | solution.py:204
  25.3 6.7 %collective-permute-start.8 = (bf16[128,512]{1,0:T(8,128)(2,1)S(1)}, bf16[128,512]{1,0:T(8,128)(2,1)S(1)}, u32[]{:S(2)}, u32[]{:S(2)}) collective-permute-start(bf16[128,512]{1,0:T(8,128)(2,1)S(1)} %get-tuple-element.30.refs_5_), channel_id=1, source_target_pairs={{0,4},{4,0},{8,12},{12,8},{16,24},{20,28},{24,16},{28,20},{1,5},{5... | collective-permute-start | bytes 393224 | tf_op jit(solution)/shard_map/ppermute | solution.py:204
  26.3 5.7 %collective-permute-start.9 = (bf16[128,512]{1,0:T(8,128)(2,1)S(1)}, bf16[128,512]{1,0:T(8,128)(2,1)S(1)}, u32[]{:S(2)}, u32[]{:S(2)}) collective-permute-start(bf16[128,512]{1,0:T(8,128)(2,1)S(1)} %get-tuple-element.31.refs_6_), channel_id=1, source_target_pairs={{0,8},{4,12},{8,0},{12,4},{16,20},{20,16},{24,28},{28,24},{1,9},{5... | collective-permute-start | bytes 393224 | tf_op jit(solution)/shard_map/ppermute | solution.py:204
  26.9 5.4 %collective-permute-start.15 = (f32[1,128]{1,0:T(1,128)S(1)}, f32[1,128]{1,0:T(1,128)S(1)}, u32[]{:S(2)}, u32[]{:S(2)}) collective-permute-start(f32[1,128]{1,0:T(1,128)S(1)} %get-tuple-element.44), channel_id=1, source_target_pairs={{0,3},{1,2},{2,1},{3,0},{4,7},{5,6},{6,5},{7,4},{8,11},{9,10},{10,... | collective-permute-start | bytes 1544 | tf_op jit(solution)/shard_map/ppermute | solution.py:293
  30.6 4.4 %collective-permute-start.16 = (f32[1,128]{1,0:T(1,128)S(1)}, f32[1,128]{1,0:T(1,128)S(1)}, u32[]{:S(2)}, u32[]{:S(2)}) collective-permute-start(f32[1,128]{1,0:T(1,128)S(1)} %get-tuple-element.43), channel_id=1, source_target_pairs={{0,2},{1,3},{2,0},{3,1},{4,6},{5,7},{6,4},{7,5},{8,10},{9,11},{10,... | collective-permute-start | bytes 1544 | tf_op jit(solution)/shard_map/ppermute | solution.py:293
  30.6 4.4 %collective-permute-start.17 = (f32[1,128]{1,0:T(1,128)S(1)}, f32[1,128]{1,0:T(1,128)S(1)}, u32[]{:S(2)}, u32[]{:S(2)}) collective-permute-start(f32[1,128]{1,0:T(1,128)S(1)} %get-tuple-element.42), channel_id=1, source_target_pairs={{0,1},{1,0},{2,3},{3,2},{4,5},{5,4},{6,7},{7,6},{8,9},{9,8},{10,11... | collective-permute-start | bytes 1544 | tf_op jit(solution)/shard_map/ppermute | solution.py:293

commit v5 on v4

--- a/solution.py
+++ b/solution.py
@@ -9,6 +9,7 @@
 
 HS = 256
 EPS = 1e-06
+ROW_TERMS = 3
 LAST = (((1,), (1,)), ((), ()))
 FIRST = (((0,), (0,)), ((), ()))
 VMEM = pl.BlockSpec(memory_space=pltpu.VMEM)
@@ -40,39 +41,60 @@
     token_ref[...] = jnp.zeros_like(token_ref)
 
 
+def project(parts, steps, chunk_refs, other_refs, gain_ref, weight, square, product_ref, started):
+    me, section = lax.axis_index("sec"), lax.axis_index("section")
+    feats = chunk_refs[0].shape[1]
+    for refs, owner in ((chunk_refs, me), (other_refs, 1 - me)):
+        for step, ref in zip(steps, refs, strict=True):
+            peer = section ^ section_step(owner, step, parts)
+            at = pl.multiple_of((owner * parts + peer) * feats, feats)
+            cols = pl.ds(at, feats)
+            x = ref[...].astype(jnp.float32)
+            scaled = (x * gain_ref[:, cols]).astype(jnp.bfloat16)
+            part = jnp.dot(scaled, weight[cols, :], preferred_element_type=jnp.float32)
+            if started:
+                product_ref[...] += part
+            else:
+                product_ref[...] = part
+                started = True
+            x = x * x
+            for i in range(0, feats, 128):
+                square = x[:, i : i + 128] if square is None else square + x[:, i : i + 128]
+    return square
+
+
+def early_kernel(parts, steps, *refs):
+    count = len(steps)
+    gain_ref, weight, product_ref, square_ref = refs[2 * count :]
+    square_ref[...] = project(
+        parts, steps, refs[:count], refs[count : 2 * count], gain_ref, weight, None, product_ref, False
+    )
+
+
 def main_kernel(
     parts,
+    steps,
     heads,
     length_ref,
     token_ref,
     *refs,
 ):
-    chunk_refs = refs[: 2 * parts]
-    (gain_ref, weight, query_ref, cot_ref) = refs[2 * parts : 2 * parts + 4]
-    (att_ref, sib_ref, kv_grad, inv_ref, row_ref) = refs[2 * parts + 4 : 2 * parts + 9]
-    (memory, kv) = refs[2 * parts + 9 :]
-    tokens, feats = chunk_refs[0].shape
+    count = len(steps)
+    chunk_refs, other_refs, refs = refs[:count], refs[count : 2 * count], refs[2 * count :]
+    (product_ref, square_ref, gain_ref, weight, query_ref, cot_ref) = refs[:6]
+    (att_hbm, sib_ref, kv_grad, inv_ref) = refs[6:10]
+    (kv, att_ref, sem) = refs[10:]
+    tokens = kv.shape[0]
     width = weight.shape[0]
     half = width // 2
-
-    square = None
-    for ref in chunk_refs:
-        x = ref[...].astype(jnp.float32)
-        x = x * x
-        for i in range(0, feats, 128):
-            square = x[:, i : i + 128] if square is None else square + x[:, i : i + 128]
-    square = jnp.sum(square, axis=1, keepdims=True)
-    inv_rms = lax.rsqrt(square / width + EPS)
+    me = lax.axis_index("sec")
+
+    kv[...] = product_ref[...]
+    square = project(
+        parts, steps, chunk_refs, other_refs, gain_ref, weight, square_ref[...], kv, True
+    )
+    inv_rms = lax.rsqrt(jnp.sum(square, axis=1, keepdims=True) / width + EPS)
     inv_ref[...] = inv_rms
-    me, section = lax.axis_index("sec"), lax.axis_index("section")
-    for j, ref in enumerate(chunk_refs):
-        owner = me if j < parts else 1 - me
-        peer = section ^ section_step(owner, j % parts, parts)
-        at = pl.multiple_of((owner * parts + peer) * feats, feats)
-        normed = ref[...].astype(jnp.float32) * inv_rms
-        memory[:, pl.ds(at, feats)] = (normed * gain_ref[:, pl.ds(at, feats)]).astype(jnp.bfloat16)
-
-    kv[...] = jnp.dot(memory[...], weight[...], preferred_element_type=jnp.float32)
 
     scale = HS ** (-0.5)
     live = lax.broadcasted_iota(jnp.int32, (query_ref.shape[0], HS), 0) < length_ref[0]
@@ -80,7 +102,7 @@
     for h in range(heads):
         cols = pl.ds(h * HS, HS)
         key_cols, value_cols = pl.ds(2 * h * HS, HS), pl.ds((2 * h + 1) * HS, HS)
-        key_full, value_full = kv[:, key_cols], kv[:, value_cols]
+        key_full, value_full = kv[:, key_cols] * inv_rms, kv[:, value_cols] * inv_rms
         key_rows, value_rows = key_full.astype(jnp.bfloat16), value_full.astype(jnp.bfloat16)
         query = query_ref[:, cols]
         cot = cot_ref[:, cols]
@@ -106,15 +128,25 @@
             keepdims=True,
         )
         row_part = here if row_part is None else row_part + here
-    row_ref[...] = jnp.transpose(jnp.broadcast_to(row_part, (tokens, 128)))[0:1, :]
+    att_out = pltpu.make_async_copy(att_ref, att_hbm, sem)
+    att_out.start()
+    rest = jnp.transpose(jnp.broadcast_to(row_part, (tokens, 128)))[0:8, :]
+    pieces = jnp.zeros_like(rest)
+    place = lax.broadcasted_iota(jnp.int32, rest.shape, 0)
+    for i in range(ROW_TERMS):
+        term = rest.astype(jnp.bfloat16).astype(jnp.float32)
+        pieces = jnp.where(place == i, term, pieces)
+        rest = rest - term
+    sib_ref[pl.ds(tokens, 8), :] = jnp.zeros((8, half), jnp.bfloat16)
+    sib_ref[pl.ds(tokens, 8), pl.ds(0, 128)] = pieces.astype(jnp.bfloat16)
 
     grad = kv_grad[...]
     tile = half // 4
     for t in range(4):
         rows = pl.ds(pl.multiple_of((1 - me) * half + t * tile, tile), tile)
-        sib_ref[:, pl.ds(t * tile, tile)] = lax.dot_general(
-            grad, weight[rows, :], LAST, preferred_element_type=jnp.float32
-        ).astype(jnp.bfloat16)
+        part = lax.dot_general(weight[rows, :], grad, LAST, preferred_element_type=jnp.float32)
+        sib_ref[pl.ds(0, tokens), pl.ds(t * tile, tile)] = jnp.transpose(part.astype(jnp.bfloat16))
+    att_out.wait()
 
 
 def back_kernel(grad_ref, weight, own_ref):
@@ -124,8 +156,8 @@
     tile = half // 4
     for t in range(4):
         rows = pl.ds(pl.multiple_of(me * half + t * tile, tile), tile)
-        own_ref[:, pl.ds(t * tile, tile)] = lax.dot_general(
-            grad, weight[rows, :], LAST, preferred_element_type=jnp.float32
+        own_ref[:, pl.ds(t * tile, tile)] = jnp.transpose(
+            lax.dot_general(weight[rows, :], grad, LAST, preferred_element_type=jnp.float32)
         )
 
 
@@ -134,7 +166,9 @@
     me, section = lax.axis_index("sec"), lax.axis_index("section")
     for k in range(parts):
         at = pl.multiple_of((section ^ section_step(me, k, parts)) * feats, feats)
-        total = own_ref[:, pl.ds(at, feats)] + sib_ref[:, pl.ds(at, feats)].astype(jnp.float32)
+        total = own_ref[:, pl.ds(at, feats)] + sib_ref[pl.ds(0, own_ref.shape[0]), pl.ds(at, feats)].astype(
+            jnp.float32
+        )
         if k == 0:
             kept_ref[...] = total
         else:
@@ -145,7 +179,11 @@
     chunk_refs, total_refs, small_refs = refs[:parts], refs[parts : 2 * parts], refs[2 * parts :]
     feats = chunk_refs[0].shape[1]
     inv_rms = inv_ref[...]
-    row = row_ref[...] + row_sib_ref[...]
+    tokens = chunk_refs[0].shape[0]
+    row = 0.0
+    for ref in (row_ref, row_sib_ref):
+        terms = ref[pl.ds(tokens, 8), pl.ds(0, 128)].astype(jnp.float32)
+        row = row + ((terms[0:1, :] + terms[1:2, :]) + terms[2:3, :])
     for k in range(parts):
         normed = chunk_refs[k][...].astype(jnp.float32) * inv_rms
         total = total_refs[k][...].astype(jnp.float32)
@@ -218,29 +256,57 @@
     chunks = [rows]
     for k in range(1, parts):
         chunks.append(lax.optimization_barrier((to_section(rows, k), token))[0])
-    others = [to_core(c) for c in chunks]
-    att, sib, kv_grad, inv_rms, row = pl.pallas_call(
-        functools.partial(main_kernel, parts, heads),
+    first, second = range(1), range(1, parts)
+    others = [to_core(chunks[k]) for k in first]
+    product, square = pl.pallas_call(
+        functools.partial(early_kernel, parts, first),
+        out_shape=(
+            jax.ShapeDtypeStruct((tokens, weight.shape[1]), jnp.float32),
+            jax.ShapeDtypeStruct((tokens, 128), jnp.float32),
+        ),
+        in_specs=[VMEM] * (2 * len(first) + 2),
+        out_specs=(VMEM, VMEM),
+        compiler_params=pltpu.CompilerParams(vmem_limit_bytes=16 << 20),
+        cost_estimate=pl.CostEstimate(
+            flops=20_000_000_000, bytes_accessed=weight.size, transcendentals=0
+        ),
+        name="early",
+    )(*[chunks[k] for k in first], *[others[k] for k in first], gain, weight)
+    for k in second:
+        chunks[k] = lax.optimization_barrier((chunks[k], square))[0]
+        others.append(to_core(chunks[k]))
+    att, sib, kv_grad, inv_rms = pl.pallas_call(
+        functools.partial(main_kernel, parts, second, heads),
         out_shape=(
             jax.ShapeDtypeStruct(query.shape, jnp.bfloat16),
-            jax.ShapeDtypeStruct((tokens, half), jnp.bfloat16),
+            jax.ShapeDtypeStruct((tokens + 8, half), jnp.bfloat16),
             jax.ShapeDtypeStruct((tokens, weight.shape[1]), jnp.bfloat16),
             jax.ShapeDtypeStruct((tokens, 1), jnp.float32),
-            jax.ShapeDtypeStruct((1, tokens), jnp.float32),
-        ),
-        in_specs=[SMEM, ANY] + [VMEM] * (2 * parts) + [VMEM, VMEM, VMEM, VMEM],
-        out_specs=(VMEM,) * 5,
+        ),
+        in_specs=[SMEM, ANY] + [VMEM] * (2 * len(second) + 6),
+        out_specs=(ANY, VMEM, VMEM, VMEM),
         scratch_shapes=[
-            pltpu.VMEM((tokens, width), jnp.bfloat16),
             pltpu.VMEM((tokens, weight.shape[1]), jnp.float32),
+            pltpu.VMEM(query.shape, jnp.bfloat16),
+            pltpu.SemaphoreType.DMA(()),
         ],
         compiler_params=pltpu.CompilerParams(vmem_limit_bytes=16 << 20),
         cost_estimate=pl.CostEstimate(
-            flops=3 * flops, bytes_accessed=2 * weight.size, transcendentals=dec * tokens * heads
+            flops=2 * flops, bytes_accessed=2 * weight.size, transcendentals=dec * tokens * heads
         ),
         name="main",
-    )(target_lengths, token, *chunks, *others, gain, weight, query, cot)
-
+    )(
+        target_lengths,
+        token,
+        *[chunks[k] for k in second],
+        *[others[k] for k in second],
+        product,
+        square,
+        gain,
+        weight,
+        query,
+        cot,
+    )
     own = pl.pallas_call(
         back_kernel,
         out_shape=jax.ShapeDtypeStruct((tokens, half), jnp.float32),
@@ -252,7 +318,6 @@
         ),
         name="back",
     )(kv_grad, weight)
-    row_sib = to_core(row)
     sib_in = to_core(sib)
 
     kept, *big = pl.pallas_call(
@@ -277,7 +342,7 @@
             flops=20_000_000_000, bytes_accessed=8 * tokens * half, transcendentals=0
         ),
         name="gain",
-    )(row, row_sib, inv_rms, *chunks, kept, *big)
+    )(sib, sib_in, inv_rms, *chunks, kept, *big)
 
     big_in = [to_section(big[k - 1], k) for k in range(1, parts)]
     small_in = [small[0]] + [to_section(small[k], k) for k in range(1, parts)]

time: 36 us -> 35.4 us (0.983)
  Pallas kernels: 6.79 us -> 6.3 us
    ppermute x9, waiting for transfers between devices: 7.04 us -> 6.25 us  [to_section(): return lax.ppermute(x, ('sec', 'section'), pairs)]
    ppermute x6 -> x5, waiting for transfers between devices: 0.36 us -> 1.14 us  [to_core(): return lax.ppermute(x, 'sec', swap)]
    ppermute x3, starting transfers between devices: 4.6 us -> 5.31 us  [per_device(): pieces.append(lax.ppermute(send, 'dp', [(i, i ^ k) for i in range(seqs)]))]
    ppermute x9, starting transfers between devices: 11.6 us -> 11.1 us  [to_section(): return lax.ppermute(x, ('sec', 'section'), pairs)]
    ppermute x6 -> x5, starting transfers between devices: 1.09 us -> 0.73 us  [to_core(): return lax.ppermute(x, 'sec', swap)]
    pallas_call x1 -> x2, Pallas kernels: 3.99 us -> 3.66 us  [the longest x1 3.19 us: per_device(): pl.pallas_call(functools.partial(main_kernel, parts, second, heads), out_...]
  transfers between devices with their start and end apart: 18 -> 17, of which waited for: 8 -> 6; matrix products, arithmetic and copies ran while one was open for 0% -> 0% of each run, Pallas kernels for 5% -> 5%
where the time goes in v5:
time: 35.4 us; the launch traced here: 35.3 us
  starting transfers between devices  17.2 us (49%)
  waiting for transfers between devices  10.3 us (29%)
  Pallas kernels  6.3 us (18%)
  between operations  1.43 us (4%)
    ppermute x9, starting transfers between devices, to_section(): return lax.ppermute(x, ('sec', 'section'), pairs)  11.1 us
    ppermute x9, waiting for transfers between devices, to_section(): return lax.ppermute(x, ('sec', 'section'), pairs)  6.25 us
    ppermute x3, starting transfers between devices, per_device(): pieces.append(lax.ppermute(send, 'dp', [(i, i ^ k) for i in range(seqs)]))  5.31 us
    pallas_call x1, Pallas kernels, per_device(): pl.pallas_call(functools.partial(main_kernel, parts, second, heads), out_...  3.19 us
    ppermute x3, waiting for transfers between devices, per_device(): pieces.append(lax.ppermute(send, 'dp', [(i, i ^ k) for i in range(seqs)]))  2.92 us
    pallas_call x1, Pallas kernels, per_device(): pl.pallas_call(back_kernel, out_shape=jax.ShapeDtypeStruct((tokens, half)...  1.35 us
    ppermute x5, waiting for transfers between devices, to_core(): return lax.ppermute(x, 'sec', swap)  1.14 us
    pallas_call x1, Pallas kernels, per_device(): pl.pallas_call(functools.partial(last_kernel, parts, width), out_shape=(j...  0.86 us
  transfers between devices with their start and end apart: 17, of which 6 were waited for; matrix products, arithmetic and copies ran while one was open for 0% of the time, Pallas kernels for 5%

profile of v5, /device:TPU:0, one launch (start us, length us, event | category | flops | bytes accessed | tf_op | source)
XLA Modules:
  0.0 35.3 jit_solution(2457698808793057706)
XLA Ops:
  0.6 0.0 slice-start
  0.6 0.0 slice-start.1
  0.7 0.0 copy-start.2
  0.7 0.0 copy-start.3
  0.7 0.5 %collective-permute-start.1 = (bf16[128,512]{1,0:T(8,128)(2,1)}, bf16[128,512]{1,0:T(8,128)(2,1)S(1)}, u32[]{:S(2)}, u32[]{:S(2)}) collective-permute-start(bf16[128,512]{1,0:T(8,128)(2,1)} %bitcast.15), channel_id=1, source_target_pairs={{0,16},{16,0},{1,17},{17,1},{2,18},{18,2},{3,19},{19,3},{4,20},{20... | collective-permute-start | bytes 393224 | tf_op jit(solution)/shard_map/ppermute | solution.py:245
  1.2 2.6 %collective-permute-start = (bf16[128,512]{1,0:T(8,128)(2,1)}, bf16[128,512]{1,0:T(8,128)(2,1)S(1)}, u32[]{:S(2)}, u32[]{:S(2)}) collective-permute-start(bf16[128,512]{1,0:T(8,128)(2,1)} %bitcast.16), channel_id=1, source_target_pairs={{0,4},{4,0},{8,12},{12,8},{16,24},{20,28},{24,16},{28,20},{1,5},{5... | collective-permute-start | bytes 393224 | tf_op jit(solution)/shard_map/ppermute | solution.py:242
  3.8 1.5 %collective-permute-start.2 = (bf16[128,512]{1,0:T(8,128)(2,1)}, bf16[128,512]{1,0:T(8,128)(2,1)S(1)}, u32[]{:S(2)}, u32[]{:S(2)}) collective-permute-start(bf16[128,512]{1,0:T(8,128)(2,1)} %bitcast.17), channel_id=1, source_target_pairs={{0,8},{4,12},{8,0},{12,4},{16,20},{20,16},{24,28},{28,24},{1,9},{5... | collective-permute-start | bytes 393224 | tf_op jit(solution)/shard_map/ppermute | solution.py:242
  5.3 0.0 collective-permute-start.3
  5.3 0.0 collective-permute-done.1.refs_1_
  5.3 0.0 slice-done.1
  5.3 0.0 copy-start
  5.3 0.0 copy-start.1
  5.4 0.5 %early.1 = (f32[128,1024]{1,0:T(8,128)S(1)}, f32[128,128]{1,0:T(8,128)S(1)}) custom-call(bf16[128,512]{1,0:T(8,128)(2,1)S(1)} %bitcast.19, bf16[128,512]{1,0:T(8,128)(2,1)S(1)} %collective-permute-done.1.refs_1_, f32[1,4096]{1,0:T(1,128)S(1)} %bitcast.22, bf16[4096,1024]{1,0:T(8,128)(2,1)S(1)} %bitcast.10), custom_call_target="tpu_custom_call" | custom-call | flops 20000000000 | bytes 4194304 | tf_op jit(solution)/shard_map/early/pallas_call | solution.py:261
  5.8 1.5 %collective-permute-done.refs_0_.refs_1_ = bf16[128,512]{1,0:T(8,128)(2,1)S(1)} collective-permute-done((bf16[128,512]{1,0:T(8,128)(2,1)}, bf16[128,512]{1,0:T(8,128)(2,1)S(1)}, u32[]{:S(2)}, u32[]{:S(2)}) %collective-permute-start) | collective-permute-done | bytes 131104 | tf_op jit(solution)/shard_map/ppermute | solution.py:242
  7.3 0.0 collective-permute-start.4
  7.3 3.6 %collective-permute-done.2.refs_1_.refs_2_ = bf16[128,512]{1,0:T(8,128)(2,1)S(1)} collective-permute-done((bf16[128,512]{1,0:T(8,128)(2,1)}, bf16[128,512]{1,0:T(8,128)(2,1)S(1)}, u32[]{:S(2)}, u32[]{:S(2)}) %collective-permute-start.2) | collective-permute-done | bytes 131104 | tf_op jit(solution)/shard_map/ppermute | solution.py:242
  10.9 0.0 collective-permute-start.5
  10.9 1.2 %collective-permute-done.3.refs_2_.refs_3_ = bf16[128,512]{1,0:T(8,128)(2,1)S(1)} collective-permute-done((bf16[128,512]{1,0:T(8,128)(2,1)}, bf16[128,512]{1,0:T(8,128)(2,1)S(1)}, u32[]{:S(2)}, u32[]{:S(2)}) %collective-permute-start.3) | collective-permute-done | bytes 131104 | tf_op jit(solution)/shard_map/ppermute | solution.py:242
  12.1 0.0 collective-permute-start.6
  12.7 0.0 collective-permute-done.4.refs_3_
  12.7 0.0 collective-permute-done.5.refs_4_
  12.8 0.7 %collective-permute-done.6.refs_5_ = bf16[128,512]{1,0:T(8,128)(2,1)S(1)} collective-permute-done((bf16[128,512]{1,0:T(8,128)(2,1)S(1)}, bf16[128,512]{1,0:T(8,128)(2,1)S(1)}, u32[]{:S(2)}, u32[]{:S(2)}) %collective-permute-start.6) | collective-permute-done | bytes 131104 | tf_op jit(solution)/shard_map/ppermute | solution.py:245
  13.4 3.2 %main.1 = (bf16[256,512]{1,0:T(8,128)(2,1)}, bf16[136,2048]{1,0:T(8,128)(2,1)S(1)}, bf16[128,1024]{1,0:T(8,128)(2,1)S(1)}, f32[128,1]{1,0:T(8,128)S(1)}) custom-call(s32[1]{0:T(128)S(6)} %copy.10.length_ref, f32[8,128]{1,0:T(8,128)S(1)} %first.1.token_ref, bf16[128,512]{1,0:T(8,128)(2,1)S(1)} %collective-permute-done.refs_0_.refs_1_, ...), custom_call_target="tpu_custom_call" | custom-call | flops 2147483648 | bytes 8388608 | tf_op jit(solution)/shard_map/main/pallas_call | solution.py:278
  16.6 0.2 collective-permute-start.7
  16.8 1.4 %back.1.own_ref = f32[128,2048]{1,0:T(8,128)S(1)} custom-call(bf16[128,1024]{1,0:T(8,128)(2,1)S(1)} %get-tuple-element.36.grad_ref, bf16[4096,1024]{1,0:T(8,128)(2,1)S(1)} %bitcast.12), custom_call_target="tpu_custom_call" | custom-call | flops 536870912 | bytes 4194304 | tf_op jit(solution)/shard_map/back/pallas_call | solution.py:310
  18.2 0.5 %collective-permute-done.7.sib_ref.row_sib_ref = bf16[136,2048]{1,0:T(8,128)(2,1)S(1)} collective-permute-done((bf16[136,2048]{1,0:T(8,128)(2,1)S(1)}, bf16[136,2048]{1,0:T(8,128)(2,1)S(1)}, u32[]{:S(2)}, u32[]{:S(2)}) %collective-permute-start.7) | collective-permute-done | bytes 557088 | tf_op jit(solution)/shard_map/ppermute | solution.py:245
  18.7 0.1 chip.1
  18.8 0.3 gain.1
  19.0 1.8 %collective-permute-start.11 = (f32[1,640]{1,0:T(1,128)S(1)}, f32[1,640]{1,0:T(1,128)S(1)}, u32[]{:S(2)}, u32[]{:S(2)}) collective-permute-start(f32[1,640]{1,0:T(1,128)S(1)} %get-tuple-element.44), channel_id=1, source_target_pairs={{0,4},{4,0},{8,12},{12,8},{16,24},{20,28},{24,16},{28,20},{1,5},{5... | collective-permute-start | bytes 7688 | tf_op jit(solution)/shard_map/ppermute | solution.py:242
  20.8 0.3 collective-permute-start.12
  21.1 1.5 %collective-permute-start.13 = (f32[1,640]{1,0:T(1,128)S(1)}, f32[1,640]{1,0:T(1,128)S(1)}, u32[]{:S(2)}, u32[]{:S(2)}) collective-permute-start(f32[1,640]{1,0:T(1,128)S(1)} %get-tuple-element.46), channel_id=1, source_target_pairs={{0,12},{4,8},{8,4},{12,0},{16,28},{20,24},{24,20},{28,16},{1,13},{... | collective-permute-start | bytes 7688 | tf_op jit(solution)/shard_map/ppermute | solution.py:242
  22.6 1.4 %collective-permute-start.10 = (bf16[128,512]{1,0:T(8,128)(2,1)S(1)}, bf16[128,512]{1,0:T(8,128)(2,1)S(1)}, u32[]{:S(2)}, u32[]{:S(2)}) collective-permute-start(bf16[128,512]{1,0:T(8,128)(2,1)S(1)} %get-tuple-element.41.refs_7_), channel_id=1, source_target_pairs={{0,12},{4,8},{8,4},{12,0},{16,28},{20,24},{24,20},{28,16},{1,13},{... | collective-permute-start | bytes 393224 | tf_op jit(solution)/shard_map/ppermute | solution.py:242
  24.0 1.4 %collective-permute-start.8 = (bf16[128,512]{1,0:T(8,128)(2,1)S(1)}, bf16[128,512]{1,0:T(8,128)(2,1)S(1)}, u32[]{:S(2)}, u32[]{:S(2)}) collective-permute-start(bf16[128,512]{1,0:T(8,128)(2,1)S(1)} %get-tuple-element.39.refs_5_), channel_id=1, source_target_pairs={{0,4},{4,0},{8,12},{12,8},{16,24},{20,28},{24,16},{28,20},{1,5},{5... | collective-permute-start | bytes 393224 | tf_op jit(solution)/shard_map/ppermute | solution.py:242
  25.4 0.0 collective-permute-done.11.refs_1_
  25.4 0.7 %collective-permute-start.9 = (bf16[128,512]{1,0:T(8,128)(2,1)S(1)}, bf16[128,512]{1,0:T(8,128)(2,1)S(1)}, u32[]{:S(2)}, u32[]{:S(2)}) collective-permute-start(bf16[128,512]{1,0:T(8,128)(2,1)S(1)} %get-tuple-element.40.refs_6_), channel_id=1, source_target_pairs={{0,8},{4,12},{8,0},{12,4},{16,20},{20,16},{24,28},{28,24},{1,9},{5... | collective-permute-start | bytes 393224 | tf_op jit(solution)/shard_map/ppermute | solution.py:242
  26.1 0.0 collective-permute-done.12.refs_2_
  26.1 0.0 collective-permute-done.13.refs_3_
  26.1 3.9 %collective-permute-start.14 = (f32[1,128]{1,0:T(1,128)S(1)}, f32[1,128]{1,0:T(1,128)S(1)}, u32[]{:S(2)}, u32[]{:S(2)}) collective-permute-start(f32[1,128]{1,0:T(1,128)S(1)} %get-tuple-element.52), channel_id=1, source_target_pairs={{0,3},{1,2},{2,1},{3,0},{4,7},{5,6},{6,5},{7,4},{8,11},{9,10},{10,... | collective-permute-start | bytes 1544 | tf_op jit(solution)/shard_map/ppermute | solution.py:358
  30.0 0.0 collective-permute-start.15
  30.0 0.0 collective-permute-done.10.refs_2_
  30.0 1.4 %collective-permute-start.16 = (f32[1,128]{1,0:T(1,128)S(1)}, f32[1,128]{1,0:T(1,128)S(1)}, u32[]{:S(2)}, u32[]{:S(2)}) collective-permute-start(f32[1,128]{1,0:T(1,128)S(1)} %get-tuple-element.50), channel_id=1, source_target_pairs={{0,1},{1,0},{2,3},{3,2},{4,5},{5,4},{6,7},{7,6},{8,9},{9,8},{10,11... | collective-permute-start | bytes 1544 | tf_op jit(solution)/shard_map/ppermute | solution.py:358
  31.4 0.0 collective-permute-done.8.refs_0_
  31.4 0.0 collective-permute-done.9.refs_1_
  31.4 0.1 total.1.grad_ref
  31.5 0.0 collective-permute-done.14.refs_5_
  31.5 2.9 %collective-permute-done.15.refs_6_ = f32[1,128]{1,0:T(1,128)S(1)} collective-permute-done((f32[1,128]{1,0:T(1,128)S(1)}, f32[1,128]{1,0:T(1,128)S(1)}, u32[]{:S(2)}, u32[]{:S(2)}) %collective-permute-start.15) | collective-permute-done | bytes 544 | tf_op jit(solution)/shard_map/ppermute | solution.py:358
  34.4 0.0 collective-permute-done.16.refs_7_
  34.4 0.9 %last.1 = (bf16[128,512]{1,0:T(8,128)(2,1)}, f32[1,128]{1,0:T(1,128)}, f32[1,128]{1,0:T(1,128)}) custom-call(f32[128,512]{1,0:T(8,128)S(1)} %total.1.grad_ref, bf16[128,512]{1,0:T(8,128)(2,1)S(1)} %bitcast.21, f32[128,1]{1,0:T(8,128)S(1)} %get-tuple-element.42.inv_ref, f32[1,4096]{1,0:T(1,128)S(1)} %bitcast.24, f32[1,640]{1,0:T(1,128)S(1)} %get-tuple-element.43.refs_0_, ...), custom_call_target="tpu_custom_call" | custom-call | flops 655360 | bytes 1048576 | tf_op jit(solution)/shard_map/last/pallas_call | solution.py:368
  (9 shorter events, 0.0 us)
Async XLA Ops:
  0.6 4.7 %slice-start = ((s8[8388608]{0:T(1024)(128)(4,1)}), s8[4194304]{0:T(1024)(128)(4,1)S(1)}, s32[]{:S(2)}) async-start(s8[8388608]{0:T(1024)(128)(4,1)} %bitcast.8), calls=%async_computation | async-start | bytes 8388608
  0.6 4.7 %slice-start.1 = ((s8[8388608]{0:T(1024)(128)(4,1)}), s8[4194304]{0:T(1024)(128)(4,1)S(1)}, s32[]{:S(2)}) async-start(s8[8388608]{0:T(1024)(128)(4,1)} %bitcast.8), calls=%async_computation.1 | async-start | bytes 8388608
  0.7 4.7 %copy-start.2 = (bf16[1,128,512]{2,1,0:T(8,128)(2,1)S(1)}, bf16[1,128,512]{2,1,0:T(8,128)(2,1)}, u32[]{:S(2)}) copy-start(bf16[1,128,512]{2,1,0:T(8,128)(2,1)} %param.6) | copy-start | bytes 393220
  0.7 4.7 %copy-start.3 = (f32[4096]{0:T(1024)S(1)}, f32[4096]{0:T(1024)}, u32[]{:S(2)}) copy-start(f32[4096]{0:T(1024)} %param.7) | copy-start | bytes 49156
  0.7 4.6 %collective-permute-start.1 = (bf16[128,512]{1,0:T(8,128)(2,1)}, bf16[128,512]{1,0:T(8,128)(2,1)S(1)}, u32[]{:S(2)}, u32[]{:S(2)}) collective-permute-start(bf16[128,512]{1,0:T(8,128)(2,1)} %bitcast.15), channel_id=1, source_target_pairs={{0,16},{16,0},{1,17},{17,1},{2,18},{18,2},{3,19},{19,3},{4,20},{20... | collective-permute-start | bytes 393224 | tf_op jit(solution)/shard_map/ppermute | solution.py:245
  1.2 6.1 %collective-permute-start = (bf16[128,512]{1,0:T(8,128)(2,1)}, bf16[128,512]{1,0:T(8,128)(2,1)S(1)}, u32[]{:S(2)}, u32[]{:S(2)}) collective-permute-start(bf16[128,512]{1,0:T(8,128)(2,1)} %bitcast.16), channel_id=1, source_target_pairs={{0,4},{4,0},{8,12},{12,8},{16,24},{20,28},{24,16},{28,20},{1,5},{5... | collective-permute-start | bytes 393224 | tf_op jit(solution)/shard_map/ppermute | solution.py:242
  3.8 7.2 %collective-permute-start.2 = (bf16[128,512]{1,0:T(8,128)(2,1)}, bf16[128,512]{1,0:T(8,128)(2,1)S(1)}, u32[]{:S(2)}, u32[]{:S(2)}) collective-permute-start(bf16[128,512]{1,0:T(8,128)(2,1)} %bitcast.17), channel_id=1, source_target_pairs={{0,8},{4,12},{8,0},{12,4},{16,20},{20,16},{24,28},{28,24},{1,9},{5... | collective-permute-start | bytes 393224 | tf_op jit(solution)/shard_map/ppermute | solution.py:242
  5.3 6.8 %collective-permute-start.3 = (bf16[128,512]{1,0:T(8,128)(2,1)}, bf16[128,512]{1,0:T(8,128)(2,1)S(1)}, u32[]{:S(2)}, u32[]{:S(2)}) collective-permute-start(bf16[128,512]{1,0:T(8,128)(2,1)} %bitcast.18), channel_id=1, source_target_pairs={{0,12},{4,8},{8,4},{12,0},{16,28},{20,24},{24,20},{28,16},{1,13},{... | collective-permute-start | bytes 393224 | tf_op jit(solution)/shard_map/ppermute | solution.py:242
  5.3 8.1 %copy-start = (bf16[1,1,256,512]{3,2,1,0:T(8,128)(2,1)S(1)}, bf16[1,1,256,512]{3,2,1,0:T(8,128)(2,1)}, u32[]{:S(2)}) copy-start(bf16[1,1,256,512]{3,2,1,0:T(8,128)(2,1)} %param.9) | copy-start | bytes 786436
  5.3 8.1 %copy-start.1 = (bf16[1,1,256,512]{3,2,1,0:T(8,128)(2,1)S(1)}, bf16[1,1,256,512]{3,2,1,0:T(8,128)(2,1)}, u32[]{:S(2)}) copy-start(bf16[1,1,256,512]{3,2,1,0:T(8,128)(2,1)} %param.10) | copy-start | bytes 786436
  7.3 5.4 %collective-permute-start.4 = (bf16[128,512]{1,0:T(8,128)(2,1)S(1)}, bf16[128,512]{1,0:T(8,128)(2,1)S(1)}, u32[]{:S(2)}, u32[]{:S(2)}) collective-permute-start(bf16[128,512]{1,0:T(8,128)(2,1)S(1)} %collective-permute-done.refs_0_.refs_1_), channel_id=1, source_target_pairs={{0,16},{16,0},{1,17},{17,1},{2,18},{18,2},{3,19},{19,3},{4,20},{20... | collective-permute-start | bytes 393224 | tf_op jit(solution)/shard_map/ppermute | solution.py:245
  10.9 1.8 %collective-permute-start.5 = (bf16[128,512]{1,0:T(8,128)(2,1)S(1)}, bf16[128,512]{1,0:T(8,128)(2,1)S(1)}, u32[]{:S(2)}, u32[]{:S(2)}) collective-permute-start(bf16[128,512]{1,0:T(8,128)(2,1)S(1)} %collective-permute-done.2.refs_1_.refs_2_), channel_id=1, source_target_pairs={{0,16},{16,0},{1,17},{17,1},{2,18},{18,2},{3,19},{19,3},{4,20},{20... | collective-permute-start | bytes 393224 | tf_op jit(solution)/shard_map/ppermute | solution.py:245
  12.1 1.3 %collective-permute-start.6 = (bf16[128,512]{1,0:T(8,128)(2,1)S(1)}, bf16[128,512]{1,0:T(8,128)(2,1)S(1)}, u32[]{:S(2)}, u32[]{:S(2)}) collective-permute-start(bf16[128,512]{1,0:T(8,128)(2,1)S(1)} %collective-permute-done.3.refs_2_.refs_3_), channel_id=1, source_target_pairs={{0,16},{16,0},{1,17},{17,1},{2,18},{18,2},{3,19},{19,3},{4,20},{20... | collective-permute-start | bytes 393224 | tf_op jit(solution)/shard_map/ppermute | solution.py:245
  16.6 2.0 %collective-permute-start.7 = (bf16[136,2048]{1,0:T(8,128)(2,1)S(1)}, bf16[136,2048]{1,0:T(8,128)(2,1)S(1)}, u32[]{:S(2)}, u32[]{:S(2)}) collective-permute-start(bf16[136,2048]{1,0:T(8,128)(2,1)S(1)} %get-tuple-element.37.row_ref), channel_id=1, source_target_pairs={{0,16},{16,0},{1,17},{17,1},{2,18},{18,2},{3,19},{19,3},{4,20},{20... | collective-permute-start | bytes 1671176 | tf_op jit(solution)/shard_map/ppermute | solution.py:245
  19.0 6.4 %collective-permute-start.11 = (f32[1,640]{1,0:T(1,128)S(1)}, f32[1,640]{1,0:T(1,128)S(1)}, u32[]{:S(2)}, u32[]{:S(2)}) collective-permute-start(f32[1,640]{1,0:T(1,128)S(1)} %get-tuple-element.44), channel_id=1, source_target_pairs={{0,4},{4,0},{8,12},{12,8},{16,24},{20,28},{24,16},{28,20},{1,5},{5... | collective-permute-start | bytes 7688 | tf_op jit(solution)/shard_map/ppermute | solution.py:242
  20.8 5.3 %collective-permute-start.12 = (f32[1,640]{1,0:T(1,128)S(1)}, f32[1,640]{1,0:T(1,128)S(1)}, u32[]{:S(2)}, u32[]{:S(2)}) collective-permute-start(f32[1,640]{1,0:T(1,128)S(1)} %get-tuple-element.45), channel_id=1, source_target_pairs={{0,8},{4,12},{8,0},{12,4},{16,20},{20,16},{24,28},{28,24},{1,9},{5... | collective-permute-start | bytes 7688 | tf_op jit(solution)/shard_map/ppermute | solution.py:242
  21.1 5.0 %collective-permute-start.13 = (f32[1,640]{1,0:T(1,128)S(1)}, f32[1,640]{1,0:T(1,128)S(1)}, u32[]{:S(2)}, u32[]{:S(2)}) collective-permute-start(f32[1,640]{1,0:T(1,128)S(1)} %get-tuple-element.46), channel_id=1, source_target_pairs={{0,12},{4,8},{8,4},{12,0},{16,28},{20,24},{24,20},{28,16},{1,13},{... | collective-permute-start | bytes 7688 | tf_op jit(solution)/shard_map/ppermute | solution.py:242
  22.6 7.4 %collective-permute-start.10 = (bf16[128,512]{1,0:T(8,128)(2,1)S(1)}, bf16[128,512]{1,0:T(8,128)(2,1)S(1)}, u32[]{:S(2)}, u32[]{:S(2)}) collective-permute-start(bf16[128,512]{1,0:T(8,128)(2,1)S(1)} %get-tuple-element.41.refs_7_), channel_id=1, source_target_pairs={{0,12},{4,8},{8,4},{12,0},{16,28},{20,24},{24,20},{28,16},{1,13},{... | collective-permute-start | bytes 393224 | tf_op jit(solution)/shard_map/ppermute | solution.py:242
  24.0 7.5 %collective-permute-start.8 = (bf16[128,512]{1,0:T(8,128)(2,1)S(1)}, bf16[128,512]{1,0:T(8,128)(2,1)S(1)}, u32[]{:S(2)}, u32[]{:S(2)}) collective-permute-start(bf16[128,512]{1,0:T(8,128)(2,1)S(1)} %get-tuple-element.39.refs_5_), channel_id=1, source_target_pairs={{0,4},{4,0},{8,12},{12,8},{16,24},{20,28},{24,16},{28,20},{1,5},{5... | collective-permute-start | bytes 393224 | tf_op jit(solution)/shard_map/ppermute | solution.py:242
  25.4 6.0 %collective-permute-start.9 = (bf16[128,512]{1,0:T(8,128)(2,1)S(1)}, bf16[128,512]{1,0:T(8,128)(2,1)S(1)}, u32[]{:S(2)}, u32[]{:S(2)}) collective-permute-start(bf16[128,512]{1,0:T(8,128)(2,1)S(1)} %get-tuple-element.40.refs_6_), channel_id=1, source_target_pairs={{0,8},{4,12},{8,0},{12,4},{16,20},{20,16},{24,28},{28,24},{1,9},{5... | collective-permute-start | bytes 393224 | tf_op jit(solution)/shard_map/ppermute | solution.py:242
  26.1 5.4 %collective-permute-start.14 = (f32[1,128]{1,0:T(1,128)S(1)}, f32[1,128]{1,0:T(1,128)S(1)}, u32[]{:S(2)}, u32[]{:S(2)}) collective-permute-start(f32[1,128]{1,0:T(1,128)S(1)} %get-tuple-element.52), channel_id=1, source_target_pairs={{0,3},{1,2},{2,1},{3,0},{4,7},{5,6},{6,5},{7,4},{8,11},{9,10},{10,... | collective-permute-start | bytes 1544 | tf_op jit(solution)/shard_map/ppermute | solution.py:358
  30.0 4.4 %collective-permute-start.15 = (f32[1,128]{1,0:T(1,128)S(1)}, f32[1,128]{1,0:T(1,128)S(1)}, u32[]{:S(2)}, u32[]{:S(2)}) collective-permute-start(f32[1,128]{1,0:T(1,128)S(1)} %get-tuple-element.51), channel_id=1, source_target_pairs={{0,2},{1,3},{2,0},{3,1},{4,6},{5,7},{6,4},{7,5},{8,10},{9,11},{10,... | collective-permute-start | bytes 1544 | tf_op jit(solution)/shard_map/ppermute | solution.py:358
  30.0 4.4 %collective-permute-start.16 = (f32[1,128]{1,0:T(1,128)S(1)}, f32[1,128]{1,0:T(1,128)S(1)}, u32[]{:S(2)}, u32[]{:S(2)}) collective-permute-start(f32[1,128]{1,0:T(1,128)S(1)} %get-tuple-element.50), channel_id=1, source_target_pairs={{0,1},{1,0},{2,3},{3,2},{4,5},{5,4},{6,7},{7,6},{8,9},{9,8},{10,11... | collective-permute-start | bytes 1544 | tf_op jit(solution)/shard_map/ppermute | solution.py:358

commit v6 on v4

--- a/solution.py
+++ b/solution.py
@@ -9,6 +9,7 @@
 
 HS = 256
 EPS = 1e-06
+ROW_TERMS = 3
 LAST = (((1,), (1,)), ((), ()))
 FIRST = (((0,), (0,)), ((), ()))
 VMEM = pl.BlockSpec(memory_space=pltpu.VMEM)
@@ -47,32 +48,35 @@
     token_ref,
     *refs,
 ):
-    chunk_refs = refs[: 2 * parts]
-    (gain_ref, weight, query_ref, cot_ref) = refs[2 * parts : 2 * parts + 4]
-    (att_ref, sib_ref, kv_grad, inv_ref, row_ref) = refs[2 * parts + 4 : 2 * parts + 9]
-    (memory, kv) = refs[2 * parts + 9 :]
+    chunk_refs, refs = refs[: 2 * parts], refs[2 * parts :]
+    (gain_ref, weight, query_ref, cot_ref) = refs[:4]
+    (att_hbm, sib_ref, kv_grad, inv_ref) = refs[4:8]
+    (kv, att_ref, sem) = refs[8:]
     tokens, feats = chunk_refs[0].shape
     width = weight.shape[0]
     half = width // 2
-
+    me = lax.axis_index("sec")
+
+    section = lax.axis_index("section")
     square = None
     for ref in chunk_refs:
         x = ref[...].astype(jnp.float32)
         x = x * x
         for i in range(0, feats, 128):
             square = x[:, i : i + 128] if square is None else square + x[:, i : i + 128]
-    square = jnp.sum(square, axis=1, keepdims=True)
-    inv_rms = lax.rsqrt(square / width + EPS)
+    inv_rms = lax.rsqrt(jnp.sum(square, axis=1, keepdims=True) / width + EPS)
     inv_ref[...] = inv_rms
-    me, section = lax.axis_index("sec"), lax.axis_index("section")
     for j, ref in enumerate(chunk_refs):
         owner = me if j < parts else 1 - me
         peer = section ^ section_step(owner, j % parts, parts)
-        at = pl.multiple_of((owner * parts + peer) * feats, feats)
+        cols = pl.ds(pl.multiple_of((owner * parts + peer) * feats, feats), feats)
         normed = ref[...].astype(jnp.float32) * inv_rms
-        memory[:, pl.ds(at, feats)] = (normed * gain_ref[:, pl.ds(at, feats)]).astype(jnp.bfloat16)
-
-    kv[...] = jnp.dot(memory[...], weight[...], preferred_element_type=jnp.float32)
+        memory = (normed * gain_ref[:, cols]).astype(jnp.bfloat16)
+        product = jnp.dot(memory, weight[cols, :], preferred_element_type=jnp.float32)
+        if j == 0:
+            kv[...] = product
+        else:
+            kv[...] += product
 
     scale = HS ** (-0.5)
     live = lax.broadcasted_iota(jnp.int32, (query_ref.shape[0], HS), 0) < length_ref[0]
@@ -106,26 +110,36 @@
             keepdims=True,
         )
         row_part = here if row_part is None else row_part + here
-    row_ref[...] = jnp.transpose(jnp.broadcast_to(row_part, (tokens, 128)))[0:1, :]
+    att_out = pltpu.make_async_copy(att_ref, att_hbm, sem)
+    att_out.start()
+    rest = jnp.transpose(jnp.broadcast_to(row_part, (tokens, 128)))[0:8, :]
+    pieces = jnp.zeros_like(rest)
+    place = lax.broadcasted_iota(jnp.int32, rest.shape, 0)
+    for i in range(ROW_TERMS):
+        term = rest.astype(jnp.bfloat16).astype(jnp.float32)
+        pieces = jnp.where(place == i, term, pieces)
+        rest = rest - term
+    sib_ref[pl.ds(tokens, 8), :] = jnp.zeros((8, half), jnp.bfloat16)
+    sib_ref[pl.ds(tokens, 8), pl.ds(0, 128)] = pieces.astype(jnp.bfloat16)
 
     grad = kv_grad[...]
     tile = half // 4
     for t in range(4):
         rows = pl.ds(pl.multiple_of((1 - me) * half + t * tile, tile), tile)
-        sib_ref[:, pl.ds(t * tile, tile)] = lax.dot_general(
-            grad, weight[rows, :], LAST, preferred_element_type=jnp.float32
-        ).astype(jnp.bfloat16)
+        part = lax.dot_general(weight[rows, :], grad, LAST, preferred_element_type=jnp.float32)
+        sib_ref[pl.ds(0, tokens), pl.ds(t * tile, tile)] = jnp.transpose(part).astype(jnp.bfloat16)
+    att_out.wait()
 
 
 def back_kernel(grad_ref, weight, own_ref):
     half = own_ref.shape[1]
     me = lax.axis_index("sec")
     grad = grad_ref[...]
-    tile = half // 4
-    for t in range(4):
+    tile = half // 8
+    for t in range(8):
         rows = pl.ds(pl.multiple_of(me * half + t * tile, tile), tile)
-        own_ref[:, pl.ds(t * tile, tile)] = lax.dot_general(
-            grad, weight[rows, :], LAST, preferred_element_type=jnp.float32
+        own_ref[:, pl.ds(t * tile, tile)] = jnp.transpose(
+            lax.dot_general(weight[rows, :], grad, LAST, preferred_element_type=jnp.float32)
         )
 
 
@@ -134,7 +148,9 @@
     me, section = lax.axis_index("sec"), lax.axis_index("section")
     for k in range(parts):
         at = pl.multiple_of((section ^ section_step(me, k, parts)) * feats, feats)
-        total = own_ref[:, pl.ds(at, feats)] + sib_ref[:, pl.ds(at, feats)].astype(jnp.float32)
+        total = own_ref[:, pl.ds(at, feats)] + sib_ref[pl.ds(0, own_ref.shape[0]), pl.ds(at, feats)].astype(
+            jnp.float32
+        )
         if k == 0:
             kept_ref[...] = total
         else:
@@ -145,7 +161,11 @@
     chunk_refs, total_refs, small_refs = refs[:parts], refs[parts : 2 * parts], refs[2 * parts :]
     feats = chunk_refs[0].shape[1]
     inv_rms = inv_ref[...]
-    row = row_ref[...] + row_sib_ref[...]
+    tokens = chunk_refs[0].shape[0]
+    row = 0.0
+    for ref in (row_ref, row_sib_ref):
+        terms = ref[pl.ds(tokens, 8), pl.ds(0, 128)].astype(jnp.float32)
+        row = row + ((terms[0:1, :] + terms[1:2, :]) + terms[2:3, :])
     for k in range(parts):
         normed = chunk_refs[k][...].astype(jnp.float32) * inv_rms
         total = total_refs[k][...].astype(jnp.float32)
@@ -219,28 +239,36 @@
     for k in range(1, parts):
         chunks.append(lax.optimization_barrier((to_section(rows, k), token))[0])
     others = [to_core(c) for c in chunks]
-    att, sib, kv_grad, inv_rms, row = pl.pallas_call(
+    att, sib, kv_grad, inv_rms = pl.pallas_call(
         functools.partial(main_kernel, parts, heads),
         out_shape=(
             jax.ShapeDtypeStruct(query.shape, jnp.bfloat16),
-            jax.ShapeDtypeStruct((tokens, half), jnp.bfloat16),
+            jax.ShapeDtypeStruct((tokens + 8, half), jnp.bfloat16),
             jax.ShapeDtypeStruct((tokens, weight.shape[1]), jnp.bfloat16),
             jax.ShapeDtypeStruct((tokens, 1), jnp.float32),
-            jax.ShapeDtypeStruct((1, tokens), jnp.float32),
-        ),
-        in_specs=[SMEM, ANY] + [VMEM] * (2 * parts) + [VMEM, VMEM, VMEM, VMEM],
-        out_specs=(VMEM,) * 5,
+        ),
+        in_specs=[SMEM, ANY] + [VMEM] * (2 * parts + 4),
+        out_specs=(ANY, VMEM, VMEM, VMEM),
         scratch_shapes=[
-            pltpu.VMEM((tokens, width), jnp.bfloat16),
             pltpu.VMEM((tokens, weight.shape[1]), jnp.float32),
+            pltpu.VMEM(query.shape, jnp.bfloat16),
+            pltpu.SemaphoreType.DMA(()),
         ],
         compiler_params=pltpu.CompilerParams(vmem_limit_bytes=16 << 20),
         cost_estimate=pl.CostEstimate(
-            flops=3 * flops, bytes_accessed=2 * weight.size, transcendentals=dec * tokens * heads
+            flops=2 * flops, bytes_accessed=2 * weight.size, transcendentals=dec * tokens * heads
         ),
         name="main",
-    )(target_lengths, token, *chunks, *others, gain, weight, query, cot)
-
+    )(
+        target_lengths,
+        token,
+        *chunks,
+        *others,
+        gain,
+        weight,
+        query,
+        cot,
+    )
     own = pl.pallas_call(
         back_kernel,
         out_shape=jax.ShapeDtypeStruct((tokens, half), jnp.float32),
@@ -252,7 +280,6 @@
         ),
         name="back",
     )(kv_grad, weight)
-    row_sib = to_core(row)
     sib_in = to_core(sib)
 
     kept, *big = pl.pallas_call(
@@ -277,7 +304,7 @@
             flops=20_000_000_000, bytes_accessed=8 * tokens * half, transcendentals=0
         ),
         name="gain",
-    )(row, row_sib, inv_rms, *chunks, kept, *big)
+    )(sib, sib_in, inv_rms, *chunks, kept, *big)
 
     big_in = [to_section(big[k - 1], k) for k in range(1, parts)]
     small_in = [small[0]] + [to_section(small[k], k) for k in range(1, parts)]

time: 36 us -> 35.6 us (0.989)
  Pallas kernels: 6.79 us -> 6.27 us
    ppermute x6 -> x5, starting transfers between devices: 1.09 us -> 0.91 us  [to_core(): return lax.ppermute(x, 'sec', swap)]
  transfers between devices with their start and end apart: 18 -> 17, of which waited for: 8 -> 9; matrix products, arithmetic and copies ran while one was open for 0% -> 0% of each run, Pallas kernels for 5% -> 4%
where the time goes in v6:
time: 35.6 us; the launch traced here: 35.5 us
  starting transfers between devices  17.1 us (48%)
  waiting for transfers between devices  10.6 us (30%)
  Pallas kernels  6.27 us (18%)
  between operations  1.43 us (4%)
    ppermute x9, starting transfers between devices, to_section(): return lax.ppermute(x, ('sec', 'section'), pairs)  11.6 us
    ppermute x9, waiting for transfers between devices, to_section(): return lax.ppermute(x, ('sec', 'section'), pairs)  7.03 us
    ppermute x3, starting transfers between devices, per_device(): pieces.append(lax.ppermute(send, 'dp', [(i, i ^ k) for i in range(seqs)]))  4.61 us
    pallas_call x1, Pallas kernels, per_device(): pl.pallas_call(functools.partial(main_kernel, parts, heads), out_shape=(j...  3.65 us
    ppermute x3, waiting for transfers between devices, per_device(): pieces.append(lax.ppermute(send, 'dp', [(i, i ^ k) for i in range(seqs)]))  2.93 us
    pallas_call x1, Pallas kernels, per_device(): pl.pallas_call(back_kernel, out_shape=jax.ShapeDtypeStruct((tokens, half)...  1.34 us
    ppermute x5, starting transfers between devices, to_core(): return lax.ppermute(x, 'sec', swap)  0.91 us
    pallas_call x1, Pallas kernels, per_device(): pl.pallas_call(functools.partial(last_kernel, parts, width), out_shape=(j...  0.86 us
  transfers between devices with their start and end apart: 17, of which 9 were waited for; matrix products, arithmetic and copies ran while one was open for 0% of the time, Pallas kernels for 4%

profile of v6, /device:TPU:0, one launch (start us, length us, event | category | flops | bytes accessed | tf_op | source)
XLA Modules:
  0.0 35.5 jit_solution(10801567331243184823)
XLA Ops:
  0.6 0.0 slice-start
  0.6 0.0 slice-start.1
  0.7 0.0 copy-start
  0.7 0.0 copy-start.1
  0.7 0.0 copy-start.2
  0.7 0.0 copy-start.3
  0.7 3.0 %collective-permute-start = (bf16[128,512]{1,0:T(8,128)(2,1)}, bf16[128,512]{1,0:T(8,128)(2,1)S(1)}, u32[]{:S(2)}, u32[]{:S(2)}) collective-permute-start(bf16[128,512]{1,0:T(8,128)(2,1)} %bitcast.12), channel_id=1, source_target_pairs={{0,4},{4,0},{8,12},{12,8},{16,24},{20,28},{24,16},{28,20},{1,5},{5... | collective-permute-start | bytes 393224 | tf_op jit(solution)/shard_map/ppermute | solution.py:224
  3.7 1.5 %collective-permute-start.1 = (bf16[128,512]{1,0:T(8,128)(2,1)}, bf16[128,512]{1,0:T(8,128)(2,1)S(1)}, u32[]{:S(2)}, u32[]{:S(2)}) collective-permute-start(bf16[128,512]{1,0:T(8,128)(2,1)} %bitcast.13), channel_id=1, source_target_pairs={{0,8},{4,12},{8,0},{12,4},{16,20},{20,16},{24,28},{28,24},{1,9},{5... | collective-permute-start | bytes 393224 | tf_op jit(solution)/shard_map/ppermute | solution.py:224
  5.2 0.0 collective-permute-start.2
  5.2 0.0 collective-permute-start.3
  5.2 2.6 %collective-permute-done.refs_1_ = bf16[128,512]{1,0:T(8,128)(2,1)S(1)} collective-permute-done((bf16[128,512]{1,0:T(8,128)(2,1)}, bf16[128,512]{1,0:T(8,128)(2,1)S(1)}, u32[]{:S(2)}, u32[]{:S(2)}) %collective-permute-start) | collective-permute-done | bytes 131104 | tf_op jit(solution)/shard_map/ppermute | solution.py:224
  7.8 0.0 collective-permute-start.4
  7.8 3.9 %collective-permute-done.1.refs_2_ = bf16[128,512]{1,0:T(8,128)(2,1)S(1)} collective-permute-done((bf16[128,512]{1,0:T(8,128)(2,1)}, bf16[128,512]{1,0:T(8,128)(2,1)S(1)}, u32[]{:S(2)}, u32[]{:S(2)}) %collective-permute-start.1) | collective-permute-done | bytes 131104 | tf_op jit(solution)/shard_map/ppermute | solution.py:224
  11.7 0.0 collective-permute-start.5
  11.7 0.0 collective-permute-done.2.refs_3_
  11.7 0.5 %collective-permute-start.6 = (bf16[128,512]{1,0:T(8,128)(2,1)S(1)}, bf16[128,512]{1,0:T(8,128)(2,1)S(1)}, u32[]{:S(2)}, u32[]{:S(2)}) collective-permute-start(bf16[128,512]{1,0:T(8,128)(2,1)S(1)} %collective-permute-done.2.refs_3_), channel_id=1, source_target_pairs={{0,16},{16,0},{1,17},{17,1},{2,18},{18,2},{3,19},{19,3},{4,20},{20... | collective-permute-start | bytes 393224 | tf_op jit(solution)/shard_map/ppermute | solution.py:227
  12.9 0.0 collective-permute-done.3.refs_4_
  12.9 0.0 collective-permute-done.4.refs_5_
  12.9 0.2 collective-permute-done.5.refs_6_
  13.0 0.2 collective-permute-done.6.refs_7_
  13.2 0.0 slice-done
  13.2 0.0 copy-done
  13.3 3.6 %main.1 = (bf16[256,512]{1,0:T(8,128)(2,1)}, bf16[136,2048]{1,0:T(8,128)(2,1)S(1)}, bf16[128,1024]{1,0:T(8,128)(2,1)S(1)}, f32[128,1]{1,0:T(8,128)S(1)}) custom-call(s32[1]{0:T(128)S(6)} %copy.10.length_ref, f32[8,128]{1,0:T(8,128)S(1)} %first.1.token_ref, bf16[128,512]{1,0:T(8,128)(2,1)S(1)} %bitcast.16, bf16[128,512]{1,0:T(8,128)(2,1)S(1)} %collective-permute-done.refs_1_, ...), custom_call_target="tpu_custom_call" | custom-call | flops 2147483648 | bytes 8388608 | tf_op jit(solution)/shard_map/main/pallas_call | solution.py:242
  16.9 0.4 %collective-permute-start.7 = (bf16[136,2048]{1,0:T(8,128)(2,1)S(1)}, bf16[136,2048]{1,0:T(8,128)(2,1)S(1)}, u32[]{:S(2)}, u32[]{:S(2)}) collective-permute-start(bf16[136,2048]{1,0:T(8,128)(2,1)S(1)} %get-tuple-element.27.row_ref), channel_id=1, source_target_pairs={{0,16},{16,0},{1,17},{17,1},{2,18},{18,2},{3,19},{19,3},{4,20},{20... | collective-permute-start | bytes 1671176 | tf_op jit(solution)/shard_map/ppermute | solution.py:227
  17.3 1.3 %back.1.own_ref = f32[128,2048]{1,0:T(8,128)S(1)} custom-call(bf16[128,1024]{1,0:T(8,128)(2,1)S(1)} %get-tuple-element.26.grad_ref, bf16[4096,1024]{1,0:T(8,128)(2,1)S(1)} %bitcast.11), custom_call_target="tpu_custom_call" | custom-call | flops 536870912 | bytes 4194304 | tf_op jit(solution)/shard_map/back/pallas_call | solution.py:272
  18.7 0.3 collective-permute-done.7.sib_ref.row_sib_ref
  18.9 0.1 chip.1
  19.1 0.3 gain.1
  19.3 1.3 %collective-permute-start.11 = (f32[1,640]{1,0:T(1,128)S(1)}, f32[1,640]{1,0:T(1,128)S(1)}, u32[]{:S(2)}, u32[]{:S(2)}) collective-permute-start(f32[1,640]{1,0:T(1,128)S(1)} %get-tuple-element.34), channel_id=1, source_target_pairs={{0,4},{4,0},{8,12},{12,8},{16,24},{20,28},{24,16},{28,20},{1,5},{5... | collective-permute-start | bytes 7688 | tf_op jit(solution)/shard_map/ppermute | solution.py:224
  20.6 1.3 %collective-permute-start.12 = (f32[1,640]{1,0:T(1,128)S(1)}, f32[1,640]{1,0:T(1,128)S(1)}, u32[]{:S(2)}, u32[]{:S(2)}) collective-permute-start(f32[1,640]{1,0:T(1,128)S(1)} %get-tuple-element.35), channel_id=1, source_target_pairs={{0,8},{4,12},{8,0},{12,4},{16,20},{20,16},{24,28},{28,24},{1,9},{5... | collective-permute-start | bytes 7688 | tf_op jit(solution)/shard_map/ppermute | solution.py:224
  22.0 0.9 %collective-permute-start.13 = (f32[1,640]{1,0:T(1,128)S(1)}, f32[1,640]{1,0:T(1,128)S(1)}, u32[]{:S(2)}, u32[]{:S(2)}) collective-permute-start(f32[1,640]{1,0:T(1,128)S(1)} %get-tuple-element.36), channel_id=1, source_target_pairs={{0,12},{4,8},{8,4},{12,0},{16,28},{20,24},{24,20},{28,16},{1,13},{... | collective-permute-start | bytes 7688 | tf_op jit(solution)/shard_map/ppermute | solution.py:224
  22.9 2.0 %collective-permute-start.10 = (bf16[128,512]{1,0:T(8,128)(2,1)S(1)}, bf16[128,512]{1,0:T(8,128)(2,1)S(1)}, u32[]{:S(2)}, u32[]{:S(2)}) collective-permute-start(bf16[128,512]{1,0:T(8,128)(2,1)S(1)} %get-tuple-element.31.refs_7_), channel_id=1, source_target_pairs={{0,12},{4,8},{8,4},{12,0},{16,28},{20,24},{24,20},{28,16},{1,13},{... | collective-permute-start | bytes 393224 | tf_op jit(solution)/shard_map/ppermute | solution.py:224
  24.9 1.0 %collective-permute-start.8 = (bf16[128,512]{1,0:T(8,128)(2,1)S(1)}, bf16[128,512]{1,0:T(8,128)(2,1)S(1)}, u32[]{:S(2)}, u32[]{:S(2)}) collective-permute-start(bf16[128,512]{1,0:T(8,128)(2,1)S(1)} %get-tuple-element.29.refs_5_), channel_id=1, source_target_pairs={{0,4},{4,0},{8,12},{12,8},{16,24},{20,28},{24,16},{28,20},{1,5},{5... | collective-permute-start | bytes 393224 | tf_op jit(solution)/shard_map/ppermute | solution.py:224
  25.9 0.0 collective-permute-done.11.refs_1_
  25.9 0.5 %collective-permute-start.9 = (bf16[128,512]{1,0:T(8,128)(2,1)S(1)}, bf16[128,512]{1,0:T(8,128)(2,1)S(1)}, u32[]{:S(2)}, u32[]{:S(2)}) collective-permute-start(bf16[128,512]{1,0:T(8,128)(2,1)S(1)} %get-tuple-element.30.refs_6_), channel_id=1, source_target_pairs={{0,8},{4,12},{8,0},{12,4},{16,20},{20,16},{24,28},{28,24},{1,9},{5... | collective-permute-start | bytes 393224 | tf_op jit(solution)/shard_map/ppermute | solution.py:224
  26.4 0.0 collective-permute-done.12.refs_2_
  26.4 0.1 collective-permute-done.13.refs_3_
  26.5 3.7 %collective-permute-start.14 = (f32[1,128]{1,0:T(1,128)S(1)}, f32[1,128]{1,0:T(1,128)S(1)}, u32[]{:S(2)}, u32[]{:S(2)}) collective-permute-start(f32[1,128]{1,0:T(1,128)S(1)} %get-tuple-element.42), channel_id=1, source_target_pairs={{0,3},{1,2},{2,1},{3,0},{4,7},{5,6},{6,5},{7,4},{8,11},{9,10},{10,... | collective-permute-start | bytes 1544 | tf_op jit(solution)/shard_map/ppermute | solution.py:320
  30.1 0.0 collective-permute-start.15
  30.1 0.0 collective-permute-done.10.refs_2_
  30.1 0.9 %collective-permute-start.16 = (f32[1,128]{1,0:T(1,128)S(1)}, f32[1,128]{1,0:T(1,128)S(1)}, u32[]{:S(2)}, u32[]{:S(2)}) collective-permute-start(f32[1,128]{1,0:T(1,128)S(1)} %get-tuple-element.40), channel_id=1, source_target_pairs={{0,1},{1,0},{2,3},{3,2},{4,5},{5,4},{6,7},{7,6},{8,9},{9,8},{10,11... | collective-permute-start | bytes 1544 | tf_op jit(solution)/shard_map/ppermute | solution.py:320
  31.1 0.5 %collective-permute-done.8.refs_0_ = bf16[128,512]{1,0:T(8,128)(2,1)S(1)} collective-permute-done((bf16[128,512]{1,0:T(8,128)(2,1)S(1)}, bf16[128,512]{1,0:T(8,128)(2,1)S(1)}, u32[]{:S(2)}, u32[]{:S(2)}) %collective-permute-start.8) | collective-permute-done | bytes 131104 | tf_op jit(solution)/shard_map/ppermute | solution.py:224
  31.6 0.0 collective-permute-done.9.refs_1_
  31.6 0.1 total.1.grad_ref
  31.7 0.2 collective-permute-done.14.refs_5_
  31.9 2.7 %collective-permute-done.15.refs_6_ = f32[1,128]{1,0:T(1,128)S(1)} collective-permute-done((f32[1,128]{1,0:T(1,128)S(1)}, f32[1,128]{1,0:T(1,128)S(1)}, u32[]{:S(2)}, u32[]{:S(2)}) %collective-permute-start.15) | collective-permute-done | bytes 544 | tf_op jit(solution)/shard_map/ppermute | solution.py:320
  34.6 0.0 collective-permute-done.16.refs_7_
  34.6 0.9 %last.1 = (bf16[128,512]{1,0:T(8,128)(2,1)}, f32[1,128]{1,0:T(1,128)}, f32[1,128]{1,0:T(1,128)}) custom-call(f32[128,512]{1,0:T(8,128)S(1)} %total.1.grad_ref, bf16[128,512]{1,0:T(8,128)(2,1)S(1)} %bitcast.18, f32[128,1]{1,0:T(8,128)S(1)} %get-tuple-element.32.inv_ref, f32[1,4096]{1,0:T(1,128)S(1)} %bitcast.22, f32[1,640]{1,0:T(1,128)S(1)} %get-tuple-element.33.refs_0_, ...), custom_call_target="tpu_custom_call" | custom-call | flops 655360 | bytes 1048576 | tf_op jit(solution)/shard_map/last/pallas_call | solution.py:330
  (8 shorter events, 0.0 us)
Async XLA Ops:
  0.6 12.6 %slice-start = ((s8[8388608]{0:T(1024)(128)(4,1)}), s8[4194304]{0:T(1024)(128)(4,1)S(1)}, s32[]{:S(2)}) async-start(s8[8388608]{0:T(1024)(128)(4,1)} %bitcast.8), calls=%async_computation | async-start | bytes 8388608
  0.6 12.6 %slice-start.1 = ((s8[8388608]{0:T(1024)(128)(4,1)}), s8[4194304]{0:T(1024)(128)(4,1)S(1)}, s32[]{:S(2)}) async-start(s8[8388608]{0:T(1024)(128)(4,1)} %bitcast.8), calls=%async_computation.1 | async-start | bytes 8388608
  0.7 12.6 %copy-start = (bf16[1,128,512]{2,1,0:T(8,128)(2,1)S(1)}, bf16[1,128,512]{2,1,0:T(8,128)(2,1)}, u32[]{:S(2)}) copy-start(bf16[1,128,512]{2,1,0:T(8,128)(2,1)} %param.6) | copy-start | bytes 393220
  0.7 12.6 %copy-start.1 = (bf16[1,1,256,512]{3,2,1,0:T(8,128)(2,1)S(1)}, bf16[1,1,256,512]{3,2,1,0:T(8,128)(2,1)}, u32[]{:S(2)}) copy-start(bf16[1,1,256,512]{3,2,1,0:T(8,128)(2,1)} %param.9) | copy-start | bytes 786436
  0.7 12.6 %copy-start.2 = (bf16[1,1,256,512]{3,2,1,0:T(8,128)(2,1)S(1)}, bf16[1,1,256,512]{3,2,1,0:T(8,128)(2,1)}, u32[]{:S(2)}) copy-start(bf16[1,1,256,512]{3,2,1,0:T(8,128)(2,1)} %param.10) | copy-start | bytes 786436
  0.7 12.6 %copy-start.3 = (f32[4096]{0:T(1024)S(1)}, f32[4096]{0:T(1024)}, u32[]{:S(2)}) copy-start(f32[4096]{0:T(1024)} %param.7) | copy-start | bytes 49156
  0.7 7.1 %collective-permute-start = (bf16[128,512]{1,0:T(8,128)(2,1)}, bf16[128,512]{1,0:T(8,128)(2,1)S(1)}, u32[]{:S(2)}, u32[]{:S(2)}) collective-permute-start(bf16[128,512]{1,0:T(8,128)(2,1)} %bitcast.12), channel_id=1, source_target_pairs={{0,4},{4,0},{8,12},{12,8},{16,24},{20,28},{24,16},{28,20},{1,5},{5... | collective-permute-start | bytes 393224 | tf_op jit(solution)/shard_map/ppermute | solution.py:224
  3.7 8.0 %collective-permute-start.1 = (bf16[128,512]{1,0:T(8,128)(2,1)}, bf16[128,512]{1,0:T(8,128)(2,1)S(1)}, u32[]{:S(2)}, u32[]{:S(2)}) collective-permute-start(bf16[128,512]{1,0:T(8,128)(2,1)} %bitcast.13), channel_id=1, source_target_pairs={{0,8},{4,12},{8,0},{12,4},{16,20},{20,16},{24,28},{28,24},{1,9},{5... | collective-permute-start | bytes 393224 | tf_op jit(solution)/shard_map/ppermute | solution.py:224
  5.2 6.5 %collective-permute-start.2 = (bf16[128,512]{1,0:T(8,128)(2,1)}, bf16[128,512]{1,0:T(8,128)(2,1)S(1)}, u32[]{:S(2)}, u32[]{:S(2)}) collective-permute-start(bf16[128,512]{1,0:T(8,128)(2,1)} %bitcast.14), channel_id=1, source_target_pairs={{0,12},{4,8},{8,4},{12,0},{16,28},{20,24},{24,20},{28,16},{1,13},{... | collective-permute-start | bytes 393224 | tf_op jit(solution)/shard_map/ppermute | solution.py:224
  5.2 7.6 %collective-permute-start.3 = (bf16[128,512]{1,0:T(8,128)(2,1)}, bf16[128,512]{1,0:T(8,128)(2,1)S(1)}, u32[]{:S(2)}, u32[]{:S(2)}) collective-permute-start(bf16[128,512]{1,0:T(8,128)(2,1)} %bitcast.15), channel_id=1, source_target_pairs={{0,16},{16,0},{1,17},{17,1},{2,18},{18,2},{3,19},{19,3},{4,20},{20... | collective-permute-start | bytes 393224 | tf_op jit(solution)/shard_map/ppermute | solution.py:227
  7.8 5.1 %collective-permute-start.4 = (bf16[128,512]{1,0:T(8,128)(2,1)S(1)}, bf16[128,512]{1,0:T(8,128)(2,1)S(1)}, u32[]{:S(2)}, u32[]{:S(2)}) collective-permute-start(bf16[128,512]{1,0:T(8,128)(2,1)S(1)} %collective-permute-done.refs_1_), channel_id=1, source_target_pairs={{0,16},{16,0},{1,17},{17,1},{2,18},{18,2},{3,19},{19,3},{4,20},{20... | collective-permute-start | bytes 393224 | tf_op jit(solution)/shard_map/ppermute | solution.py:227
  11.7 1.3 %collective-permute-start.5 = (bf16[128,512]{1,0:T(8,128)(2,1)S(1)}, bf16[128,512]{1,0:T(8,128)(2,1)S(1)}, u32[]{:S(2)}, u32[]{:S(2)}) collective-permute-start(bf16[128,512]{1,0:T(8,128)(2,1)S(1)} %collective-permute-done.1.refs_2_), channel_id=1, source_target_pairs={{0,16},{16,0},{1,17},{17,1},{2,18},{18,2},{3,19},{19,3},{4,20},{20... | collective-permute-start | bytes 393224 | tf_op jit(solution)/shard_map/ppermute | solution.py:227
  11.7 1.5 %collective-permute-start.6 = (bf16[128,512]{1,0:T(8,128)(2,1)S(1)}, bf16[128,512]{1,0:T(8,128)(2,1)S(1)}, u32[]{:S(2)}, u32[]{:S(2)}) collective-permute-start(bf16[128,512]{1,0:T(8,128)(2,1)S(1)} %collective-permute-done.2.refs_3_), channel_id=1, source_target_pairs={{0,16},{16,0},{1,17},{17,1},{2,18},{18,2},{3,19},{19,3},{4,20},{20... | collective-permute-start | bytes 393224 | tf_op jit(solution)/shard_map/ppermute | solution.py:227
  16.9 2.0 %collective-permute-start.7 = (bf16[136,2048]{1,0:T(8,128)(2,1)S(1)}, bf16[136,2048]{1,0:T(8,128)(2,1)S(1)}, u32[]{:S(2)}, u32[]{:S(2)}) collective-permute-start(bf16[136,2048]{1,0:T(8,128)(2,1)S(1)} %get-tuple-element.27.row_ref), channel_id=1, source_target_pairs={{0,16},{16,0},{1,17},{17,1},{2,18},{18,2},{3,19},{19,3},{4,20},{20... | collective-permute-start | bytes 1671176 | tf_op jit(solution)/shard_map/ppermute | solution.py:227
  19.3 6.5 %collective-permute-start.11 = (f32[1,640]{1,0:T(1,128)S(1)}, f32[1,640]{1,0:T(1,128)S(1)}, u32[]{:S(2)}, u32[]{:S(2)}) collective-permute-start(f32[1,640]{1,0:T(1,128)S(1)} %get-tuple-element.34), channel_id=1, source_target_pairs={{0,4},{4,0},{8,12},{12,8},{16,24},{20,28},{24,16},{28,20},{1,5},{5... | collective-permute-start | bytes 7688 | tf_op jit(solution)/shard_map/ppermute | solution.py:224
  20.6 5.7 %collective-permute-start.12 = (f32[1,640]{1,0:T(1,128)S(1)}, f32[1,640]{1,0:T(1,128)S(1)}, u32[]{:S(2)}, u32[]{:S(2)}) collective-permute-start(f32[1,640]{1,0:T(1,128)S(1)} %get-tuple-element.35), channel_id=1, source_target_pairs={{0,8},{4,12},{8,0},{12,4},{16,20},{20,16},{24,28},{28,24},{1,9},{5... | collective-permute-start | bytes 7688 | tf_op jit(solution)/shard_map/ppermute | solution.py:224
  22.0 4.5 %collective-permute-start.13 = (f32[1,640]{1,0:T(1,128)S(1)}, f32[1,640]{1,0:T(1,128)S(1)}, u32[]{:S(2)}, u32[]{:S(2)}) collective-permute-start(f32[1,640]{1,0:T(1,128)S(1)} %get-tuple-element.36), channel_id=1, source_target_pairs={{0,12},{4,8},{8,4},{12,0},{16,28},{20,24},{24,20},{28,16},{1,13},{... | collective-permute-start | bytes 7688 | tf_op jit(solution)/shard_map/ppermute | solution.py:224
  22.9 7.3 %collective-permute-start.10 = (bf16[128,512]{1,0:T(8,128)(2,1)S(1)}, bf16[128,512]{1,0:T(8,128)(2,1)S(1)}, u32[]{:S(2)}, u32[]{:S(2)}) collective-permute-start(bf16[128,512]{1,0:T(8,128)(2,1)S(1)} %get-tuple-element.31.refs_7_), channel_id=1, source_target_pairs={{0,12},{4,8},{8,4},{12,0},{16,28},{20,24},{24,20},{28,16},{1,13},{... | collective-permute-start | bytes 393224 | tf_op jit(solution)/shard_map/ppermute | solution.py:224
  24.9 6.7 %collective-permute-start.8 = (bf16[128,512]{1,0:T(8,128)(2,1)S(1)}, bf16[128,512]{1,0:T(8,128)(2,1)S(1)}, u32[]{:S(2)}, u32[]{:S(2)}) collective-permute-start(bf16[128,512]{1,0:T(8,128)(2,1)S(1)} %get-tuple-element.29.refs_5_), channel_id=1, source_target_pairs={{0,4},{4,0},{8,12},{12,8},{16,24},{20,28},{24,16},{28,20},{1,5},{5... | collective-permute-start | bytes 393224 | tf_op jit(solution)/shard_map/ppermute | solution.py:224
  25.9 5.7 %collective-permute-start.9 = (bf16[128,512]{1,0:T(8,128)(2,1)S(1)}, bf16[128,512]{1,0:T(8,128)(2,1)S(1)}, u32[]{:S(2)}, u32[]{:S(2)}) collective-permute-start(bf16[128,512]{1,0:T(8,128)(2,1)S(1)} %get-tuple-element.30.refs_6_), channel_id=1, source_target_pairs={{0,8},{4,12},{8,0},{12,4},{16,20},{20,16},{24,28},{28,24},{1,9},{5... | collective-permute-start | bytes 393224 | tf_op jit(solution)/shard_map/ppermute | solution.py:224
  26.5 5.4 %collective-permute-start.14 = (f32[1,128]{1,0:T(1,128)S(1)}, f32[1,128]{1,0:T(1,128)S(1)}, u32[]{:S(2)}, u32[]{:S(2)}) collective-permute-start(f32[1,128]{1,0:T(1,128)S(1)} %get-tuple-element.42), channel_id=1, source_target_pairs={{0,3},{1,2},{2,1},{3,0},{4,7},{5,6},{6,5},{7,4},{8,11},{9,10},{10,... | collective-permute-start | bytes 1544 | tf_op jit(solution)/shard_map/ppermute | solution.py:320
  30.1 4.4 %collective-permute-start.15 = (f32[1,128]{1,0:T(1,128)S(1)}, f32[1,128]{1,0:T(1,128)S(1)}, u32[]{:S(2)}, u32[]{:S(2)}) collective-permute-start(f32[1,128]{1,0:T(1,128)S(1)} %get-tuple-element.41), channel_id=1, source_target_pairs={{0,2},{1,3},{2,0},{3,1},{4,6},{5,7},{6,4},{7,5},{8,10},{9,11},{10,... | collective-permute-start | bytes 1544 | tf_op jit(solution)/shard_map/ppermute | solution.py:320
  30.1 4.4 %collective-permute-start.16 = (f32[1,128]{1,0:T(1,128)S(1)}, f32[1,128]{1,0:T(1,128)S(1)}, u32[]{:S(2)}, u32[]{:S(2)}) collective-permute-start(f32[1,128]{1,0:T(1,128)S(1)} %get-tuple-element.40), channel_id=1, source_target_pairs={{0,1},{1,0},{2,3},{3,2},{4,5},{5,4},{6,7},{7,6},{8,9},{9,8},{10,11... | collective-permute-start | bytes 1544 | tf_op jit(solution)/shard_map/ppermute | solution.py:320

commit v7 on v6

--- a/solution.py
+++ b/solution.py
@@ -91,7 +91,7 @@
         masked = jnp.where(live, cot, jnp.zeros_like(cot))
         scores = lax.dot_general(key_rows, query, LAST, preferred_element_type=jnp.float32) * scale
         exponent = jnp.exp(scores)
-        attention = exponent * (1.0 / jnp.sum(exponent, axis=0, keepdims=True))
+        attention = exponent / jnp.sum(exponent, axis=0, keepdims=True)
         weights_b = attention.astype(jnp.bfloat16)
         att_ref[:, cols] = lax.dot_general(
             weights_b, value_rows, FIRST, preferred_element_type=jnp.float32
@@ -173,17 +173,9 @@
         small_refs[k][:, pl.ds(feats, row.shape[1])] = row
 
 
-def total_kernel(kept_ref, *refs):
-    total = kept_ref[...]
-    for ref in refs[:-1]:
-        total = total + ref[...].astype(jnp.float32)
-    refs[-1][...] = total
-
-
-def last_kernel(parts, width, grad_ref, chunk_ref, inv_ref, gain_ref, *refs):
-    small_refs, gain_refs, (enc_ref, row_ref, *gain_out) = refs[:parts], refs[parts:-3], refs[-3:]
-    if not gain_refs:
-        small_refs, (enc_ref, row_ref), gain_out = refs[:parts], refs[-2:], ()
+def last_kernel(parts, width, kept_ref, *refs):
+    big_refs, (chunk_ref, inv_ref, gain_ref) = refs[: parts - 1], refs[parts - 1 : parts + 2]
+    small_refs, (enc_ref, row_ref) = refs[parts + 2 : 2 * parts + 2], refs[2 * parts + 2 :]
     tokens, feats = chunk_ref.shape
     core = lax.axis_index("sec")
     rows = [ref[:, pl.ds(feats, tokens)] for ref in small_refs]
@@ -191,15 +183,15 @@
         [jnp.where(core == 0, rows[k], rows[reverse_bits(k, parts)]) for k in range(parts)]
     )
     row_ref[...] = row
-    grad = grad_ref[...]
+    grad = kept_ref[...]
+    for ref in big_refs:
+        grad = grad + ref[...].astype(jnp.float32)
     inv_rms = inv_ref[...]
     at = pl.multiple_of((core * parts + lax.axis_index("section")) * feats, feats)
     gain = gain_ref[:, pl.ds(at, feats)]
     normed = chunk_ref[...].astype(jnp.float32) * inv_rms
     row_dot = jnp.transpose(jnp.broadcast_to(row, (128, tokens)))[:, 0:1]
     enc_ref[...] = (inv_rms * (gain * grad - normed * (row_dot / width))).astype(jnp.bfloat16)
-    for ref in gain_out:
-        ref[...] = tree_sum([g[...] for g in gain_refs])
 
 
 def per_device(sizes, enc_states, norm_gain, kv_weight, queries, attn_cotangent, target_lengths):
@@ -318,32 +310,21 @@
         for k in reversed(range(1, seqs)):
             send = lax.dynamic_slice_in_dim(gain_term, (dp ^ k) * piece, piece, 1)
             pieces.append(lax.ppermute(send, "dp", [(i, i ^ k) for i in range(seqs)]))
-    total = pl.pallas_call(
-        total_kernel,
-        out_shape=jax.ShapeDtypeStruct((tokens, feats), jnp.float32),
-        in_specs=[VMEM] * parts,
-        out_specs=VMEM,
-        compiler_params=pltpu.CompilerParams(vmem_limit_bytes=8 << 20),
-        cost_estimate=pl.CostEstimate(flops=20_000_000_000, bytes_accessed=4096, transcendentals=0),
-        name="total",
-    )(kept, *big_in)
-    enc_grad, row_dot, *gain_grad = pl.pallas_call(
+    enc_grad, row_dot = pl.pallas_call(
         functools.partial(last_kernel, parts, width),
         out_shape=(
             jax.ShapeDtypeStruct((tokens, feats), jnp.bfloat16),
             jax.ShapeDtypeStruct((1, tokens), jnp.float32),
-        )
-        + ((jax.ShapeDtypeStruct(pieces[0].shape, jnp.float32),) if direct else ()),
-        in_specs=[VMEM] * (4 + parts + len(pieces)),
-        out_specs=(VMEM,) * (3 if direct else 2),
+        ),
+        in_specs=[VMEM] * (2 * parts + 3),
+        out_specs=(VMEM, VMEM),
         compiler_params=pltpu.CompilerParams(vmem_limit_bytes=8 << 20),
-        cost_estimate=pl.CostEstimate(
-            flops=10 * tokens * feats, bytes_accessed=16 * tokens * feats, transcendentals=0
-        ),
+        cost_estimate=pl.CostEstimate(flops=20_000_000_000, bytes_accessed=4096, transcendentals=0),
         name="last",
-    )(total, rows, inv_rms, gain, *small_in, *pieces)
+    )(kept, *big_in, rows, inv_rms, gain, *small_in)
     if direct:
-        gain_grad = gain_grad[0][0]
+        enc_grad, pieces[0] = lax.optimization_barrier((enc_grad, pieces[0]))
+        gain_grad = tree_sum(pieces)[0]
     else:
         gain_grad = lax.psum_scatter(gain_term[0], "dp", scatter_dimension=0, tiled=True)
     return (att[None, None], enc_grad[None], gain_grad, row_dot)

time: 35.6 us -> 35.3 us (level)
  waiting for transfers between devices: 10.6 us -> 9.78 us
  other arithmetic: 0.01 us -> 0.52 us
    ppermute x3, waiting for transfers between devices: 2.93 us -> 2.12 us  [per_device(): pieces.append(lax.ppermute(send, 'dp', [(i, i ^ k) for i in range(seqs)]))]
    squeeze x0 -> x1, other arithmetic: none -> 0.52 us  [per_device(): gain_grad = tree_sum(pieces)[0]]
  transfers between devices with their start and end apart: 17 -> 17, of which waited for: 9 -> 8; matrix products, arithmetic and copies ran while one was open for 0% -> 0% of each run, Pallas kernels for 4% -> 6%
where the time goes in v7:
time: 35.3 us; the launch traced here: 35.1 us
  starting transfers between devices  17.1 us (48%)
  waiting for transfers between devices  9.78 us (28%)
  Pallas kernels  6.22 us (18%)
  between operations  1.43 us (4%)
  other arithmetic  0.52 us (1%)
    ppermute x9, starting transfers between devices, to_section(): return lax.ppermute(x, ('sec', 'section'), pairs)  11.6 us
    ppermute x9, waiting for transfers between devices, to_section(): return lax.ppermute(x, ('sec', 'section'), pairs)  7.03 us
    ppermute x3, starting transfers between devices, per_device(): pieces.append(lax.ppermute(send, 'dp', [(i, i ^ k) for i in range(seqs)]))  4.61 us
    pallas_call x1, Pallas kernels, per_device(): pl.pallas_call(functools.partial(main_kernel, parts, heads), out_shape=(j...  3.65 us
    ppermute x3, waiting for transfers between devices, per_device(): pieces.append(lax.ppermute(send, 'dp', [(i, i ^ k) for i in range(seqs)]))  2.12 us
    pallas_call x1, Pallas kernels, per_device(): pl.pallas_call(back_kernel, out_shape=jax.ShapeDtypeStruct((tokens, half)...  1.34 us
    ppermute x5, starting transfers between devices, to_core(): return lax.ppermute(x, 'sec', swap)  0.91 us
    pallas_call x1, Pallas kernels, per_device(): pl.pallas_call(functools.partial(last_kernel, parts, width), out_shape=(j...  0.87 us
  transfers between devices with their start and end apart: 17, of which 8 were waited for; matrix products, arithmetic and copies ran while one was open for 0% of the time, Pallas kernels for 6%

profile of v7, /device:TPU:0, one launch (start us, length us, event | category | flops | bytes accessed | tf_op | source)
XLA Modules:
  0.0 35.1 jit_solution(1115599852833852064)
XLA Ops:
  0.6 0.0 slice-start
  0.6 0.0 slice-start.1
  0.7 0.0 copy-start
  0.7 0.0 copy-start.1
  0.7 0.0 copy-start.2
  0.7 3.0 %collective-permute-start = (bf16[128,512]{1,0:T(8,128)(2,1)}, bf16[128,512]{1,0:T(8,128)(2,1)S(1)}, u32[]{:S(2)}, u32[]{:S(2)}) collective-permute-start(bf16[128,512]{1,0:T(8,128)(2,1)} %bitcast.15), channel_id=1, source_target_pairs={{0,4},{4,0},{8,12},{12,8},{16,24},{20,28},{24,16},{28,20},{1,5},{5... | collective-permute-start | bytes 393224 | tf_op jit(solution)/shard_map/ppermute | solution.py:216
  3.7 1.5 %collective-permute-start.1 = (bf16[128,512]{1,0:T(8,128)(2,1)}, bf16[128,512]{1,0:T(8,128)(2,1)S(1)}, u32[]{:S(2)}, u32[]{:S(2)}) collective-permute-start(bf16[128,512]{1,0:T(8,128)(2,1)} %bitcast.16), channel_id=1, source_target_pairs={{0,8},{4,12},{8,0},{12,4},{16,20},{20,16},{24,28},{28,24},{1,9},{5... | collective-permute-start | bytes 393224 | tf_op jit(solution)/shard_map/ppermute | solution.py:216
  5.2 0.0 collective-permute-start.2
  5.2 0.0 collective-permute-start.3
  5.2 2.6 %collective-permute-done.refs_1_ = bf16[128,512]{1,0:T(8,128)(2,1)S(1)} collective-permute-done((bf16[128,512]{1,0:T(8,128)(2,1)}, bf16[128,512]{1,0:T(8,128)(2,1)S(1)}, u32[]{:S(2)}, u32[]{:S(2)}) %collective-permute-start) | collective-permute-done | bytes 131104 | tf_op jit(solution)/shard_map/ppermute | solution.py:216
  7.8 0.0 collective-permute-start.4
  7.8 3.9 %collective-permute-done.1.refs_2_ = bf16[128,512]{1,0:T(8,128)(2,1)S(1)} collective-permute-done((bf16[128,512]{1,0:T(8,128)(2,1)}, bf16[128,512]{1,0:T(8,128)(2,1)S(1)}, u32[]{:S(2)}, u32[]{:S(2)}) %collective-permute-start.1) | collective-permute-done | bytes 131104 | tf_op jit(solution)/shard_map/ppermute | solution.py:216
  11.7 0.0 collective-permute-start.5
  11.7 0.0 collective-permute-done.2.refs_3_
  11.7 0.5 %collective-permute-start.6 = (bf16[128,512]{1,0:T(8,128)(2,1)S(1)}, bf16[128,512]{1,0:T(8,128)(2,1)S(1)}, u32[]{:S(2)}, u32[]{:S(2)}) collective-permute-start(bf16[128,512]{1,0:T(8,128)(2,1)S(1)} %collective-permute-done.2.refs_3_), channel_id=1, source_target_pairs={{0,16},{16,0},{1,17},{17,1},{2,18},{18,2},{3,19},{19,3},{4,20},{20... | collective-permute-start | bytes 393224 | tf_op jit(solution)/shard_map/ppermute | solution.py:219
  12.9 0.0 collective-permute-done.3.refs_4_
  12.9 0.0 collective-permute-done.4.refs_5_
  12.9 0.2 collective-permute-done.5.refs_6_
  13.0 0.2 collective-permute-done.6.refs_7_
  13.2 0.0 copy-done.1
  13.2 0.0 copy-done.2
  13.3 0.0 copy-done.3
  13.3 3.6 %main.1 = (bf16[256,512]{1,0:T(8,128)(2,1)}, bf16[136,2048]{1,0:T(8,128)(2,1)S(1)}, bf16[128,1024]{1,0:T(8,128)(2,1)S(1)}, f32[128,1]{1,0:T(8,128)S(1)}) custom-call(s32[1]{0:T(128)S(6)} %copy.10.length_ref, f32[8,128]{1,0:T(8,128)S(1)} %first.1.token_ref, bf16[128,512]{1,0:T(8,128)(2,1)S(1)} %bitcast.19, bf16[128,512]{1,0:T(8,128)(2,1)S(1)} %collective-permute-done.refs_1_, ...), custom_call_target="tpu_custom_call" | custom-call | flops 2147483648 | bytes 8388608 | tf_op jit(solution)/shard_map/main/pallas_call | solution.py:234
  16.9 0.4 %collective-permute-start.7 = (bf16[136,2048]{1,0:T(8,128)(2,1)S(1)}, bf16[136,2048]{1,0:T(8,128)(2,1)S(1)}, u32[]{:S(2)}, u32[]{:S(2)}) collective-permute-start(bf16[136,2048]{1,0:T(8,128)(2,1)S(1)} %get-tuple-element.28.row_ref), channel_id=1, source_target_pairs={{0,16},{16,0},{1,17},{17,1},{2,18},{18,2},{3,19},{19,3},{4,20},{20... | collective-permute-start | bytes 1671176 | tf_op jit(solution)/shard_map/ppermute | solution.py:219
  17.3 1.3 %back.1.own_ref = f32[128,2048]{1,0:T(8,128)S(1)} custom-call(bf16[128,1024]{1,0:T(8,128)(2,1)S(1)} %get-tuple-element.27.grad_ref, bf16[4096,1024]{1,0:T(8,128)(2,1)S(1)} %bitcast.12), custom_call_target="tpu_custom_call" | custom-call | flops 536870912 | bytes 4194304 | tf_op jit(solution)/shard_map/back/pallas_call | solution.py:264
  18.7 0.3 collective-permute-done.7.sib_ref.row_sib_ref
  18.9 0.1 chip.1
  19.1 0.3 gain.1
  19.3 1.3 %collective-permute-start.11 = (f32[1,640]{1,0:T(1,128)S(1)}, f32[1,640]{1,0:T(1,128)S(1)}, u32[]{:S(2)}, u32[]{:S(2)}) collective-permute-start(f32[1,640]{1,0:T(1,128)S(1)} %get-tuple-element.35), channel_id=1, source_target_pairs={{0,4},{4,0},{8,12},{12,8},{16,24},{20,28},{24,16},{28,20},{1,5},{5... | collective-permute-start | bytes 7688 | tf_op jit(solution)/shard_map/ppermute | solution.py:216
  20.6 1.3 %collective-permute-start.12 = (f32[1,640]{1,0:T(1,128)S(1)}, f32[1,640]{1,0:T(1,128)S(1)}, u32[]{:S(2)}, u32[]{:S(2)}) collective-permute-start(f32[1,640]{1,0:T(1,128)S(1)} %get-tuple-element.36), channel_id=1, source_target_pairs={{0,8},{4,12},{8,0},{12,4},{16,20},{20,16},{24,28},{28,24},{1,9},{5... | collective-permute-start | bytes 7688 | tf_op jit(solution)/shard_map/ppermute | solution.py:216
  22.0 0.9 %collective-permute-start.13 = (f32[1,640]{1,0:T(1,128)S(1)}, f32[1,640]{1,0:T(1,128)S(1)}, u32[]{:S(2)}, u32[]{:S(2)}) collective-permute-start(f32[1,640]{1,0:T(1,128)S(1)} %get-tuple-element.37), channel_id=1, source_target_pairs={{0,12},{4,8},{8,4},{12,0},{16,28},{20,24},{24,20},{28,16},{1,13},{... | collective-permute-start | bytes 7688 | tf_op jit(solution)/shard_map/ppermute | solution.py:216
  22.9 2.0 %collective-permute-start.10 = (bf16[128,512]{1,0:T(8,128)(2,1)S(1)}, bf16[128,512]{1,0:T(8,128)(2,1)S(1)}, u32[]{:S(2)}, u32[]{:S(2)}) collective-permute-start(bf16[128,512]{1,0:T(8,128)(2,1)S(1)} %get-tuple-element.32.refs_7_), channel_id=1, source_target_pairs={{0,12},{4,8},{8,4},{12,0},{16,28},{20,24},{24,20},{28,16},{1,13},{... | collective-permute-start | bytes 393224 | tf_op jit(solution)/shard_map/ppermute | solution.py:216
  24.9 1.0 %collective-permute-start.8 = (bf16[128,512]{1,0:T(8,128)(2,1)S(1)}, bf16[128,512]{1,0:T(8,128)(2,1)S(1)}, u32[]{:S(2)}, u32[]{:S(2)}) collective-permute-start(bf16[128,512]{1,0:T(8,128)(2,1)S(1)} %get-tuple-element.30.refs_5_), channel_id=1, source_target_pairs={{0,4},{4,0},{8,12},{12,8},{16,24},{20,28},{24,16},{28,20},{1,5},{5... | collective-permute-start | bytes 393224 | tf_op jit(solution)/shard_map/ppermute | solution.py:216
  25.9 0.0 collective-permute-done.11.refs_7_
  25.9 0.5 %collective-permute-start.9 = (bf16[128,512]{1,0:T(8,128)(2,1)S(1)}, bf16[128,512]{1,0:T(8,128)(2,1)S(1)}, u32[]{:S(2)}, u32[]{:S(2)}) collective-permute-start(bf16[128,512]{1,0:T(8,128)(2,1)S(1)} %get-tuple-element.31.refs_6_), channel_id=1, source_target_pairs={{0,8},{4,12},{8,0},{12,4},{16,20},{20,16},{24,28},{28,24},{1,9},{5... | collective-permute-start | bytes 393224 | tf_op jit(solution)/shard_map/ppermute | solution.py:216
  26.4 0.0 collective-permute-done.12.refs_8_
  26.4 0.1 collective-permute-done.13.refs_9_
  26.5 3.7 %collective-permute-start.14 = (f32[1,128]{1,0:T(1,128)S(1)}, f32[1,128]{1,0:T(1,128)S(1)}, u32[]{:S(2)}, u32[]{:S(2)}) collective-permute-start(f32[1,128]{1,0:T(1,128)S(1)} %get-tuple-element.42), channel_id=1, source_target_pairs={{0,3},{1,2},{2,1},{3,0},{4,7},{5,6},{6,5},{7,4},{8,11},{9,10},{10,... | collective-permute-start | bytes 1544 | tf_op jit(solution)/shard_map/ppermute | solution.py:312
  30.1 0.0 collective-permute-start.15
  30.1 0.0 collective-permute-done.10.refs_2_
  30.1 0.9 %collective-permute-start.16 = (f32[1,128]{1,0:T(1,128)S(1)}, f32[1,128]{1,0:T(1,128)S(1)}, u32[]{:S(2)}, u32[]{:S(2)}) collective-permute-start(f32[1,128]{1,0:T(1,128)S(1)} %get-tuple-element.43), channel_id=1, source_target_pairs={{0,1},{1,0},{2,3},{3,2},{4,5},{5,4},{6,7},{7,6},{8,9},{9,8},{10,11... | collective-permute-start | bytes 1544 | tf_op jit(solution)/shard_map/ppermute | solution.py:312
  31.1 0.5 %collective-permute-done.8.refs_0_ = bf16[128,512]{1,0:T(8,128)(2,1)S(1)} collective-permute-done((bf16[128,512]{1,0:T(8,128)(2,1)S(1)}, bf16[128,512]{1,0:T(8,128)(2,1)S(1)}, u32[]{:S(2)}, u32[]{:S(2)}) %collective-permute-start.8) | collective-permute-done | bytes 131104 | tf_op jit(solution)/shard_map/ppermute | solution.py:216
  31.6 0.0 collective-permute-done.9.refs_1_
  31.6 0.9 %last.1 = (bf16[128,512]{1,0:T(8,128)(2,1)}, f32[1,128]{1,0:T(1,128)}) custom-call(f32[128,512]{1,0:T(8,128)S(1)} %get-tuple-element.29.refs_4_.kept_ref, bf16[128,512]{1,0:T(8,128)(2,1)S(1)} %collective-permute-done.8.refs_0_, bf16[128,512]{1,0:T(8,128)(2,1)S(1)} %collective-permute-done.9.refs_1_, bf16[128,512]{1,0:T(8,128)(2,1)S(1)} %collective-permute-done.10.refs_2_, ...), custom_call_target="tpu_custom_call" | custom-call | flops 20000000000 | bytes 4096 | tf_op jit(solution)/shard_map/last/pallas_call | solution.py:313
  32.5 0.0 collective-permute-done.14
  32.5 2.1 %collective-permute-done.15 = f32[1,128]{1,0:T(1,128)S(1)} collective-permute-done((f32[1,128]{1,0:T(1,128)S(1)}, f32[1,128]{1,0:T(1,128)S(1)}, u32[]{:S(2)}, u32[]{:S(2)}) %collective-permute-start.15) | collective-permute-done | bytes 544 | tf_op jit(solution)/shard_map/ppermute | solution.py:312
  34.6 0.0 collective-permute-done.16
  34.6 0.5 %add_bitcast_fusion = f32[128]{0:T(128)} fusion(f32[1,128]{1,0:T(1,128)S(1)} %collective-permute-done.15, f32[1,128]{1,0:T(1,128)S(1)} %collective-permute-done.16, f32[1,128]{1,0:T(1,128)S(1)} %get-tuple-element.40, f32[1,128]{1,0:T(1,128)S(1)} %collective-permute-done.14), kind=kLoop, calls=%fused_computation.7 | loop fusion | flops 384 | bytes 2560 | tf_op jit(solution)/shard_map/squeeze | solution.py:327
  (8 shorter events, 0.0 us)
Async XLA Ops:
  0.6 12.6 %slice-start = ((s8[8388608]{0:T(1024)(128)(4,1)}), s8[4194304]{0:T(1024)(128)(4,1)S(1)}, s32[]{:S(2)}) async-start(s8[8388608]{0:T(1024)(128)(4,1)} %bitcast.9), calls=%async_computation | async-start | bytes 8388608
  0.6 12.6 %slice-start.1 = ((s8[8388608]{0:T(1024)(128)(4,1)}), s8[4194304]{0:T(1024)(128)(4,1)S(1)}, s32[]{:S(2)}) async-start(s8[8388608]{0:T(1024)(128)(4,1)} %bitcast.9), calls=%async_computation.1 | async-start | bytes 8388608
  0.7 12.6 %copy-start = (bf16[1,1,256,512]{3,2,1,0:T(8,128)(2,1)S(1)}, bf16[1,1,256,512]{3,2,1,0:T(8,128)(2,1)}, u32[]{:S(2)}) copy-start(bf16[1,1,256,512]{3,2,1,0:T(8,128)(2,1)} %param.9) | copy-start | bytes 786436
  0.7 12.6 %copy-start.1 = (bf16[1,1,256,512]{3,2,1,0:T(8,128)(2,1)S(1)}, bf16[1,1,256,512]{3,2,1,0:T(8,128)(2,1)}, u32[]{:S(2)}) copy-start(bf16[1,1,256,512]{3,2,1,0:T(8,128)(2,1)} %param.10) | copy-start | bytes 786436
  0.7 12.6 %copy-start.2 = (bf16[1,128,512]{2,1,0:T(8,128)(2,1)S(1)}, bf16[1,128,512]{2,1,0:T(8,128)(2,1)}, u32[]{:S(2)}) copy-start(bf16[1,128,512]{2,1,0:T(8,128)(2,1)} %param.6) | copy-start | bytes 393220
  0.7 12.6 %copy-start.3 = (f32[4096]{0:T(1024)S(1)}, f32[4096]{0:T(1024)}, u32[]{:S(2)}) copy-start(f32[4096]{0:T(1024)} %param.7) | copy-start | bytes 49156
  0.7 7.1 %collective-permute-start = (bf16[128,512]{1,0:T(8,128)(2,1)}, bf16[128,512]{1,0:T(8,128)(2,1)S(1)}, u32[]{:S(2)}, u32[]{:S(2)}) collective-permute-start(bf16[128,512]{1,0:T(8,128)(2,1)} %bitcast.15), channel_id=1, source_target_pairs={{0,4},{4,0},{8,12},{12,8},{16,24},{20,28},{24,16},{28,20},{1,5},{5... | collective-permute-start | bytes 393224 | tf_op jit(solution)/shard_map/ppermute | solution.py:216
  3.7 8.0 %collective-permute-start.1 = (bf16[128,512]{1,0:T(8,128)(2,1)}, bf16[128,512]{1,0:T(8,128)(2,1)S(1)}, u32[]{:S(2)}, u32[]{:S(2)}) collective-permute-start(bf16[128,512]{1,0:T(8,128)(2,1)} %bitcast.16), channel_id=1, source_target_pairs={{0,8},{4,12},{8,0},{12,4},{16,20},{20,16},{24,28},{28,24},{1,9},{5... | collective-permute-start | bytes 393224 | tf_op jit(solution)/shard_map/ppermute | solution.py:216
  5.2 6.5 %collective-permute-start.2 = (bf16[128,512]{1,0:T(8,128)(2,1)}, bf16[128,512]{1,0:T(8,128)(2,1)S(1)}, u32[]{:S(2)}, u32[]{:S(2)}) collective-permute-start(bf16[128,512]{1,0:T(8,128)(2,1)} %bitcast.17), channel_id=1, source_target_pairs={{0,12},{4,8},{8,4},{12,0},{16,28},{20,24},{24,20},{28,16},{1,13},{... | collective-permute-start | bytes 393224 | tf_op jit(solution)/shard_map/ppermute | solution.py:216
  5.2 7.6 %collective-permute-start.3 = (bf16[128,512]{1,0:T(8,128)(2,1)}, bf16[128,512]{1,0:T(8,128)(2,1)S(1)}, u32[]{:S(2)}, u32[]{:S(2)}) collective-permute-start(bf16[128,512]{1,0:T(8,128)(2,1)} %bitcast.18), channel_id=1, source_target_pairs={{0,16},{16,0},{1,17},{17,1},{2,18},{18,2},{3,19},{19,3},{4,20},{20... | collective-permute-start | bytes 393224 | tf_op jit(solution)/shard_map/ppermute | solution.py:219
  7.8 5.1 %collective-permute-start.4 = (bf16[128,512]{1,0:T(8,128)(2,1)S(1)}, bf16[128,512]{1,0:T(8,128)(2,1)S(1)}, u32[]{:S(2)}, u32[]{:S(2)}) collective-permute-start(bf16[128,512]{1,0:T(8,128)(2,1)S(1)} %collective-permute-done.refs_1_), channel_id=1, source_target_pairs={{0,16},{16,0},{1,17},{17,1},{2,18},{18,2},{3,19},{19,3},{4,20},{20... | collective-permute-start | bytes 393224 | tf_op jit(solution)/shard_map/ppermute | solution.py:219
  11.7 1.3 %collective-permute-start.5 = (bf16[128,512]{1,0:T(8,128)(2,1)S(1)}, bf16[128,512]{1,0:T(8,128)(2,1)S(1)}, u32[]{:S(2)}, u32[]{:S(2)}) collective-permute-start(bf16[128,512]{1,0:T(8,128)(2,1)S(1)} %collective-permute-done.1.refs_2_), channel_id=1, source_target_pairs={{0,16},{16,0},{1,17},{17,1},{2,18},{18,2},{3,19},{19,3},{4,20},{20... | collective-permute-start | bytes 393224 | tf_op jit(solution)/shard_map/ppermute | solution.py:219
  11.7 1.5 %collective-permute-start.6 = (bf16[128,512]{1,0:T(8,128)(2,1)S(1)}, bf16[128,512]{1,0:T(8,128)(2,1)S(1)}, u32[]{:S(2)}, u32[]{:S(2)}) collective-permute-start(bf16[128,512]{1,0:T(8,128)(2,1)S(1)} %collective-permute-done.2.refs_3_), channel_id=1, source_target_pairs={{0,16},{16,0},{1,17},{17,1},{2,18},{18,2},{3,19},{19,3},{4,20},{20... | collective-permute-start | bytes 393224 | tf_op jit(solution)/shard_map/ppermute | solution.py:219
  16.9 2.0 %collective-permute-start.7 = (bf16[136,2048]{1,0:T(8,128)(2,1)S(1)}, bf16[136,2048]{1,0:T(8,128)(2,1)S(1)}, u32[]{:S(2)}, u32[]{:S(2)}) collective-permute-start(bf16[136,2048]{1,0:T(8,128)(2,1)S(1)} %get-tuple-element.28.row_ref), channel_id=1, source_target_pairs={{0,16},{16,0},{1,17},{17,1},{2,18},{18,2},{3,19},{19,3},{4,20},{20... | collective-permute-start | bytes 1671176 | tf_op jit(solution)/shard_map/ppermute | solution.py:219
  19.3 6.5 %collective-permute-start.11 = (f32[1,640]{1,0:T(1,128)S(1)}, f32[1,640]{1,0:T(1,128)S(1)}, u32[]{:S(2)}, u32[]{:S(2)}) collective-permute-start(f32[1,640]{1,0:T(1,128)S(1)} %get-tuple-element.35), channel_id=1, source_target_pairs={{0,4},{4,0},{8,12},{12,8},{16,24},{20,28},{24,16},{28,20},{1,5},{5... | collective-permute-start | bytes 7688 | tf_op jit(solution)/shard_map/ppermute | solution.py:216
  20.6 5.7 %collective-permute-start.12 = (f32[1,640]{1,0:T(1,128)S(1)}, f32[1,640]{1,0:T(1,128)S(1)}, u32[]{:S(2)}, u32[]{:S(2)}) collective-permute-start(f32[1,640]{1,0:T(1,128)S(1)} %get-tuple-element.36), channel_id=1, source_target_pairs={{0,8},{4,12},{8,0},{12,4},{16,20},{20,16},{24,28},{28,24},{1,9},{5... | collective-permute-start | bytes 7688 | tf_op jit(solution)/shard_map/ppermute | solution.py:216
  22.0 4.5 %collective-permute-start.13 = (f32[1,640]{1,0:T(1,128)S(1)}, f32[1,640]{1,0:T(1,128)S(1)}, u32[]{:S(2)}, u32[]{:S(2)}) collective-permute-start(f32[1,640]{1,0:T(1,128)S(1)} %get-tuple-element.37), channel_id=1, source_target_pairs={{0,12},{4,8},{8,4},{12,0},{16,28},{20,24},{24,20},{28,16},{1,13},{... | collective-permute-start | bytes 7688 | tf_op jit(solution)/shard_map/ppermute | solution.py:216
  22.9 7.3 %collective-permute-start.10 = (bf16[128,512]{1,0:T(8,128)(2,1)S(1)}, bf16[128,512]{1,0:T(8,128)(2,1)S(1)}, u32[]{:S(2)}, u32[]{:S(2)}) collective-permute-start(bf16[128,512]{1,0:T(8,128)(2,1)S(1)} %get-tuple-element.32.refs_7_), channel_id=1, source_target_pairs={{0,12},{4,8},{8,4},{12,0},{16,28},{20,24},{24,20},{28,16},{1,13},{... | collective-permute-start | bytes 393224 | tf_op jit(solution)/shard_map/ppermute | solution.py:216
  24.9 6.7 %collective-permute-start.8 = (bf16[128,512]{1,0:T(8,128)(2,1)S(1)}, bf16[128,512]{1,0:T(8,128)(2,1)S(1)}, u32[]{:S(2)}, u32[]{:S(2)}) collective-permute-start(bf16[128,512]{1,0:T(8,128)(2,1)S(1)} %get-tuple-element.30.refs_5_), channel_id=1, source_target_pairs={{0,4},{4,0},{8,12},{12,8},{16,24},{20,28},{24,16},{28,20},{1,5},{5... | collective-permute-start | bytes 393224 | tf_op jit(solution)/shard_map/ppermute | solution.py:216
  25.9 5.7 %collective-permute-start.9 = (bf16[128,512]{1,0:T(8,128)(2,1)S(1)}, bf16[128,512]{1,0:T(8,128)(2,1)S(1)}, u32[]{:S(2)}, u32[]{:S(2)}) collective-permute-start(bf16[128,512]{1,0:T(8,128)(2,1)S(1)} %get-tuple-element.31.refs_6_), channel_id=1, source_target_pairs={{0,8},{4,12},{8,0},{12,4},{16,20},{20,16},{24,28},{28,24},{1,9},{5... | collective-permute-start | bytes 393224 | tf_op jit(solution)/shard_map/ppermute | solution.py:216
  26.5 6.0 %collective-permute-start.14 = (f32[1,128]{1,0:T(1,128)S(1)}, f32[1,128]{1,0:T(1,128)S(1)}, u32[]{:S(2)}, u32[]{:S(2)}) collective-permute-start(f32[1,128]{1,0:T(1,128)S(1)} %get-tuple-element.42), channel_id=1, source_target_pairs={{0,3},{1,2},{2,1},{3,0},{4,7},{5,6},{6,5},{7,4},{8,11},{9,10},{10,... | collective-permute-start | bytes 1544 | tf_op jit(solution)/shard_map/ppermute | solution.py:312
  30.1 4.4 %collective-permute-start.15 = (f32[1,128]{1,0:T(1,128)S(1)}, f32[1,128]{1,0:T(1,128)S(1)}, u32[]{:S(2)}, u32[]{:S(2)}) collective-permute-start(f32[1,128]{1,0:T(1,128)S(1)} %get-tuple-element.44), channel_id=1, source_target_pairs={{0,2},{1,3},{2,0},{3,1},{4,6},{5,7},{6,4},{7,5},{8,10},{9,11},{10,... | collective-permute-start | bytes 1544 | tf_op jit(solution)/shard_map/ppermute | solution.py:312
  30.1 4.4 %collective-permute-start.16 = (f32[1,128]{1,0:T(1,128)S(1)}, f32[1,128]{1,0:T(1,128)S(1)}, u32[]{:S(2)}, u32[]{:S(2)}) collective-permute-start(f32[1,128]{1,0:T(1,128)S(1)} %get-tuple-element.43), channel_id=1, source_target_pairs={{0,1},{1,0},{2,3},{3,2},{4,5},{5,4},{6,7},{7,6},{8,9},{9,8},{10,11... | collective-permute-start | bytes 1544 | tf_op jit(solution)/shard_map/ppermute | solution.py:312

commit v8 on v7

--- a/solution.py
+++ b/solution.py
@@ -80,36 +80,49 @@
 
     scale = HS ** (-0.5)
     live = lax.broadcasted_iota(jnp.int32, (query_ref.shape[0], HS), 0) < length_ref[0]
+    every = range(heads)
+    cols = [pl.ds(h * HS, HS) for h in every]
+    key_cols = [pl.ds(2 * h * HS, HS) for h in every]
+    value_cols = [pl.ds((2 * h + 1) * HS, HS) for h in every]
+    key_rows = [kv[:, c].astype(jnp.bfloat16) for c in key_cols]
+    value_rows = [kv[:, c].astype(jnp.bfloat16) for c in value_cols]
+    query = [query_ref[:, c] for c in cols]
+    masked = [jnp.where(live, cot_ref[:, c], jnp.zeros((), jnp.bfloat16)) for c in cols]
+    scores = [
+        lax.dot_general(key_rows[h], query[h], LAST, preferred_element_type=jnp.float32) * scale
+        for h in every
+    ]
+    back = [
+        lax.dot_general(value_rows[h], masked[h], LAST, preferred_element_type=jnp.float32)
+        for h in every
+    ]
+    exponent = [jnp.exp(x) for x in scores]
+    attention = [x / jnp.sum(x, axis=0, keepdims=True) for x in exponent]
+    weights_b = [x.astype(jnp.bfloat16) for x in attention]
+    mean = [jnp.sum(attention[h] * back[h], axis=0, keepdims=True) for h in every]
+    score_grad = [
+        (attention[h] * (back[h] - mean[h]) * scale).astype(jnp.bfloat16) for h in every
+    ]
+    for h in every:
+        att_ref[:, cols[h]] = lax.dot_general(
+            weights_b[h], value_rows[h], FIRST, preferred_element_type=jnp.float32
+        ).astype(jnp.bfloat16)
+    key_grad = [
+        jnp.dot(score_grad[h], query[h], preferred_element_type=jnp.float32).astype(jnp.bfloat16)
+        for h in every
+    ]
+    value_grad = [
+        jnp.dot(weights_b[h], masked[h], preferred_element_type=jnp.float32).astype(jnp.bfloat16)
+        for h in every
+    ]
     row_part = None
-    for h in range(heads):
-        cols = pl.ds(h * HS, HS)
-        key_cols, value_cols = pl.ds(2 * h * HS, HS), pl.ds((2 * h + 1) * HS, HS)
-        key_full, value_full = kv[:, key_cols], kv[:, value_cols]
-        key_rows, value_rows = key_full.astype(jnp.bfloat16), value_full.astype(jnp.bfloat16)
-        query = query_ref[:, cols]
-        cot = cot_ref[:, cols]
-        masked = jnp.where(live, cot, jnp.zeros_like(cot))
-        scores = lax.dot_general(key_rows, query, LAST, preferred_element_type=jnp.float32) * scale
-        exponent = jnp.exp(scores)
-        attention = exponent / jnp.sum(exponent, axis=0, keepdims=True)
-        weights_b = attention.astype(jnp.bfloat16)
-        att_ref[:, cols] = lax.dot_general(
-            weights_b, value_rows, FIRST, preferred_element_type=jnp.float32
-        ).astype(jnp.bfloat16)
-        back = lax.dot_general(value_rows, masked, LAST, preferred_element_type=jnp.float32)
-        mean = jnp.sum(attention * back, axis=0, keepdims=True)
-        score_grad = (attention * (back - mean) * scale).astype(jnp.bfloat16)
-        key_grad = jnp.dot(score_grad, query, preferred_element_type=jnp.float32)
-        value_grad = jnp.dot(weights_b, masked, preferred_element_type=jnp.float32)
-        key_grad, value_grad = key_grad.astype(jnp.bfloat16), value_grad.astype(jnp.bfloat16)
-        kv_grad[:, key_cols] = key_grad
-        kv_grad[:, value_cols] = value_grad
-        here = jnp.sum(
-            key_grad.astype(jnp.float32) * key_full + value_grad.astype(jnp.float32) * value_full,
-            axis=1,
-            keepdims=True,
-        )
+    for h in every:
+        kv_grad[:, key_cols[h]] = key_grad[h]
+        kv_grad[:, value_cols[h]] = value_grad[h]
+        here = key_grad[h].astype(jnp.float32) * kv[:, key_cols[h]]
+        here = here + value_grad[h].astype(jnp.float32) * kv[:, value_cols[h]]
         row_part = here if row_part is None else row_part + here
+    row_part = jnp.sum(row_part, axis=1, keepdims=True)
     att_out = pltpu.make_async_copy(att_ref, att_hbm, sem)
     att_out.start()
     rest = jnp.transpose(jnp.broadcast_to(row_part, (tokens, 128)))[0:8, :]

time: 35.3 us -> 34.9 us (0.989)
  Pallas kernels: 6.22 us -> 5.84 us
    pallas_call x1, Pallas kernels: 3.65 us -> 3.26 us  [per_device(): pl.pallas_call(functools.partial(main_kernel, parts, heads), out_shape=(j...]
where the time goes in v8:
time: 34.9 us; the launch traced here: 34.7 us
  starting transfers between devices  17.1 us (49%)
  waiting for transfers between devices  9.77 us (28%)
  Pallas kernels  5.84 us (17%)
  between operations  1.43 us (4%)
  other arithmetic  0.52 us (1%)
    ppermute x9, starting transfers between devices, to_section(): return lax.ppermute(x, ('sec', 'section'), pairs)  11.6 us
    ppermute x9, waiting for transfers between devices, to_section(): return lax.ppermute(x, ('sec', 'section'), pairs)  7.02 us
    ppermute x3, starting transfers between devices, per_device(): pieces.append(lax.ppermute(send, 'dp', [(i, i ^ k) for i in range(seqs)]))  4.62 us
    pallas_call x1, Pallas kernels, per_device(): pl.pallas_call(functools.partial(main_kernel, parts, heads), out_shape=(j...  3.26 us
    ppermute x3, waiting for transfers between devices, per_device(): pieces.append(lax.ppermute(send, 'dp', [(i, i ^ k) for i in range(seqs)]))  2.13 us
    pallas_call x1, Pallas kernels, per_device(): pl.pallas_call(back_kernel, out_shape=jax.ShapeDtypeStruct((tokens, half)...  1.34 us
    ppermute x5, starting transfers between devices, to_core(): return lax.ppermute(x, 'sec', swap)  0.91 us
    pallas_call x1, Pallas kernels, per_device(): pl.pallas_call(functools.partial(last_kernel, parts, width), out_shape=(j...  0.87 us
  transfers between devices with their start and end apart: 17, of which 8 were waited for; matrix products, arithmetic and copies ran while one was open for 0% of the time, Pallas kernels for 6%

profile of v8, /device:TPU:0, one launch (start us, length us, event | category | flops | bytes accessed | tf_op | source)
XLA Modules:
  0.0 34.7 jit_solution(2678518236261989863)
XLA Ops:
  0.6 0.0 slice-start
  0.6 0.0 slice-start.1
  0.7 0.0 copy-start
  0.7 0.0 copy-start.1
  0.7 0.0 copy-start.2
  0.7 0.0 copy-start.3
  0.7 3.0 %collective-permute-start = (bf16[128,512]{1,0:T(8,128)(2,1)}, bf16[128,512]{1,0:T(8,128)(2,1)S(1)}, u32[]{:S(2)}, u32[]{:S(2)}) collective-permute-start(bf16[128,512]{1,0:T(8,128)(2,1)} %bitcast.15), channel_id=1, source_target_pairs={{0,4},{4,0},{8,12},{12,8},{16,24},{20,28},{24,16},{28,20},{1,5},{5... | collective-permute-start | bytes 393224 | tf_op jit(solution)/shard_map/ppermute | solution.py:229
  3.7 1.5 %collective-permute-start.1 = (bf16[128,512]{1,0:T(8,128)(2,1)}, bf16[128,512]{1,0:T(8,128)(2,1)S(1)}, u32[]{:S(2)}, u32[]{:S(2)}) collective-permute-start(bf16[128,512]{1,0:T(8,128)(2,1)} %bitcast.16), channel_id=1, source_target_pairs={{0,8},{4,12},{8,0},{12,4},{16,20},{20,16},{24,28},{28,24},{1,9},{5... | collective-permute-start | bytes 393224 | tf_op jit(solution)/shard_map/ppermute | solution.py:229
  5.2 0.0 collective-permute-start.2
  5.2 0.0 collective-permute-start.3
  5.2 2.6 %collective-permute-done.refs_1_ = bf16[128,512]{1,0:T(8,128)(2,1)S(1)} collective-permute-done((bf16[128,512]{1,0:T(8,128)(2,1)}, bf16[128,512]{1,0:T(8,128)(2,1)S(1)}, u32[]{:S(2)}, u32[]{:S(2)}) %collective-permute-start) | collective-permute-done | bytes 131104 | tf_op jit(solution)/shard_map/ppermute | solution.py:229
  7.8 0.0 collective-permute-start.4
  7.8 3.9 %collective-permute-done.1.refs_2_ = bf16[128,512]{1,0:T(8,128)(2,1)S(1)} collective-permute-done((bf16[128,512]{1,0:T(8,128)(2,1)}, bf16[128,512]{1,0:T(8,128)(2,1)S(1)}, u32[]{:S(2)}, u32[]{:S(2)}) %collective-permute-start.1) | collective-permute-done | bytes 131104 | tf_op jit(solution)/shard_map/ppermute | solution.py:229
  11.7 0.0 collective-permute-start.5
  11.7 0.0 collective-permute-done.2.refs_3_
  11.7 0.5 %collective-permute-start.6 = (bf16[128,512]{1,0:T(8,128)(2,1)S(1)}, bf16[128,512]{1,0:T(8,128)(2,1)S(1)}, u32[]{:S(2)}, u32[]{:S(2)}) collective-permute-start(bf16[128,512]{1,0:T(8,128)(2,1)S(1)} %collective-permute-done.2.refs_3_), channel_id=1, source_target_pairs={{0,16},{16,0},{1,17},{17,1},{2,18},{18,2},{3,19},{19,3},{4,20},{20... | collective-permute-start | bytes 393224 | tf_op jit(solution)/shard_map/ppermute | solution.py:232
  12.9 0.0 collective-permute-done.3.refs_4_
  12.9 0.0 collective-permute-done.4.refs_5_
  12.9 0.2 collective-permute-done.5.refs_6_
  13.0 0.2 collective-permute-done.6.refs_7_
  13.2 0.0 slice-done
  13.2 0.0 slice-done.1
  13.3 3.3 %main.1 = (bf16[256,512]{1,0:T(8,128)(2,1)}, bf16[136,2048]{1,0:T(8,128)(2,1)S(1)}, bf16[128,1024]{1,0:T(8,128)(2,1)S(1)}, f32[128,1]{1,0:T(8,128)S(1)}) custom-call(s32[1]{0:T(128)S(6)} %copy.10.length_ref, f32[8,128]{1,0:T(8,128)S(1)} %first.1.token_ref, bf16[128,512]{1,0:T(8,128)(2,1)S(1)} %bitcast.19, bf16[128,512]{1,0:T(8,128)(2,1)S(1)} %collective-permute-done.refs_1_, ...), custom_call_target="tpu_custom_call" | custom-call | flops 2147483648 | bytes 8388608 | tf_op jit(solution)/shard_map/main/pallas_call | solution.py:247
  16.5 0.4 %collective-permute-start.7 = (bf16[136,2048]{1,0:T(8,128)(2,1)S(1)}, bf16[136,2048]{1,0:T(8,128)(2,1)S(1)}, u32[]{:S(2)}, u32[]{:S(2)}) collective-permute-start(bf16[136,2048]{1,0:T(8,128)(2,1)S(1)} %get-tuple-element.28.row_ref), channel_id=1, source_target_pairs={{0,16},{16,0},{1,17},{17,1},{2,18},{18,2},{3,19},{19,3},{4,20},{20... | collective-permute-start | bytes 1671176 | tf_op jit(solution)/shard_map/ppermute | solution.py:232
  16.9 1.3 %back.1.own_ref = f32[128,2048]{1,0:T(8,128)S(1)} custom-call(bf16[128,1024]{1,0:T(8,128)(2,1)S(1)} %get-tuple-element.27.grad_ref, bf16[4096,1024]{1,0:T(8,128)(2,1)S(1)} %bitcast.12), custom_call_target="tpu_custom_call" | custom-call | flops 536870912 | bytes 4194304 | tf_op jit(solution)/shard_map/back/pallas_call | solution.py:277
  18.3 0.3 collective-permute-done.7.sib_ref.row_sib_ref
  18.6 0.1 chip.1
  18.7 0.3 gain.1
  18.9 1.3 %collective-permute-start.11 = (f32[1,640]{1,0:T(1,128)S(1)}, f32[1,640]{1,0:T(1,128)S(1)}, u32[]{:S(2)}, u32[]{:S(2)}) collective-permute-start(f32[1,640]{1,0:T(1,128)S(1)} %get-tuple-element.35), channel_id=1, source_target_pairs={{0,4},{4,0},{8,12},{12,8},{16,24},{20,28},{24,16},{28,20},{1,5},{5... | collective-permute-start | bytes 7688 | tf_op jit(solution)/shard_map/ppermute | solution.py:229
  20.3 1.3 %collective-permute-start.12 = (f32[1,640]{1,0:T(1,128)S(1)}, f32[1,640]{1,0:T(1,128)S(1)}, u32[]{:S(2)}, u32[]{:S(2)}) collective-permute-start(f32[1,640]{1,0:T(1,128)S(1)} %get-tuple-element.36), channel_id=1, source_target_pairs={{0,8},{4,12},{8,0},{12,4},{16,20},{20,16},{24,28},{28,24},{1,9},{5... | collective-permute-start | bytes 7688 | tf_op jit(solution)/shard_map/ppermute | solution.py:229
  21.6 0.9 %collective-permute-start.13 = (f32[1,640]{1,0:T(1,128)S(1)}, f32[1,640]{1,0:T(1,128)S(1)}, u32[]{:S(2)}, u32[]{:S(2)}) collective-permute-start(f32[1,640]{1,0:T(1,128)S(1)} %get-tuple-element.37), channel_id=1, source_target_pairs={{0,12},{4,8},{8,4},{12,0},{16,28},{20,24},{24,20},{28,16},{1,13},{... | collective-permute-start | bytes 7688 | tf_op jit(solution)/shard_map/ppermute | solution.py:229
  22.5 2.0 %collective-permute-start.10 = (bf16[128,512]{1,0:T(8,128)(2,1)S(1)}, bf16[128,512]{1,0:T(8,128)(2,1)S(1)}, u32[]{:S(2)}, u32[]{:S(2)}) collective-permute-start(bf16[128,512]{1,0:T(8,128)(2,1)S(1)} %get-tuple-element.32.refs_7_), channel_id=1, source_target_pairs={{0,12},{4,8},{8,4},{12,0},{16,28},{20,24},{24,20},{28,16},{1,13},{... | collective-permute-start | bytes 393224 | tf_op jit(solution)/shard_map/ppermute | solution.py:229
  24.5 1.0 %collective-permute-start.8 = (bf16[128,512]{1,0:T(8,128)(2,1)S(1)}, bf16[128,512]{1,0:T(8,128)(2,1)S(1)}, u32[]{:S(2)}, u32[]{:S(2)}) collective-permute-start(bf16[128,512]{1,0:T(8,128)(2,1)S(1)} %get-tuple-element.30.refs_5_), channel_id=1, source_target_pairs={{0,4},{4,0},{8,12},{12,8},{16,24},{20,28},{24,16},{28,20},{1,5},{5... | collective-permute-start | bytes 393224 | tf_op jit(solution)/shard_map/ppermute | solution.py:229
  25.5 0.0 collective-permute-done.11.refs_7_
  25.5 0.5 %collective-permute-start.9 = (bf16[128,512]{1,0:T(8,128)(2,1)S(1)}, bf16[128,512]{1,0:T(8,128)(2,1)S(1)}, u32[]{:S(2)}, u32[]{:S(2)}) collective-permute-start(bf16[128,512]{1,0:T(8,128)(2,1)S(1)} %get-tuple-element.31.refs_6_), channel_id=1, source_target_pairs={{0,8},{4,12},{8,0},{12,4},{16,20},{20,16},{24,28},{28,24},{1,9},{5... | collective-permute-start | bytes 393224 | tf_op jit(solution)/shard_map/ppermute | solution.py:229
  26.0 0.0 collective-permute-done.12.refs_8_
  26.0 0.1 collective-permute-done.13.refs_9_
  26.1 3.7 %collective-permute-start.14 = (f32[1,128]{1,0:T(1,128)S(1)}, f32[1,128]{1,0:T(1,128)S(1)}, u32[]{:S(2)}, u32[]{:S(2)}) collective-permute-start(f32[1,128]{1,0:T(1,128)S(1)} %get-tuple-element.42), channel_id=1, source_target_pairs={{0,3},{1,2},{2,1},{3,0},{4,7},{5,6},{6,5},{7,4},{8,11},{9,10},{10,... | collective-permute-start | bytes 1544 | tf_op jit(solution)/shard_map/ppermute | solution.py:325
  29.8 0.0 collective-permute-start.15
  29.8 0.0 collective-permute-done.10.refs_2_
  29.8 0.9 %collective-permute-start.16 = (f32[1,128]{1,0:T(1,128)S(1)}, f32[1,128]{1,0:T(1,128)S(1)}, u32[]{:S(2)}, u32[]{:S(2)}) collective-permute-start(f32[1,128]{1,0:T(1,128)S(1)} %get-tuple-element.43), channel_id=1, source_target_pairs={{0,1},{1,0},{2,3},{3,2},{4,5},{5,4},{6,7},{7,6},{8,9},{9,8},{10,11... | collective-permute-start | bytes 1544 | tf_op jit(solution)/shard_map/ppermute | solution.py:325
  30.7 0.5 %collective-permute-done.8.refs_0_ = bf16[128,512]{1,0:T(8,128)(2,1)S(1)} collective-permute-done((bf16[128,512]{1,0:T(8,128)(2,1)S(1)}, bf16[128,512]{1,0:T(8,128)(2,1)S(1)}, u32[]{:S(2)}, u32[]{:S(2)}) %collective-permute-start.8) | collective-permute-done | bytes 131104 | tf_op jit(solution)/shard_map/ppermute | solution.py:229
  31.2 0.0 collective-permute-done.9.refs_1_
  31.2 0.9 %last.1 = (bf16[128,512]{1,0:T(8,128)(2,1)}, f32[1,128]{1,0:T(1,128)}) custom-call(f32[128,512]{1,0:T(8,128)S(1)} %get-tuple-element.29.refs_4_.kept_ref, bf16[128,512]{1,0:T(8,128)(2,1)S(1)} %collective-permute-done.8.refs_0_, bf16[128,512]{1,0:T(8,128)(2,1)S(1)} %collective-permute-done.9.refs_1_, bf16[128,512]{1,0:T(8,128)(2,1)S(1)} %collective-permute-done.10.refs_2_, ...), custom_call_target="tpu_custom_call" | custom-call | flops 20000000000 | bytes 4096 | tf_op jit(solution)/shard_map/last/pallas_call | solution.py:326
  32.1 0.0 collective-permute-done.14
  32.1 2.1 %collective-permute-done.15 = f32[1,128]{1,0:T(1,128)S(1)} collective-permute-done((f32[1,128]{1,0:T(1,128)S(1)}, f32[1,128]{1,0:T(1,128)S(1)}, u32[]{:S(2)}, u32[]{:S(2)}) %collective-permute-start.15) | collective-permute-done | bytes 544 | tf_op jit(solution)/shard_map/ppermute | solution.py:325
  34.2 0.0 collective-permute-done.16
  34.2 0.5 %add_bitcast_fusion = f32[128]{0:T(128)} fusion(f32[1,128]{1,0:T(1,128)S(1)} %collective-permute-done.15, f32[1,128]{1,0:T(1,128)S(1)} %collective-permute-done.16, f32[1,128]{1,0:T(1,128)S(1)} %get-tuple-element.40, f32[1,128]{1,0:T(1,128)S(1)} %collective-permute-done.14), kind=kLoop, calls=%fused_computation.7 | loop fusion | flops 384 | bytes 2560 | tf_op jit(solution)/shard_map/squeeze | solution.py:340
  (8 shorter events, 0.0 us)
Async XLA Ops:
  0.6 12.6 %slice-start = ((s8[8388608]{0:T(1024)(128)(4,1)}), s8[4194304]{0:T(1024)(128)(4,1)S(1)}, s32[]{:S(2)}) async-start(s8[8388608]{0:T(1024)(128)(4,1)} %bitcast.9), calls=%async_computation | async-start | bytes 8388608
  0.6 12.6 %slice-start.1 = ((s8[8388608]{0:T(1024)(128)(4,1)}), s8[4194304]{0:T(1024)(128)(4,1)S(1)}, s32[]{:S(2)}) async-start(s8[8388608]{0:T(1024)(128)(4,1)} %bitcast.9), calls=%async_computation.1 | async-start | bytes 8388608
  0.7 12.6 %copy-start = (bf16[1,1,256,512]{3,2,1,0:T(8,128)(2,1)S(1)}, bf16[1,1,256,512]{3,2,1,0:T(8,128)(2,1)}, u32[]{:S(2)}) copy-start(bf16[1,1,256,512]{3,2,1,0:T(8,128)(2,1)} %param.9) | copy-start | bytes 786436
  0.7 12.6 %copy-start.1 = (bf16[1,1,256,512]{3,2,1,0:T(8,128)(2,1)S(1)}, bf16[1,1,256,512]{3,2,1,0:T(8,128)(2,1)}, u32[]{:S(2)}) copy-start(bf16[1,1,256,512]{3,2,1,0:T(8,128)(2,1)} %param.10) | copy-start | bytes 786436
  0.7 12.6 %copy-start.2 = (bf16[1,128,512]{2,1,0:T(8,128)(2,1)S(1)}, bf16[1,128,512]{2,1,0:T(8,128)(2,1)}, u32[]{:S(2)}) copy-start(bf16[1,128,512]{2,1,0:T(8,128)(2,1)} %param.6) | copy-start | bytes 393220
  0.7 12.6 %copy-start.3 = (f32[4096]{0:T(1024)S(1)}, f32[4096]{0:T(1024)}, u32[]{:S(2)}) copy-start(f32[4096]{0:T(1024)} %param.7) | copy-start | bytes 49156
  0.7 7.1 %collective-permute-start = (bf16[128,512]{1,0:T(8,128)(2,1)}, bf16[128,512]{1,0:T(8,128)(2,1)S(1)}, u32[]{:S(2)}, u32[]{:S(2)}) collective-permute-start(bf16[128,512]{1,0:T(8,128)(2,1)} %bitcast.15), channel_id=1, source_target_pairs={{0,4},{4,0},{8,12},{12,8},{16,24},{20,28},{24,16},{28,20},{1,5},{5... | collective-permute-start | bytes 393224 | tf_op jit(solution)/shard_map/ppermute | solution.py:229
  3.7 8.0 %collective-permute-start.1 = (bf16[128,512]{1,0:T(8,128)(2,1)}, bf16[128,512]{1,0:T(8,128)(2,1)S(1)}, u32[]{:S(2)}, u32[]{:S(2)}) collective-permute-start(bf16[128,512]{1,0:T(8,128)(2,1)} %bitcast.16), channel_id=1, source_target_pairs={{0,8},{4,12},{8,0},{12,4},{16,20},{20,16},{24,28},{28,24},{1,9},{5... | collective-permute-start | bytes 393224 | tf_op jit(solution)/shard_map/ppermute | solution.py:229
  5.2 6.5 %collective-permute-start.2 = (bf16[128,512]{1,0:T(8,128)(2,1)}, bf16[128,512]{1,0:T(8,128)(2,1)S(1)}, u32[]{:S(2)}, u32[]{:S(2)}) collective-permute-start(bf16[128,512]{1,0:T(8,128)(2,1)} %bitcast.17), channel_id=1, source_target_pairs={{0,12},{4,8},{8,4},{12,0},{16,28},{20,24},{24,20},{28,16},{1,13},{... | collective-permute-start | bytes 393224 | tf_op jit(solution)/shard_map/ppermute | solution.py:229
  5.2 7.6 %collective-permute-start.3 = (bf16[128,512]{1,0:T(8,128)(2,1)}, bf16[128,512]{1,0:T(8,128)(2,1)S(1)}, u32[]{:S(2)}, u32[]{:S(2)}) collective-permute-start(bf16[128,512]{1,0:T(8,128)(2,1)} %bitcast.18), channel_id=1, source_target_pairs={{0,16},{16,0},{1,17},{17,1},{2,18},{18,2},{3,19},{19,3},{4,20},{20... | collective-permute-start | bytes 393224 | tf_op jit(solution)/shard_map/ppermute | solution.py:232
  7.8 5.1 %collective-permute-start.4 = (bf16[128,512]{1,0:T(8,128)(2,1)S(1)}, bf16[128,512]{1,0:T(8,128)(2,1)S(1)}, u32[]{:S(2)}, u32[]{:S(2)}) collective-permute-start(bf16[128,512]{1,0:T(8,128)(2,1)S(1)} %collective-permute-done.refs_1_), channel_id=1, source_target_pairs={{0,16},{16,0},{1,17},{17,1},{2,18},{18,2},{3,19},{19,3},{4,20},{20... | collective-permute-start | bytes 393224 | tf_op jit(solution)/shard_map/ppermute | solution.py:232
  11.7 1.3 %collective-permute-start.5 = (bf16[128,512]{1,0:T(8,128)(2,1)S(1)}, bf16[128,512]{1,0:T(8,128)(2,1)S(1)}, u32[]{:S(2)}, u32[]{:S(2)}) collective-permute-start(bf16[128,512]{1,0:T(8,128)(2,1)S(1)} %collective-permute-done.1.refs_2_), channel_id=1, source_target_pairs={{0,16},{16,0},{1,17},{17,1},{2,18},{18,2},{3,19},{19,3},{4,20},{20... | collective-permute-start | bytes 393224 | tf_op jit(solution)/shard_map/ppermute | solution.py:232
  11.7 1.5 %collective-permute-start.6 = (bf16[128,512]{1,0:T(8,128)(2,1)S(1)}, bf16[128,512]{1,0:T(8,128)(2,1)S(1)}, u32[]{:S(2)}, u32[]{:S(2)}) collective-permute-start(bf16[128,512]{1,0:T(8,128)(2,1)S(1)} %collective-permute-done.2.refs_3_), channel_id=1, source_target_pairs={{0,16},{16,0},{1,17},{17,1},{2,18},{18,2},{3,19},{19,3},{4,20},{20... | collective-permute-start | bytes 393224 | tf_op jit(solution)/shard_map/ppermute | solution.py:232
  16.5 2.0 %collective-permute-start.7 = (bf16[136,2048]{1,0:T(8,128)(2,1)S(1)}, bf16[136,2048]{1,0:T(8,128)(2,1)S(1)}, u32[]{:S(2)}, u32[]{:S(2)}) collective-permute-start(bf16[136,2048]{1,0:T(8,128)(2,1)S(1)} %get-tuple-element.28.row_ref), channel_id=1, source_target_pairs={{0,16},{16,0},{1,17},{17,1},{2,18},{18,2},{3,19},{19,3},{4,20},{20... | collective-permute-start | bytes 1671176 | tf_op jit(solution)/shard_map/ppermute | solution.py:232
  18.9 6.5 %collective-permute-start.11 = (f32[1,640]{1,0:T(1,128)S(1)}, f32[1,640]{1,0:T(1,128)S(1)}, u32[]{:S(2)}, u32[]{:S(2)}) collective-permute-start(f32[1,640]{1,0:T(1,128)S(1)} %get-tuple-element.35), channel_id=1, source_target_pairs={{0,4},{4,0},{8,12},{12,8},{16,24},{20,28},{24,16},{28,20},{1,5},{5... | collective-permute-start | bytes 7688 | tf_op jit(solution)/shard_map/ppermute | solution.py:229
  20.3 5.7 %collective-permute-start.12 = (f32[1,640]{1,0:T(1,128)S(1)}, f32[1,640]{1,0:T(1,128)S(1)}, u32[]{:S(2)}, u32[]{:S(2)}) collective-permute-start(f32[1,640]{1,0:T(1,128)S(1)} %get-tuple-element.36), channel_id=1, source_target_pairs={{0,8},{4,12},{8,0},{12,4},{16,20},{20,16},{24,28},{28,24},{1,9},{5... | collective-permute-start | bytes 7688 | tf_op jit(solution)/shard_map/ppermute | solution.py:229
  21.6 4.5 %collective-permute-start.13 = (f32[1,640]{1,0:T(1,128)S(1)}, f32[1,640]{1,0:T(1,128)S(1)}, u32[]{:S(2)}, u32[]{:S(2)}) collective-permute-start(f32[1,640]{1,0:T(1,128)S(1)} %get-tuple-element.37), channel_id=1, source_target_pairs={{0,12},{4,8},{8,4},{12,0},{16,28},{20,24},{24,20},{28,16},{1,13},{... | collective-permute-start | bytes 7688 | tf_op jit(solution)/shard_map/ppermute | solution.py:229
  22.5 7.3 %collective-permute-start.10 = (bf16[128,512]{1,0:T(8,128)(2,1)S(1)}, bf16[128,512]{1,0:T(8,128)(2,1)S(1)}, u32[]{:S(2)}, u32[]{:S(2)}) collective-permute-start(bf16[128,512]{1,0:T(8,128)(2,1)S(1)} %get-tuple-element.32.refs_7_), channel_id=1, source_target_pairs={{0,12},{4,8},{8,4},{12,0},{16,28},{20,24},{24,20},{28,16},{1,13},{... | collective-permute-start | bytes 393224 | tf_op jit(solution)/shard_map/ppermute | solution.py:229
  24.5 6.7 %collective-permute-start.8 = (bf16[128,512]{1,0:T(8,128)(2,1)S(1)}, bf16[128,512]{1,0:T(8,128)(2,1)S(1)}, u32[]{:S(2)}, u32[]{:S(2)}) collective-permute-start(bf16[128,512]{1,0:T(8,128)(2,1)S(1)} %get-tuple-element.30.refs_5_), channel_id=1, source_target_pairs={{0,4},{4,0},{8,12},{12,8},{16,24},{20,28},{24,16},{28,20},{1,5},{5... | collective-permute-start | bytes 393224 | tf_op jit(solution)/shard_map/ppermute | solution.py:229
  25.5 5.7 %collective-permute-start.9 = (bf16[128,512]{1,0:T(8,128)(2,1)S(1)}, bf16[128,512]{1,0:T(8,128)(2,1)S(1)}, u32[]{:S(2)}, u32[]{:S(2)}) collective-permute-start(bf16[128,512]{1,0:T(8,128)(2,1)S(1)} %get-tuple-element.31.refs_6_), channel_id=1, source_target_pairs={{0,8},{4,12},{8,0},{12,4},{16,20},{20,16},{24,28},{28,24},{1,9},{5... | collective-permute-start | bytes 393224 | tf_op jit(solution)/shard_map/ppermute | solution.py:229
  26.1 6.0 %collective-permute-start.14 = (f32[1,128]{1,0:T(1,128)S(1)}, f32[1,128]{1,0:T(1,128)S(1)}, u32[]{:S(2)}, u32[]{:S(2)}) collective-permute-start(f32[1,128]{1,0:T(1,128)S(1)} %get-tuple-element.42), channel_id=1, source_target_pairs={{0,3},{1,2},{2,1},{3,0},{4,7},{5,6},{6,5},{7,4},{8,11},{9,10},{10,... | collective-permute-start | bytes 1544 | tf_op jit(solution)/shard_map/ppermute | solution.py:325
  29.8 4.4 %collective-permute-start.15 = (f32[1,128]{1,0:T(1,128)S(1)}, f32[1,128]{1,0:T(1,128)S(1)}, u32[]{:S(2)}, u32[]{:S(2)}) collective-permute-start(f32[1,128]{1,0:T(1,128)S(1)} %get-tuple-element.44), channel_id=1, source_target_pairs={{0,2},{1,3},{2,0},{3,1},{4,6},{5,7},{6,4},{7,5},{8,10},{9,11},{10,... | collective-permute-start | bytes 1544 | tf_op jit(solution)/shard_map/ppermute | solution.py:325
  29.8 4.4 %collective-permute-start.16 = (f32[1,128]{1,0:T(1,128)S(1)}, f32[1,128]{1,0:T(1,128)S(1)}, u32[]{:S(2)}, u32[]{:S(2)}) collective-permute-start(f32[1,128]{1,0:T(1,128)S(1)} %get-tuple-element.43), channel_id=1, source_target_pairs={{0,1},{1,0},{2,3},{3,2},{4,5},{5,4},{6,7},{7,6},{8,9},{9,8},{10,11... | collective-permute-start | bytes 1544 | tf_op jit(solution)/shard_map/ppermute | solution.py:325

commit v9 on v8

--- a/solution.py
+++ b/solution.py
@@ -15,20 +15,6 @@
 VMEM = pl.BlockSpec(memory_space=pltpu.VMEM)
 SMEM = pl.BlockSpec(memory_space=pltpu.SMEM)
 ANY = pl.BlockSpec(memory_space=pl.ANY)
-
-
-def reverse_bits(step, count):
-    out, bit = 0, 1
-    while bit < count:
-        out = 2 * out + (1 if step & bit else 0)
-        bit *= 2
-    return out
-
-
-def section_step(core, step, count):
-    if isinstance(core, int):
-        return reverse_bits(step, count) if core else step
-    return jnp.where(core == 0, step, reverse_bits(step, count))
 
 
 def tree_sum(terms):
@@ -50,8 +36,8 @@
 ):
     chunk_refs, refs = refs[: 2 * parts], refs[2 * parts :]
     (gain_ref, weight, query_ref, cot_ref) = refs[:4]
-    (att_hbm, sib_ref, kv_grad, inv_ref) = refs[4:8]
-    (kv, att_ref, sem) = refs[8:]
+    (att_hbm, sib_ref, kv_grad, inv_ref, normed_ref) = refs[4:9]
+    (kv, att_ref, sem) = refs[9:]
     tokens, feats = chunk_refs[0].shape
     width = weight.shape[0]
     half = width // 2
@@ -68,9 +54,11 @@
     inv_ref[...] = inv_rms
     for j, ref in enumerate(chunk_refs):
         owner = me if j < parts else 1 - me
-        peer = section ^ section_step(owner, j % parts, parts)
+        peer = section ^ (j % parts)
         cols = pl.ds(pl.multiple_of((owner * parts + peer) * feats, feats), feats)
         normed = ref[...].astype(jnp.float32) * inv_rms
+        if j < parts:
+            normed_ref[:, pl.ds(j * feats, feats)] = normed
         memory = (normed * gain_ref[:, cols]).astype(jnp.bfloat16)
         product = jnp.dot(memory, weight[cols, :], preferred_element_type=jnp.float32)
         if j == 0:
@@ -103,10 +91,6 @@
     score_grad = [
         (attention[h] * (back[h] - mean[h]) * scale).astype(jnp.bfloat16) for h in every
     ]
-    for h in every:
-        att_ref[:, cols[h]] = lax.dot_general(
-            weights_b[h], value_rows[h], FIRST, preferred_element_type=jnp.float32
-        ).astype(jnp.bfloat16)
     key_grad = [
         jnp.dot(score_grad[h], query[h], preferred_element_type=jnp.float32).astype(jnp.bfloat16)
         for h in every
@@ -123,6 +107,10 @@
         here = here + value_grad[h].astype(jnp.float32) * kv[:, value_cols[h]]
         row_part = here if row_part is None else row_part + here
     row_part = jnp.sum(row_part, axis=1, keepdims=True)
+    for h in every:
+        att_ref[:, cols[h]] = lax.dot_general(
+            weights_b[h], value_rows[h], FIRST, preferred_element_type=jnp.float32
+        ).astype(jnp.bfloat16)
     att_out = pltpu.make_async_copy(att_ref, att_hbm, sem)
     att_out.start()
     rest = jnp.transpose(jnp.broadcast_to(row_part, (tokens, 128)))[0:8, :]
@@ -156,34 +144,24 @@
         )
 
 
-def chip_kernel(parts, own_ref, sib_ref, kept_ref, *big_refs):
-    feats = kept_ref.shape[1]
+def chip_kernel(parts, own_ref, sent_ref, sib_ref, normed_ref, *refs):
+    kept_ref, big_refs, small_refs = refs[0], refs[1:parts], refs[parts:]
+    tokens, feats = kept_ref.shape
     me, section = lax.axis_index("sec"), lax.axis_index("section")
+    row = 0.0
+    for ref in (sent_ref, sib_ref):
+        terms = ref[pl.ds(tokens, 8), pl.ds(0, 128)].astype(jnp.float32)
+        row = row + ((terms[0:1, :] + terms[1:2, :]) + terms[2:3, :])
     for k in range(parts):
-        at = pl.multiple_of((section ^ section_step(me, k, parts)) * feats, feats)
-        total = own_ref[:, pl.ds(at, feats)] + sib_ref[pl.ds(0, own_ref.shape[0]), pl.ds(at, feats)].astype(
-            jnp.float32
-        )
+        cols = pl.ds(pl.multiple_of((section ^ k) * feats, feats), feats)
+        total = own_ref[:, cols] + sib_ref[pl.ds(0, tokens), cols].astype(jnp.float32)
         if k == 0:
             kept_ref[...] = total
         else:
             big_refs[k - 1][...] = total.astype(jnp.bfloat16)
-
-
-def gain_kernel(parts, row_ref, row_sib_ref, inv_ref, *refs):
-    chunk_refs, total_refs, small_refs = refs[:parts], refs[parts : 2 * parts], refs[2 * parts :]
-    feats = chunk_refs[0].shape[1]
-    inv_rms = inv_ref[...]
-    tokens = chunk_refs[0].shape[0]
-    row = 0.0
-    for ref in (row_ref, row_sib_ref):
-        terms = ref[pl.ds(tokens, 8), pl.ds(0, 128)].astype(jnp.float32)
-        row = row + ((terms[0:1, :] + terms[1:2, :]) + terms[2:3, :])
-    for k in range(parts):
-        normed = chunk_refs[k][...].astype(jnp.float32) * inv_rms
-        total = total_refs[k][...].astype(jnp.float32)
+        normed = normed_ref[:, pl.ds(k * feats, feats)]
         small_refs[k][:, pl.ds(0, feats)] = jnp.sum(total * normed, axis=0, keepdims=True)
-        small_refs[k][:, pl.ds(feats, row.shape[1])] = row
+        small_refs[k][:, pl.ds(feats, tokens)] = row
 
 
 def last_kernel(parts, width, kept_ref, *refs):
@@ -192,9 +170,7 @@
     tokens, feats = chunk_ref.shape
     core = lax.axis_index("sec")
     rows = [ref[:, pl.ds(feats, tokens)] for ref in small_refs]
-    row = tree_sum(
-        [jnp.where(core == 0, rows[k], rows[reverse_bits(k, parts)]) for k in range(parts)]
-    )
+    row = tree_sum(rows)
     row_ref[...] = row
     grad = kept_ref[...]
     for ref in big_refs:
@@ -222,7 +198,7 @@
 
     def to_section(x, step):
         pairs = [
-            (c * parts + i, c * parts + (i ^ section_step(c, step, parts)))
+            (c * parts + i, c * parts + (i ^ step))
             for c in range(cores)
             for i in range(parts)
         ]
@@ -244,16 +220,17 @@
     for k in range(1, parts):
         chunks.append(lax.optimization_barrier((to_section(rows, k), token))[0])
     others = [to_core(c) for c in chunks]
-    att, sib, kv_grad, inv_rms = pl.pallas_call(
+    att, sib, kv_grad, inv_rms, normed = pl.pallas_call(
         functools.partial(main_kernel, parts, heads),
         out_shape=(
             jax.ShapeDtypeStruct(query.shape, jnp.bfloat16),
             jax.ShapeDtypeStruct((tokens + 8, half), jnp.bfloat16),
             jax.ShapeDtypeStruct((tokens, weight.shape[1]), jnp.bfloat16),
             jax.ShapeDtypeStruct((tokens, 1), jnp.float32),
+            jax.ShapeDtypeStruct((tokens, half), jnp.float32),
         ),
         in_specs=[SMEM, ANY] + [VMEM] * (2 * parts + 4),
-        out_specs=(ANY, VMEM, VMEM, VMEM),
+        out_specs=(ANY, VMEM, VMEM, VMEM, VMEM),
         scratch_shapes=[
             pltpu.VMEM((tokens, weight.shape[1]), jnp.float32),
             pltpu.VMEM(query.shape, jnp.bfloat16),
@@ -287,31 +264,21 @@
     )(kv_grad, weight)
     sib_in = to_core(sib)
 
-    kept, *big = pl.pallas_call(
+    pieces = pl.pallas_call(
         functools.partial(chip_kernel, parts),
         out_shape=(jax.ShapeDtypeStruct((tokens, feats), jnp.float32),)
-        + (jax.ShapeDtypeStruct((tokens, feats), jnp.bfloat16),) * (parts - 1),
-        in_specs=[VMEM] * 2,
-        out_specs=(VMEM,) * parts,
+        + (jax.ShapeDtypeStruct((tokens, feats), jnp.bfloat16),) * (parts - 1)
+        + (jax.ShapeDtypeStruct((1, feats + tokens), jnp.float32),) * parts,
+        in_specs=[VMEM] * 4,
+        out_specs=(VMEM,) * (2 * parts),
         compiler_params=pltpu.CompilerParams(vmem_limit_bytes=16 << 20),
         cost_estimate=pl.CostEstimate(
-            flops=2 * tokens * half, bytes_accessed=8 * tokens * half, transcendentals=0
+            flops=4 * tokens * half, bytes_accessed=12 * tokens * half, transcendentals=0
         ),
         name="chip",
-    )(own, sib_in)
-    small = pl.pallas_call(
-        functools.partial(gain_kernel, parts),
-        out_shape=(jax.ShapeDtypeStruct((1, feats + tokens), jnp.float32),) * parts,
-        in_specs=[VMEM] * (3 + 2 * parts),
-        out_specs=(VMEM,) * parts,
-        compiler_params=pltpu.CompilerParams(vmem_limit_bytes=16 << 20),
-        cost_estimate=pl.CostEstimate(
-            flops=20_000_000_000, bytes_accessed=8 * tokens * half, transcendentals=0
-        ),
-        name="gain",
-    )(sib, sib_in, inv_rms, *chunks, kept, *big)
-
-    big_in = [to_section(big[k - 1], k) for k in range(1, parts)]
+    )(own, sib, sib_in, normed)
+    kept, big, small = pieces[0], pieces[1:parts], pieces[parts:]
+    big_in = [to_section(big[k - 1], k) for k in (parts - 1, *range(1, parts - 1))]
     small_in = [small[0]] + [to_section(small[k], k) for k in range(1, parts)]
     gain_term = tree_sum([x[:, :feats] for x in small_in])
     direct = seqs <= 8 and (feats // seqs) % 128 == 0

time: 34.9 us -> 34.6 us (level)
  no operation moved by 1% of the time
where the time goes in v9:
time: 34.6 us; the launch traced here: 34.4 us
  starting transfers between devices  17.3 us (50%)
  waiting for transfers between devices  9.49 us (27%)
  Pallas kernels  5.61 us (16%)
  between operations  1.43 us (4%)
  other arithmetic  0.52 us (2%)
    ppermute x9, starting transfers between devices, to_section(): return lax.ppermute(x, ('sec', 'section'), pairs)  11.6 us
    ppermute x9, waiting for transfers between devices, to_section(): return lax.ppermute(x, ('sec', 'section'), pairs)  7.02 us
    ppermute x3, starting transfers between devices, per_device(): pieces.append(lax.ppermute(send, 'dp', [(i, i ^ k) for i in range(seqs)]))  4.82 us
    pallas_call x1, Pallas kernels, per_device(): pl.pallas_call(functools.partial(main_kernel, parts, heads), out_shape=(j...  3.17 us
    ppermute x3, waiting for transfers between devices, per_device(): pieces.append(lax.ppermute(send, 'dp', [(i, i ^ k) for i in range(seqs)]))  1.84 us
    pallas_call x1, Pallas kernels, per_device(): pl.pallas_call(back_kernel, out_shape=jax.ShapeDtypeStruct((tokens, half)...  1.34 us
    ppermute x5, starting transfers between devices, to_core(): return lax.ppermute(x, 'sec', swap)  0.91 us
    pallas_call x1, Pallas kernels, per_device(): pl.pallas_call(functools.partial(last_kernel, parts, width), out_shape=(j...  0.87 us
  transfers between devices with their start and end apart: 17, of which 8 were waited for; matrix products, arithmetic and copies ran while one was open for 0% of the time, Pallas kernels for 6%

profile of v9, /device:TPU:0, one launch (start us, length us, event | category | flops | bytes accessed | tf_op | source)
XLA Modules:
  0.0 34.4 jit_solution(8339780899726012677)
XLA Ops:
  0.6 0.0 slice-start
  0.6 0.0 slice-start.1
  0.7 0.0 copy-start
  0.7 0.0 copy-start.1
  0.7 0.0 copy-start.2
  0.7 0.0 copy-start.3
  0.7 3.0 %collective-permute-start = (bf16[128,512]{1,0:T(8,128)(2,1)}, bf16[128,512]{1,0:T(8,128)(2,1)S(1)}, u32[]{:S(2)}, u32[]{:S(2)}) collective-permute-start(bf16[128,512]{1,0:T(8,128)(2,1)} %bitcast.15), channel_id=1, source_target_pairs={{0,4},{4,0},{8,12},{12,8},{16,20},{20,16},{24,28},{28,24},{1,5},{5... | collective-permute-start | bytes 393224 | tf_op jit(solution)/shard_map/ppermute | solution.py:205
  3.7 1.5 %collective-permute-start.1 = (bf16[128,512]{1,0:T(8,128)(2,1)}, bf16[128,512]{1,0:T(8,128)(2,1)S(1)}, u32[]{:S(2)}, u32[]{:S(2)}) collective-permute-start(bf16[128,512]{1,0:T(8,128)(2,1)} %bitcast.16), channel_id=1, source_target_pairs={{0,8},{4,12},{8,0},{12,4},{16,24},{20,28},{24,16},{28,20},{1,9},{5... | collective-permute-start | bytes 393224 | tf_op jit(solution)/shard_map/ppermute | solution.py:205
  5.2 0.0 collective-permute-start.2
  5.2 0.0 collective-permute-start.3
  5.2 2.7 %collective-permute-done.refs_1_ = bf16[128,512]{1,0:T(8,128)(2,1)S(1)} collective-permute-done((bf16[128,512]{1,0:T(8,128)(2,1)}, bf16[128,512]{1,0:T(8,128)(2,1)S(1)}, u32[]{:S(2)}, u32[]{:S(2)}) %collective-permute-start) | collective-permute-done | bytes 131104 | tf_op jit(solution)/shard_map/ppermute | solution.py:205
  7.9 0.0 collective-permute-start.4
  7.9 3.8 %collective-permute-done.1.refs_2_ = bf16[128,512]{1,0:T(8,128)(2,1)S(1)} collective-permute-done((bf16[128,512]{1,0:T(8,128)(2,1)}, bf16[128,512]{1,0:T(8,128)(2,1)S(1)}, u32[]{:S(2)}, u32[]{:S(2)}) %collective-permute-start.1) | collective-permute-done | bytes 131104 | tf_op jit(solution)/shard_map/ppermute | solution.py:205
  11.7 0.0 collective-permute-start.5
  11.7 0.0 collective-permute-done.2.refs_3_
  11.7 0.5 %collective-permute-start.6 = (bf16[128,512]{1,0:T(8,128)(2,1)S(1)}, bf16[128,512]{1,0:T(8,128)(2,1)S(1)}, u32[]{:S(2)}, u32[]{:S(2)}) collective-permute-start(bf16[128,512]{1,0:T(8,128)(2,1)S(1)} %collective-permute-done.2.refs_3_), channel_id=1, source_target_pairs={{0,16},{16,0},{1,17},{17,1},{2,18},{18,2},{3,19},{19,3},{4,20},{20... | collective-permute-start | bytes 393224 | tf_op jit(solution)/shard_map/ppermute | solution.py:208
  12.9 0.0 collective-permute-done.3.refs_4_
  12.9 0.0 collective-permute-done.4.refs_5_
  12.9 0.2 collective-permute-done.5.refs_6_
  13.0 0.2 collective-permute-done.6.refs_7_
  13.2 0.0 copy-done.1
  13.2 0.0 copy-done.2
  13.3 0.0 copy-done.3
  13.3 3.2 %main.1 = (bf16[256,512]{1,0:T(8,128)(2,1)}, bf16[136,2048]{1,0:T(8,128)(2,1)S(1)}, bf16[128,1024]{1,0:T(8,128)(2,1)S(1)}, f32[128,1]{1,0:T(8,128)S(1)}, f32[128,2048]{1,0:T(8,128)S(1)}) custom-call(s32[1]{0:T(128)S(6)} %copy.10.length_ref, f32[8,128]{1,0:T(8,128)S(1)} %first.1.token_ref, bf16[128,512]{1,0:T(8,128)(2,1)S(1)} %bitcast.19, ...), custom_call_target="tpu_custom_call" | custom-call | flops 2147483648 | bytes 8388608 | tf_op jit(solution)/shard_map/main/pallas_call | solution.py:223
  16.4 0.4 %collective-permute-start.7 = (bf16[136,2048]{1,0:T(8,128)(2,1)S(1)}, bf16[136,2048]{1,0:T(8,128)(2,1)S(1)}, u32[]{:S(2)}, u32[]{:S(2)}) collective-permute-start(bf16[136,2048]{1,0:T(8,128)(2,1)S(1)} %get-tuple-element.29.sent_ref), channel_id=1, source_target_pairs={{0,16},{16,0},{1,17},{17,1},{2,18},{18,2},{3,19},{19,3},{4,20},{20... | collective-permute-start | bytes 1671176 | tf_op jit(solution)/shard_map/ppermute | solution.py:208
  16.8 1.3 %back.1.own_ref = f32[128,2048]{1,0:T(8,128)S(1)} custom-call(bf16[128,1024]{1,0:T(8,128)(2,1)S(1)} %get-tuple-element.28.grad_ref, bf16[4096,1024]{1,0:T(8,128)(2,1)S(1)} %bitcast.12), custom_call_target="tpu_custom_call" | custom-call | flops 536870912 | bytes 4194304 | tf_op jit(solution)/shard_map/back/pallas_call | solution.py:254
  18.2 0.3 collective-permute-done.7.sib_ref
  18.5 0.2 chip.1
  18.7 1.1 %collective-permute-start.11 = (f32[1,640]{1,0:T(1,128)S(1)}, f32[1,640]{1,0:T(1,128)S(1)}, u32[]{:S(2)}, u32[]{:S(2)}) collective-permute-start(f32[1,640]{1,0:T(1,128)S(1)} %get-tuple-element.37), channel_id=1, source_target_pairs={{0,4},{4,0},{8,12},{12,8},{16,20},{20,16},{24,28},{28,24},{1,5},{5... | collective-permute-start | bytes 7688 | tf_op jit(solution)/shard_map/ppermute | solution.py:205
  19.8 1.0 %collective-permute-start.12 = (f32[1,640]{1,0:T(1,128)S(1)}, f32[1,640]{1,0:T(1,128)S(1)}, u32[]{:S(2)}, u32[]{:S(2)}) collective-permute-start(f32[1,640]{1,0:T(1,128)S(1)} %get-tuple-element.38), channel_id=1, source_target_pairs={{0,8},{4,12},{8,0},{12,4},{16,24},{20,28},{24,16},{28,20},{1,9},{5... | collective-permute-start | bytes 7688 | tf_op jit(solution)/shard_map/ppermute | solution.py:205
  20.8 1.4 %collective-permute-start.13 = (f32[1,640]{1,0:T(1,128)S(1)}, f32[1,640]{1,0:T(1,128)S(1)}, u32[]{:S(2)}, u32[]{:S(2)}) collective-permute-start(f32[1,640]{1,0:T(1,128)S(1)} %get-tuple-element.39), channel_id=1, source_target_pairs={{0,12},{4,8},{8,4},{12,0},{16,28},{20,24},{24,20},{28,16},{1,13},{... | collective-permute-start | bytes 7688 | tf_op jit(solution)/shard_map/ppermute | solution.py:205
  22.2 1.5 %collective-permute-start.10 = (bf16[128,512]{1,0:T(8,128)(2,1)S(1)}, bf16[128,512]{1,0:T(8,128)(2,1)S(1)}, u32[]{:S(2)}, u32[]{:S(2)}) collective-permute-start(bf16[128,512]{1,0:T(8,128)(2,1)S(1)} %get-tuple-element.34), channel_id=1, source_target_pairs={{0,8},{4,12},{8,0},{12,4},{16,24},{20,28},{24,16},{28,20},{1,9},{5... | collective-permute-start | bytes 393224 | tf_op jit(solution)/shard_map/ppermute | solution.py:205
  23.8 1.0 %collective-permute-start.8 = (bf16[128,512]{1,0:T(8,128)(2,1)S(1)}, bf16[128,512]{1,0:T(8,128)(2,1)S(1)}, u32[]{:S(2)}, u32[]{:S(2)}) collective-permute-start(bf16[128,512]{1,0:T(8,128)(2,1)S(1)} %get-tuple-element.32), channel_id=1, source_target_pairs={{0,12},{4,8},{8,4},{12,0},{16,28},{20,24},{24,20},{28,16},{1,13},{... | collective-permute-start | bytes 393224 | tf_op jit(solution)/shard_map/ppermute | solution.py:205
  24.7 0.0 collective-permute-done.11.refs_7_
  24.8 1.0 %collective-permute-start.9 = (bf16[128,512]{1,0:T(8,128)(2,1)S(1)}, bf16[128,512]{1,0:T(8,128)(2,1)S(1)}, u32[]{:S(2)}, u32[]{:S(2)}) collective-permute-start(bf16[128,512]{1,0:T(8,128)(2,1)S(1)} %get-tuple-element.33), channel_id=1, source_target_pairs={{0,4},{4,0},{8,12},{12,8},{16,20},{20,16},{24,28},{28,24},{1,5},{5... | collective-permute-start | bytes 393224 | tf_op jit(solution)/shard_map/ppermute | solution.py:205
  25.7 0.0 collective-permute-done.12.refs_8_
  25.7 0.0 collective-permute-done.13.refs_9_
  25.8 3.7 %collective-permute-start.14 = (f32[1,128]{1,0:T(1,128)S(1)}, f32[1,128]{1,0:T(1,128)S(1)}, u32[]{:S(2)}, u32[]{:S(2)}) collective-permute-start(f32[1,128]{1,0:T(1,128)S(1)} %get-tuple-element.44), channel_id=1, source_target_pairs={{0,3},{1,2},{2,1},{3,0},{4,7},{5,6},{6,5},{7,4},{8,11},{9,10},{10,... | collective-permute-start | bytes 1544 | tf_op jit(solution)/shard_map/ppermute | solution.py:292
  29.5 0.0 collective-permute-start.15
  29.5 0.0 collective-permute-done.10.refs_2_
  29.5 1.2 %collective-permute-start.16 = (f32[1,128]{1,0:T(1,128)S(1)}, f32[1,128]{1,0:T(1,128)S(1)}, u32[]{:S(2)}, u32[]{:S(2)}) collective-permute-start(f32[1,128]{1,0:T(1,128)S(1)} %get-tuple-element.45), channel_id=1, source_target_pairs={{0,1},{1,0},{2,3},{3,2},{4,5},{5,4},{6,7},{7,6},{8,9},{9,8},{10,11... | collective-permute-start | bytes 1544 | tf_op jit(solution)/shard_map/ppermute | solution.py:292
  30.6 0.1 collective-permute-done.8.refs_0_
  30.7 0.5 %collective-permute-done.9.refs_1_ = bf16[128,512]{1,0:T(8,128)(2,1)S(1)} collective-permute-done((bf16[128,512]{1,0:T(8,128)(2,1)S(1)}, bf16[128,512]{1,0:T(8,128)(2,1)S(1)}, u32[]{:S(2)}, u32[]{:S(2)}) %collective-permute-start.9) | collective-permute-done | bytes 131104 | tf_op jit(solution)/shard_map/ppermute | solution.py:205
  31.2 0.9 %last.1 = (bf16[128,512]{1,0:T(8,128)(2,1)}, f32[1,128]{1,0:T(1,128)}) custom-call(f32[128,512]{1,0:T(8,128)S(1)} %get-tuple-element.31.kept_ref, bf16[128,512]{1,0:T(8,128)(2,1)S(1)} %collective-permute-done.8.refs_0_, bf16[128,512]{1,0:T(8,128)(2,1)S(1)} %collective-permute-done.9.refs_1_, bf16[128,512]{1,0:T(8,128)(2,1)S(1)} %collective-permute-done.10.refs_2_, ...), custom_call_target="tpu_custom_call" | custom-call | flops 20000000000 | bytes 4096 | tf_op jit(solution)/shard_map/last/pallas_call | solution.py:293
  32.1 0.0 collective-permute-done.14
  32.1 1.8 %collective-permute-done.15 = f32[1,128]{1,0:T(1,128)S(1)} collective-permute-done((f32[1,128]{1,0:T(1,128)S(1)}, f32[1,128]{1,0:T(1,128)S(1)}, u32[]{:S(2)}, u32[]{:S(2)}) %collective-permute-start.15) | collective-permute-done | bytes 544 | tf_op jit(solution)/shard_map/ppermute | solution.py:292
  33.9 0.0 collective-permute-done.16
  33.9 0.5 %add_bitcast_fusion = f32[128]{0:T(128)} fusion(f32[1,128]{1,0:T(1,128)S(1)} %collective-permute-done.15, f32[1,128]{1,0:T(1,128)S(1)} %collective-permute-done.16, f32[1,128]{1,0:T(1,128)S(1)} %get-tuple-element.42, f32[1,128]{1,0:T(1,128)S(1)} %collective-permute-done.14), kind=kLoop, calls=%fused_computation.7 | loop fusion | flops 384 | bytes 2560 | tf_op jit(solution)/shard_map/squeeze | solution.py:307
  (7 shorter events, 0.0 us)
Async XLA Ops:
  0.6 12.6 %slice-start = ((s8[8388608]{0:T(1024)(128)(4,1)}), s8[4194304]{0:T(1024)(128)(4,1)S(1)}, s32[]{:S(2)}) async-start(s8[8388608]{0:T(1024)(128)(4,1)} %bitcast.9), calls=%async_computation | async-start | bytes 8388608
  0.6 12.6 %slice-start.1 = ((s8[8388608]{0:T(1024)(128)(4,1)}), s8[4194304]{0:T(1024)(128)(4,1)S(1)}, s32[]{:S(2)}) async-start(s8[8388608]{0:T(1024)(128)(4,1)} %bitcast.9), calls=%async_computation.1 | async-start | bytes 8388608
  0.7 12.6 %copy-start = (bf16[1,1,256,512]{3,2,1,0:T(8,128)(2,1)S(1)}, bf16[1,1,256,512]{3,2,1,0:T(8,128)(2,1)}, u32[]{:S(2)}) copy-start(bf16[1,1,256,512]{3,2,1,0:T(8,128)(2,1)} %param.9) | copy-start | bytes 786436
  0.7 12.6 %copy-start.1 = (bf16[1,1,256,512]{3,2,1,0:T(8,128)(2,1)S(1)}, bf16[1,1,256,512]{3,2,1,0:T(8,128)(2,1)}, u32[]{:S(2)}) copy-start(bf16[1,1,256,512]{3,2,1,0:T(8,128)(2,1)} %param.10) | copy-start | bytes 786436
  0.7 12.6 %copy-start.2 = (bf16[1,128,512]{2,1,0:T(8,128)(2,1)S(1)}, bf16[1,128,512]{2,1,0:T(8,128)(2,1)}, u32[]{:S(2)}) copy-start(bf16[1,128,512]{2,1,0:T(8,128)(2,1)} %param.6) | copy-start | bytes 393220
  0.7 12.6 %copy-start.3 = (f32[4096]{0:T(1024)S(1)}, f32[4096]{0:T(1024)}, u32[]{:S(2)}) copy-start(f32[4096]{0:T(1024)} %param.7) | copy-start | bytes 49156
  0.7 7.2 %collective-permute-start = (bf16[128,512]{1,0:T(8,128)(2,1)}, bf16[128,512]{1,0:T(8,128)(2,1)S(1)}, u32[]{:S(2)}, u32[]{:S(2)}) collective-permute-start(bf16[128,512]{1,0:T(8,128)(2,1)} %bitcast.15), channel_id=1, source_target_pairs={{0,4},{4,0},{8,12},{12,8},{16,20},{20,16},{24,28},{28,24},{1,5},{5... | collective-permute-start | bytes 393224 | tf_op jit(solution)/shard_map/ppermute | solution.py:205
  3.7 8.0 %collective-permute-start.1 = (bf16[128,512]{1,0:T(8,128)(2,1)}, bf16[128,512]{1,0:T(8,128)(2,1)S(1)}, u32[]{:S(2)}, u32[]{:S(2)}) collective-permute-start(bf16[128,512]{1,0:T(8,128)(2,1)} %bitcast.16), channel_id=1, source_target_pairs={{0,8},{4,12},{8,0},{12,4},{16,24},{20,28},{24,16},{28,20},{1,9},{5... | collective-permute-start | bytes 393224 | tf_op jit(solution)/shard_map/ppermute | solution.py:205
  5.2 6.5 %collective-permute-start.2 = (bf16[128,512]{1,0:T(8,128)(2,1)}, bf16[128,512]{1,0:T(8,128)(2,1)S(1)}, u32[]{:S(2)}, u32[]{:S(2)}) collective-permute-start(bf16[128,512]{1,0:T(8,128)(2,1)} %bitcast.17), channel_id=1, source_target_pairs={{0,12},{4,8},{8,4},{12,0},{16,28},{20,24},{24,20},{28,16},{1,13},{... | collective-permute-start | bytes 393224 | tf_op jit(solution)/shard_map/ppermute | solution.py:205
  5.2 7.6 %collective-permute-start.3 = (bf16[128,512]{1,0:T(8,128)(2,1)}, bf16[128,512]{1,0:T(8,128)(2,1)S(1)}, u32[]{:S(2)}, u32[]{:S(2)}) collective-permute-start(bf16[128,512]{1,0:T(8,128)(2,1)} %bitcast.18), channel_id=1, source_target_pairs={{0,16},{16,0},{1,17},{17,1},{2,18},{18,2},{3,19},{19,3},{4,20},{20... | collective-permute-start | bytes 393224 | tf_op jit(solution)/shard_map/ppermute | solution.py:208
  7.9 4.9 %collective-permute-start.4 = (bf16[128,512]{1,0:T(8,128)(2,1)S(1)}, bf16[128,512]{1,0:T(8,128)(2,1)S(1)}, u32[]{:S(2)}, u32[]{:S(2)}) collective-permute-start(bf16[128,512]{1,0:T(8,128)(2,1)S(1)} %collective-permute-done.refs_1_), channel_id=1, source_target_pairs={{0,16},{16,0},{1,17},{17,1},{2,18},{18,2},{3,19},{19,3},{4,20},{20... | collective-permute-start | bytes 393224 | tf_op jit(solution)/shard_map/ppermute | solution.py:208
  11.7 1.3 %collective-permute-start.5 = (bf16[128,512]{1,0:T(8,128)(2,1)S(1)}, bf16[128,512]{1,0:T(8,128)(2,1)S(1)}, u32[]{:S(2)}, u32[]{:S(2)}) collective-permute-start(bf16[128,512]{1,0:T(8,128)(2,1)S(1)} %collective-permute-done.1.refs_2_), channel_id=1, source_target_pairs={{0,16},{16,0},{1,17},{17,1},{2,18},{18,2},{3,19},{19,3},{4,20},{20... | collective-permute-start | bytes 393224 | tf_op jit(solution)/shard_map/ppermute | solution.py:208
  11.7 1.5 %collective-permute-start.6 = (bf16[128,512]{1,0:T(8,128)(2,1)S(1)}, bf16[128,512]{1,0:T(8,128)(2,1)S(1)}, u32[]{:S(2)}, u32[]{:S(2)}) collective-permute-start(bf16[128,512]{1,0:T(8,128)(2,1)S(1)} %collective-permute-done.2.refs_3_), channel_id=1, source_target_pairs={{0,16},{16,0},{1,17},{17,1},{2,18},{18,2},{3,19},{19,3},{4,20},{20... | collective-permute-start | bytes 393224 | tf_op jit(solution)/shard_map/ppermute | solution.py:208
  16.4 2.0 %collective-permute-start.7 = (bf16[136,2048]{1,0:T(8,128)(2,1)S(1)}, bf16[136,2048]{1,0:T(8,128)(2,1)S(1)}, u32[]{:S(2)}, u32[]{:S(2)}) collective-permute-start(bf16[136,2048]{1,0:T(8,128)(2,1)S(1)} %get-tuple-element.29.sent_ref), channel_id=1, source_target_pairs={{0,16},{16,0},{1,17},{17,1},{2,18},{18,2},{3,19},{19,3},{4,20},{20... | collective-permute-start | bytes 1671176 | tf_op jit(solution)/shard_map/ppermute | solution.py:208
  18.7 6.1 %collective-permute-start.11 = (f32[1,640]{1,0:T(1,128)S(1)}, f32[1,640]{1,0:T(1,128)S(1)}, u32[]{:S(2)}, u32[]{:S(2)}) collective-permute-start(f32[1,640]{1,0:T(1,128)S(1)} %get-tuple-element.37), channel_id=1, source_target_pairs={{0,4},{4,0},{8,12},{12,8},{16,20},{20,16},{24,28},{28,24},{1,5},{5... | collective-permute-start | bytes 7688 | tf_op jit(solution)/shard_map/ppermute | solution.py:205
  19.8 5.9 %collective-permute-start.12 = (f32[1,640]{1,0:T(1,128)S(1)}, f32[1,640]{1,0:T(1,128)S(1)}, u32[]{:S(2)}, u32[]{:S(2)}) collective-permute-start(f32[1,640]{1,0:T(1,128)S(1)} %get-tuple-element.38), channel_id=1, source_target_pairs={{0,8},{4,12},{8,0},{12,4},{16,24},{20,28},{24,16},{28,20},{1,9},{5... | collective-permute-start | bytes 7688 | tf_op jit(solution)/shard_map/ppermute | solution.py:205
  20.8 4.9 %collective-permute-start.13 = (f32[1,640]{1,0:T(1,128)S(1)}, f32[1,640]{1,0:T(1,128)S(1)}, u32[]{:S(2)}, u32[]{:S(2)}) collective-permute-start(f32[1,640]{1,0:T(1,128)S(1)} %get-tuple-element.39), channel_id=1, source_target_pairs={{0,12},{4,8},{8,4},{12,0},{16,28},{20,24},{24,20},{28,16},{1,13},{... | collective-permute-start | bytes 7688 | tf_op jit(solution)/shard_map/ppermute | solution.py:205
  22.2 7.2 %collective-permute-start.10 = (bf16[128,512]{1,0:T(8,128)(2,1)S(1)}, bf16[128,512]{1,0:T(8,128)(2,1)S(1)}, u32[]{:S(2)}, u32[]{:S(2)}) collective-permute-start(bf16[128,512]{1,0:T(8,128)(2,1)S(1)} %get-tuple-element.34), channel_id=1, source_target_pairs={{0,8},{4,12},{8,0},{12,4},{16,24},{20,28},{24,16},{28,20},{1,9},{5... | collective-permute-start | bytes 393224 | tf_op jit(solution)/shard_map/ppermute | solution.py:205
  23.8 7.0 %collective-permute-start.8 = (bf16[128,512]{1,0:T(8,128)(2,1)S(1)}, bf16[128,512]{1,0:T(8,128)(2,1)S(1)}, u32[]{:S(2)}, u32[]{:S(2)}) collective-permute-start(bf16[128,512]{1,0:T(8,128)(2,1)S(1)} %get-tuple-element.32), channel_id=1, source_target_pairs={{0,12},{4,8},{8,4},{12,0},{16,28},{20,24},{24,20},{28,16},{1,13},{... | collective-permute-start | bytes 393224 | tf_op jit(solution)/shard_map/ppermute | solution.py:205
  24.8 6.4 %collective-permute-start.9 = (bf16[128,512]{1,0:T(8,128)(2,1)S(1)}, bf16[128,512]{1,0:T(8,128)(2,1)S(1)}, u32[]{:S(2)}, u32[]{:S(2)}) collective-permute-start(bf16[128,512]{1,0:T(8,128)(2,1)S(1)} %get-tuple-element.33), channel_id=1, source_target_pairs={{0,4},{4,0},{8,12},{12,8},{16,20},{20,16},{24,28},{28,24},{1,5},{5... | collective-permute-start | bytes 393224 | tf_op jit(solution)/shard_map/ppermute | solution.py:205
  25.8 6.3 %collective-permute-start.14 = (f32[1,128]{1,0:T(1,128)S(1)}, f32[1,128]{1,0:T(1,128)S(1)}, u32[]{:S(2)}, u32[]{:S(2)}) collective-permute-start(f32[1,128]{1,0:T(1,128)S(1)} %get-tuple-element.44), channel_id=1, source_target_pairs={{0,3},{1,2},{2,1},{3,0},{4,7},{5,6},{6,5},{7,4},{8,11},{9,10},{10,... | collective-permute-start | bytes 1544 | tf_op jit(solution)/shard_map/ppermute | solution.py:292
  29.5 4.4 %collective-permute-start.15 = (f32[1,128]{1,0:T(1,128)S(1)}, f32[1,128]{1,0:T(1,128)S(1)}, u32[]{:S(2)}, u32[]{:S(2)}) collective-permute-start(f32[1,128]{1,0:T(1,128)S(1)} %get-tuple-element.46), channel_id=1, source_target_pairs={{0,2},{1,3},{2,0},{3,1},{4,6},{5,7},{6,4},{7,5},{8,10},{9,11},{10,... | collective-permute-start | bytes 1544 | tf_op jit(solution)/shard_map/ppermute | solution.py:292
  29.5 4.4 %collective-permute-start.16 = (f32[1,128]{1,0:T(1,128)S(1)}, f32[1,128]{1,0:T(1,128)S(1)}, u32[]{:S(2)}, u32[]{:S(2)}) collective-permute-start(f32[1,128]{1,0:T(1,128)S(1)} %get-tuple-element.45), channel_id=1, source_target_pairs={{0,1},{1,0},{2,3},{3,2},{4,5},{5,4},{6,7},{7,6},{8,9},{9,8},{10,11... | collective-permute-start | bytes 1544 | tf_op jit(solution)/shard_map/ppermute | solution.py:292

commit v10 on v9

--- a/solution.py
+++ b/solution.py
@@ -287,7 +287,7 @@
         piece = feats // seqs
         dp = lax.axis_index("dp")
         pieces = [lax.dynamic_slice_in_dim(gain_term, dp * piece, piece, 1)]
-        for k in reversed(range(1, seqs)):
+        for k in ((2, 3, 1) if seqs == 4 else range(1, seqs)):
             send = lax.dynamic_slice_in_dim(gain_term, (dp ^ k) * piece, piece, 1)
             pieces.append(lax.ppermute(send, "dp", [(i, i ^ k) for i in range(seqs)]))
     enc_grad, row_dot = pl.pallas_call(

time: 34.6 us -> 34.5 us (level)
  no operation moved by 1% of the time
where the time goes in v10:
time: 34.5 us; the launch traced here: 34.3 us
  starting transfers between devices  17.3 us (50%)
  waiting for transfers between devices  9.37 us (27%)
  Pallas kernels  5.61 us (16%)
  between operations  1.43 us (4%)
  other arithmetic  0.52 us (2%)
    ppermute x9, starting transfers between devices, to_section(): return lax.ppermute(x, ('sec', 'section'), pairs)  11.6 us
    ppermute x9, waiting for transfers between devices, to_section(): return lax.ppermute(x, ('sec', 'section'), pairs)  7.02 us
    ppermute x3, starting transfers between devices, per_device(): pieces.append(lax.ppermute(send, 'dp', [(i, i ^ k) for i in range(seqs)]))  4.82 us
    pallas_call x1, Pallas kernels, per_device(): pl.pallas_call(functools.partial(main_kernel, parts, heads), out_shape=(j...  3.17 us
    ppermute x3, waiting for transfers between devices, per_device(): pieces.append(lax.ppermute(send, 'dp', [(i, i ^ k) for i in range(seqs)]))  1.73 us
    pallas_call x1, Pallas kernels, per_device(): pl.pallas_call(back_kernel, out_shape=jax.ShapeDtypeStruct((tokens, half)...  1.34 us
    ppermute x5, starting transfers between devices, to_core(): return lax.ppermute(x, 'sec', swap)  0.91 us
    pallas_call x1, Pallas kernels, per_device(): pl.pallas_call(functools.partial(last_kernel, parts, width), out_shape=(j...  0.87 us
  transfers between devices with their start and end apart: 17, of which 8 were waited for; matrix products, arithmetic and copies ran while one was open for 0% of the time, Pallas kernels for 6%

profile of v10, /device:TPU:0, one launch (start us, length us, event | category | flops | bytes accessed | tf_op | source)
XLA Modules:
  0.0 34.3 jit_solution(3468696985676276019)
XLA Ops:
  0.6 0.0 slice-start
  0.6 0.0 slice-start.1
  0.7 0.0 copy-start
  0.7 0.0 copy-start.1
  0.7 0.0 copy-start.2
  0.7 0.0 copy-start.3
  0.7 3.0 %collective-permute-start = (bf16[128,512]{1,0:T(8,128)(2,1)}, bf16[128,512]{1,0:T(8,128)(2,1)S(1)}, u32[]{:S(2)}, u32[]{:S(2)}) collective-permute-start(bf16[128,512]{1,0:T(8,128)(2,1)} %bitcast.15), channel_id=1, source_target_pairs={{0,4},{4,0},{8,12},{12,8},{16,20},{20,16},{24,28},{28,24},{1,5},{5... | collective-permute-start | bytes 393224 | tf_op jit(solution)/shard_map/ppermute | solution.py:205
  3.7 1.5 %collective-permute-start.1 = (bf16[128,512]{1,0:T(8,128)(2,1)}, bf16[128,512]{1,0:T(8,128)(2,1)S(1)}, u32[]{:S(2)}, u32[]{:S(2)}) collective-permute-start(bf16[128,512]{1,0:T(8,128)(2,1)} %bitcast.16), channel_id=1, source_target_pairs={{0,8},{4,12},{8,0},{12,4},{16,24},{20,28},{24,16},{28,20},{1,9},{5... | collective-permute-start | bytes 393224 | tf_op jit(solution)/shard_map/ppermute | solution.py:205
  5.2 0.0 collective-permute-start.2
  5.2 0.0 collective-permute-start.3
  5.2 2.7 %collective-permute-done.refs_1_ = bf16[128,512]{1,0:T(8,128)(2,1)S(1)} collective-permute-done((bf16[128,512]{1,0:T(8,128)(2,1)}, bf16[128,512]{1,0:T(8,128)(2,1)S(1)}, u32[]{:S(2)}, u32[]{:S(2)}) %collective-permute-start) | collective-permute-done | bytes 131104 | tf_op jit(solution)/shard_map/ppermute | solution.py:205
  7.9 0.0 collective-permute-start.4
  7.9 3.8 %collective-permute-done.1.refs_2_ = bf16[128,512]{1,0:T(8,128)(2,1)S(1)} collective-permute-done((bf16[128,512]{1,0:T(8,128)(2,1)}, bf16[128,512]{1,0:T(8,128)(2,1)S(1)}, u32[]{:S(2)}, u32[]{:S(2)}) %collective-permute-start.1) | collective-permute-done | bytes 131104 | tf_op jit(solution)/shard_map/ppermute | solution.py:205
  11.7 0.0 collective-permute-start.5
  11.7 0.0 collective-permute-done.2.refs_3_
  11.7 0.5 %collective-permute-start.6 = (bf16[128,512]{1,0:T(8,128)(2,1)S(1)}, bf16[128,512]{1,0:T(8,128)(2,1)S(1)}, u32[]{:S(2)}, u32[]{:S(2)}) collective-permute-start(bf16[128,512]{1,0:T(8,128)(2,1)S(1)} %collective-permute-done.2.refs_3_), channel_id=1, source_target_pairs={{0,16},{16,0},{1,17},{17,1},{2,18},{18,2},{3,19},{19,3},{4,20},{20... | collective-permute-start | bytes 393224 | tf_op jit(solution)/shard_map/ppermute | solution.py:208
  12.9 0.0 collective-permute-done.3.refs_4_
  12.9 0.0 collective-permute-done.4.refs_5_
  12.9 0.2 collective-permute-done.5.refs_6_
  13.0 0.2 collective-permute-done.6.refs_7_
  13.2 0.0 slice-done
  13.2 0.0 slice-done.1
  13.2 0.0 copy-done
  13.3 3.2 %main.1 = (bf16[256,512]{1,0:T(8,128)(2,1)}, bf16[136,2048]{1,0:T(8,128)(2,1)S(1)}, bf16[128,1024]{1,0:T(8,128)(2,1)S(1)}, f32[128,1]{1,0:T(8,128)S(1)}, f32[128,2048]{1,0:T(8,128)S(1)}) custom-call(s32[1]{0:T(128)S(6)} %copy.10.length_ref, f32[8,128]{1,0:T(8,128)S(1)} %first.1.token_ref, bf16[128,512]{1,0:T(8,128)(2,1)S(1)} %bitcast.19, ...), custom_call_target="tpu_custom_call" | custom-call | flops 2147483648 | bytes 8388608 | tf_op jit(solution)/shard_map/main/pallas_call | solution.py:223
  16.4 0.4 %collective-permute-start.7 = (bf16[136,2048]{1,0:T(8,128)(2,1)S(1)}, bf16[136,2048]{1,0:T(8,128)(2,1)S(1)}, u32[]{:S(2)}, u32[]{:S(2)}) collective-permute-start(bf16[136,2048]{1,0:T(8,128)(2,1)S(1)} %get-tuple-element.29.sent_ref), channel_id=1, source_target_pairs={{0,16},{16,0},{1,17},{17,1},{2,18},{18,2},{3,19},{19,3},{4,20},{20... | collective-permute-start | bytes 1671176 | tf_op jit(solution)/shard_map/ppermute | solution.py:208
  16.8 1.3 %back.1.own_ref = f32[128,2048]{1,0:T(8,128)S(1)} custom-call(bf16[128,1024]{1,0:T(8,128)(2,1)S(1)} %get-tuple-element.28.grad_ref, bf16[4096,1024]{1,0:T(8,128)(2,1)S(1)} %bitcast.12), custom_call_target="tpu_custom_call" | custom-call | flops 536870912 | bytes 4194304 | tf_op jit(solution)/shard_map/back/pallas_call | solution.py:254
  18.2 0.3 collective-permute-done.7.sib_ref
  18.5 0.2 chip.1
  18.7 1.1 %collective-permute-start.11 = (f32[1,640]{1,0:T(1,128)S(1)}, f32[1,640]{1,0:T(1,128)S(1)}, u32[]{:S(2)}, u32[]{:S(2)}) collective-permute-start(f32[1,640]{1,0:T(1,128)S(1)} %get-tuple-element.37), channel_id=1, source_target_pairs={{0,4},{4,0},{8,12},{12,8},{16,20},{20,16},{24,28},{28,24},{1,5},{5... | collective-permute-start | bytes 7688 | tf_op jit(solution)/shard_map/ppermute | solution.py:205
  19.8 1.0 %collective-permute-start.12 = (f32[1,640]{1,0:T(1,128)S(1)}, f32[1,640]{1,0:T(1,128)S(1)}, u32[]{:S(2)}, u32[]{:S(2)}) collective-permute-start(f32[1,640]{1,0:T(1,128)S(1)} %get-tuple-element.38), channel_id=1, source_target_pairs={{0,8},{4,12},{8,0},{12,4},{16,24},{20,28},{24,16},{28,20},{1,9},{5... | collective-permute-start | bytes 7688 | tf_op jit(solution)/shard_map/ppermute | solution.py:205
  20.8 1.4 %collective-permute-start.13 = (f32[1,640]{1,0:T(1,128)S(1)}, f32[1,640]{1,0:T(1,128)S(1)}, u32[]{:S(2)}, u32[]{:S(2)}) collective-permute-start(f32[1,640]{1,0:T(1,128)S(1)} %get-tuple-element.39), channel_id=1, source_target_pairs={{0,12},{4,8},{8,4},{12,0},{16,28},{20,24},{24,20},{28,16},{1,13},{... | collective-permute-start | bytes 7688 | tf_op jit(solution)/shard_map/ppermute | solution.py:205
  22.2 1.5 %collective-permute-start.10 = (bf16[128,512]{1,0:T(8,128)(2,1)S(1)}, bf16[128,512]{1,0:T(8,128)(2,1)S(1)}, u32[]{:S(2)}, u32[]{:S(2)}) collective-permute-start(bf16[128,512]{1,0:T(8,128)(2,1)S(1)} %get-tuple-element.34), channel_id=1, source_target_pairs={{0,8},{4,12},{8,0},{12,4},{16,24},{20,28},{24,16},{28,20},{1,9},{5... | collective-permute-start | bytes 393224 | tf_op jit(solution)/shard_map/ppermute | solution.py:205
  23.8 1.0 %collective-permute-start.8 = (bf16[128,512]{1,0:T(8,128)(2,1)S(1)}, bf16[128,512]{1,0:T(8,128)(2,1)S(1)}, u32[]{:S(2)}, u32[]{:S(2)}) collective-permute-start(bf16[128,512]{1,0:T(8,128)(2,1)S(1)} %get-tuple-element.32), channel_id=1, source_target_pairs={{0,12},{4,8},{8,4},{12,0},{16,28},{20,24},{24,20},{28,16},{1,13},{... | collective-permute-start | bytes 393224 | tf_op jit(solution)/shard_map/ppermute | solution.py:205
  24.7 0.0 collective-permute-done.11.refs_7_
  24.8 1.0 %collective-permute-start.9 = (bf16[128,512]{1,0:T(8,128)(2,1)S(1)}, bf16[128,512]{1,0:T(8,128)(2,1)S(1)}, u32[]{:S(2)}, u32[]{:S(2)}) collective-permute-start(bf16[128,512]{1,0:T(8,128)(2,1)S(1)} %get-tuple-element.33), channel_id=1, source_target_pairs={{0,4},{4,0},{8,12},{12,8},{16,20},{20,16},{24,28},{28,24},{1,5},{5... | collective-permute-start | bytes 393224 | tf_op jit(solution)/shard_map/ppermute | solution.py:205
  25.7 0.0 collective-permute-done.12.refs_8_
  25.7 0.0 collective-permute-done.13.refs_9_
  25.8 2.7 %collective-permute-start.14 = (f32[1,128]{1,0:T(1,128)S(1)}, f32[1,128]{1,0:T(1,128)S(1)}, u32[]{:S(2)}, u32[]{:S(2)}) collective-permute-start(f32[1,128]{1,0:T(1,128)S(1)} %get-tuple-element.44), channel_id=1, source_target_pairs={{0,2},{1,3},{2,0},{3,1},{4,6},{5,7},{6,4},{7,5},{8,10},{9,11},{10,... | collective-permute-start | bytes 1544 | tf_op jit(solution)/shard_map/ppermute | solution.py:292
  28.4 1.3 %collective-permute-start.15 = (f32[1,128]{1,0:T(1,128)S(1)}, f32[1,128]{1,0:T(1,128)S(1)}, u32[]{:S(2)}, u32[]{:S(2)}) collective-permute-start(f32[1,128]{1,0:T(1,128)S(1)} %get-tuple-element.46), channel_id=1, source_target_pairs={{0,3},{1,2},{2,1},{3,0},{4,7},{5,6},{6,5},{7,4},{8,11},{9,10},{10,... | collective-permute-start | bytes 1544 | tf_op jit(solution)/shard_map/ppermute | solution.py:292
  29.8 0.0 collective-permute-done.10.refs_2_
  29.8 0.8 %collective-permute-start.16 = (f32[1,128]{1,0:T(1,128)S(1)}, f32[1,128]{1,0:T(1,128)S(1)}, u32[]{:S(2)}, u32[]{:S(2)}) collective-permute-start(f32[1,128]{1,0:T(1,128)S(1)} %get-tuple-element.45), channel_id=1, source_target_pairs={{0,1},{1,0},{2,3},{3,2},{4,5},{5,4},{6,7},{7,6},{8,9},{9,8},{10,11... | collective-permute-start | bytes 1544 | tf_op jit(solution)/shard_map/ppermute | solution.py:292
  30.6 0.1 collective-permute-done.8.refs_0_
  30.7 0.5 %collective-permute-done.9.refs_1_ = bf16[128,512]{1,0:T(8,128)(2,1)S(1)} collective-permute-done((bf16[128,512]{1,0:T(8,128)(2,1)S(1)}, bf16[128,512]{1,0:T(8,128)(2,1)S(1)}, u32[]{:S(2)}, u32[]{:S(2)}) %collective-permute-start.9) | collective-permute-done | bytes 131104 | tf_op jit(solution)/shard_map/ppermute | solution.py:205
  31.2 0.9 %last.1 = (bf16[128,512]{1,0:T(8,128)(2,1)}, f32[1,128]{1,0:T(1,128)}) custom-call(f32[128,512]{1,0:T(8,128)S(1)} %get-tuple-element.31.kept_ref, bf16[128,512]{1,0:T(8,128)(2,1)S(1)} %collective-permute-done.8.refs_0_, bf16[128,512]{1,0:T(8,128)(2,1)S(1)} %collective-permute-done.9.refs_1_, bf16[128,512]{1,0:T(8,128)(2,1)S(1)} %collective-permute-done.10.refs_2_, ...), custom_call_target="tpu_custom_call" | custom-call | flops 20000000000 | bytes 4096 | tf_op jit(solution)/shard_map/last/pallas_call | solution.py:293
  32.1 0.0 collective-permute-done.14
  32.1 1.7 %collective-permute-done.15 = f32[1,128]{1,0:T(1,128)S(1)} collective-permute-done((f32[1,128]{1,0:T(1,128)S(1)}, f32[1,128]{1,0:T(1,128)S(1)}, u32[]{:S(2)}, u32[]{:S(2)}) %collective-permute-start.15) | collective-permute-done | bytes 544 | tf_op jit(solution)/shard_map/ppermute | solution.py:292
  33.8 0.0 collective-permute-done.16
  33.8 0.5 %add_bitcast_fusion = f32[128]{0:T(128)} fusion(f32[1,128]{1,0:T(1,128)S(1)} %collective-permute-done.15, f32[1,128]{1,0:T(1,128)S(1)} %collective-permute-done.16, f32[1,128]{1,0:T(1,128)S(1)} %get-tuple-element.42, f32[1,128]{1,0:T(1,128)S(1)} %collective-permute-done.14), kind=kLoop, calls=%fused_computation.7 | loop fusion | flops 384 | bytes 2560 | tf_op jit(solution)/shard_map/squeeze | solution.py:307
  (7 shorter events, 0.0 us)
Async XLA Ops:
  0.6 12.6 %slice-start = ((s8[8388608]{0:T(1024)(128)(4,1)}), s8[4194304]{0:T(1024)(128)(4,1)S(1)}, s32[]{:S(2)}) async-start(s8[8388608]{0:T(1024)(128)(4,1)} %bitcast.9), calls=%async_computation | async-start | bytes 8388608
  0.6 12.6 %slice-start.1 = ((s8[8388608]{0:T(1024)(128)(4,1)}), s8[4194304]{0:T(1024)(128)(4,1)S(1)}, s32[]{:S(2)}) async-start(s8[8388608]{0:T(1024)(128)(4,1)} %bitcast.9), calls=%async_computation.1 | async-start | bytes 8388608
  0.7 12.6 %copy-start = (bf16[1,1,256,512]{3,2,1,0:T(8,128)(2,1)S(1)}, bf16[1,1,256,512]{3,2,1,0:T(8,128)(2,1)}, u32[]{:S(2)}) copy-start(bf16[1,1,256,512]{3,2,1,0:T(8,128)(2,1)} %param.9) | copy-start | bytes 786436
  0.7 12.6 %copy-start.1 = (bf16[1,1,256,512]{3,2,1,0:T(8,128)(2,1)S(1)}, bf16[1,1,256,512]{3,2,1,0:T(8,128)(2,1)}, u32[]{:S(2)}) copy-start(bf16[1,1,256,512]{3,2,1,0:T(8,128)(2,1)} %param.10) | copy-start | bytes 786436
  0.7 12.6 %copy-start.2 = (bf16[1,128,512]{2,1,0:T(8,128)(2,1)S(1)}, bf16[1,128,512]{2,1,0:T(8,128)(2,1)}, u32[]{:S(2)}) copy-start(bf16[1,128,512]{2,1,0:T(8,128)(2,1)} %param.6) | copy-start | bytes 393220
  0.7 12.6 %copy-start.3 = (f32[4096]{0:T(1024)S(1)}, f32[4096]{0:T(1024)}, u32[]{:S(2)}) copy-start(f32[4096]{0:T(1024)} %param.7) | copy-start | bytes 49156
  0.7 7.2 %collective-permute-start = (bf16[128,512]{1,0:T(8,128)(2,1)}, bf16[128,512]{1,0:T(8,128)(2,1)S(1)}, u32[]{:S(2)}, u32[]{:S(2)}) collective-permute-start(bf16[128,512]{1,0:T(8,128)(2,1)} %bitcast.15), channel_id=1, source_target_pairs={{0,4},{4,0},{8,12},{12,8},{16,20},{20,16},{24,28},{28,24},{1,5},{5... | collective-permute-start | bytes 393224 | tf_op jit(solution)/shard_map/ppermute | solution.py:205
  3.7 8.0 %collective-permute-start.1 = (bf16[128,512]{1,0:T(8,128)(2,1)}, bf16[128,512]{1,0:T(8,128)(2,1)S(1)}, u32[]{:S(2)}, u32[]{:S(2)}) collective-permute-start(bf16[128,512]{1,0:T(8,128)(2,1)} %bitcast.16), channel_id=1, source_target_pairs={{0,8},{4,12},{8,0},{12,4},{16,24},{20,28},{24,16},{28,20},{1,9},{5... | collective-permute-start | bytes 393224 | tf_op jit(solution)/shard_map/ppermute | solution.py:205
  5.2 6.5 %collective-permute-start.2 = (bf16[128,512]{1,0:T(8,128)(2,1)}, bf16[128,512]{1,0:T(8,128)(2,1)S(1)}, u32[]{:S(2)}, u32[]{:S(2)}) collective-permute-start(bf16[128,512]{1,0:T(8,128)(2,1)} %bitcast.17), channel_id=1, source_target_pairs={{0,12},{4,8},{8,4},{12,0},{16,28},{20,24},{24,20},{28,16},{1,13},{... | collective-permute-start | bytes 393224 | tf_op jit(solution)/shard_map/ppermute | solution.py:205
  5.2 7.6 %collective-permute-start.3 = (bf16[128,512]{1,0:T(8,128)(2,1)}, bf16[128,512]{1,0:T(8,128)(2,1)S(1)}, u32[]{:S(2)}, u32[]{:S(2)}) collective-permute-start(bf16[128,512]{1,0:T(8,128)(2,1)} %bitcast.18), channel_id=1, source_target_pairs={{0,16},{16,0},{1,17},{17,1},{2,18},{18,2},{3,19},{19,3},{4,20},{20... | collective-permute-start | bytes 393224 | tf_op jit(solution)/shard_map/ppermute | solution.py:208
  7.9 4.9 %collective-permute-start.4 = (bf16[128,512]{1,0:T(8,128)(2,1)S(1)}, bf16[128,512]{1,0:T(8,128)(2,1)S(1)}, u32[]{:S(2)}, u32[]{:S(2)}) collective-permute-start(bf16[128,512]{1,0:T(8,128)(2,1)S(1)} %collective-permute-done.refs_1_), channel_id=1, source_target_pairs={{0,16},{16,0},{1,17},{17,1},{2,18},{18,2},{3,19},{19,3},{4,20},{20... | collective-permute-start | bytes 393224 | tf_op jit(solution)/shard_map/ppermute | solution.py:208
  11.7 1.3 %collective-permute-start.5 = (bf16[128,512]{1,0:T(8,128)(2,1)S(1)}, bf16[128,512]{1,0:T(8,128)(2,1)S(1)}, u32[]{:S(2)}, u32[]{:S(2)}) collective-permute-start(bf16[128,512]{1,0:T(8,128)(2,1)S(1)} %collective-permute-done.1.refs_2_), channel_id=1, source_target_pairs={{0,16},{16,0},{1,17},{17,1},{2,18},{18,2},{3,19},{19,3},{4,20},{20... | collective-permute-start | bytes 393224 | tf_op jit(solution)/shard_map/ppermute | solution.py:208
  11.7 1.5 %collective-permute-start.6 = (bf16[128,512]{1,0:T(8,128)(2,1)S(1)}, bf16[128,512]{1,0:T(8,128)(2,1)S(1)}, u32[]{:S(2)}, u32[]{:S(2)}) collective-permute-start(bf16[128,512]{1,0:T(8,128)(2,1)S(1)} %collective-permute-done.2.refs_3_), channel_id=1, source_target_pairs={{0,16},{16,0},{1,17},{17,1},{2,18},{18,2},{3,19},{19,3},{4,20},{20... | collective-permute-start | bytes 393224 | tf_op jit(solution)/shard_map/ppermute | solution.py:208
  16.4 2.0 %collective-permute-start.7 = (bf16[136,2048]{1,0:T(8,128)(2,1)S(1)}, bf16[136,2048]{1,0:T(8,128)(2,1)S(1)}, u32[]{:S(2)}, u32[]{:S(2)}) collective-permute-start(bf16[136,2048]{1,0:T(8,128)(2,1)S(1)} %get-tuple-element.29.sent_ref), channel_id=1, source_target_pairs={{0,16},{16,0},{1,17},{17,1},{2,18},{18,2},{3,19},{19,3},{4,20},{20... | collective-permute-start | bytes 1671176 | tf_op jit(solution)/shard_map/ppermute | solution.py:208
  18.7 6.1 %collective-permute-start.11 = (f32[1,640]{1,0:T(1,128)S(1)}, f32[1,640]{1,0:T(1,128)S(1)}, u32[]{:S(2)}, u32[]{:S(2)}) collective-permute-start(f32[1,640]{1,0:T(1,128)S(1)} %get-tuple-element.37), channel_id=1, source_target_pairs={{0,4},{4,0},{8,12},{12,8},{16,20},{20,16},{24,28},{28,24},{1,5},{5... | collective-permute-start | bytes 7688 | tf_op jit(solution)/shard_map/ppermute | solution.py:205
  19.8 5.9 %collective-permute-start.12 = (f32[1,640]{1,0:T(1,128)S(1)}, f32[1,640]{1,0:T(1,128)S(1)}, u32[]{:S(2)}, u32[]{:S(2)}) collective-permute-start(f32[1,640]{1,0:T(1,128)S(1)} %get-tuple-element.38), channel_id=1, source_target_pairs={{0,8},{4,12},{8,0},{12,4},{16,24},{20,28},{24,16},{28,20},{1,9},{5... | collective-permute-start | bytes 7688 | tf_op jit(solution)/shard_map/ppermute | solution.py:205
  20.8 4.9 %collective-permute-start.13 = (f32[1,640]{1,0:T(1,128)S(1)}, f32[1,640]{1,0:T(1,128)S(1)}, u32[]{:S(2)}, u32[]{:S(2)}) collective-permute-start(f32[1,640]{1,0:T(1,128)S(1)} %get-tuple-element.39), channel_id=1, source_target_pairs={{0,12},{4,8},{8,4},{12,0},{16,28},{20,24},{24,20},{28,16},{1,13},{... | collective-permute-start | bytes 7688 | tf_op jit(solution)/shard_map/ppermute | solution.py:205
  22.2 7.5 %collective-permute-start.10 = (bf16[128,512]{1,0:T(8,128)(2,1)S(1)}, bf16[128,512]{1,0:T(8,128)(2,1)S(1)}, u32[]{:S(2)}, u32[]{:S(2)}) collective-permute-start(bf16[128,512]{1,0:T(8,128)(2,1)S(1)} %get-tuple-element.34), channel_id=1, source_target_pairs={{0,8},{4,12},{8,0},{12,4},{16,24},{20,28},{24,16},{28,20},{1,9},{5... | collective-permute-start | bytes 393224 | tf_op jit(solution)/shard_map/ppermute | solution.py:205
  23.8 7.0 %collective-permute-start.8 = (bf16[128,512]{1,0:T(8,128)(2,1)S(1)}, bf16[128,512]{1,0:T(8,128)(2,1)S(1)}, u32[]{:S(2)}, u32[]{:S(2)}) collective-permute-start(bf16[128,512]{1,0:T(8,128)(2,1)S(1)} %get-tuple-element.32), channel_id=1, source_target_pairs={{0,12},{4,8},{8,4},{12,0},{16,28},{20,24},{24,20},{28,16},{1,13},{... | collective-permute-start | bytes 393224 | tf_op jit(solution)/shard_map/ppermute | solution.py:205
  24.8 6.4 %collective-permute-start.9 = (bf16[128,512]{1,0:T(8,128)(2,1)S(1)}, bf16[128,512]{1,0:T(8,128)(2,1)S(1)}, u32[]{:S(2)}, u32[]{:S(2)}) collective-permute-start(bf16[128,512]{1,0:T(8,128)(2,1)S(1)} %get-tuple-element.33), channel_id=1, source_target_pairs={{0,4},{4,0},{8,12},{12,8},{16,20},{20,16},{24,28},{28,24},{1,5},{5... | collective-permute-start | bytes 393224 | tf_op jit(solution)/shard_map/ppermute | solution.py:205
  25.8 6.3 %collective-permute-start.14 = (f32[1,128]{1,0:T(1,128)S(1)}, f32[1,128]{1,0:T(1,128)S(1)}, u32[]{:S(2)}, u32[]{:S(2)}) collective-permute-start(f32[1,128]{1,0:T(1,128)S(1)} %get-tuple-element.44), channel_id=1, source_target_pairs={{0,2},{1,3},{2,0},{3,1},{4,6},{5,7},{6,4},{7,5},{8,10},{9,11},{10,... | collective-permute-start | bytes 1544 | tf_op jit(solution)/shard_map/ppermute | solution.py:292
  28.4 5.3 %collective-permute-start.15 = (f32[1,128]{1,0:T(1,128)S(1)}, f32[1,128]{1,0:T(1,128)S(1)}, u32[]{:S(2)}, u32[]{:S(2)}) collective-permute-start(f32[1,128]{1,0:T(1,128)S(1)} %get-tuple-element.46), channel_id=1, source_target_pairs={{0,3},{1,2},{2,1},{3,0},{4,7},{5,6},{6,5},{7,4},{8,11},{9,10},{10,... | collective-permute-start | bytes 1544 | tf_op jit(solution)/shard_map/ppermute | solution.py:292
  29.8 4.0 %collective-permute-start.16 = (f32[1,128]{1,0:T(1,128)S(1)}, f32[1,128]{1,0:T(1,128)S(1)}, u32[]{:S(2)}, u32[]{:S(2)}) collective-permute-start(f32[1,128]{1,0:T(1,128)S(1)} %get-tuple-element.45), channel_id=1, source_target_pairs={{0,1},{1,0},{2,3},{3,2},{4,5},{5,4},{6,7},{7,6},{8,9},{9,8},{10,11... | collective-permute-start | bytes 1544 | tf_op jit(solution)/shard_map/ppermute | solution.py:292

commit v11 on v9

--- a/solution.py
+++ b/solution.py
@@ -124,8 +124,8 @@
     sib_ref[pl.ds(tokens, 8), pl.ds(0, 128)] = pieces.astype(jnp.bfloat16)
 
     grad = kv_grad[...]
-    tile = half // 4
-    for t in range(4):
+    tile = half // 8
+    for t in range(8):
         rows = pl.ds(pl.multiple_of((1 - me) * half + t * tile, tile), tile)
         part = lax.dot_general(weight[rows, :], grad, LAST, preferred_element_type=jnp.float32)
         sib_ref[pl.ds(0, tokens), pl.ds(t * tile, tile)] = jnp.transpose(part).astype(jnp.bfloat16)

time: 34.6 us -> 34.6 us (level)
  no operation moved by 1% of the time
where the time goes in v11:
time: 34.6 us; the launch traced here: 34.4 us
  starting transfers between devices  17.3 us (50%)
  waiting for transfers between devices  9.5 us (27%)
  Pallas kernels  5.6 us (16%)
  between operations  1.43 us (4%)
  other arithmetic  0.52 us (2%)
    ppermute x9, starting transfers between devices, to_section(): return lax.ppermute(x, ('sec', 'section'), pairs)  11.6 us
    ppermute x9, waiting for transfers between devices, to_section(): return lax.ppermute(x, ('sec', 'section'), pairs)  7.02 us
    ppermute x3, starting transfers between devices, per_device(): pieces.append(lax.ppermute(send, 'dp', [(i, i ^ k) for i in range(seqs)]))  4.82 us
    pallas_call x1, Pallas kernels, per_device(): pl.pallas_call(functools.partial(main_kernel, parts, heads), out_shape=(j...  3.17 us
    ppermute x3, waiting for transfers between devices, per_device(): pieces.append(lax.ppermute(send, 'dp', [(i, i ^ k) for i in range(seqs)]))  1.84 us
    pallas_call x1, Pallas kernels, per_device(): pl.pallas_call(back_kernel, out_shape=jax.ShapeDtypeStruct((tokens, half)...  1.33 us
    ppermute x5, starting transfers between devices, to_core(): return lax.ppermute(x, 'sec', swap)  0.91 us
    pallas_call x1, Pallas kernels, per_device(): pl.pallas_call(functools.partial(last_kernel, parts, width), out_shape=(j...  0.87 us
  transfers between devices with their start and end apart: 17, of which 8 were waited for; matrix products, arithmetic and copies ran while one was open for 0% of the time, Pallas kernels for 6%

profile of v11, /device:TPU:0, one launch (start us, length us, event | category | flops | bytes accessed | tf_op | source)
XLA Modules:
  0.0 34.4 jit_solution(3421759577903675298)
XLA Ops:
  0.6 0.0 slice-start
  0.6 0.0 slice-start.1
  0.7 0.0 copy-start
  0.7 0.0 copy-start.1
  0.7 0.0 copy-start.2
  0.7 0.0 copy-start.3
  0.7 3.0 %collective-permute-start = (bf16[128,512]{1,0:T(8,128)(2,1)}, bf16[128,512]{1,0:T(8,128)(2,1)S(1)}, u32[]{:S(2)}, u32[]{:S(2)}) collective-permute-start(bf16[128,512]{1,0:T(8,128)(2,1)} %bitcast.15), channel_id=1, source_target_pairs={{0,4},{4,0},{8,12},{12,8},{16,20},{20,16},{24,28},{28,24},{1,5},{5... | collective-permute-start | bytes 393224 | tf_op jit(solution)/shard_map/ppermute | solution.py:205
  3.7 1.5 %collective-permute-start.1 = (bf16[128,512]{1,0:T(8,128)(2,1)}, bf16[128,512]{1,0:T(8,128)(2,1)S(1)}, u32[]{:S(2)}, u32[]{:S(2)}) collective-permute-start(bf16[128,512]{1,0:T(8,128)(2,1)} %bitcast.16), channel_id=1, source_target_pairs={{0,8},{4,12},{8,0},{12,4},{16,24},{20,28},{24,16},{28,20},{1,9},{5... | collective-permute-start | bytes 393224 | tf_op jit(solution)/shard_map/ppermute | solution.py:205
  5.2 0.0 collective-permute-start.2
  5.2 0.0 collective-permute-start.3
  5.2 2.7 %collective-permute-done.refs_1_ = bf16[128,512]{1,0:T(8,128)(2,1)S(1)} collective-permute-done((bf16[128,512]{1,0:T(8,128)(2,1)}, bf16[128,512]{1,0:T(8,128)(2,1)S(1)}, u32[]{:S(2)}, u32[]{:S(2)}) %collective-permute-start) | collective-permute-done | bytes 131104 | tf_op jit(solution)/shard_map/ppermute | solution.py:205
  7.9 0.0 collective-permute-start.4
  7.9 3.8 %collective-permute-done.1.refs_2_ = bf16[128,512]{1,0:T(8,128)(2,1)S(1)} collective-permute-done((bf16[128,512]{1,0:T(8,128)(2,1)}, bf16[128,512]{1,0:T(8,128)(2,1)S(1)}, u32[]{:S(2)}, u32[]{:S(2)}) %collective-permute-start.1) | collective-permute-done | bytes 131104 | tf_op jit(solution)/shard_map/ppermute | solution.py:205
  11.7 0.0 collective-permute-start.5
  11.7 0.0 collective-permute-done.2.refs_3_
  11.7 0.5 %collective-permute-start.6 = (bf16[128,512]{1,0:T(8,128)(2,1)S(1)}, bf16[128,512]{1,0:T(8,128)(2,1)S(1)}, u32[]{:S(2)}, u32[]{:S(2)}) collective-permute-start(bf16[128,512]{1,0:T(8,128)(2,1)S(1)} %collective-permute-done.2.refs_3_), channel_id=1, source_target_pairs={{0,16},{16,0},{1,17},{17,1},{2,18},{18,2},{3,19},{19,3},{4,20},{20... | collective-permute-start | bytes 393224 | tf_op jit(solution)/shard_map/ppermute | solution.py:208
  12.9 0.0 collective-permute-done.3.refs_4_
  12.9 0.0 collective-permute-done.4.refs_5_
  12.9 0.2 collective-permute-done.5.refs_6_
  13.0 0.2 collective-permute-done.6.refs_7_
  13.2 0.0 copy-done.1
  13.2 0.0 copy-done.2
  13.3 0.0 copy-done.3
  13.3 3.2 %main.1 = (bf16[256,512]{1,0:T(8,128)(2,1)}, bf16[136,2048]{1,0:T(8,128)(2,1)S(1)}, bf16[128,1024]{1,0:T(8,128)(2,1)S(1)}, f32[128,1]{1,0:T(8,128)S(1)}, f32[128,2048]{1,0:T(8,128)S(1)}) custom-call(s32[1]{0:T(128)S(6)} %copy.10.length_ref, f32[8,128]{1,0:T(8,128)S(1)} %first.1.token_ref, bf16[128,512]{1,0:T(8,128)(2,1)S(1)} %bitcast.19, ...), custom_call_target="tpu_custom_call" | custom-call | flops 2147483648 | bytes 8388608 | tf_op jit(solution)/shard_map/main/pallas_call | solution.py:223
  16.4 0.4 %collective-permute-start.7 = (bf16[136,2048]{1,0:T(8,128)(2,1)S(1)}, bf16[136,2048]{1,0:T(8,128)(2,1)S(1)}, u32[]{:S(2)}, u32[]{:S(2)}) collective-permute-start(bf16[136,2048]{1,0:T(8,128)(2,1)S(1)} %get-tuple-element.29.sent_ref), channel_id=1, source_target_pairs={{0,16},{16,0},{1,17},{17,1},{2,18},{18,2},{3,19},{19,3},{4,20},{20... | collective-permute-start | bytes 1671176 | tf_op jit(solution)/shard_map/ppermute | solution.py:208
  16.8 1.3 %back.1.own_ref = f32[128,2048]{1,0:T(8,128)S(1)} custom-call(bf16[128,1024]{1,0:T(8,128)(2,1)S(1)} %get-tuple-element.28.grad_ref, bf16[4096,1024]{1,0:T(8,128)(2,1)S(1)} %bitcast.12), custom_call_target="tpu_custom_call" | custom-call | flops 536870912 | bytes 4194304 | tf_op jit(solution)/shard_map/back/pallas_call | solution.py:254
  18.2 0.3 collective-permute-done.7.sib_ref
  18.5 0.2 chip.1
  18.7 1.1 %collective-permute-start.11 = (f32[1,640]{1,0:T(1,128)S(1)}, f32[1,640]{1,0:T(1,128)S(1)}, u32[]{:S(2)}, u32[]{:S(2)}) collective-permute-start(f32[1,640]{1,0:T(1,128)S(1)} %get-tuple-element.37), channel_id=1, source_target_pairs={{0,4},{4,0},{8,12},{12,8},{16,20},{20,16},{24,28},{28,24},{1,5},{5... | collective-permute-start | bytes 7688 | tf_op jit(solution)/shard_map/ppermute | solution.py:205
  19.8 1.0 %collective-permute-start.12 = (f32[1,640]{1,0:T(1,128)S(1)}, f32[1,640]{1,0:T(1,128)S(1)}, u32[]{:S(2)}, u32[]{:S(2)}) collective-permute-start(f32[1,640]{1,0:T(1,128)S(1)} %get-tuple-element.38), channel_id=1, source_target_pairs={{0,8},{4,12},{8,0},{12,4},{16,24},{20,28},{24,16},{28,20},{1,9},{5... | collective-permute-start | bytes 7688 | tf_op jit(solution)/shard_map/ppermute | solution.py:205
  20.8 1.4 %collective-permute-start.13 = (f32[1,640]{1,0:T(1,128)S(1)}, f32[1,640]{1,0:T(1,128)S(1)}, u32[]{:S(2)}, u32[]{:S(2)}) collective-permute-start(f32[1,640]{1,0:T(1,128)S(1)} %get-tuple-element.39), channel_id=1, source_target_pairs={{0,12},{4,8},{8,4},{12,0},{16,28},{20,24},{24,20},{28,16},{1,13},{... | collective-permute-start | bytes 7688 | tf_op jit(solution)/shard_map/ppermute | solution.py:205
  22.2 1.5 %collective-permute-start.10 = (bf16[128,512]{1,0:T(8,128)(2,1)S(1)}, bf16[128,512]{1,0:T(8,128)(2,1)S(1)}, u32[]{:S(2)}, u32[]{:S(2)}) collective-permute-start(bf16[128,512]{1,0:T(8,128)(2,1)S(1)} %get-tuple-element.34), channel_id=1, source_target_pairs={{0,8},{4,12},{8,0},{12,4},{16,24},{20,28},{24,16},{28,20},{1,9},{5... | collective-permute-start | bytes 393224 | tf_op jit(solution)/shard_map/ppermute | solution.py:205
  23.8 1.0 %collective-permute-start.8 = (bf16[128,512]{1,0:T(8,128)(2,1)S(1)}, bf16[128,512]{1,0:T(8,128)(2,1)S(1)}, u32[]{:S(2)}, u32[]{:S(2)}) collective-permute-start(bf16[128,512]{1,0:T(8,128)(2,1)S(1)} %get-tuple-element.32), channel_id=1, source_target_pairs={{0,12},{4,8},{8,4},{12,0},{16,28},{20,24},{24,20},{28,16},{1,13},{... | collective-permute-start | bytes 393224 | tf_op jit(solution)/shard_map/ppermute | solution.py:205
  24.7 0.0 collective-permute-done.11.refs_7_
  24.7 1.0 %collective-permute-start.9 = (bf16[128,512]{1,0:T(8,128)(2,1)S(1)}, bf16[128,512]{1,0:T(8,128)(2,1)S(1)}, u32[]{:S(2)}, u32[]{:S(2)}) collective-permute-start(bf16[128,512]{1,0:T(8,128)(2,1)S(1)} %get-tuple-element.33), channel_id=1, source_target_pairs={{0,4},{4,0},{8,12},{12,8},{16,20},{20,16},{24,28},{28,24},{1,5},{5... | collective-permute-start | bytes 393224 | tf_op jit(solution)/shard_map/ppermute | solution.py:205
  25.7 0.0 collective-permute-done.12.refs_8_
  25.7 0.0 collective-permute-done.13.refs_9_
  25.8 3.7 %collective-permute-start.14 = (f32[1,128]{1,0:T(1,128)S(1)}, f32[1,128]{1,0:T(1,128)S(1)}, u32[]{:S(2)}, u32[]{:S(2)}) collective-permute-start(f32[1,128]{1,0:T(1,128)S(1)} %get-tuple-element.44), channel_id=1, source_target_pairs={{0,3},{1,2},{2,1},{3,0},{4,7},{5,6},{6,5},{7,4},{8,11},{9,10},{10,... | collective-permute-start | bytes 1544 | tf_op jit(solution)/shard_map/ppermute | solution.py:292
  29.5 0.0 collective-permute-start.15
  29.5 0.0 collective-permute-done.10.refs_2_
  29.5 1.2 %collective-permute-start.16 = (f32[1,128]{1,0:T(1,128)S(1)}, f32[1,128]{1,0:T(1,128)S(1)}, u32[]{:S(2)}, u32[]{:S(2)}) collective-permute-start(f32[1,128]{1,0:T(1,128)S(1)} %get-tuple-element.45), channel_id=1, source_target_pairs={{0,1},{1,0},{2,3},{3,2},{4,5},{5,4},{6,7},{7,6},{8,9},{9,8},{10,11... | collective-permute-start | bytes 1544 | tf_op jit(solution)/shard_map/ppermute | solution.py:292
  30.6 0.1 collective-permute-done.8.refs_0_
  30.7 0.5 %collective-permute-done.9.refs_1_ = bf16[128,512]{1,0:T(8,128)(2,1)S(1)} collective-permute-done((bf16[128,512]{1,0:T(8,128)(2,1)S(1)}, bf16[128,512]{1,0:T(8,128)(2,1)S(1)}, u32[]{:S(2)}, u32[]{:S(2)}) %collective-permute-start.9) | collective-permute-done | bytes 131104 | tf_op jit(solution)/shard_map/ppermute | solution.py:205
  31.2 0.9 %last.1 = (bf16[128,512]{1,0:T(8,128)(2,1)}, f32[1,128]{1,0:T(1,128)}) custom-call(f32[128,512]{1,0:T(8,128)S(1)} %get-tuple-element.31.kept_ref, bf16[128,512]{1,0:T(8,128)(2,1)S(1)} %collective-permute-done.8.refs_0_, bf16[128,512]{1,0:T(8,128)(2,1)S(1)} %collective-permute-done.9.refs_1_, bf16[128,512]{1,0:T(8,128)(2,1)S(1)} %collective-permute-done.10.refs_2_, ...), custom_call_target="tpu_custom_call" | custom-call | flops 20000000000 | bytes 4096 | tf_op jit(solution)/shard_map/last/pallas_call | solution.py:293
  32.1 0.0 collective-permute-done.14
  32.1 1.8 %collective-permute-done.15 = f32[1,128]{1,0:T(1,128)S(1)} collective-permute-done((f32[1,128]{1,0:T(1,128)S(1)}, f32[1,128]{1,0:T(1,128)S(1)}, u32[]{:S(2)}, u32[]{:S(2)}) %collective-permute-start.15) | collective-permute-done | bytes 544 | tf_op jit(solution)/shard_map/ppermute | solution.py:292
  33.9 0.0 collective-permute-done.16
  33.9 0.5 %add_bitcast_fusion = f32[128]{0:T(128)} fusion(f32[1,128]{1,0:T(1,128)S(1)} %collective-permute-done.15, f32[1,128]{1,0:T(1,128)S(1)} %collective-permute-done.16, f32[1,128]{1,0:T(1,128)S(1)} %get-tuple-element.42, f32[1,128]{1,0:T(1,128)S(1)} %collective-permute-done.14), kind=kLoop, calls=%fused_computation.7 | loop fusion | flops 384 | bytes 2560 | tf_op jit(solution)/shard_map/squeeze | solution.py:307
  (7 shorter events, 0.0 us)
Async XLA Ops:
  0.6 12.6 %slice-start = ((s8[8388608]{0:T(1024)(128)(4,1)}), s8[4194304]{0:T(1024)(128)(4,1)S(1)}, s32[]{:S(2)}) async-start(s8[8388608]{0:T(1024)(128)(4,1)} %bitcast.9), calls=%async_computation | async-start | bytes 8388608
  0.6 12.6 %slice-start.1 = ((s8[8388608]{0:T(1024)(128)(4,1)}), s8[4194304]{0:T(1024)(128)(4,1)S(1)}, s32[]{:S(2)}) async-start(s8[8388608]{0:T(1024)(128)(4,1)} %bitcast.9), calls=%async_computation.1 | async-start | bytes 8388608
  0.7 12.6 %copy-start = (bf16[1,1,256,512]{3,2,1,0:T(8,128)(2,1)S(1)}, bf16[1,1,256,512]{3,2,1,0:T(8,128)(2,1)}, u32[]{:S(2)}) copy-start(bf16[1,1,256,512]{3,2,1,0:T(8,128)(2,1)} %param.9) | copy-start | bytes 786436
  0.7 12.6 %copy-start.1 = (bf16[1,1,256,512]{3,2,1,0:T(8,128)(2,1)S(1)}, bf16[1,1,256,512]{3,2,1,0:T(8,128)(2,1)}, u32[]{:S(2)}) copy-start(bf16[1,1,256,512]{3,2,1,0:T(8,128)(2,1)} %param.10) | copy-start | bytes 786436
  0.7 12.6 %copy-start.2 = (bf16[1,128,512]{2,1,0:T(8,128)(2,1)S(1)}, bf16[1,128,512]{2,1,0:T(8,128)(2,1)}, u32[]{:S(2)}) copy-start(bf16[1,128,512]{2,1,0:T(8,128)(2,1)} %param.6) | copy-start | bytes 393220
  0.7 12.6 %copy-start.3 = (f32[4096]{0:T(1024)S(1)}, f32[4096]{0:T(1024)}, u32[]{:S(2)}) copy-start(f32[4096]{0:T(1024)} %param.7) | copy-start | bytes 49156
  0.7 7.2 %collective-permute-start = (bf16[128,512]{1,0:T(8,128)(2,1)}, bf16[128,512]{1,0:T(8,128)(2,1)S(1)}, u32[]{:S(2)}, u32[]{:S(2)}) collective-permute-start(bf16[128,512]{1,0:T(8,128)(2,1)} %bitcast.15), channel_id=1, source_target_pairs={{0,4},{4,0},{8,12},{12,8},{16,20},{20,16},{24,28},{28,24},{1,5},{5... | collective-permute-start | bytes 393224 | tf_op jit(solution)/shard_map/ppermute | solution.py:205
  3.7 8.0 %collective-permute-start.1 = (bf16[128,512]{1,0:T(8,128)(2,1)}, bf16[128,512]{1,0:T(8,128)(2,1)S(1)}, u32[]{:S(2)}, u32[]{:S(2)}) collective-permute-start(bf16[128,512]{1,0:T(8,128)(2,1)} %bitcast.16), channel_id=1, source_target_pairs={{0,8},{4,12},{8,0},{12,4},{16,24},{20,28},{24,16},{28,20},{1,9},{5... | collective-permute-start | bytes 393224 | tf_op jit(solution)/shard_map/ppermute | solution.py:205
  5.2 6.5 %collective-permute-start.2 = (bf16[128,512]{1,0:T(8,128)(2,1)}, bf16[128,512]{1,0:T(8,128)(2,1)S(1)}, u32[]{:S(2)}, u32[]{:S(2)}) collective-permute-start(bf16[128,512]{1,0:T(8,128)(2,1)} %bitcast.17), channel_id=1, source_target_pairs={{0,12},{4,8},{8,4},{12,0},{16,28},{20,24},{24,20},{28,16},{1,13},{... | collective-permute-start | bytes 393224 | tf_op jit(solution)/shard_map/ppermute | solution.py:205
  5.2 7.6 %collective-permute-start.3 = (bf16[128,512]{1,0:T(8,128)(2,1)}, bf16[128,512]{1,0:T(8,128)(2,1)S(1)}, u32[]{:S(2)}, u32[]{:S(2)}) collective-permute-start(bf16[128,512]{1,0:T(8,128)(2,1)} %bitcast.18), channel_id=1, source_target_pairs={{0,16},{16,0},{1,17},{17,1},{2,18},{18,2},{3,19},{19,3},{4,20},{20... | collective-permute-start | bytes 393224 | tf_op jit(solution)/shard_map/ppermute | solution.py:208
  7.9 4.9 %collective-permute-start.4 = (bf16[128,512]{1,0:T(8,128)(2,1)S(1)}, bf16[128,512]{1,0:T(8,128)(2,1)S(1)}, u32[]{:S(2)}, u32[]{:S(2)}) collective-permute-start(bf16[128,512]{1,0:T(8,128)(2,1)S(1)} %collective-permute-done.refs_1_), channel_id=1, source_target_pairs={{0,16},{16,0},{1,17},{17,1},{2,18},{18,2},{3,19},{19,3},{4,20},{20... | collective-permute-start | bytes 393224 | tf_op jit(solution)/shard_map/ppermute | solution.py:208
  11.7 1.3 %collective-permute-start.5 = (bf16[128,512]{1,0:T(8,128)(2,1)S(1)}, bf16[128,512]{1,0:T(8,128)(2,1)S(1)}, u32[]{:S(2)}, u32[]{:S(2)}) collective-permute-start(bf16[128,512]{1,0:T(8,128)(2,1)S(1)} %collective-permute-done.1.refs_2_), channel_id=1, source_target_pairs={{0,16},{16,0},{1,17},{17,1},{2,18},{18,2},{3,19},{19,3},{4,20},{20... | collective-permute-start | bytes 393224 | tf_op jit(solution)/shard_map/ppermute | solution.py:208
  11.7 1.5 %collective-permute-start.6 = (bf16[128,512]{1,0:T(8,128)(2,1)S(1)}, bf16[128,512]{1,0:T(8,128)(2,1)S(1)}, u32[]{:S(2)}, u32[]{:S(2)}) collective-permute-start(bf16[128,512]{1,0:T(8,128)(2,1)S(1)} %collective-permute-done.2.refs_3_), channel_id=1, source_target_pairs={{0,16},{16,0},{1,17},{17,1},{2,18},{18,2},{3,19},{19,3},{4,20},{20... | collective-permute-start | bytes 393224 | tf_op jit(solution)/shard_map/ppermute | solution.py:208
  16.4 2.0 %collective-permute-start.7 = (bf16[136,2048]{1,0:T(8,128)(2,1)S(1)}, bf16[136,2048]{1,0:T(8,128)(2,1)S(1)}, u32[]{:S(2)}, u32[]{:S(2)}) collective-permute-start(bf16[136,2048]{1,0:T(8,128)(2,1)S(1)} %get-tuple-element.29.sent_ref), channel_id=1, source_target_pairs={{0,16},{16,0},{1,17},{17,1},{2,18},{18,2},{3,19},{19,3},{4,20},{20... | collective-permute-start | bytes 1671176 | tf_op jit(solution)/shard_map/ppermute | solution.py:208
  18.7 6.1 %collective-permute-start.11 = (f32[1,640]{1,0:T(1,128)S(1)}, f32[1,640]{1,0:T(1,128)S(1)}, u32[]{:S(2)}, u32[]{:S(2)}) collective-permute-start(f32[1,640]{1,0:T(1,128)S(1)} %get-tuple-element.37), channel_id=1, source_target_pairs={{0,4},{4,0},{8,12},{12,8},{16,20},{20,16},{24,28},{28,24},{1,5},{5... | collective-permute-start | bytes 7688 | tf_op jit(solution)/shard_map/ppermute | solution.py:205
  19.8 5.9 %collective-permute-start.12 = (f32[1,640]{1,0:T(1,128)S(1)}, f32[1,640]{1,0:T(1,128)S(1)}, u32[]{:S(2)}, u32[]{:S(2)}) collective-permute-start(f32[1,640]{1,0:T(1,128)S(1)} %get-tuple-element.38), channel_id=1, source_target_pairs={{0,8},{4,12},{8,0},{12,4},{16,24},{20,28},{24,16},{28,20},{1,9},{5... | collective-permute-start | bytes 7688 | tf_op jit(solution)/shard_map/ppermute | solution.py:205
  20.8 4.9 %collective-permute-start.13 = (f32[1,640]{1,0:T(1,128)S(1)}, f32[1,640]{1,0:T(1,128)S(1)}, u32[]{:S(2)}, u32[]{:S(2)}) collective-permute-start(f32[1,640]{1,0:T(1,128)S(1)} %get-tuple-element.39), channel_id=1, source_target_pairs={{0,12},{4,8},{8,4},{12,0},{16,28},{20,24},{24,20},{28,16},{1,13},{... | collective-permute-start | bytes 7688 | tf_op jit(solution)/shard_map/ppermute | solution.py:205
  22.2 7.2 %collective-permute-start.10 = (bf16[128,512]{1,0:T(8,128)(2,1)S(1)}, bf16[128,512]{1,0:T(8,128)(2,1)S(1)}, u32[]{:S(2)}, u32[]{:S(2)}) collective-permute-start(bf16[128,512]{1,0:T(8,128)(2,1)S(1)} %get-tuple-element.34), channel_id=1, source_target_pairs={{0,8},{4,12},{8,0},{12,4},{16,24},{20,28},{24,16},{28,20},{1,9},{5... | collective-permute-start | bytes 393224 | tf_op jit(solution)/shard_map/ppermute | solution.py:205
  23.8 7.0 %collective-permute-start.8 = (bf16[128,512]{1,0:T(8,128)(2,1)S(1)}, bf16[128,512]{1,0:T(8,128)(2,1)S(1)}, u32[]{:S(2)}, u32[]{:S(2)}) collective-permute-start(bf16[128,512]{1,0:T(8,128)(2,1)S(1)} %get-tuple-element.32), channel_id=1, source_target_pairs={{0,12},{4,8},{8,4},{12,0},{16,28},{20,24},{24,20},{28,16},{1,13},{... | collective-permute-start | bytes 393224 | tf_op jit(solution)/shard_map/ppermute | solution.py:205
  24.7 6.4 %collective-permute-start.9 = (bf16[128,512]{1,0:T(8,128)(2,1)S(1)}, bf16[128,512]{1,0:T(8,128)(2,1)S(1)}, u32[]{:S(2)}, u32[]{:S(2)}) collective-permute-start(bf16[128,512]{1,0:T(8,128)(2,1)S(1)} %get-tuple-element.33), channel_id=1, source_target_pairs={{0,4},{4,0},{8,12},{12,8},{16,20},{20,16},{24,28},{28,24},{1,5},{5... | collective-permute-start | bytes 393224 | tf_op jit(solution)/shard_map/ppermute | solution.py:205
  25.8 6.3 %collective-permute-start.14 = (f32[1,128]{1,0:T(1,128)S(1)}, f32[1,128]{1,0:T(1,128)S(1)}, u32[]{:S(2)}, u32[]{:S(2)}) collective-permute-start(f32[1,128]{1,0:T(1,128)S(1)} %get-tuple-element.44), channel_id=1, source_target_pairs={{0,3},{1,2},{2,1},{3,0},{4,7},{5,6},{6,5},{7,4},{8,11},{9,10},{10,... | collective-permute-start | bytes 1544 | tf_op jit(solution)/shard_map/ppermute | solution.py:292
  29.5 4.4 %collective-permute-start.15 = (f32[1,128]{1,0:T(1,128)S(1)}, f32[1,128]{1,0:T(1,128)S(1)}, u32[]{:S(2)}, u32[]{:S(2)}) collective-permute-start(f32[1,128]{1,0:T(1,128)S(1)} %get-tuple-element.46), channel_id=1, source_target_pairs={{0,2},{1,3},{2,0},{3,1},{4,6},{5,7},{6,4},{7,5},{8,10},{9,11},{10,... | collective-permute-start | bytes 1544 | tf_op jit(solution)/shard_map/ppermute | solution.py:292
  29.5 4.4 %collective-permute-start.16 = (f32[1,128]{1,0:T(1,128)S(1)}, f32[1,128]{1,0:T(1,128)S(1)}, u32[]{:S(2)}, u32[]{:S(2)}) collective-permute-start(f32[1,128]{1,0:T(1,128)S(1)} %get-tuple-element.45), channel_id=1, source_target_pairs={{0,1},{1,0},{2,3},{3,2},{4,5},{5,4},{6,7},{7,6},{8,9},{9,8},{10,11... | collective-permute-start | bytes 1544 | tf_op jit(solution)/shard_map/ppermute | solution.py:292
